TPU v7x, 128 devices: a whole 4x4x4 slice. The times are simulated.
128 devices in a mesh: qn: 4 (over y), blk: 32 (over z, x, core).
Axes of the slice: x: 4, y: 4, z: 4, core: 2. Of those that a mesh axis runs over, the one named last changes fastest.
Arguments:
- wavefunction: bfloat16 [4096, 256, 256], P(('qn', 'blk')), may hold values from -6 to 6
- pair_left: int32 [4096], P(('qn', 'blk')), may hold values from 0 to 1
- pair_right: int32 [4096], P(('qn', 'blk')), may hold values from 0 to 1
- left_env: bfloat16 [256, 8, 256, 256], P(('qn', 'blk')), may hold values from -0.375 to 0.375
- left_dims: int32 [256], P(('qn', 'blk')), may hold values from 128 to 256, as said below
- right_env: bfloat16 [256, 8, 256, 256], P(('qn', 'blk')), may hold values from -0.125 to 0.125
- right_dims: int32 [256], P(('qn', 'blk')), may hold values from 128 to 256, as said below
Outputs:
- applied: bfloat16 [4096, 256, 256], P(('qn', 'blk'))
Inputs may be any that keep to these rules, and one draw needn't show every extreme that they name: `left_dims`: multiples of 8; the largest entry equals 256. `right_dims`: multiples of 8; the largest entry equals 256.
All inputs are finite; a program needn't handle non-finite values.
Results may differ from a plain program's by a relative error of at most 0.005.
Values may be sent and summed in bfloat16 or wider, within the bound.
No kernel may reach another device: no remote copies, remote signals or barrier semaphores. Data moves between devices by JAX's collectives and lax.ppermute only.
A program may use at most 384 MiB of HBM per device.

v0:
```python
import jax
import jax.numpy as jnp
from jax import lax
from jax.sharding import PartitionSpec as P


def shortened(shard):

    def short(part):
        return part.astype(jnp.bfloat16) if part.dtype == jnp.float32 else part

    return jax.tree.map(short, shard)


def right_combine(terms_flat, sector_pick, environment, live_sizes):
    block_width = terms_flat.shape[-1]
    cols_live = jnp.take(live_sizes, sector_pick, axis=0)
    col_index = lax.broadcasted_iota(jnp.int32, (1, 1, block_width), 2)
    keep = col_index < cols_live[:, None, None]
    running = jnp.zeros((terms_flat.shape[0], block_width, block_width), jnp.float32)
    for term_index in range(terms_flat.shape[1]):
        masked = jnp.where(
            keep, terms_flat[:, term_index], jnp.zeros_like(terms_flat[:, term_index])
        )
        chosen = jnp.take(environment[:, term_index], sector_pick, axis=0)
        running = running + jnp.einsum(
            "sij,sjk->sik", masked, chosen, preferred_element_type=jnp.float32
        )
    return running


def body(wavefunction, pair_left, pair_right, left_env, left_dims, right_env, right_dims):
    group_count = lax.axis_size("qn")
    block_count = lax.axis_size("blk")
    slot_count = wavefunction.shape[0]
    block_width = wavefunction.shape[1]
    per_group = slot_count // group_count
    per_peer = slot_count // block_count
    term_count = left_env.shape[1]
    blocks = lax.all_to_all(
        wavefunction.reshape(group_count, per_group, block_width, block_width),
        "qn",
        split_axis=0,
        concat_axis=0,
        tiled=True,
    )
    left_pick = lax.all_to_all(
        pair_left.reshape(group_count, per_group), "qn", split_axis=0, concat_axis=0, tiled=True
    )
    right_pick = lax.all_to_all(
        pair_right.reshape(group_count, per_group), "qn", split_axis=0, concat_axis=0, tiled=True
    )
    leading = blocks.shape[:2]
    flattened = blocks.reshape((-1, block_width, block_width))
    sector_pick = left_pick.reshape(-1)
    rows_live = jnp.take(left_dims, sector_pick, axis=0)
    row_index = lax.broadcasted_iota(jnp.int32, (1, block_width, 1), 1)
    masked = jnp.where(row_index < rows_live[:, None, None], flattened, jnp.zeros_like(flattened))
    products_list = []
    for term_index in range(term_count):
        chosen = jnp.take(left_env[:, term_index], sector_pick, axis=0)
        product = jnp.einsum("sij,sjk->sik", chosen, masked, preferred_element_type=jnp.float32)
        products_list.append(product.astype(jnp.bfloat16))
    stacked = jnp.stack(products_list, axis=1)
    routed_terms = stacked.reshape(leading + (term_count, block_width, block_width))
    routed_pick = right_pick
    terms_flat = routed_terms.reshape(slot_count, term_count, block_width, block_width)
    right_pick = routed_pick.reshape(slot_count)
    terms_in = lax.all_to_all(
        terms_flat.reshape(block_count, per_peer, term_count, block_width, block_width),
        "blk",
        split_axis=0,
        concat_axis=0,
        tiled=True,
    )
    pick_in = lax.all_to_all(
        shortened(right_pick.reshape(block_count, per_peer)),
        "blk",
        split_axis=0,
        concat_axis=0,
        tiled=True,
    )
    leading = terms_in.shape[:2]
    flattened = terms_in.reshape((-1, term_count, block_width, block_width))
    running = right_combine(flattened, pick_in.reshape(-1), right_env, right_dims)
    finished = running.astype(jnp.bfloat16).reshape(leading + (block_width, block_width))
    return finished.reshape(slot_count, block_width, block_width)


def solution(mesh):
    return jax.shard_map(
        body,
        mesh=mesh,
        in_specs=(
            P(("qn", "blk"), None, None),
            P(("qn", "blk")),
            P(("qn", "blk")),
            P(("qn", "blk"), None, None, None),
            P(("qn", "blk")),
            P(("qn", "blk"), None, None, None),
            P(("qn", "blk")),
        ),
        out_specs=P(("qn", "blk"), None, None),
        check_vma=False,
    )
```

profile of v0, /device:TPU:0, one launch (start us, length us, event | category | flops | bytes accessed | tf_op | source)
XLA Modules:
  0.0 652.5 jit_solution(17090352079171606391)
XLA Ops:
  0.0 1.3 all_to_all.28
  1.3 4.5 all-to-all-start.2
  5.9 0.7 all_to_all.24
  6.6 4.4 all-to-all-done.2
  11.0 7.6 %all_to_all.38 = s32[4,1,8]{2,1,0:T(1,128)S(1)} all-to-all(s32[4,1,8]{2,1,0:T(1,128)S(1)} %bitcast.125), channel_id=1, replica_groups=mesh['qn'=4,'blk'=32] {'qn'}, dimensions={0} | all-to-all | bytes 256 | tf_op jit(solution)/shard_map/all_to_all | solution.py:50
  18.6 5.0 all-to-all-start.3
  24.2 1.6 slice_bitcast_fusion.16
  27.2 1.3 compare_select_fusion
  28.6 2.8 gather_fusion
  31.4 2.7 gather_fusion.1
  34.2 2.8 gather_fusion.2
  37.0 2.9 gather_fusion.3
  39.8 2.8 gather_fusion.4
  42.6 2.7 gather_fusion.5
  45.3 2.8 gather_fusion.6
  48.1 2.9 gather_fusion.7
  52.5 17.7 %all-to-all-done.3 = bf16[4,8,256,256]{3,2,1,0:T(8,128)(2,1)} async-done(((bf16[4,8,256,256]{3,2,1,0:T(8,128)(2,1)}), bf16[4,8,256,256]{3,2,1,0:T(8,128)(2,1)}, u32[]{:S(2)}, u32[]{:S(2)}) %all-to-all-start.3) | async-done | bytes 4194336 | tf_op jit(solution)/shard_map/all_to_all | solution.py:40
  70.2 8.3 %all-to-all-start.1 = ((s32[32,1,1]{2,1,0:T(1,128)}), s32[32,1,1]{2,1,0:T(1,128)S(1)}, u32[]{:S(2)}, u32[]{:S(2)}) async-start(s32[32,1,1]{2,1,0:T(1,128)} %all_to_all.32), calls=%async_computation.1 | async-start | bytes 32768 | tf_op jit(solution)/shard_map/all_to_all | solution.py:76
  78.6 3.8 bitcast_select_fusion
  82.4 3.3 bitcast_dynamic-update-slice_fusion.7
  85.7 3.3 bitcast_dynamic-update-slice_fusion.6
  89.0 3.3 bitcast_dynamic-update-slice_fusion.5
  92.3 3.3 bitcast_dynamic-update-slice_fusion.4
  95.6 3.3 bitcast_dynamic-update-slice_fusion.3
  98.8 3.3 bitcast_dynamic-update-slice_fusion.2
  102.1 3.3 bitcast_dynamic-update-slice_fusion.1
  105.4 3.3 bitcast_dynamic-update-slice_fusion
  108.7 23.0 %copy.22 = bf16[32,1,8,256,256]{4,3,2,1,0:T(8,128)(2,1)} copy(bf16[32,1,8,256,256]{4,3,0,2,1:T(8,128)(2,1)} %bitcast.123) | data formatting | bytes 67108864 | tf_op jit(solution)/shard_map/reshape;reshape;reshape | solution.py:70
  131.7 7.6 %all-to-all-start.4 = ((bf16[32,1,8,256,256]{4,3,2,1,0:T(8,128)(2,1)}), bf16[32,1,8,256,256]{4,3,2,1,0:T(8,128)(2,1)}, u32[]{:S(2)}, u32[]{:S(2)}) async-start(bf16[32,1,8,256,256]{4,3,2,1,0:T(8,128)(2,1)} %copy.22), calls=%async_computation.4 | async-start | bytes 67108864 | tf_op jit(solution)/shard_map/all_to_all | solution.py:69
  139.8 1.6 slice_bitcast_fusion.15
  142.1 1.3 fusion.116
  143.4 2.8 gather_fusion.12
  146.3 2.8 gather_fusion.11
  149.0 2.8 gather_fusion.10
  151.8 2.8 gather_fusion.9
  154.6 2.8 gather_fusion.14
  157.4 2.8 gather_fusion.13
  160.2 2.8 gather_fusion.15
  163.0 2.8 gather_fusion.8
  165.9 412.8 %all-to-all-done.4 = bf16[32,1,8,256,256]{4,3,2,1,0:T(8,128)(2,1)} async-done(((bf16[32,1,8,256,256]{4,3,2,1,0:T(8,128)(2,1)}), bf16[32,1,8,256,256]{4,3,2,1,0:T(8,128)(2,1)}, u32[]{:S(2)}, u32[]{:S(2)}) %all-to-all-start.4) | async-done | bytes 33554464 | tf_op jit(solution)/shard_map/all_to_all | solution.py:69
  578.6 8.2 %fusion.10 = f32[32,256,256]{2,1,0:T(8,128)} fusion(bf16[32,8,256,256]{3,2,1,0:T(8,128)(2,1)} %bitcast.25, bf16[32,256,256]{2,1,0:T(8,128)(2,1)} %gather_fusion.12, pred[32]{0:T(512)(128)(4,1)S(1)} %compare_and_fusion.1, pred[32,256]{1,0:T(8,128)(4,1)S(1)} %iota_compare_fusion.1), kind=kOutput, calls=%fused_computation.28 | convolution fusion | flops 1077936128 | bytes 16785440 | tf_op jit(solution)/shard_map/sij,sjk->sik/dot_general | solution.py:26
  586.9 6.9 %fusion.13 = f32[32,256,256]{2,1,0:T(8,128)} fusion(bf16[32,8,256,256]{3,2,1,0:T(8,128)(2,1)} %bitcast.25, bf16[32,256,256]{2,1,0:T(8,128)(2,1)S(1)} %copy-done.8, pred[32]{0:T(512)(128)(4,1)S(1)} %compare_and_fusion.1, pred[32,256]{1,0:T(8,128)(4,1)S(1)} %iota_compare_fusion.1), kind=kOutput, calls=%fused_computation.31 | convolution fusion | flops 1077936128 | bytes 16785440 | tf_op jit(solution)/shard_map/sij,sjk->sik/dot_general | solution.py:26
  593.8 7.0 %fusion.16 = f32[32,256,256]{2,1,0:T(8,128)} fusion(bf16[32,8,256,256]{3,2,1,0:T(8,128)(2,1)} %bitcast.25, bf16[32,256,256]{2,1,0:T(8,128)(2,1)S(1)} %copy-done.9, pred[32]{0:T(512)(128)(4,1)S(1)} %compare_and_fusion.1, pred[32,256]{1,0:T(8,128)(4,1)S(1)} %iota_compare_fusion.1), kind=kOutput, calls=%fused_computation.34 | convolution fusion | flops 1077936128 | bytes 16785440 | tf_op jit(solution)/shard_map/sij,sjk->sik/dot_general | solution.py:26
  600.8 6.9 %fusion.19 = f32[32,256,256]{2,1,0:T(8,128)} fusion(bf16[32,8,256,256]{3,2,1,0:T(8,128)(2,1)} %bitcast.25, bf16[32,256,256]{2,1,0:T(8,128)(2,1)S(1)} %copy-done.10, pred[32]{0:T(512)(128)(4,1)S(1)} %compare_and_fusion.1, pred[32,256]{1,0:T(8,128)(4,1)S(1)} %iota_compare_fusion.1), kind=kOutput, calls=%fused_computation.37 | convolution fusion | flops 1077936128 | bytes 16785440 | tf_op jit(solution)/shard_map/sij,sjk->sik/dot_general | solution.py:26
  607.7 6.9 %fusion.4 = f32[32,256,256]{2,1,0:T(8,128)} fusion(bf16[32,8,256,256]{3,2,1,0:T(8,128)(2,1)} %bitcast.25, bf16[32,256,256]{2,1,0:T(8,128)(2,1)S(1)} %copy-done.11, pred[32]{0:T(512)(128)(4,1)S(1)} %compare_and_fusion.1, pred[32,256]{1,0:T(8,128)(4,1)S(1)} %iota_compare_fusion.1), kind=kOutput, calls=%fused_computation.22 | convolution fusion | flops 1077936128 | bytes 16785440 | tf_op jit(solution)/shard_map/sij,sjk->sik/dot_general | solution.py:26
  614.6 6.9 %fusion.7 = f32[32,256,256]{2,1,0:T(8,128)} fusion(bf16[32,8,256,256]{3,2,1,0:T(8,128)(2,1)} %bitcast.25, bf16[32,256,256]{2,1,0:T(8,128)(2,1)S(1)} %copy-done.12, pred[32]{0:T(512)(128)(4,1)S(1)} %compare_and_fusion.1, pred[32,256]{1,0:T(8,128)(4,1)S(1)} %iota_compare_fusion.1), kind=kOutput, calls=%fused_computation.25 | convolution fusion | flops 1077936128 | bytes 16785440 | tf_op jit(solution)/shard_map/sij,sjk->sik/dot_general | solution.py:26
  621.6 6.9 %fusion.1 = f32[32,256,256]{2,1,0:T(8,128)} fusion(bf16[32,8,256,256]{3,2,1,0:T(8,128)(2,1)} %bitcast.25, bf16[32,256,256]{2,1,0:T(8,128)(2,1)S(1)} %copy-done.13, pred[32]{0:T(512)(128)(4,1)S(1)} %compare_and_fusion.1, pred[32,256]{1,0:T(8,128)(4,1)S(1)} %iota_compare_fusion.1), kind=kOutput, calls=%fused_computation.19 | convolution fusion | flops 1077936128 | bytes 16785440 | tf_op jit(solution)/shard_map/sij,sjk->sik/dot_general | solution.py:26
  628.4 24.1 %add_convert_fusion = bf16[32,256,256]{2,1,0:T(8,128)(2,1)} fusion(f32[32,256,256]{2,1,0:T(8,128)} %fusion.1, f32[32,256,256]{2,1,0:T(8,128)} %fusion.4, f32[32,256,256]{2,1,0:T(8,128)} %fusion.7, f32[32,256,256]{2,1,0:T(8,128)} %fusion.10, f32[32,256,256]{2,1,0:T(8,128)} %fusion.13, f32[32,256,256]{2,1,0:T(8,128)} %fusion.16, f32[32,256,256]{2,1,0:T(8,128)} %fusion.19, ...), kind=kOutput, calls=%fused_computation.16 | convolution fusion | flops 1094713344 | bytes 71311392 | tf_op jit(solution)/shard_map/sij,sjk->sik/dot_general | solution.py:26
  (47 shorter events, 4.8 us)
Async XLA Ops:
  1.3 9.7 %all-to-all-start.2 = ((s32[4,1,8]{2,1,0:T(1,128)}), s32[4,1,8]{2,1,0:T(1,128)S(1)}, u32[]{:S(2)}, u32[]{:S(2)}) async-start(s32[4,1,8]{2,1,0:T(1,128)} %bitcast.3), calls=%async_computation.2 | async-start | bytes 4096 | tf_op jit(solution)/shard_map/all_to_all | solution.py:47
  18.6 5.0 copy-start.14
  18.6 51.6 %all-to-all-start.3 = ((bf16[4,8,256,256]{3,2,1,0:T(8,128)(2,1)}), bf16[4,8,256,256]{3,2,1,0:T(8,128)(2,1)}, u32[]{:S(2)}, u32[]{:S(2)}) async-start(bf16[4,8,256,256]{3,2,1,0:T(8,128)(2,1)} %bitcast.124), calls=%async_computation.3 | async-start | bytes 8388608 | tf_op jit(solution)/shard_map/all_to_all | solution.py:40
  70.2 61.5 %all-to-all-start.1 = ((s32[32,1,1]{2,1,0:T(1,128)}), s32[32,1,1]{2,1,0:T(1,128)S(1)}, u32[]{:S(2)}, u32[]{:S(2)}) async-start(s32[32,1,1]{2,1,0:T(1,128)} %all_to_all.32), calls=%async_computation.1 | async-start | bytes 32768 | tf_op jit(solution)/shard_map/all_to_all | solution.py:76
  78.5 3.9 copy-start.6
  82.4 3.3 copy-start.7
  85.7 3.3 copy-start.5
  89.0 3.3 copy-start.4
  92.3 3.3 copy-start.3
  95.6 3.3 copy-start.2
  98.8 3.3 copy-start
  102.1 3.3 copy-start.1
  131.7 7.6 %copy-start.15 = (s32[2]{0:T(128)S(1)}, s32[2]{0:T(128)}, u32[]{:S(2)}) copy-start(s32[2]{0:T(128)} %param.17) | copy-start | bytes 28
  131.7 447.0 %all-to-all-start.4 = ((bf16[32,1,8,256,256]{4,3,2,1,0:T(8,128)(2,1)}), bf16[32,1,8,256,256]{4,3,2,1,0:T(8,128)(2,1)}, u32[]{:S(2)}, u32[]{:S(2)}) async-start(bf16[32,1,8,256,256]{4,3,2,1,0:T(8,128)(2,1)} %copy.22), calls=%async_computation.4 | async-start | bytes 67108864 | tf_op jit(solution)/shard_map/all_to_all | solution.py:69
  578.6 8.2 %copy-start.8 = (bf16[32,256,256]{2,1,0:T(8,128)(2,1)S(1)}, bf16[32,256,256]{2,1,0:T(8,128)(2,1)}, u32[]{:S(2)}) copy-start(bf16[32,256,256]{2,1,0:T(8,128)(2,1)} %gather_fusion.11) | copy-start | bytes 12582916
  586.9 6.9 %copy-start.9 = (bf16[32,256,256]{2,1,0:T(8,128)(2,1)S(1)}, bf16[32,256,256]{2,1,0:T(8,128)(2,1)}, u32[]{:S(2)}) copy-start(bf16[32,256,256]{2,1,0:T(8,128)(2,1)} %gather_fusion.10) | copy-start | bytes 12582916
  593.8 7.0 %copy-start.10 = (bf16[32,256,256]{2,1,0:T(8,128)(2,1)S(1)}, bf16[32,256,256]{2,1,0:T(8,128)(2,1)}, u32[]{:S(2)}) copy-start(bf16[32,256,256]{2,1,0:T(8,128)(2,1)} %gather_fusion.9) | copy-start | bytes 12582916
  600.8 6.9 %copy-start.11 = (bf16[32,256,256]{2,1,0:T(8,128)(2,1)S(1)}, bf16[32,256,256]{2,1,0:T(8,128)(2,1)}, u32[]{:S(2)}) copy-start(bf16[32,256,256]{2,1,0:T(8,128)(2,1)} %gather_fusion.14) | copy-start | bytes 12582916
  607.7 6.9 %copy-start.12 = (bf16[32,256,256]{2,1,0:T(8,128)(2,1)S(1)}, bf16[32,256,256]{2,1,0:T(8,128)(2,1)}, u32[]{:S(2)}) copy-start(bf16[32,256,256]{2,1,0:T(8,128)(2,1)} %gather_fusion.13) | copy-start | bytes 12582916
  614.6 6.9 %copy-start.13 = (bf16[32,256,256]{2,1,0:T(8,128)(2,1)S(1)}, bf16[32,256,256]{2,1,0:T(8,128)(2,1)}, u32[]{:S(2)}) copy-start(bf16[32,256,256]{2,1,0:T(8,128)(2,1)} %gather_fusion.15) | copy-start | bytes 12582916
where the time goes:
time: 653 us
  waiting for transfers between devices  435 us (67%)
  matrix products  100 us (15%)
  local copies, waits for them, and re-layouts  75.7 us (12%)
  starting transfers between devices  25.5 us (4%)
  other arithmetic  8.67 us (1%)
  blocking collectives  7.58 us (1%)
    all_to_all x1, waiting for transfers between devices, body(): lax.all_to_all(terms_flat.reshape(block_count, per_peer, term_count, bloc...  413 us
    dot_general x8, matrix products, right_combine(): jnp.einsum('sij,sjk->sik', masked, chosen, preferred_element_type=jnp.flo...  73.9 us
    dot_general x8, matrix products, body(): jnp.einsum('sij,sjk->sik', chosen, masked, preferred_element_type=jnp.flo...  26.2 us
    another operation x1, local copies, waits for them, and re-layouts, body(): terms_flat.reshape(block_count, per_peer, term_count, block_width, block_...  23 us
    gather x8, local copies, waits for them, and re-layouts, body(): chosen = jnp.take(left_env[:, term_index], sector_pick, axis=0)  22.4 us
    gather x8, local copies, waits for them, and re-layouts, right_combine(): chosen = jnp.take(environment[:, term_index], sector_pick, axis=0)  22.3 us
    all_to_all x1, waiting for transfers between devices, body(): lax.all_to_all(wavefunction.reshape(group_count, per_group, block_width,...  17.7 us
  transfers between devices with their start and end apart: 4, of which 3 were waited for; matrix products, arithmetic and copies ran while one was open for 17% of the time, Pallas kernels for 0%

commit v1 on v0

v1 whole, which is shorter than its diff:
```python
import jax
import jax.numpy as jnp
import numpy as np
from jax import lax
from jax.experimental import pallas as pl
from jax.experimental.pallas import tpu as pltpu
from jax.sharding import Mesh, PartitionSpec as P

AXES = ("y", "z", "x", "c")
OFFSETS = (0, 3, 1, 2)
BF16 = jnp.bfloat16


def ring_positions():
    rows = []
    for y, z, x, c in np.ndindex(4, 4, 4, 2):
        rows.append([(z + o) % 4 for o in OFFSETS] + [(x + o) % 4 for o in OFFSETS] + [y, z, x, c])
    return np.asarray(rows, np.int32)


def exchange(array, axis):
    return lax.all_to_all(array, axis, split_axis=0, concat_axis=0, tiled=True)


def shift(array, axis, step, size=4):
    return lax.ppermute(array, axis, [(i, (i + step) % size) for i in range(size)])


def both_ways(array, axis):
    return shift(array, axis, 1), shift(array, axis, 3)


def onward(from_low, from_high, axis):
    half = from_low.shape[1] // 2
    return shift(from_low[:, :half], axis, 1), shift(from_high[:, half:], axis, 3)


def combine(where, meta, psi, lefts, rights, first):
    width = psi.shape[-1]
    depth = sum(a.shape[1] for a in lefts[0])
    terms = depth // width
    count = len(lefts)
    left_parts = [a for group in lefts for a in group]
    right_parts = [a for group in rights for a in group]

    def place(i, where):
        source, k = i // count, i % count
        g = where[source // 2]
        c_r = where[11] ^ (source % 2)
        x_j = where[4 + first + k]
        return g, c_r, x_j, k

    def picks(i, where, meta):
        g, c_r, x_j, k = place(i, where)
        y, z, x, c = where[8], where[9], where[10], where[11]
        sender = ((g * 4 + z) * 4 + x_j) * 2 + c
        slot = y * 8 + x * 2 + c_r
        left = meta[sender * 128 + slot]
        right = meta[sender * 128 + 32 + slot]
        rows = meta[(((y * 4 + z) * 4 + x_j) * 2 + c) * 128 + 64 + left]
        cols = meta[(((y * 4 + g) * 4 + x) * 2 + c_r) * 128 + 66 + right]
        return left, right, rows, cols

    def psi_index(i, where, meta):
        g, c_r, x_j, k = place(i, where)
        return (g * 4 + x_j) * 2 + c_r, 0, 0

    def out_index(i, where, meta):
        g, c_r, x_j, k = place(i, where)
        return (g * 2 + c_r) * count + k, 0, 0

    def kernel(where, meta, psi_ref, *refs):
        left_refs = refs[: len(left_parts)]
        right_refs = refs[len(left_parts) : len(left_parts) + len(right_parts)]
        out_ref, right_buf, partial, sems = refs[len(left_parts) + len(right_parts) :]
        i = pl.program_id(0)
        steps = pl.num_programs(0)

        def fetch(step, go):
            _, right, _, _ = picks(step, where, meta)
            slot = lax.rem(step, 2)
            at = 0
            for source, group in enumerate(rights):

                @pl.when(step // count == source)
                def _(at=at, group=group):
                    row = 0
                    for n in range(len(group)):
                        size = group[n].shape[1]
                        copy = pltpu.make_async_copy(
                            right_refs[at + n].at[right],
                            right_buf.at[slot, pl.ds(row, size)],
                            sems.at[slot, n],
                        )
                        copy.start() if go else copy.wait()
                        row += size

                at += len(group)

        @pl.when(i == 0)
        def _():
            fetch(i, True)

        @pl.when(i + 1 < steps)
        def _():
            fetch(i + 1, True)

        left, _, rows, cols = picks(i, where, meta)
        keep = (lax.broadcasted_iota(jnp.int32, (width, width), 0) < rows) & (
            lax.broadcasted_iota(jnp.int32, (width, width), 1) < cols
        )
        masked = jnp.where(keep, psi_ref[0].astype(jnp.float32), 0.0).astype(BF16)

        def first_half(group):
            t = 0
            for ref in group:
                for n in range(ref.shape[1] // width):
                    block = ref[left, pl.ds(n * width, width)]
                    product = jnp.dot(block, masked, preferred_element_type=jnp.float32)
                    partial[:, t * width : (t + 1) * width] = product.astype(BF16)
                    t += 1

        at = 0
        for k, group in enumerate(lefts):
            here = left_refs[at : at + len(group)]
            at += len(group)
            if count == 1:
                first_half(here)
            else:
                pl.when(i % count == k)(lambda here=here: first_half(here))

        fetch(i, False)
        total = jnp.dot(partial[...], right_buf[lax.rem(i, 2)], preferred_element_type=jnp.float32)
        out_ref[0] = total.astype(BF16)

    blocks = 2 * 4 * count
    whole = lambda i, where, meta: (0, 0, 0)
    parts = max(len(group) for group in rights)
    moved = blocks * (depth * width * 2 + 2 * width * width * 2) + count * 2 * depth * width * 2
    return pl.pallas_call(
        kernel,
        out_shape=jax.ShapeDtypeStruct((blocks, width, width), BF16),
        grid_spec=pltpu.PrefetchScalarGridSpec(
            num_scalar_prefetch=2,
            grid=(blocks,),
            in_specs=[pl.BlockSpec((1, width, width), psi_index)]
            + [pl.BlockSpec(a.shape, whole) for a in left_parts]
            + [pl.BlockSpec(memory_space=pl.ANY) for _ in right_parts],
            out_specs=pl.BlockSpec((1, width, width), out_index),
            scratch_shapes=[
                pltpu.VMEM((2, depth, width), BF16),
                pltpu.VMEM((width, depth), BF16),
                pltpu.SemaphoreType.DMA((2, parts)),
            ],
        ),
        compiler_params=pltpu.CompilerParams(
            dimension_semantics=("arbitrary",), vmem_limit_bytes=32 * 2**20
        ),
        cost_estimate=pl.CostEstimate(
            flops=blocks * terms * 4 * width**3, bytes_accessed=moved, transcendentals=0
        ),
        name=f"combine_{first}",
    )(where, meta, psi, *left_parts, *right_parts)


def after(array, *others):
    return lax.optimization_barrier((array, *others))[0]


def body(wavefunction, pair_left, pair_right, left_env, left_dims, right_env, right_dims):
    width = wavefunction.shape[-1]
    sectors, terms = left_env.shape[:2]
    me = lax.axis_index(AXES)
    where = lax.dynamic_index_in_dim(jnp.asarray(ring_positions()), me, 0, keepdims=False)
    mine = jnp.concatenate([pair_left, pair_right, left_dims, right_dims])
    mine = jnp.pad(mine, (0, 128 - mine.shape[0]))
    meta = lax.all_gather(mine, AXES, axis=0, tiled=True)

    left_own = left_env.reshape(sectors, terms * width, width)
    right_own = right_env.reshape(sectors, terms * width, width)
    psi = exchange(wavefunction, ("y", "x"))

    right_low, right_high = both_ways(right_own, "z")
    far = onward(right_low, right_high, "z")
    rights = []
    for group in ((right_own,), (right_low,), (right_high,), far):
        rights.append(group)
        rights.append(tuple(shift(a, "c", 1, 2) for a in group))

    left_low, left_high = both_ways(after(left_own, psi), "x")
    left_far = onward(left_low, left_high, "x")

    def home(first, lefts):
        out = combine(where, meta, psi, lefts, rights, first)
        out = exchange(out, ("z", "c"))
        return out.reshape(4, 2, len(lefts), width, width)

    own = home(0, [(left_own,)])
    near = home(1, [(left_low,), (left_high,)])
    opposite = home(3, [left_far])

    applied = jnp.zeros((4, 4, 2, width, width), BF16)
    for position, piece in ((0, own[:, :, 0]), (1, near[:, :, 0]), (2, near[:, :, 1]), (3, opposite[:, :, 0])):
        applied = lax.dynamic_update_slice(
            applied, piece[:, None], (0, where[4 + position], 0, 0, 0)
        )
    return applied.reshape(wavefunction.shape)


def solution(mesh):
    fine = Mesh(mesh.devices.reshape(4, 4, 4, 2), AXES)
    return jax.shard_map(
        body, mesh=fine, in_specs=P(AXES), out_specs=P(AXES), check_vma=False
    )
```

time: 653 us -> 279 us (0.43)
  waiting for transfers between devices: 435 us -> 88.1 us
  matrix products: 100 us -> 0 us
  blocking collectives: 7.58 us -> 70.4 us
  local copies, waits for them, and re-layouts: 75.7 us -> 22.8 us
  Pallas kernels: 0 us -> 51.9 us
  starting transfers between devices: 25.5 us -> 35.7 us
  other arithmetic: 8.67 us -> 0.08 us
  between operations: 0.15 us -> 7.63 us
    all_to_all x4, waiting for transfers between devices: 435 us -> 0.01 us  [exchange(): return lax.all_to_all(array, axis, split_axis=0, concat_axis=0, tiled=True)]
    dot_general x16 -> x0, matrix products: 100 us -> none  [the longest x8 73.9 us: right_combine(): jnp.einsum('sij,sjk->sik', masked, chosen, preferred_element_type=jnp.flo...]
    ppermute x0 -> x13, waiting for transfers between devices: none -> 88.1 us  [shift(): lax.ppermute(array, axis, [(i, (i + step) % size) for i in range(size)])]
    all_gather x0 -> x1, blocking collectives: none -> 70.4 us  [body(): meta = lax.all_gather(mine, AXES, axis=0, tiled=True)]
    pallas_call x0 -> x3, Pallas kernels: none -> 51.9 us  [combine(): pl.pallas_call(kernel, out_shape=jax.ShapeDtypeStruct((blocks, width, wid...]
    gather x18 -> x0, local copies, waits for them, and re-layouts: 45.9 us -> none  [the longest x8 22.4 us: body(): chosen = jnp.take(left_env[:, term_index], sector_pick, axis=0)]
    another operation x1 -> x0, local copies, waits for them, and re-layouts: 23 us -> none  [body(): terms_flat.reshape(block_count, per_peer, term_count, block_width, block_...]
    ppermute x0 -> x13, starting transfers between devices: none -> 15.2 us  [shift(): lax.ppermute(array, axis, [(i, (i + step) % size) for i in range(size)])]
  transfers between devices with their start and end apart: 4 -> 17, of which waited for: 3 -> 4; matrix products, arithmetic and copies ran while one was open for 17% -> 6% of each run, Pallas kernels for 0% -> 19%
where the time goes in v1:
time: 279 us; the launch traced here: 277 us
  waiting for transfers between devices  88.1 us (32%)
  blocking collectives  70.4 us (25%)
  Pallas kernels  51.9 us (19%)
  starting transfers between devices  35.7 us (13%)
  local copies, waits for them, and re-layouts  22.8 us (8%)
  between operations  7.63 us (3%)
    ppermute x13, waiting for transfers between devices, shift(): lax.ppermute(array, axis, [(i, (i + step) % size) for i in range(size)])  88.1 us
    all_gather x1, blocking collectives, body(): meta = lax.all_gather(mine, AXES, axis=0, tiled=True)  70.4 us
    pallas_call x3, Pallas kernels, combine(): pl.pallas_call(kernel, out_shape=jax.ShapeDtypeStruct((blocks, width, wid...  51.9 us
    all_to_all x4, starting transfers between devices, exchange(): return lax.all_to_all(array, axis, split_axis=0, concat_axis=0, tiled=True)  20.6 us
    ppermute x13, starting transfers between devices, shift(): lax.ppermute(array, axis, [(i, (i + step) % size) for i in range(size)])  15.2 us
    dynamic_update_slice x4, local copies, waits for them, and re-layouts, body(): lax.dynamic_update_slice(applied, piece[:, None], (0, where[4 + position]...  7.82 us
    unnamed x19, local copies, waits for them, and re-layouts  6.11 us
  transfers between devices with their start and end apart: 17, of which 4 were waited for; matrix products, arithmetic and copies ran while one was open for 6% of the time, Pallas kernels for 19%

profile of v1, /device:TPU:0, one launch (start us, length us, event | category | flops | bytes accessed | tf_op | source)
XLA Modules:
  0.0 276.7 jit_solution(3151073575863708653)
XLA Ops:
  0.0 7.2 %all-to-all-start = ((bf16[32,256,256]{2,1,0:T(8,128)(2,1)}), bf16[32,256,256]{2,1,0:T(8,128)(2,1)}, u32[]{:S(2)}, u32[]{:S(2)}) async-start(bf16[32,256,256]{2,1,0:T(8,128)(2,1)} %param.8), calls=%async_computation | async-start | bytes 8388608 | tf_op jit(solution)/shard_map/all_to_all | solution.py:22
  7.2 0.0 copy-start.5
  7.2 0.0 copy-start.6
  7.2 0.0 copy-start.7
  7.2 0.0 copy-start.8
  7.2 2.0 collective-permute-start.1
  9.2 2.2 collective-permute-start.3
  11.4 0.0 collective-permute-start
  11.4 45.5 %collective-permute-done.1.refs_3_.refs_4_ = bf16[2,2048,256]{2,1,0:T(8,128)(2,1)S(1)} collective-permute-done((bf16[2,2048,256]{2,1,0:T(8,128)(2,1)}, bf16[2,2048,256]{2,1,0:T(8,128)(2,1)S(1)}, u32[]{:S(2)}, u32[]{:S(2)}) %collective-permute-start.1) | collective-permute-done | bytes 2097184 | tf_op jit(solution)/shard_map/ppermute | solution.py:26
  56.9 0.1 slice.44
  57.0 0.1 collective-permute-start.5
  57.0 0.0 collective-permute-done.3.refs_5_.refs_6_
  57.1 2.3 slice.45
  59.3 3.2 %collective-permute-start.6 = (bf16[2,1024,256]{2,1,0:T(8,128)(2,1)}, bf16[2,1024,256]{2,1,0:T(8,128)(2,1)}, u32[]{:S(2)}, u32[]{:S(2)}) collective-permute-start(bf16[2,1024,256]{2,1,0:T(8,128)(2,1)} %slice.45), channel_id=1, source_target_pairs={{0,24},{8,0},{16,8},{24,16},{1,25},{9,1},{17,9},{25,17},{2,26},{10... | collective-permute-start | bytes 3145736 | tf_op jit(solution)/shard_map/ppermute | solution.py:26
  62.5 19.8 %collective-permute-done.5.refs_7_.refs_8_ = bf16[2,1024,256]{2,1,0:T(8,128)(2,1)S(1)} collective-permute-done((bf16[2,1024,256]{2,1,0:T(8,128)(2,1)S(1)}, bf16[2,1024,256]{2,1,0:T(8,128)(2,1)S(1)}, u32[]{:S(2)}, u32[]{:S(2)}) %collective-permute-start.5) | collective-permute-done | bytes 1048608 | tf_op jit(solution)/shard_map/ppermute | solution.py:26
  82.4 0.0 collective-permute-start.7
  82.4 0.5 collective-permute-start.2
  82.9 0.0 collective-permute-start.4
  82.9 1.3 collective-permute-start.9
  84.2 2.5 collective-permute-start.10
  86.8 0.1 pad_add_fusion
  86.8 70.4 %all-gather = s32[128,1,128]{2,1,0:T(1,128)S(1)} all-gather(s32[1,1,128]{2,1,0:T(1,128)S(1)} %pad_bitcast_fusion), channel_id=1, replica_groups=mesh['y'=4,'z'=4,'x'=4,'c'=2] {'y','z','x','c'}, dimensions={0}, use_global_device_ids=true | all-gather | bytes 66048 | tf_op jit(solution)/shard_map/all_gather | solution.py:177
  157.2 0.7 constant_dynamic-slice_fusion
  157.9 0.0 copy-start
  157.9 1.6 copy-done
  159.5 1.6 copy-done.4
  161.1 15.4 %combine_0.1 = bf16[8,256,256]{2,1,0:T(8,128)(2,1)} custom-call(s32[12]{0:T(128)S(1)} %get-tuple-element.8.where, s32[16384]{0:T(1024)S(1)} %bitcast.40, bf16[32,256,256]{2,1,0:T(8,128)(2,1)} %all-to-all-done.psi_ref, bf16[2,2048,256]{2,1,0:T(8,128)(2,1)S(1)} %bitcast.39, bf16[2,2048,256]{2,1,0:T(8,128)(2,1)S(1)} %bitcast.34, ...), custom_call_target="tpu_custom_call" | custom-call | flops 4294967296 | bytes 12582912 | tf_op jit(solution)/shard_map/combine_0/pallas_call | solution.py:140
  176.5 4.2 %all-to-all-start.1 = ((bf16[8,256,256]{2,1,0:T(8,128)(2,1)}), bf16[8,256,256]{2,1,0:T(8,128)(2,1)}, u32[]{:S(2)}, u32[]{:S(2)}) async-start(bf16[8,256,256]{2,1,0:T(8,128)(2,1)} %combine_0.1), calls=%async_computation.1 | async-start | bytes 2097152 | tf_op jit(solution)/shard_map/all_to_all | solution.py:22
  180.7 0.0 copy-start.1
  180.7 1.6 copy-done.1
  182.3 21.2 %combine_1.1 = bf16[16,256,256]{2,1,0:T(8,128)(2,1)S(1)} custom-call(s32[12]{0:T(128)S(1)} %get-tuple-element.8.where, s32[16384]{0:T(1024)S(1)} %bitcast.41, bf16[32,256,256]{2,1,0:T(8,128)(2,1)} %all-to-all-done.psi_ref, bf16[2,2048,256]{2,1,0:T(8,128)(2,1)} %collective-permute-done.9.refs_0_, bf16[2,2048,256]{2,1,0:T(8,128)(2,1)} %collective-permute-done.10.refs_1_, ...), custom_call_target="tpu_custom_call" | custom-call | flops 8589934592 | bytes 25165824 | tf_op jit(solution)/shard_map/combine_1/pallas_call | solution.py:140
  203.6 0.0 copy-start.3
  203.6 1.3 copy-done.3
  204.9 4.7 %all-to-all-start.2 = ((bf16[16,256,256]{2,1,0:T(8,128)(2,1)}), bf16[16,256,256]{2,1,0:T(8,128)(2,1)}, u32[]{:S(2)}, u32[]{:S(2)}) async-start(bf16[16,256,256]{2,1,0:T(8,128)(2,1)} %copy-done.3), calls=%async_computation.2 | async-start | bytes 4194304 | tf_op jit(solution)/shard_map/all_to_all | solution.py:22
  209.6 1.4 slice.48
  211.0 0.5 collective-permute-start.11
  211.5 1.3 slice.49
  212.8 2.8 %collective-permute-start.12 = (bf16[2,1024,256]{2,1,0:T(8,128)(2,1)S(1)}, bf16[2,1024,256]{2,1,0:T(8,128)(2,1)S(1)}, u32[]{:S(2)}, u32[]{:S(2)}) collective-permute-start(bf16[2,1024,256]{2,1,0:T(8,128)(2,1)S(1)} %slice.49), channel_id=1, source_target_pairs={{0,6},{2,0},{4,2},{6,4},{1,7},{3,1},{5,3},{7,5},{8,14},{10,8},{12,... | collective-permute-start | bytes 3145736 | tf_op jit(solution)/shard_map/ppermute | solution.py:26
  215.7 22.2 %collective-permute-done.11.refs_0_ = bf16[2,1024,256]{2,1,0:T(8,128)(2,1)S(1)} collective-permute-done((bf16[2,1024,256]{2,1,0:T(8,128)(2,1)S(1)}, bf16[2,1024,256]{2,1,0:T(8,128)(2,1)S(1)}, u32[]{:S(2)}, u32[]{:S(2)}) %collective-permute-start.11) | collective-permute-done | bytes 1048608 | tf_op jit(solution)/shard_map/ppermute | solution.py:26
  237.9 0.6 collective-permute-done.12.refs_1_
  238.5 15.4 %combine_3.1 = bf16[8,256,256]{2,1,0:T(8,128)(2,1)} custom-call(s32[12]{0:T(128)S(1)} %get-tuple-element.8.where, s32[16384]{0:T(1024)S(1)} %bitcast.42, bf16[32,256,256]{2,1,0:T(8,128)(2,1)} %all-to-all-done.psi_ref, bf16[2,1024,256]{2,1,0:T(8,128)(2,1)S(1)} %collective-permute-done.11.refs_0_, bf16[2,1024,256]{2,1,0:T(8,128)(2,1)S(1)} %collective-permute-done.12.refs_1_, ...), custom_call_target="tpu_custom_call" | custom-call | flops 4294967296 | bytes 12582912 | tf_op jit(solution)/shard_map/combine_3/pallas_call | solution.py:140
  253.9 4.5 %all-to-all-start.3 = ((bf16[8,256,256]{2,1,0:T(8,128)(2,1)}), bf16[8,256,256]{2,1,0:T(8,128)(2,1)S(1)}, u32[]{:S(2)}, u32[]{:S(2)}) async-start(bf16[8,256,256]{2,1,0:T(8,128)(2,1)} %combine_3.1), calls=%async_computation.3 | async-start | bytes 2097152 | tf_op jit(solution)/shard_map/all_to_all | solution.py:22
  258.3 0.6 fusion.3
  266.4 2.5 broadcast_in_dim.3
  268.9 2.3 constant_dynamic-update-slice_fusion.1
  271.1 2.3 fusion.1
  273.4 2.3 fusion
  275.6 1.0 constant_dynamic-update-slice_fusion
  (21 shorter events, 0.1 us)
Async XLA Ops:
  0.0 82.9 %all-to-all-start = ((bf16[32,256,256]{2,1,0:T(8,128)(2,1)}), bf16[32,256,256]{2,1,0:T(8,128)(2,1)}, u32[]{:S(2)}, u32[]{:S(2)}) async-start(bf16[32,256,256]{2,1,0:T(8,128)(2,1)} %param.8), calls=%async_computation | async-start | bytes 8388608 | tf_op jit(solution)/shard_map/all_to_all | solution.py:22
  7.2 79.5 %copy-start.5 = (s32[2]{0:T(128)S(1)}, s32[2]{0:T(128)}, u32[]{:S(2)}) copy-start(s32[2]{0:T(128)} %param.14) | copy-start | bytes 28
  7.2 79.5 %copy-start.6 = (s32[2]{0:T(128)S(1)}, s32[2]{0:T(128)}, u32[]{:S(2)}) copy-start(s32[2]{0:T(128)} %param.12) | copy-start | bytes 28
  7.2 79.5 %copy-start.7 = (s32[32]{0:T(128)S(1)}, s32[32]{0:T(128)}, u32[]{:S(2)}) copy-start(s32[32]{0:T(128)} %param.10) | copy-start | bytes 388
  7.2 79.5 %copy-start.8 = (s32[32]{0:T(128)S(1)}, s32[32]{0:T(128)}, u32[]{:S(2)}) copy-start(s32[32]{0:T(128)} %param.9) | copy-start | bytes 388
  7.2 49.7 %collective-permute-start.1 = (bf16[2,2048,256]{2,1,0:T(8,128)(2,1)}, bf16[2,2048,256]{2,1,0:T(8,128)(2,1)S(1)}, u32[]{:S(2)}, u32[]{:S(2)}) collective-permute-start(bf16[2,2048,256]{2,1,0:T(8,128)(2,1)} %bitcast.31), channel_id=1, source_target_pairs={{0,8},{8,16},{16,24},{24,0},{1,9},{9,17},{17,25},{25,1},{2,10},{10... | collective-permute-start | bytes 6291464 | tf_op jit(solution)/shard_map/ppermute | solution.py:26
  9.2 47.8 %collective-permute-start.3 = (bf16[2,2048,256]{2,1,0:T(8,128)(2,1)}, bf16[2,2048,256]{2,1,0:T(8,128)(2,1)}, u32[]{:S(2)}, u32[]{:S(2)}) collective-permute-start(bf16[2,2048,256]{2,1,0:T(8,128)(2,1)} %bitcast.32), channel_id=1, source_target_pairs={{0,24},{8,0},{16,8},{24,16},{1,25},{9,1},{17,9},{25,17},{2,26},{10... | collective-permute-start | bytes 6291464 | tf_op jit(solution)/shard_map/ppermute | solution.py:26
  11.4 71.5 %collective-permute-start = (bf16[2,2048,256]{2,1,0:T(8,128)(2,1)}, bf16[2,2048,256]{2,1,0:T(8,128)(2,1)}, u32[]{:S(2)}, u32[]{:S(2)}) collective-permute-start(bf16[2,2048,256]{2,1,0:T(8,128)(2,1)} %bitcast.33), channel_id=1, source_target_pairs={{0,1},{1,0},{2,3},{3,2},{4,5},{5,4},{6,7},{7,6},{8,9},{9,8},{10,11... | collective-permute-start | bytes 6291464 | tf_op jit(solution)/shard_map/ppermute | solution.py:26
  57.0 25.4 %collective-permute-start.5 = (bf16[2,1024,256]{2,1,0:T(8,128)(2,1)S(1)}, bf16[2,1024,256]{2,1,0:T(8,128)(2,1)S(1)}, u32[]{:S(2)}, u32[]{:S(2)}) collective-permute-start(bf16[2,1024,256]{2,1,0:T(8,128)(2,1)S(1)} %slice.44), channel_id=1, source_target_pairs={{0,8},{8,16},{16,24},{24,0},{1,9},{9,17},{17,25},{25,1},{2,10},{10... | collective-permute-start | bytes 3145736 | tf_op jit(solution)/shard_map/ppermute | solution.py:26
  59.3 24.9 %collective-permute-start.6 = (bf16[2,1024,256]{2,1,0:T(8,128)(2,1)}, bf16[2,1024,256]{2,1,0:T(8,128)(2,1)}, u32[]{:S(2)}, u32[]{:S(2)}) collective-permute-start(bf16[2,1024,256]{2,1,0:T(8,128)(2,1)} %slice.45), channel_id=1, source_target_pairs={{0,24},{8,0},{16,8},{24,16},{1,25},{9,1},{17,9},{25,17},{2,26},{10... | collective-permute-start | bytes 3145736 | tf_op jit(solution)/shard_map/ppermute | solution.py:26
  82.4 4.3 %collective-permute-start.7 = (bf16[2,1024,256]{2,1,0:T(8,128)(2,1)S(1)}, bf16[2,1024,256]{2,1,0:T(8,128)(2,1)}, u32[]{:S(2)}, u32[]{:S(2)}) collective-permute-start(bf16[2,1024,256]{2,1,0:T(8,128)(2,1)S(1)} %collective-permute-done.5.refs_7_.refs_8_), channel_id=1, source_target_pairs={{0,1},{1,0},{2,3},{3,2},{4,5},{5,4},{6,7},{7,6},{8,9},{9,8},{10,11... | collective-permute-start | bytes 3145736 | tf_op jit(solution)/shard_map/ppermute | solution.py:26
  82.4 75.5 %collective-permute-start.2 = (bf16[2,2048,256]{2,1,0:T(8,128)(2,1)S(1)}, bf16[2,2048,256]{2,1,0:T(8,128)(2,1)}, u32[]{:S(2)}, u32[]{:S(2)}) collective-permute-start(bf16[2,2048,256]{2,1,0:T(8,128)(2,1)S(1)} %collective-permute-done.1.refs_3_.refs_4_), channel_id=1, source_target_pairs={{0,1},{1,0},{2,3},{3,2},{4,5},{5,4},{6,7},{7,6},{8,9},{9,8},{10,11... | collective-permute-start | bytes 6291464 | tf_op jit(solution)/shard_map/ppermute | solution.py:26
  82.9 75.0 %collective-permute-start.4 = (bf16[2,2048,256]{2,1,0:T(8,128)(2,1)}, bf16[2,2048,256]{2,1,0:T(8,128)(2,1)}, u32[]{:S(2)}, u32[]{:S(2)}) collective-permute-start(bf16[2,2048,256]{2,1,0:T(8,128)(2,1)} %collective-permute-done.3.refs_5_.refs_6_), channel_id=1, source_target_pairs={{0,1},{1,0},{2,3},{3,2},{4,5},{5,4},{6,7},{7,6},{8,9},{9,8},{10,11... | collective-permute-start | bytes 6291464 | tf_op jit(solution)/shard_map/ppermute | solution.py:26
  82.9 97.8 %collective-permute-start.9 = (bf16[2,2048,256]{2,1,0:T(8,128)(2,1)}, bf16[2,2048,256]{2,1,0:T(8,128)(2,1)}, u32[]{:S(2)}, u32[]{:S(2)}) collective-permute-start(bf16[2,2048,256]{2,1,0:T(8,128)(2,1)} %bitcast.37), channel_id=1, source_target_pairs={{0,2},{2,4},{4,6},{6,0},{1,3},{3,5},{5,7},{7,1},{8,10},{10,12},{12... | collective-permute-start | bytes 6291464 | tf_op jit(solution)/shard_map/ppermute | solution.py:26
  84.2 96.5 %collective-permute-start.10 = (bf16[2,2048,256]{2,1,0:T(8,128)(2,1)}, bf16[2,2048,256]{2,1,0:T(8,128)(2,1)}, u32[]{:S(2)}, u32[]{:S(2)}) collective-permute-start(bf16[2,2048,256]{2,1,0:T(8,128)(2,1)} %bitcast.38), channel_id=1, source_target_pairs={{0,6},{2,0},{4,2},{6,4},{1,7},{3,1},{5,3},{7,5},{8,14},{10,8},{12,... | collective-permute-start | bytes 6291464 | tf_op jit(solution)/shard_map/ppermute | solution.py:26
  86.7 71.2 %collective-permute-start.8 = (bf16[2,1024,256]{2,1,0:T(8,128)(2,1)}, bf16[2,1024,256]{2,1,0:T(8,128)(2,1)}, u32[]{:S(2)}, u32[]{:S(2)}) collective-permute-start(bf16[2,1024,256]{2,1,0:T(8,128)(2,1)} %collective-permute-done.6.refs_8_.refs_9_), channel_id=1, source_target_pairs={{0,1},{1,0},{2,3},{3,2},{4,5},{5,4},{6,7},{7,6},{8,9},{9,8},{10,11... | collective-permute-start | bytes 3145736 | tf_op jit(solution)/shard_map/ppermute | solution.py:26
  157.9 1.6 copy-start
  159.5 1.6 copy-start.4
  176.5 28.4 %all-to-all-start.1 = ((bf16[8,256,256]{2,1,0:T(8,128)(2,1)}), bf16[8,256,256]{2,1,0:T(8,128)(2,1)}, u32[]{:S(2)}, u32[]{:S(2)}) async-start(bf16[8,256,256]{2,1,0:T(8,128)(2,1)} %combine_0.1), calls=%async_computation.1 | async-start | bytes 2097152 | tf_op jit(solution)/shard_map/all_to_all | solution.py:22
  180.7 1.6 copy-start.1
  203.6 1.3 copy-start.3
  204.9 49.0 %all-to-all-start.2 = ((bf16[16,256,256]{2,1,0:T(8,128)(2,1)}), bf16[16,256,256]{2,1,0:T(8,128)(2,1)}, u32[]{:S(2)}, u32[]{:S(2)}) async-start(bf16[16,256,256]{2,1,0:T(8,128)(2,1)} %copy-done.3), calls=%async_computation.2 | async-start | bytes 4194304 | tf_op jit(solution)/shard_map/all_to_all | solution.py:22
  209.6 28.9 %copy-start.2 = (bf16[2,8,256,256]{3,2,1,0:T(8,128)(2,1)S(1)}, bf16[2,8,256,256]{3,2,1,0:T(8,128)(2,1)}, u32[]{:S(2)}) copy-start(bf16[2,8,256,256]{3,2,1,0:T(8,128)(2,1)} %param.13) | copy-start | bytes 6291460
  211.0 26.8 %collective-permute-start.11 = (bf16[2,1024,256]{2,1,0:T(8,128)(2,1)S(1)}, bf16[2,1024,256]{2,1,0:T(8,128)(2,1)S(1)}, u32[]{:S(2)}, u32[]{:S(2)}) collective-permute-start(bf16[2,1024,256]{2,1,0:T(8,128)(2,1)S(1)} %slice.48), channel_id=1, source_target_pairs={{0,2},{2,4},{4,6},{6,0},{1,3},{3,5},{5,7},{7,1},{8,10},{10,12},{12... | collective-permute-start | bytes 3145736 | tf_op jit(solution)/shard_map/ppermute | solution.py:26
  212.8 25.6 %collective-permute-start.12 = (bf16[2,1024,256]{2,1,0:T(8,128)(2,1)S(1)}, bf16[2,1024,256]{2,1,0:T(8,128)(2,1)S(1)}, u32[]{:S(2)}, u32[]{:S(2)}) collective-permute-start(bf16[2,1024,256]{2,1,0:T(8,128)(2,1)S(1)} %slice.49), channel_id=1, source_target_pairs={{0,6},{2,0},{4,2},{6,4},{1,7},{3,1},{5,3},{7,5},{8,14},{10,8},{12,... | collective-permute-start | bytes 3145736 | tf_op jit(solution)/shard_map/ppermute | solution.py:26
  253.9 21.8 %all-to-all-start.3 = ((bf16[8,256,256]{2,1,0:T(8,128)(2,1)}), bf16[8,256,256]{2,1,0:T(8,128)(2,1)S(1)}, u32[]{:S(2)}, u32[]{:S(2)}) async-start(bf16[8,256,256]{2,1,0:T(8,128)(2,1)} %combine_3.1), calls=%async_computation.3 | async-start | bytes 2097152 | tf_op jit(solution)/shard_map/all_to_all | solution.py:22

commit v2 on v1

v2 whole, which is shorter than its diff:
```python
import jax
import jax.numpy as jnp
import numpy as np
from jax import lax
from jax.experimental import pallas as pl
from jax.experimental.pallas import tpu as pltpu
from jax.sharding import Mesh, PartitionSpec as P

AXES = ("y", "z", "x", "c")
OFFSETS = (0, 3, 1, 2)
BF16 = jnp.bfloat16
BRIEF = pl.CostEstimate(flops=1, bytes_accessed=1, transcendentals=0)
LONG = pl.CostEstimate(flops=10**12, bytes_accessed=1, transcendentals=0)
VMEM = 56 * 2**20


def ring_positions():
    rows = []
    for y, z, x, c in np.ndindex(4, 4, 4, 2):
        seen = [OFFSETS.index((z + o - y) % 4) for o in OFFSETS]
        rows.append(
            [(z + o) % 4 for o in OFFSETS]
            + [(x + o) % 4 for o in OFFSETS]
            + [32 * s + y * 8 + x * 2 for s in seen]
            + [c]
        )
    return np.asarray(rows, np.int32)


def exchange(array, axis):
    return lax.all_to_all(array, axis, split_axis=0, concat_axis=0, tiled=True)


def shift(array, axis, step, size=4):
    return lax.ppermute(array, axis, [(i, (i + step) % size) for i in range(size)])


def both_ways(array, axis):
    return shift(array, axis, 1), shift(array, axis, 3)


def all_around(array, axis):
    return jnp.concatenate([array, *both_ways(array, axis), shift(array, axis, 2)])


def onward(from_low, from_high, axis):
    half = from_low.shape[1] // 2
    return shift(from_low[:, :half], axis, 1), shift(from_high[:, half:], axis, 3)


def combine(where, codes, psi, lefts, rights, first):
    width = psi.shape[-1]
    depth = sum(a.shape[1] for a in lefts[0])
    terms = depth // width
    count = len(lefts)
    left_parts = [a for group in lefts for a in group]
    right_parts = [a for group in rights for a in group]

    def place(i, where):
        source, k = i // count, i % count
        return where[source // 2], where[12] ^ (source % 2), where[4 + first + k], k

    def code_at(i, where):
        source, k = i // count, i % count
        return 128 * (first + k) + where[8 + source // 2] + (where[12] ^ (source % 2))

    def psi_at(i, where):
        g, c_r, x_j, _ = place(i, where)
        return (g * 4 + x_j) * 2 + c_r

    def out_index(i, where, codes):
        g, c_r, _, k = place(i, where)
        return (g * 2 + c_r) * count + k, 0, 0

    def kernel(where, codes, psi_ref, *refs):
        left_refs = refs[: len(left_parts)]
        right_refs = refs[len(left_parts) : len(left_parts) + len(right_parts)]
        out_ref, left_buf, right_buf, partial, left_sems, sems = refs[len(left_parts) + len(right_parts) :]
        i = pl.program_id(0)
        steps = pl.num_programs(0)

        def load_left(k, go):
            at = sum(len(group) for group in lefts[:k])
            row = 0
            for n, a in enumerate(lefts[k]):
                copy = pltpu.make_async_copy(
                    left_refs[at + n], left_buf.at[k, :, pl.ds(row, a.shape[1])], left_sems.at[k, n]
                )
                copy.start() if go else copy.wait()
                row += a.shape[1]

        def fetch(step, go):
            right = codes[code_at(step, where)] // 2
            slot = lax.rem(step, 2)
            at = 0
            for source, group in enumerate(rights):

                @pl.when(step // count == source)
                def _(at=at, group=group):
                    row = 0
                    for n, a in enumerate(group):
                        copy = pltpu.make_async_copy(
                            right_refs[at + n].at[right],
                            right_buf.at[slot, pl.ds(row, a.shape[1])],
                            sems.at[slot, n],
                        )
                        copy.start() if go else copy.wait()
                        row += a.shape[1]

                at += len(group)

        @pl.when(i == 0)
        def _():
            load_left(0, True)
            fetch(i, True)
            for k in range(1, count):
                load_left(k, True)

        @pl.when(i + 1 < steps)
        def _():
            fetch(i + 1, True)

        for k in range(count):

            @pl.when(i == k)
            def _(k=k):
                load_left(k, False)

        left = codes[code_at(i, where)] % 2
        k = lax.rem(i, count)
        for t in range(terms):
            block = left_buf[k, left, t * width : (t + 1) * width]
            product = jnp.dot(block, psi_ref[0], preferred_element_type=jnp.float32)
            partial[:, t * width : (t + 1) * width] = product.astype(BF16)
        fetch(i, False)
        total = jnp.dot(partial[...], right_buf[lax.rem(i, 2)], preferred_element_type=jnp.float32)
        out_ref[0] = total.astype(BF16)

    blocks = 2 * 4 * count
    parts = max(len(group) for group in rights + lefts)
    in_place = pl.BlockSpec(memory_space=pl.ANY)
    return pl.pallas_call(
        kernel,
        out_shape=jax.ShapeDtypeStruct((blocks, width, width), BF16),
        grid_spec=pltpu.PrefetchScalarGridSpec(
            num_scalar_prefetch=2,
            grid=(blocks,),
            in_specs=[pl.BlockSpec((1, width, width), lambda i, where, codes: (psi_at(i, where), 0, 0))]
            + [in_place] * (len(left_parts) + len(right_parts)),
            out_specs=pl.BlockSpec((1, width, width), out_index),
            scratch_shapes=[
                pltpu.VMEM((count, 2, depth, width), BF16),
                pltpu.VMEM((2, depth, width), BF16),
                pltpu.VMEM((width, depth), BF16),
                pltpu.SemaphoreType.DMA((count, parts)),
                pltpu.SemaphoreType.DMA((2, parts)),
            ],
        ),
        compiler_params=pltpu.CompilerParams(
            dimension_semantics=("arbitrary",), vmem_limit_bytes=VMEM
        ),
        cost_estimate=LONG if first else BRIEF,
        name=f"combine_{first}",
    )(where, codes, psi, *left_parts, *right_parts)


def assemble(where, pieces, applied=None):
    shape = pieces[0][2].shape
    kept = [] if applied is None else [applied]

    def kernel(where, *refs):
        piece_refs = refs[: len(pieces)]
        out_ref, sems = refs[len(pieces) + len(kept) :]
        copies = []
        for (first, count, _), ref in zip(pieces, piece_refs):
            size = 2 if count == 1 else 1
            for n in range(0, 8 * count, size):
                owner, k = n // count, n % count
                z_j, c_j = owner // 2, owner % 2
                to = z_j * 8 + where[4 + first + k] * 2 + c_j
                copies.append(
                    pltpu.make_async_copy(
                        ref.at[pl.ds(n, size)], out_ref.at[pl.ds(to, size)], sems.at[len(copies)]
                    )
                )
        for copy in copies:
            copy.start()
        for copy in copies:
            copy.wait()

    number = sum(4 if count == 1 else 8 * count for _, count, _ in pieces)
    in_place = pl.BlockSpec(memory_space=pltpu.HBM)
    return pl.pallas_call(
        kernel,
        out_shape=jax.ShapeDtypeStruct((32,) + shape[1:], BF16),
        grid_spec=pltpu.PrefetchScalarGridSpec(
            num_scalar_prefetch=1,
            grid=(1,),
            in_specs=[in_place] * (len(pieces) + len(kept)),
            out_specs=in_place,
            scratch_shapes=[pltpu.SemaphoreType.DMA((number,))],
        ),
        input_output_aliases={1 + len(pieces): 0} if kept else {},
        cost_estimate=BRIEF,
        compiler_params=pltpu.CompilerParams(vmem_limit_bytes=62 * 2**20),
        name=f"assemble_{len(kept)}",
    )(where, *[piece for _, _, piece in pieces], *kept)


def after(array, *others):
    return lax.optimization_barrier((array, *others))[0]


def body(where, wavefunction, pair_left, pair_right, left_env, left_dims, right_env, right_dims):
    width = wavefunction.shape[-1]
    sectors, terms = left_env.shape[:2]
    where = where.reshape(-1)

    psi = exchange(wavefunction, ("y", "x"))
    codes = all_around(all_around(pair_left + 2 * pair_right, "y"), "x")

    index = lax.broadcasted_iota(jnp.int32, right_env.shape, 2)
    right_own = jnp.where(index < right_dims[:, None, None, None], right_env, jnp.zeros_like(right_env))
    index = lax.broadcasted_iota(jnp.int32, left_env.shape, 3)
    left_own = jnp.where(index < left_dims[:, None, None, None], left_env, jnp.zeros_like(left_env))
    left_own = left_own.reshape(sectors, terms * width, width)
    right_own = right_own.reshape(sectors, terms * width, width)

    right_low, right_high = both_ways(right_own, "z")
    far = onward(*lax.optimization_barrier((right_low, right_high, psi))[:2], "z")
    rights = []
    for group in ((right_own,), (right_low,), (right_high,), far):
        rights.append(group)
        rights.append(tuple(shift(a, "c", 1, 2) for a in group))

    left_low, left_high = both_ways(after(left_own, psi), "x")
    left_far = onward(left_low, left_high, "x")

    def home(first, lefts):
        out = combine(where, codes, psi, lefts, rights, first)
        return first, len(lefts), exchange(out, ("z", "c"))

    own = home(0, [(left_own,)])
    near = home(1, [(left_low,), (left_high,)])
    opposite = home(3, [left_far])
    applied = assemble(where, [own, near])
    return assemble(where, [opposite], applied)


def solution(mesh):
    fine = Mesh(mesh.devices.reshape(4, 4, 4, 2), AXES)
    mapped = jax.shard_map(
        body, mesh=fine, in_specs=P(AXES), out_specs=P(AXES), check_vma=False
    )

    def run(*arrays):
        return mapped(jnp.asarray(ring_positions()), *arrays)

    return run
```

time: 279 us -> 334 us (1.20)
  Pallas kernels: 51.9 us -> 191 us
  blocking collectives: 70.4 us -> 0 us
  local copies, waits for them, and re-layouts: 22.8 us -> 11.1 us
  waiting for transfers between devices: 88.1 us -> 77.6 us
  starting transfers between devices: 35.7 us -> 46.1 us
  between operations: 7.63 us -> 0.22 us
  other arithmetic: 0.08 us -> 6.2 us
    pallas_call x0 -> x2, Pallas kernels: none -> 131 us  [assemble(): pl.pallas_call(kernel, out_shape=jax.ShapeDtypeStruct((32,) + shape[1:],...]
    all_gather x1 -> x0, blocking collectives: 70.4 us -> none  [body(): meta = lax.all_gather(mine, AXES, axis=0, tiled=True)]
    ppermute x13 -> x19, waiting for transfers between devices: 88.1 us -> 62.3 us  [shift(): lax.ppermute(array, axis, [(i, (i + step) % size) for i in range(size)])]
    all_to_all x4, waiting for transfers between devices: 0.01 us -> 15.2 us  [exchange(): return lax.all_to_all(array, axis, split_axis=0, concat_axis=0, tiled=True)]
    ppermute x13 -> x19, starting transfers between devices: 15.2 us -> 26.5 us  [shift(): lax.ppermute(array, axis, [(i, (i + step) % size) for i in range(size)])]
    pallas_call x3, Pallas kernels: 51.9 us -> 59.9 us  [combine(): pl.pallas_call(kernel, out_shape=jax.ShapeDtypeStruct((blocks, width, wid...]
    dynamic_update_slice x4 -> x0, local copies, waits for them, and re-layouts: 7.82 us -> none  [body(): lax.dynamic_update_slice(applied, piece[:, None], (0, where[4 + position]...]
    select_n x0 -> x2, other arithmetic: none -> 6.12 us  [the longest x1 3.74 us: body(): jnp.where(index < left_dims[:, None, None, None], left_env, jnp.zeros_lik...]
  transfers between devices with their start and end apart: 17 -> 23, of which waited for: 4 -> 7; matrix products, arithmetic and copies ran while one was open for 6% -> 4% of each run, Pallas kernels for 19% -> 47%
where the time goes in v2:
time: 334 us; the launch traced here: 332 us
  Pallas kernels  191 us (57%)
  waiting for transfers between devices  77.6 us (23%)
  starting transfers between devices  46.1 us (14%)
  local copies, waits for them, and re-layouts  11.1 us (3%)
  other arithmetic  6.2 us (2%)
    pallas_call x2, Pallas kernels, assemble(): pl.pallas_call(kernel, out_shape=jax.ShapeDtypeStruct((32,) + shape[1:],...  131 us
    ppermute x19, waiting for transfers between devices, shift(): lax.ppermute(array, axis, [(i, (i + step) % size) for i in range(size)])  62.3 us
    pallas_call x3, Pallas kernels, combine(): pl.pallas_call(kernel, out_shape=jax.ShapeDtypeStruct((blocks, width, wid...  59.9 us
    ppermute x19, starting transfers between devices, shift(): lax.ppermute(array, axis, [(i, (i + step) % size) for i in range(size)])  26.5 us
    all_to_all x4, starting transfers between devices, exchange(): return lax.all_to_all(array, axis, split_axis=0, concat_axis=0, tiled=True)  19.6 us
    all_to_all x4, waiting for transfers between devices, exchange(): return lax.all_to_all(array, axis, split_axis=0, concat_axis=0, tiled=True)  15.2 us
  transfers between devices with their start and end apart: 23, of which 7 were waited for; matrix products, arithmetic and copies ran while one was open for 4% of the time, Pallas kernels for 47%

profile of v2, /device:TPU:0, one launch (start us, length us, event | category | flops | bytes accessed | tf_op | source)
XLA Modules:
  0.0 332.0 jit_solution(2402928906878835220)
XLA Ops:
  0.0 2.4 fusion.1
  2.4 0.0 copy-start.6
  2.4 0.0 copy-start.7
  2.4 0.0 copy-start.5
  2.4 4.2 %collective-permute-start.13 = (bf16[2,2048,256]{2,1,0:T(8,128)(2,1)S(1)}, bf16[2,2048,256]{2,1,0:T(8,128)(2,1)}, u32[]{:S(2)}, u32[]{:S(2)}) collective-permute-start(bf16[2,2048,256]{2,1,0:T(8,128)(2,1)S(1)} %bitcast.4), channel_id=1, source_target_pairs={{0,24},{8,0},{16,8},{24,16},{1,25},{9,1},{17,9},{25,17},{2,26},{10... | collective-permute-start | bytes 6291464 | tf_op jit(solution)/shard_map/ppermute | solution.py:35
  6.6 7.1 %all-to-all-start = ((bf16[32,256,256]{2,1,0:T(8,128)(2,1)}), bf16[32,256,256]{2,1,0:T(8,128)(2,1)}, u32[]{:S(2)}, u32[]{:S(2)}) async-start(bf16[32,256,256]{2,1,0:T(8,128)(2,1)} %param.8), calls=%async_computation | async-start | bytes 8388608 | tf_op jit(solution)/shard_map/all_to_all | solution.py:31
  13.7 0.1 collective-permute-start.11
  13.8 0.1 collective-permute-start.10
  13.9 37.6 %collective-permute-done.13.refs_6_.refs_5_ = bf16[2,2048,256]{2,1,0:T(8,128)(2,1)} collective-permute-done((bf16[2,2048,256]{2,1,0:T(8,128)(2,1)S(1)}, bf16[2,2048,256]{2,1,0:T(8,128)(2,1)}, u32[]{:S(2)}, u32[]{:S(2)}) %collective-permute-start.13) | collective-permute-done | bytes 2097184 | tf_op jit(solution)/shard_map/ppermute | solution.py:35
  51.5 3.3 collective-permute-start.2
  54.8 1.1 collective-permute-start.1
  55.9 0.8 collective-permute-done.2
  56.7 3.4 %collective-permute-start = (s32[32]{0:T(128)S(1)}, s32[32]{0:T(128)S(1)}, u32[]{:S(2)}, u32[]{:S(2)}) collective-permute-start(s32[32]{0:T(128)S(1)} %multiply_add_fusion), channel_id=1, source_target_pairs={{0,32},{32,64},{64,96},{96,0},{1,33},{33,65},{65,97},{97,1},{2,34}... | collective-permute-start | bytes 392 | tf_op jit(solution)/shard_map/ppermute | solution.py:35
  60.1 3.7 %fusion = bf16[2,8,256,256]{3,2,1,0:T(8,128)(2,1)} fusion(bf16[2,8,256,256]{3,2,1,0:T(8,128)(2,1)} %param.11, s32[2]{0:T(128)S(1)} %copy-done.5), kind=kLoop, calls=%fused_computation.2 | loop fusion | flops 2097152 | bytes 4194312 | tf_op jit(solution)/shard_map/jit(_where)/select_n | solution.py:225
  63.8 0.1 pad_add_fusion
  63.9 6.1 %collective-permute-start.5 = (s32[128]{0:T(128)S(1)}, s32[128]{0:T(128)S(1)}, u32[]{:S(2)}, u32[]{:S(2)}) collective-permute-start(s32[128]{0:T(128)S(1)} %pad_add_fusion), channel_id=1, source_target_pairs={{0,4},{2,6},{4,0},{6,2},{1,5},{3,7},{5,1},{7,3},{8,12},{10,14},{12... | collective-permute-start | bytes 1544 | tf_op jit(solution)/shard_map/ppermute | solution.py:35
  70.0 2.0 collective-permute-start.3
  72.0 4.1 %all-to-all-done.psi_ref = bf16[32,256,256]{2,1,0:T(8,128)(2,1)} async-done(((bf16[32,256,256]{2,1,0:T(8,128)(2,1)}), bf16[32,256,256]{2,1,0:T(8,128)(2,1)}, u32[]{:S(2)}, u32[]{:S(2)}) %all-to-all-start) | async-done | bytes 4194336 | tf_op jit(solution)/shard_map/all_to_all | solution.py:31
  76.2 1.3 slice.14
  77.5 1.3 slice.15
  78.8 0.0 collective-permute-done.5
  78.8 0.1 collective-permute-start.12
  78.9 0.5 collective-permute-start.16
  79.3 0.0 collective-permute-done.3
  79.3 1.6 collective-permute-start.15
  81.0 0.0 collective-permute-done.10.refs_3_.refs_2_
  81.0 0.9 collective-permute-start.8
  81.9 1.1 collective-permute-start.6
  83.0 21.4 %collective-permute-done.16.refs_9_.refs_8_ = bf16[2,1024,256]{2,1,0:T(8,128)(2,1)S(1)} collective-permute-done((bf16[2,1024,256]{2,1,0:T(8,128)(2,1)S(1)}, bf16[2,1024,256]{2,1,0:T(8,128)(2,1)S(1)}, u32[]{:S(2)}, u32[]{:S(2)}) %collective-permute-start.16) | collective-permute-done | bytes 1048608 | tf_op jit(solution)/shard_map/ppermute | solution.py:35
  104.4 1.4 collective-permute-done.15.refs_8_.refs_7_
  105.9 1.3 dynamic-slice_bitcast_fusion.where
  107.1 0.6 concatenate.8.codes
  107.8 1.0 collective-permute-done.17.refs_10_.refs_9_
  108.8 1.1 copy-done.4
  109.9 15.9 %combine_0.1 = bf16[8,256,256]{2,1,0:T(8,128)(2,1)} custom-call(s32[13]{0:T(128)} %dynamic-slice_bitcast_fusion.where, s32[512]{0:T(512)} %concatenate.8.codes, bf16[32,256,256]{2,1,0:T(8,128)(2,1)} %all-to-all-done.psi_ref, bf16[2,2048,256]{2,1,0:T(8,128)(2,1)} %bitcast.1.refs_0_, bf16[2,2048,256]{2,1,0:T(8,128)(2,1)} %bitcast.7, ...), custom_call_target="tpu_custom_call" | custom-call | flops 1 | bytes 1 | tf_op jit(solution)/shard_map/combine_0/pallas_call | solution.py:142
  125.8 4.3 %all-to-all-start.2 = ((bf16[8,256,256]{2,1,0:T(8,128)(2,1)}), bf16[8,256,256]{2,1,0:T(8,128)(2,1)}, u32[]{:S(2)}, u32[]{:S(2)}) async-start(bf16[8,256,256]{2,1,0:T(8,128)(2,1)} %combine_0.1), calls=%async_computation.2 | async-start | bytes 2097152 | tf_op jit(solution)/shard_map/all_to_all | solution.py:31
  130.1 2.3 slice.17
  132.4 1.0 collective-permute-start.9
  133.4 2.3 slice.16
  135.6 1.1 collective-permute-start.7
  136.7 27.9 %combine_1.1 = bf16[16,256,256]{2,1,0:T(8,128)(2,1)} custom-call(s32[13]{0:T(128)} %dynamic-slice_bitcast_fusion.where, s32[512]{0:T(512)} %concatenate.8.codes, bf16[32,256,256]{2,1,0:T(8,128)(2,1)} %all-to-all-done.psi_ref, bf16[2,2048,256]{2,1,0:T(8,128)(2,1)} %collective-permute-done.6.refs_0_, bf16[2,2048,256]{2,1,0:T(8,128)(2,1)} %collective-permute-done.8.refs_1_, ...), custom_call_target="tpu_custom_call" | custom-call | flops 999999995904 | bytes 1 | tf_op jit(solution)/shard_map/combine_1/pallas_call | solution.py:142
  164.6 4.7 %all-to-all-start.3 = ((bf16[16,256,256]{2,1,0:T(8,128)(2,1)}), bf16[16,256,256]{2,1,0:T(8,128)(2,1)}, u32[]{:S(2)}, u32[]{:S(2)}) async-start(bf16[16,256,256]{2,1,0:T(8,128)(2,1)} %combine_1.1), calls=%async_computation.3 | async-start | bytes 4194304 | tf_op jit(solution)/shard_map/all_to_all | solution.py:31
  169.3 16.2 %combine_3.1 = bf16[8,256,256]{2,1,0:T(8,128)(2,1)} custom-call(s32[13]{0:T(128)} %dynamic-slice_bitcast_fusion.where, s32[512]{0:T(512)} %concatenate.8.codes, bf16[32,256,256]{2,1,0:T(8,128)(2,1)} %all-to-all-done.psi_ref, bf16[2,1024,256]{2,1,0:T(8,128)(2,1)} %collective-permute-done.7.refs_0_, bf16[2,1024,256]{2,1,0:T(8,128)(2,1)} %collective-permute-done.9.refs_1_, ...), custom_call_target="tpu_custom_call" | custom-call | flops 999999995904 | bytes 1 | tf_op jit(solution)/shard_map/combine_3/pallas_call | solution.py:142
  185.5 11.1 %all-to-all-done.3.refs_1_ = bf16[16,256,256]{2,1,0:T(8,128)(2,1)} async-done(((bf16[16,256,256]{2,1,0:T(8,128)(2,1)}), bf16[16,256,256]{2,1,0:T(8,128)(2,1)}, u32[]{:S(2)}, u32[]{:S(2)}) %all-to-all-start.3) | async-done | bytes 2097184 | tf_op jit(solution)/shard_map/all_to_all | solution.py:31
  196.6 3.6 %all-to-all-start.1 = ((bf16[8,256,256]{2,1,0:T(8,128)(2,1)}), bf16[8,256,256]{2,1,0:T(8,128)(2,1)S(1)}, u32[]{:S(2)}, u32[]{:S(2)}) async-start(bf16[8,256,256]{2,1,0:T(8,128)(2,1)} %combine_3.1), calls=%async_computation.1 | async-start | bytes 2097152 | tf_op jit(solution)/shard_map/all_to_all | solution.py:31
  200.2 97.2 %assemble_0.1.refs_1_ = bf16[32,256,256]{2,1,0:T(8,128)(2,1)} custom-call(s32[13]{0:T(128)} %dynamic-slice_bitcast_fusion.where, bf16[8,256,256]{2,1,0:T(8,128)(2,1)} %all-to-all-done.2.refs_0_, bf16[16,256,256]{2,1,0:T(8,128)(2,1)} %all-to-all-done.3.refs_1_), custom_call_target="tpu_custom_call" | custom-call | flops 1 | bytes 1 | tf_op jit(solution)/shard_map/assemble_0/pallas_call | solution.py:193
  297.4 1.0 copy-done.1
  298.4 33.6 %assemble_1.1 = bf16[32,256,256]{2,1,0:T(8,128)(2,1)} custom-call(s32[13]{0:T(128)} %dynamic-slice_bitcast_fusion.where, bf16[8,256,256]{2,1,0:T(8,128)(2,1)} %copy-done.1, bf16[32,256,256]{2,1,0:T(8,128)(2,1)} %assemble_0.1.refs_1_), custom_call_target="tpu_custom_call", output_to_operand_aliasing={{}: (2, {})} | custom-call | flops 1 | bytes 1 | tf_op jit(solution)/shard_map/assemble_1/pallas_call | solution.py:193
  (29 shorter events, 0.1 us)
Async XLA Ops:
  2.4 11.4 %copy-start = (bf16[2,8,256,256]{3,2,1,0:T(8,128)(2,1)}, bf16[2,8,256,256]{3,2,1,0:T(8,128)(2,1)S(1)}, u32[]{:S(2)}) copy-start(bf16[2,8,256,256]{3,2,1,0:T(8,128)(2,1)S(1)} %fusion.1) | copy-start | bytes 6291460
  2.4 49.1 %copy-start.6 = (s32[32]{0:T(128)S(1)}, s32[32]{0:T(128)}, u32[]{:S(2)}) copy-start(s32[32]{0:T(128)} %param.9) | copy-start | bytes 388
  2.4 49.1 %copy-start.7 = (s32[32]{0:T(128)S(1)}, s32[32]{0:T(128)}, u32[]{:S(2)}) copy-start(s32[32]{0:T(128)} %param.10) | copy-start | bytes 388
  2.4 57.7 %copy-start.5 = (s32[2]{0:T(128)S(1)}, s32[2]{0:T(128)}, u32[]{:S(2)}) copy-start(s32[2]{0:T(128)} %param.12) | copy-start | bytes 28
  2.4 49.1 %collective-permute-start.13 = (bf16[2,2048,256]{2,1,0:T(8,128)(2,1)S(1)}, bf16[2,2048,256]{2,1,0:T(8,128)(2,1)}, u32[]{:S(2)}, u32[]{:S(2)}) collective-permute-start(bf16[2,2048,256]{2,1,0:T(8,128)(2,1)S(1)} %bitcast.4), channel_id=1, source_target_pairs={{0,24},{8,0},{16,8},{24,16},{1,25},{9,1},{17,9},{25,17},{2,26},{10... | collective-permute-start | bytes 6291464 | tf_op jit(solution)/shard_map/ppermute | solution.py:35
  6.6 69.5 %all-to-all-start = ((bf16[32,256,256]{2,1,0:T(8,128)(2,1)}), bf16[32,256,256]{2,1,0:T(8,128)(2,1)}, u32[]{:S(2)}, u32[]{:S(2)}) async-start(bf16[32,256,256]{2,1,0:T(8,128)(2,1)} %param.8), calls=%async_computation | async-start | bytes 8388608 | tf_op jit(solution)/shard_map/all_to_all | solution.py:31
  13.7 56.3 %collective-permute-start.11 = (bf16[2,2048,256]{2,1,0:T(8,128)(2,1)S(1)}, bf16[2,2048,256]{2,1,0:T(8,128)(2,1)}, u32[]{:S(2)}, u32[]{:S(2)}) collective-permute-start(bf16[2,2048,256]{2,1,0:T(8,128)(2,1)S(1)} %bitcast.5), channel_id=1, source_target_pairs={{0,8},{8,16},{16,24},{24,0},{1,9},{9,17},{17,25},{25,1},{2,10},{10... | collective-permute-start | bytes 6291464 | tf_op jit(solution)/shard_map/ppermute | solution.py:35
  13.8 67.2 %collective-permute-start.10 = (bf16[2,2048,256]{2,1,0:T(8,128)(2,1)S(1)}, bf16[2,2048,256]{2,1,0:T(8,128)(2,1)}, u32[]{:S(2)}, u32[]{:S(2)}) collective-permute-start(bf16[2,2048,256]{2,1,0:T(8,128)(2,1)S(1)} %bitcast.6), channel_id=1, source_target_pairs={{0,1},{1,0},{2,3},{3,2},{4,5},{5,4},{6,7},{7,6},{8,9},{9,8},{10,11... | collective-permute-start | bytes 6291464 | tf_op jit(solution)/shard_map/ppermute | solution.py:35
  51.5 30.4 %collective-permute-start.14 = (bf16[2,2048,256]{2,1,0:T(8,128)(2,1)}, bf16[2,2048,256]{2,1,0:T(8,128)(2,1)}, u32[]{:S(2)}, u32[]{:S(2)}) collective-permute-start(bf16[2,2048,256]{2,1,0:T(8,128)(2,1)} %collective-permute-done.13.refs_6_.refs_5_), channel_id=1, source_target_pairs={{0,1},{1,0},{2,3},{3,2},{4,5},{5,4},{6,7},{7,6},{8,9},{9,8},{10,11... | collective-permute-start | bytes 6291464 | tf_op jit(solution)/shard_map/ppermute | solution.py:35
  51.5 5.1 %collective-permute-start.2 = (s32[32]{0:T(128)S(1)}, s32[32]{0:T(128)S(1)}, u32[]{:S(2)}, u32[]{:S(2)}) collective-permute-start(s32[32]{0:T(128)S(1)} %multiply_add_fusion), channel_id=1, source_target_pairs={{0,64},{32,96},{64,0},{96,32},{1,65},{33,97},{65,1},{97,33},{2,66}... | collective-permute-start | bytes 392 | tf_op jit(solution)/shard_map/ppermute | solution.py:35
  54.8 9.0 %collective-permute-start.1 = (s32[32]{0:T(128)S(1)}, s32[32]{0:T(128)S(1)}, u32[]{:S(2)}, u32[]{:S(2)}) collective-permute-start(s32[32]{0:T(128)S(1)} %multiply_add_fusion), channel_id=1, source_target_pairs={{0,96},{32,0},{64,32},{96,64},{1,97},{33,1},{65,33},{97,65},{2,98}... | collective-permute-start | bytes 392 | tf_op jit(solution)/shard_map/ppermute | solution.py:35
  56.7 7.2 %collective-permute-start = (s32[32]{0:T(128)S(1)}, s32[32]{0:T(128)S(1)}, u32[]{:S(2)}, u32[]{:S(2)}) collective-permute-start(s32[32]{0:T(128)S(1)} %multiply_add_fusion), channel_id=1, source_target_pairs={{0,32},{32,64},{64,96},{96,0},{1,33},{33,65},{65,97},{97,1},{2,34}... | collective-permute-start | bytes 392 | tf_op jit(solution)/shard_map/ppermute | solution.py:35
  63.9 14.8 %collective-permute-start.5 = (s32[128]{0:T(128)S(1)}, s32[128]{0:T(128)S(1)}, u32[]{:S(2)}, u32[]{:S(2)}) collective-permute-start(s32[128]{0:T(128)S(1)} %pad_add_fusion), channel_id=1, source_target_pairs={{0,4},{2,6},{4,0},{6,2},{1,5},{3,7},{5,1},{7,3},{8,12},{10,14},{12... | collective-permute-start | bytes 1544 | tf_op jit(solution)/shard_map/ppermute | solution.py:35
  70.0 8.8 %collective-permute-start.4 = (s32[128]{0:T(128)S(1)}, s32[128]{0:T(128)S(1)}, u32[]{:S(2)}, u32[]{:S(2)}) collective-permute-start(s32[128]{0:T(128)S(1)} %pad_add_fusion), channel_id=1, source_target_pairs={{0,6},{2,0},{4,2},{6,4},{1,7},{3,1},{5,3},{7,5},{8,14},{10,8},{12,... | collective-permute-start | bytes 1544 | tf_op jit(solution)/shard_map/ppermute | solution.py:35
  70.0 9.3 %collective-permute-start.3 = (s32[128]{0:T(128)S(1)}, s32[128]{0:T(128)S(1)}, u32[]{:S(2)}, u32[]{:S(2)}) collective-permute-start(s32[128]{0:T(128)S(1)} %pad_add_fusion), channel_id=1, source_target_pairs={{0,2},{2,4},{4,6},{6,0},{1,3},{3,5},{5,7},{7,1},{8,10},{10,12},{12... | collective-permute-start | bytes 1544 | tf_op jit(solution)/shard_map/ppermute | solution.py:35
  78.8 29.0 %collective-permute-start.12 = (bf16[2,2048,256]{2,1,0:T(8,128)(2,1)}, bf16[2,2048,256]{2,1,0:T(8,128)(2,1)}, u32[]{:S(2)}, u32[]{:S(2)}) collective-permute-start(bf16[2,2048,256]{2,1,0:T(8,128)(2,1)} %collective-permute-done.11.refs_4_.refs_3_), channel_id=1, source_target_pairs={{0,1},{1,0},{2,3},{3,2},{4,5},{5,4},{6,7},{7,6},{8,9},{9,8},{10,11... | collective-permute-start | bytes 6291464 | tf_op jit(solution)/shard_map/ppermute | solution.py:35
  78.9 25.6 %collective-permute-start.16 = (bf16[2,1024,256]{2,1,0:T(8,128)(2,1)S(1)}, bf16[2,1024,256]{2,1,0:T(8,128)(2,1)S(1)}, u32[]{:S(2)}, u32[]{:S(2)}) collective-permute-start(bf16[2,1024,256]{2,1,0:T(8,128)(2,1)S(1)} %slice.15), channel_id=1, source_target_pairs={{0,24},{8,0},{16,8},{24,16},{1,25},{9,1},{17,9},{25,17},{2,26},{10... | collective-permute-start | bytes 3145736 | tf_op jit(solution)/shard_map/ppermute | solution.py:35
  79.3 26.5 %collective-permute-start.15 = (bf16[2,1024,256]{2,1,0:T(8,128)(2,1)S(1)}, bf16[2,1024,256]{2,1,0:T(8,128)(2,1)}, u32[]{:S(2)}, u32[]{:S(2)}) collective-permute-start(bf16[2,1024,256]{2,1,0:T(8,128)(2,1)S(1)} %slice.14), channel_id=1, source_target_pairs={{0,8},{8,16},{16,24},{24,0},{1,9},{9,17},{17,25},{25,1},{2,10},{10... | collective-permute-start | bytes 3145736 | tf_op jit(solution)/shard_map/ppermute | solution.py:35
  81.0 49.1 %collective-permute-start.8 = (bf16[2,2048,256]{2,1,0:T(8,128)(2,1)}, bf16[2,2048,256]{2,1,0:T(8,128)(2,1)}, u32[]{:S(2)}, u32[]{:S(2)}) collective-permute-start(bf16[2,2048,256]{2,1,0:T(8,128)(2,1)} %bitcast.1.refs_0_), channel_id=1, source_target_pairs={{0,6},{2,0},{4,2},{6,4},{1,7},{3,1},{5,3},{7,5},{8,14},{10,8},{12,... | collective-permute-start | bytes 6291464 | tf_op jit(solution)/shard_map/ppermute | solution.py:35
  81.9 51.4 %collective-permute-start.6 = (bf16[2,2048,256]{2,1,0:T(8,128)(2,1)}, bf16[2,2048,256]{2,1,0:T(8,128)(2,1)}, u32[]{:S(2)}, u32[]{:S(2)}) collective-permute-start(bf16[2,2048,256]{2,1,0:T(8,128)(2,1)} %bitcast.1.refs_0_), channel_id=1, source_target_pairs={{0,2},{2,4},{4,6},{6,0},{1,3},{3,5},{5,7},{7,1},{8,10},{10,12},{12... | collective-permute-start | bytes 6291464 | tf_op jit(solution)/shard_map/ppermute | solution.py:35
  104.4 4.4 %copy-start.2 = (bf16[2,1024,256]{2,1,0:T(8,128)(2,1)}, bf16[2,1024,256]{2,1,0:T(8,128)(2,1)S(1)}, u32[]{:S(2)}) copy-start(bf16[2,1024,256]{2,1,0:T(8,128)(2,1)S(1)} %collective-permute-done.16.refs_9_.refs_8_) | copy-start | bytes 3145732
  104.4 3.3 %collective-permute-start.18 = (bf16[2,1024,256]{2,1,0:T(8,128)(2,1)S(1)}, bf16[2,1024,256]{2,1,0:T(8,128)(2,1)S(1)}, u32[]{:S(2)}, u32[]{:S(2)}) collective-permute-start(bf16[2,1024,256]{2,1,0:T(8,128)(2,1)S(1)} %collective-permute-done.16.refs_9_.refs_8_), channel_id=1, source_target_pairs={{0,1},{1,0},{2,3},{3,2},{4,5},{5,4},{6,7},{7,6},{8,9},{9,8},{10,11... | collective-permute-start | bytes 3145736 | tf_op jit(solution)/shard_map/ppermute | solution.py:35
  105.9 2.9 collective-permute-start.17
  107.8 1.0 copy-start.3
  108.8 1.1 copy-start.4
  125.8 38.8 %all-to-all-start.2 = ((bf16[8,256,256]{2,1,0:T(8,128)(2,1)}), bf16[8,256,256]{2,1,0:T(8,128)(2,1)}, u32[]{:S(2)}, u32[]{:S(2)}) async-start(bf16[8,256,256]{2,1,0:T(8,128)(2,1)} %combine_0.1), calls=%async_computation.2 | async-start | bytes 2097152 | tf_op jit(solution)/shard_map/all_to_all | solution.py:31
  132.4 36.9 %collective-permute-start.9 = (bf16[2,1024,256]{2,1,0:T(8,128)(2,1)}, bf16[2,1024,256]{2,1,0:T(8,128)(2,1)}, u32[]{:S(2)}, u32[]{:S(2)}) collective-permute-start(bf16[2,1024,256]{2,1,0:T(8,128)(2,1)} %slice.17), channel_id=1, source_target_pairs={{0,6},{2,0},{4,2},{6,4},{1,7},{3,1},{5,3},{7,5},{8,14},{10,8},{12,... | collective-permute-start | bytes 3145736 | tf_op jit(solution)/shard_map/ppermute | solution.py:35
  135.6 33.7 %collective-permute-start.7 = (bf16[2,1024,256]{2,1,0:T(8,128)(2,1)}, bf16[2,1024,256]{2,1,0:T(8,128)(2,1)}, u32[]{:S(2)}, u32[]{:S(2)}) collective-permute-start(bf16[2,1024,256]{2,1,0:T(8,128)(2,1)} %slice.16), channel_id=1, source_target_pairs={{0,2},{2,4},{4,6},{6,0},{1,3},{3,5},{5,7},{7,1},{8,10},{10,12},{12... | collective-permute-start | bytes 3145736 | tf_op jit(solution)/shard_map/ppermute | solution.py:35
  164.6 32.0 %all-to-all-start.3 = ((bf16[16,256,256]{2,1,0:T(8,128)(2,1)}), bf16[16,256,256]{2,1,0:T(8,128)(2,1)}, u32[]{:S(2)}, u32[]{:S(2)}) async-start(bf16[16,256,256]{2,1,0:T(8,128)(2,1)} %combine_1.1), calls=%async_computation.3 | async-start | bytes 4194304 | tf_op jit(solution)/shard_map/all_to_all | solution.py:31
  196.6 100.8 %all-to-all-start.1 = ((bf16[8,256,256]{2,1,0:T(8,128)(2,1)}), bf16[8,256,256]{2,1,0:T(8,128)(2,1)S(1)}, u32[]{:S(2)}, u32[]{:S(2)}) async-start(bf16[8,256,256]{2,1,0:T(8,128)(2,1)} %combine_3.1), calls=%async_computation.1 | async-start | bytes 2097152 | tf_op jit(solution)/shard_map/all_to_all | solution.py:31
  297.4 1.0 copy-start.1

commit v3 on v2

v3 whole, which is shorter than its diff:
```python
import jax
import jax.numpy as jnp
import numpy as np
from jax import lax
from jax.experimental import pallas as pl
from jax.experimental.pallas import tpu as pltpu
from jax.sharding import Mesh, PartitionSpec as P

AXES = ("y", "z", "x", "c")
OFFSETS = (0, 3, 1, 2)
STEPS = (0, 1, 3, 2)
SLOTS = 3
BF16 = jnp.bfloat16
BRIEF = pl.CostEstimate(flops=1, bytes_accessed=1, transcendentals=0)
LONG = pl.CostEstimate(flops=10**12, bytes_accessed=1, transcendentals=0)
VMEM = 60 * 2**20


def ring_positions():
    rows = []
    for y, z, x, c in np.ndindex(4, 4, 4, 2):
        rows.append(
            [(z + o) % 4 for o in OFFSETS]
            + [(x + o) % 4 for o in OFFSETS]
            + [c]
            + [(x + o) % 4 for o in STEPS]
        )
    return np.asarray(rows, np.int32)


def exchange(array, axis):
    return lax.all_to_all(array, axis, split_axis=0, concat_axis=0, tiled=True)


def shift(array, axis, step, size=4):
    return lax.ppermute(array, axis, [(i, (i + step) % size) for i in range(size)])


def both_ways(array, axis):
    return shift(array, axis, 1), shift(array, axis, 3)


def onward(from_low, from_high, axis):
    half = from_low.shape[1] // 2
    return shift(from_low[:, :half], axis, 1), shift(from_high[:, half:], axis, 3)


def combine(where, codes, psi, lefts, rights, position):
    width = psi.shape[-1]
    depth = sum(a.shape[1] for a in lefts)
    terms = depth // width
    depth_of = SLOTS
    right_parts = [a for group in rights for a in group]

    def block_of(n, where):
        g, c_r = where[n // 2], where[8] ^ (n % 2)
        return g * 2 + c_r, (g * 4 + where[4 + position]) * 2 + c_r

    def kernel(where, codes, psi_ref, *refs):
        refs = list(refs)
        left_refs = [refs.pop(0) for _ in lefts]
        right_refs = [[refs.pop(0) for _ in group] for group in rights]
        out_ref, left_buf, right_buf, partial, left_sems, sems = refs
        step = pl.program_id(0)
        steps = pl.num_programs(0)

        def left_copies():
            row = 0
            for n, ref in enumerate(left_refs):
                size = ref.shape[1]
                yield pltpu.make_async_copy(ref, left_buf.at[:, pl.ds(row, size)], left_sems.at[n])
                row += size

        def fetch(at, go):
            slot = lax.rem(at, depth_of)
            for z_step in range(4):

                @pl.when(at == z_step)
                def _(z_step=z_step):
                    for core in range(2):
                        right = codes[block_of(2 * z_step + core, where)[1]] // 2
                        row = 0
                        for n, ref in enumerate(right_refs[2 * z_step + core]):
                            size = ref.shape[1]
                            copy = pltpu.make_async_copy(
                                ref.at[right],
                                right_buf.at[slot, core, pl.ds(row, size)],
                                sems.at[slot, core, n],
                            )
                            copy.start() if go else copy.wait()
                            row += size

        @pl.when(step == 0)
        def _():
            for copy in left_copies():
                copy.start()
            for ahead in range(depth_of - 1):
                fetch(ahead, True)

        @pl.when(step + depth_of - 1 < steps)
        def _():
            fetch(step + depth_of - 1, True)

        @pl.when(step == 0)
        def _():
            for copy in left_copies():
                copy.wait()

        fetch(step, False)
        slot = lax.rem(step, depth_of)
        for core in range(2):
            at, code_at = block_of(2 * step + core, where)
            left = codes[code_at] % 2
            block = psi_ref[at]
            for t in range(terms):
                product = jnp.dot(
                    left_buf[left, t * width : (t + 1) * width],
                    block,
                    preferred_element_type=jnp.float32,
                )
                partial[core, :, t * width : (t + 1) * width] = product.astype(BF16)
        for core in range(2):
            at, _ = block_of(2 * step + core, where)
            total = jnp.dot(partial[core], right_buf[slot, core], preferred_element_type=jnp.float32)
            out_ref[at] = total.astype(BF16)

    in_place = pl.BlockSpec(memory_space=pl.ANY)
    whole = lambda step, where, codes: (0, 0, 0)
    parts = max(len(group) for group in rights)
    return pl.pallas_call(
        kernel,
        out_shape=jax.ShapeDtypeStruct((8, width, width), BF16),
        grid_spec=pltpu.PrefetchScalarGridSpec(
            num_scalar_prefetch=2,
            grid=(4,),
            in_specs=[pl.BlockSpec((8, width, width), whole)]
            + [in_place] * (len(lefts) + len(right_parts)),
            out_specs=pl.BlockSpec((8, width, width), whole),
            scratch_shapes=[
                pltpu.VMEM((2, depth, width), BF16),
                pltpu.VMEM((depth_of, 2, depth, width), BF16),
                pltpu.VMEM((2, width, depth), BF16),
                pltpu.SemaphoreType.DMA((len(lefts),)),
                pltpu.SemaphoreType.DMA((depth_of, 2, parts)),
            ],
        ),
        compiler_params=pltpu.CompilerParams(
            dimension_semantics=("arbitrary",), vmem_limit_bytes=VMEM
        ),
        cost_estimate=LONG,
        name=f"combine_{position}",
    )(where, codes, psi, *lefts, *right_parts)


def assemble(where, pieces, applied=None):
    width = pieces[0][2].shape[-1]
    kept = [] if applied is None else [applied]
    steps = [(first + k, count, k) for first, count, _ in pieces for k in range(count)]

    def kernel(where, *refs):
        *piece_refs, out_ref = refs[: len(pieces)] + refs[-1:]
        p = pl.program_id(0)
        for n, ref in enumerate(r for (_, count, _), r in zip(pieces, piece_refs) for _ in range(count)):

            @pl.when(p == n)
            def _(ref=ref, k=steps[n][2]):
                out_ref[0, 0] = ref[0, :, k]

    def spec(count):
        return pl.BlockSpec((1, 2, count, width, width), lambda p, z_j, where: (z_j, 0, 0, 0, 0))

    def slot(p, z_j, where):
        return z_j, where[4 + pieces[0][0] + p], 0, 0, 0

    shaped = [piece.reshape(4, 2, count, width, width) for _, count, piece in pieces]
    return pl.pallas_call(
        kernel,
        out_shape=jax.ShapeDtypeStruct((4, 4, 2, width, width), BF16),
        grid_spec=pltpu.PrefetchScalarGridSpec(
            num_scalar_prefetch=1,
            grid=(len(steps), 4),
            in_specs=[spec(count) for _, count, _ in pieces]
            + [pl.BlockSpec(memory_space=pl.ANY)] * len(kept),
            out_specs=pl.BlockSpec((1, 1, 2, width, width), slot),
        ),
        input_output_aliases={1 + len(pieces): 0} if kept else {},
        compiler_params=pltpu.CompilerParams(vmem_limit_bytes=63 * 2**20 + 2**19),
        cost_estimate=BRIEF,
        name=f"assemble_{len(kept)}",
    )(where, *shaped, *kept)


def pick(where, psi, columns, cost):
    width = psi.shape[-1]

    def kernel(where, *refs):
        for n in range(len(columns)):
            refs[len(columns) + n][...] = refs[n][0, 0]

    def column(n):
        return pl.BlockSpec((1, 1, 2, width, width), lambda g, where: (g, where[9 + n], 0, 0, 0))

    return pl.pallas_call(
        kernel,
        out_shape=[jax.ShapeDtypeStruct((8, width, width), BF16)] * len(columns),
        grid_spec=pltpu.PrefetchScalarGridSpec(
            num_scalar_prefetch=1,
            grid=(4,),
            in_specs=[column(n) for n in columns],
            out_specs=[pl.BlockSpec((2, width, width), lambda g, where: (g, 0, 0))] * len(columns),
        ),
        compiler_params=pltpu.CompilerParams(vmem_limit_bytes=VMEM),
        cost_estimate=cost,
        name=f"pick_{columns[0]}",
    )(where, *[psi] * len(columns))


def together(*arrays):
    return lax.optimization_barrier(arrays)


def body(where, wavefunction, pair_left, pair_right, left_env, left_dims, right_env, right_dims):
    width = wavefunction.shape[-1]
    sectors, terms = left_env.shape[:2]
    where = where.reshape(-1)

    index = lax.broadcasted_iota(jnp.int32, right_env.shape, 2)
    right_own = jnp.where(index < right_dims[:, None, None, None], right_env, jnp.zeros_like(right_env))
    index = lax.broadcasted_iota(jnp.int32, left_env.shape, 3)
    left_own = jnp.where(index < left_dims[:, None, None, None], left_env, jnp.zeros_like(left_env))
    left_own = left_own.reshape(sectors, terms * width, width)
    right_own = right_own.reshape(sectors, terms * width, width)

    psi = exchange(wavefunction, "y").reshape(4, 4, 2, width, width)
    right_low, right_high = both_ways(right_own, "z")
    left_low, left_high = both_ways(left_own, "x")
    other_own = shift(right_own, "c", 1, 2)
    picks = pair_left + 2 * pair_right
    psi, right_low, right_high, left_low, left_high, other_own, picks = together(
        psi, right_low, right_high, left_low, left_high, other_own, picks
    )

    codes = exchange(picks, ("y", "x"))
    for_low, for_high = pick(where, psi, (1, 2), BRIEF)
    psi_own, psi_rest = pick(where, psi, (0, 3), LONG)
    psi_low, psi_high = shift(for_low, "x", 1), shift(for_high, "x", 3)
    far = onward(right_low, right_high, "z")
    others = [other_own, shift(right_low, "c", 1, 2), shift(right_high, "c", 1, 2)]
    psi_own, psi_rest, psi_low, psi_high, codes, others[1], others[2], *far = together(
        psi_own, psi_rest, psi_low, psi_high, codes, others[1], others[2], *far
    )

    left_far = onward(*together(left_low, left_high, psi_low)[:2], "x")
    psi_far = shift(psi_rest, "x", 2)
    rights = []
    for group, other in (
        ((right_own,), (others[0],)),
        ((right_low,), (others[1],)),
        ((right_high,), (others[2],)),
        (tuple(far), tuple(shift(a, "c", 1, 2) for a in far)),
    ):
        rights += [group, other]

    def home(position, psi, lefts):
        out = combine(where, codes, psi, lefts, rights, position)
        return position, 1, exchange(out, ("z", "c"))

    own = home(0, psi_own, (left_own,))
    low = home(1, psi_low, (left_low,))
    high = home(2, psi_high, (left_high,))
    applied = assemble(where, [own, low, high])
    rest = home(3, psi_far, left_far)
    return assemble(where, [rest], applied).reshape(wavefunction.shape)


def solution(mesh):
    fine = Mesh(mesh.devices.reshape(4, 4, 4, 2), AXES)
    mapped = jax.shard_map(
        body, mesh=fine, in_specs=P(AXES), out_specs=P(AXES), check_vma=False
    )

    def run(*arrays):
        return mapped(jnp.asarray(ring_positions()), *arrays)

    return run
```

time: 334 us -> 220 us (0.66)
  Pallas kernels: 191 us -> 64.9 us
  waiting for transfers between devices: 77.6 us -> 88.5 us
    pallas_call x5 -> x8, Pallas kernels: 191 us -> 64.9 us  [the longest x4 42.2 us: combine(): pl.pallas_call(kernel, out_shape=jax.ShapeDtypeStruct((8, width, width),...]
    all_to_all x4 -> x6, starting transfers between devices: 19.6 us -> 28.5 us  [exchange(): return lax.all_to_all(array, axis, split_axis=0, concat_axis=0, tiled=True)]
    all_to_all x4 -> x6, waiting for transfers between devices: 15.2 us -> 22.4 us  [exchange(): return lax.all_to_all(array, axis, split_axis=0, concat_axis=0, tiled=True)]
    ppermute x19 -> x16, starting transfers between devices: 26.5 us -> 19.7 us  [shift(): lax.ppermute(array, axis, [(i, (i + step) % size) for i in range(size)])]
    ppermute x19 -> x16, waiting for transfers between devices: 62.3 us -> 66.1 us  [shift(): lax.ppermute(array, axis, [(i, (i + step) % size) for i in range(size)])]
  transfers between devices with their start and end apart: 23 -> 22, of which waited for: 7 -> 11; matrix products, arithmetic and copies ran while one was open for 4% -> 5% of each run, Pallas kernels for 47% -> 28%
where the time goes in v3:
time: 220 us; the launch traced here: 217 us
  waiting for transfers between devices  88.5 us (40%)
  Pallas kernels  64.9 us (30%)
  starting transfers between devices  48.1 us (22%)
  local copies, waits for them, and re-layouts  12.6 us (6%)
  other arithmetic  3.11 us (1%)
    ppermute x16, waiting for transfers between devices, shift(): lax.ppermute(array, axis, [(i, (i + step) % size) for i in range(size)])  66.1 us
    pallas_call x4, Pallas kernels, combine(): pl.pallas_call(kernel, out_shape=jax.ShapeDtypeStruct((8, width, width),...  42.2 us
    all_to_all x6, starting transfers between devices, exchange(): return lax.all_to_all(array, axis, split_axis=0, concat_axis=0, tiled=True)  28.5 us
    all_to_all x6, waiting for transfers between devices, exchange(): return lax.all_to_all(array, axis, split_axis=0, concat_axis=0, tiled=True)  22.4 us
    ppermute x16, starting transfers between devices, shift(): lax.ppermute(array, axis, [(i, (i + step) % size) for i in range(size)])  19.7 us
    pallas_call x2, Pallas kernels, assemble(): pl.pallas_call(kernel, out_shape=jax.ShapeDtypeStruct((4, 4, 2, width, wi...  13.7 us
    pallas_call x2, Pallas kernels, pick(): pl.pallas_call(kernel, out_shape=[jax.ShapeDtypeStruct((8, width, width),...  8.93 us
    slice x2, local copies, waits for them, and re-layouts, onward(): from_low[:, :half]  4.68 us
  transfers between devices with their start and end apart: 22, of which 11 were waited for; matrix products, arithmetic and copies ran while one was open for 5% of the time, Pallas kernels for 28%

profile of v3, /device:TPU:0, one launch (start us, length us, event | category | flops | bytes accessed | tf_op | source)
XLA Modules:
  0.0 217.5 jit_solution(1828988203983359281)
XLA Ops:
  0.0 5.0 %all-to-all-start = ((bf16[32,256,256]{2,1,0:T(8,128)(2,1)}), bf16[32,256,256]{2,1,0:T(8,128)(2,1)}, u32[]{:S(2)}, u32[]{:S(2)}) async-start(bf16[32,256,256]{2,1,0:T(8,128)(2,1)} %param.8), calls=%async_computation | async-start | bytes 8388608 | tf_op jit(solution)/shard_map/all_to_all | solution.py:32
  5.0 0.8 fusion
  5.9 0.1 collective-permute-start.4
  6.0 4.2 %collective-permute-start.1 = (bf16[2,2048,256]{2,1,0:T(8,128)(2,1)S(1)}, bf16[2,2048,256]{2,1,0:T(8,128)(2,1)}, u32[]{:S(2)}, u32[]{:S(2)}) collective-permute-start(bf16[2,2048,256]{2,1,0:T(8,128)(2,1)S(1)} %bitcast.13), channel_id=1, source_target_pairs={{0,24},{8,0},{16,8},{24,16},{1,25},{9,1},{17,9},{25,17},{2,26},{10... | collective-permute-start | bytes 6291464 | tf_op jit(solution)/shard_map/ppermute | solution.py:36
  10.2 0.9 fusion.1
  11.1 2.8 %collective-permute-start.3 = (bf16[2,2048,256]{2,1,0:T(8,128)(2,1)S(1)}, bf16[2,2048,256]{2,1,0:T(8,128)(2,1)S(1)}, u32[]{:S(2)}, u32[]{:S(2)}) collective-permute-start(bf16[2,2048,256]{2,1,0:T(8,128)(2,1)S(1)} %bitcast.19), channel_id=1, source_target_pairs={{0,6},{2,0},{4,2},{6,4},{1,7},{3,1},{5,3},{7,5},{8,14},{10,8},{12,... | collective-permute-start | bytes 6291464 | tf_op jit(solution)/shard_map/ppermute | solution.py:36
  13.9 41.7 %collective-permute-done.1.refs_6_.refs_5_ = bf16[2,2048,256]{2,1,0:T(8,128)(2,1)} collective-permute-done((bf16[2,2048,256]{2,1,0:T(8,128)(2,1)S(1)}, bf16[2,2048,256]{2,1,0:T(8,128)(2,1)}, u32[]{:S(2)}, u32[]{:S(2)}) %collective-permute-start.1) | collective-permute-done | bytes 2097184 | tf_op jit(solution)/shard_map/ppermute | solution.py:36
  55.6 3.5 %collective-permute-done.refs_4_.refs_3_ = bf16[2,2048,256]{2,1,0:T(8,128)(2,1)} collective-permute-done((bf16[2,2048,256]{2,1,0:T(8,128)(2,1)S(1)}, bf16[2,2048,256]{2,1,0:T(8,128)(2,1)}, u32[]{:S(2)}, u32[]{:S(2)}) %collective-permute-start) | collective-permute-done | bytes 2097184 | tf_op jit(solution)/shard_map/ppermute | solution.py:36
  59.2 1.3 copy-done.4
  60.5 2.1 collective-permute-done.2.refs_0_
  62.6 1.3 slice.13
  63.9 3.0 %collective-permute-start.10 = (bf16[2,1024,256]{2,1,0:T(8,128)(2,1)S(1)}, bf16[2,1024,256]{2,1,0:T(8,128)(2,1)S(1)}, u32[]{:S(2)}, u32[]{:S(2)}) collective-permute-start(bf16[2,1024,256]{2,1,0:T(8,128)(2,1)S(1)} %slice.13), channel_id=1, source_target_pairs={{0,24},{8,0},{16,8},{24,16},{1,25},{9,1},{17,9},{25,17},{2,26},{10... | collective-permute-start | bytes 3145736 | tf_op jit(solution)/shard_map/ppermute | solution.py:36
  66.9 1.2 dynamic-slice_bitcast_fusion.where
  68.1 2.4 %slice.12 = bf16[2,1024,256]{2,1,0:T(8,128)(2,1)} slice(bf16[2,2048,256]{2,1,0:T(8,128)(2,1)} %collective-permute-done.refs_4_.refs_3_), slice={[0:2], [0:1024], [0:256]} | slice | bytes 2097152 | tf_op jit(solution)/shard_map/slice | solution.py:45
  70.5 0.5 collective-permute-start.8
  71.0 0.7 all_to_all.24
  71.7 5.8 %all-to-all-start.1 = ((s32[16,2,1]{1,2,0:T(1,128)}), s32[16,2,1]{1,2,0:T(1,128)}, u32[]{:S(2)}, u32[]{:S(2)}) async-start(s32[16,2,1]{1,2,0:T(1,128)} %bitcast.4), calls=%async_computation.1 | async-start | bytes 16384 | tf_op jit(solution)/shard_map/all_to_all | solution.py:32
  77.6 4.5 %pick_1.1 = (bf16[8,256,256]{2,1,0:T(8,128)(2,1)}, bf16[8,256,256]{2,1,0:T(8,128)(2,1)}) custom-call(s32[13]{0:T(128)} %dynamic-slice_bitcast_fusion.where, bf16[4,4,2,256,256]{4,3,2,1,0:T(8,128)(2,1)} %bitcast.1.refs_0_.refs_1_, bf16[4,4,2,256,256]{4,3,2,1,0:T(8,128)(2,1)} %bitcast.1.refs_0_.refs_1_), custom_call_target="tpu_custom_call" | custom-call | flops 1 | bytes 1 | tf_op jit(solution)/shard_map/pick_1/pallas_call | solution.py:203
  82.1 1.8 collective-permute-start.5
  83.9 4.3 %collective-permute-done.10.refs_9_.refs_8_ = bf16[2,1024,256]{2,1,0:T(8,128)(2,1)S(1)} collective-permute-done((bf16[2,1024,256]{2,1,0:T(8,128)(2,1)S(1)}, bf16[2,1024,256]{2,1,0:T(8,128)(2,1)S(1)}, u32[]{:S(2)}, u32[]{:S(2)}) %collective-permute-start.10) | collective-permute-done | bytes 1048608 | tf_op jit(solution)/shard_map/ppermute | solution.py:36
  88.2 1.8 collective-permute-start.6
  90.0 4.5 %pick_0.1 = (bf16[8,256,256]{2,1,0:T(8,128)(2,1)}, bf16[8,256,256]{2,1,0:T(8,128)(2,1)}) custom-call(s32[13]{0:T(128)} %dynamic-slice_bitcast_fusion.where, bf16[4,4,2,256,256]{4,3,2,1,0:T(8,128)(2,1)} %bitcast.1.refs_0_.refs_1_, bf16[4,4,2,256,256]{4,3,2,1,0:T(8,128)(2,1)} %bitcast.1.refs_0_.refs_1_), custom_call_target="tpu_custom_call" | custom-call | flops 999999995904 | bytes 1 | tf_op jit(solution)/shard_map/pick_0/pallas_call | solution.py:203
  94.5 0.6 broadcast.11
  95.1 1.4 reduce.3
  96.6 0.7 all_to_all.26.codes
  97.2 6.7 %collective-permute-done.9.refs_8_.refs_7_ = bf16[2,1024,256]{2,1,0:T(8,128)(2,1)} collective-permute-done((bf16[2,1024,256]{2,1,0:T(8,128)(2,1)}, bf16[2,1024,256]{2,1,0:T(8,128)(2,1)}, u32[]{:S(2)}, u32[]{:S(2)}) %collective-permute-start.9) | collective-permute-done | bytes 1048608 | tf_op jit(solution)/shard_map/ppermute | solution.py:36
  103.9 4.5 %collective-permute-done.5.psi_ref = bf16[8,256,256]{2,1,0:T(8,128)(2,1)} collective-permute-done((bf16[8,256,256]{2,1,0:T(8,128)(2,1)}, bf16[8,256,256]{2,1,0:T(8,128)(2,1)}, u32[]{:S(2)}, u32[]{:S(2)}) %collective-permute-start.5) | collective-permute-done | bytes 1048608 | tf_op jit(solution)/shard_map/ppermute | solution.py:36
  108.4 3.2 %collective-permute-done.6.psi_ref = bf16[8,256,256]{2,1,0:T(8,128)(2,1)} collective-permute-done((bf16[8,256,256]{2,1,0:T(8,128)(2,1)}, bf16[8,256,256]{2,1,0:T(8,128)(2,1)}, u32[]{:S(2)}, u32[]{:S(2)}) %collective-permute-start.6) | collective-permute-done | bytes 1048608 | tf_op jit(solution)/shard_map/ppermute | solution.py:36
  111.7 0.5 collective-permute-start.15
  112.2 2.3 %slice.14 = bf16[2,1024,256]{2,1,0:T(8,128)(2,1)} slice(bf16[2,2048,256]{2,1,0:T(8,128)(2,1)} %collective-permute-done.2.refs_0_), slice={[0:2], [0:1024], [0:256]} | slice | bytes 2097152 | tf_op jit(solution)/shard_map/slice | solution.py:45
  114.5 1.0 slice.15
  115.5 3.3 %collective-permute-start.13 = (bf16[2,1024,256]{2,1,0:T(8,128)(2,1)}, bf16[2,1024,256]{2,1,0:T(8,128)(2,1)}, u32[]{:S(2)}, u32[]{:S(2)}) collective-permute-start(bf16[2,1024,256]{2,1,0:T(8,128)(2,1)} %slice.15), channel_id=1, source_target_pairs={{0,6},{2,0},{4,2},{6,4},{1,7},{3,1},{5,3},{7,5},{8,14},{10,8},{12,... | collective-permute-start | bytes 3145736 | tf_op jit(solution)/shard_map/ppermute | solution.py:36
  118.9 1.5 collective-permute-start.11
  120.3 1.1 copy-done.10
  121.4 10.6 %combine_0.1 = bf16[8,256,256]{2,1,0:T(8,128)(2,1)} custom-call(s32[13]{0:T(128)} %dynamic-slice_bitcast_fusion.where, s32[32]{0:T(128)} %all_to_all.26.codes, bf16[8,256,256]{2,1,0:T(8,128)(2,1)} %get-tuple-element.47.psi_ref, bf16[2,2048,256]{2,1,0:T(8,128)(2,1)} %bitcast.21, bf16[2,2048,256]{2,1,0:T(8,128)(2,1)} %bitcast.15, ...), custom_call_target="tpu_custom_call" | custom-call | flops 999999995904 | bytes 1 | tf_op jit(solution)/shard_map/combine_0/pallas_call | solution.py:130
  132.0 4.7 %all-to-all-start.3 = ((bf16[8,256,256]{2,1,0:T(8,128)(2,1)}), bf16[8,256,256]{2,1,0:T(8,128)(2,1)}, u32[]{:S(2)}, u32[]{:S(2)}) async-start(bf16[8,256,256]{2,1,0:T(8,128)(2,1)} %combine_0.1), calls=%async_computation.3 | async-start | bytes 2097152 | tf_op jit(solution)/shard_map/all_to_all | solution.py:32
  136.7 10.5 %combine_1.1 = bf16[8,256,256]{2,1,0:T(8,128)(2,1)} custom-call(s32[13]{0:T(128)} %dynamic-slice_bitcast_fusion.where, s32[32]{0:T(128)} %all_to_all.26.codes, bf16[8,256,256]{2,1,0:T(8,128)(2,1)} %collective-permute-done.5.psi_ref, bf16[2,2048,256]{2,1,0:T(8,128)(2,1)} %collective-permute-done.2.refs_0_, bf16[2,2048,256]{2,1,0:T(8,128)(2,1)} %bitcast.16, ...), custom_call_target="tpu_custom_call" | custom-call | flops 999999995904 | bytes 1 | tf_op jit(solution)/shard_map/combine_1/pallas_call | solution.py:130
  147.3 5.5 %all-to-all-done.3 = bf16[8,256,256]{2,1,0:T(8,128)(2,1)} async-done(((bf16[8,256,256]{2,1,0:T(8,128)(2,1)}), bf16[8,256,256]{2,1,0:T(8,128)(2,1)}, u32[]{:S(2)}, u32[]{:S(2)}) %all-to-all-start.3) | async-done | bytes 1048608 | tf_op jit(solution)/shard_map/all_to_all | solution.py:32
  152.8 4.4 %all-to-all-start.4 = ((bf16[8,256,256]{2,1,0:T(8,128)(2,1)}), bf16[8,256,256]{2,1,0:T(8,128)(2,1)}, u32[]{:S(2)}, u32[]{:S(2)}) async-start(bf16[8,256,256]{2,1,0:T(8,128)(2,1)} %combine_1.1), calls=%async_computation.4 | async-start | bytes 2097152 | tf_op jit(solution)/shard_map/all_to_all | solution.py:32
  157.2 10.5 %combine_2.1 = bf16[8,256,256]{2,1,0:T(8,128)(2,1)} custom-call(s32[13]{0:T(128)} %dynamic-slice_bitcast_fusion.where, s32[32]{0:T(128)} %all_to_all.26.codes, bf16[8,256,256]{2,1,0:T(8,128)(2,1)} %collective-permute-done.6.psi_ref, bf16[2,2048,256]{2,1,0:T(8,128)(2,1)} %copy-done.4, bf16[2,2048,256]{2,1,0:T(8,128)(2,1)} %bitcast.17, ...), custom_call_target="tpu_custom_call" | custom-call | flops 999999995904 | bytes 1 | tf_op jit(solution)/shard_map/combine_2/pallas_call | solution.py:130
  167.8 5.2 %all-to-all-done.4 = bf16[8,256,256]{2,1,0:T(8,128)(2,1)} async-done(((bf16[8,256,256]{2,1,0:T(8,128)(2,1)}), bf16[8,256,256]{2,1,0:T(8,128)(2,1)}, u32[]{:S(2)}, u32[]{:S(2)}) %all-to-all-start.4) | async-done | bytes 1048608 | tf_op jit(solution)/shard_map/all_to_all | solution.py:32
  173.0 4.3 %all-to-all-start.5 = ((bf16[8,256,256]{2,1,0:T(8,128)(2,1)}), bf16[8,256,256]{2,1,0:T(8,128)(2,1)}, u32[]{:S(2)}, u32[]{:S(2)}) async-start(bf16[8,256,256]{2,1,0:T(8,128)(2,1)} %combine_2.1), calls=%async_computation.5 | async-start | bytes 2097152 | tf_op jit(solution)/shard_map/all_to_all | solution.py:32
  177.3 10.6 %combine_3.1 = bf16[8,256,256]{2,1,0:T(8,128)(2,1)} custom-call(s32[13]{0:T(128)} %dynamic-slice_bitcast_fusion.where, s32[32]{0:T(128)} %all_to_all.26.codes, bf16[8,256,256]{2,1,0:T(8,128)(2,1)} %collective-permute-done.11.psi_ref, bf16[2,1024,256]{2,1,0:T(8,128)(2,1)} %collective-permute-done.12.refs_0_, ...), custom_call_target="tpu_custom_call" | custom-call | flops 999999995904 | bytes 1 | tf_op jit(solution)/shard_map/combine_3/pallas_call | solution.py:130
  187.9 5.3 %all-to-all-done.5 = bf16[8,256,256]{2,1,0:T(8,128)(2,1)} async-done(((bf16[8,256,256]{2,1,0:T(8,128)(2,1)}), bf16[8,256,256]{2,1,0:T(8,128)(2,1)}, u32[]{:S(2)}, u32[]{:S(2)}) %all-to-all-start.5) | async-done | bytes 1048608 | tf_op jit(solution)/shard_map/all_to_all | solution.py:32
  193.2 4.3 %all-to-all-start.2 = ((bf16[8,256,256]{2,1,0:T(8,128)(2,1)}), bf16[8,256,256]{2,1,0:T(8,128)(2,1)}, u32[]{:S(2)}, u32[]{:S(2)}) async-start(bf16[8,256,256]{2,1,0:T(8,128)(2,1)} %combine_3.1), calls=%async_computation.2 | async-start | bytes 2097152 | tf_op jit(solution)/shard_map/all_to_all | solution.py:32
  197.5 9.7 %assemble_0.1.refs_1_ = bf16[4,4,2,256,256]{4,3,2,1,0:T(8,128)(2,1)} custom-call(s32[13]{0:T(128)} %dynamic-slice_bitcast_fusion.where, bf16[4,2,1,256,256]{4,3,2,1,0:T(8,128)(2,1)} %bitcast.6.refs_0_, bf16[4,2,1,256,256]{4,3,2,1,0:T(8,128)(2,1)} %bitcast.7.refs_1_, bf16[4,2,1,256,256]{4,3,2,1,0:T(8,128)(2,1)} %bitcast.8.refs_2_), custom_call_target="tpu_custom_call" | custom-call | flops 1 | bytes 1 | tf_op jit(solution)/shard_map/assemble_0/pallas_call | solution.py:176
  207.2 6.3 %all-to-all-done.2 = bf16[8,256,256]{2,1,0:T(8,128)(2,1)} async-done(((bf16[8,256,256]{2,1,0:T(8,128)(2,1)}), bf16[8,256,256]{2,1,0:T(8,128)(2,1)}, u32[]{:S(2)}, u32[]{:S(2)}) %all-to-all-start.2) | async-done | bytes 1048608 | tf_op jit(solution)/shard_map/all_to_all | solution.py:32
  213.4 4.0 %assemble_1.1 = bf16[4,4,2,256,256]{4,3,2,1,0:T(8,128)(2,1)} custom-call(s32[13]{0:T(128)} %dynamic-slice_bitcast_fusion.where, bf16[4,2,1,256,256]{4,3,2,1,0:T(8,128)(2,1)} %bitcast.5.refs_0_, bf16[4,4,2,256,256]{4,3,2,1,0:T(8,128)(2,1)} %assemble_0.1.refs_1_), custom_call_target="tpu_custom_call", output_to_operand_aliasing={{}: (2, {})} | custom-call | flops 1 | bytes 1 | tf_op jit(solution)/shard_map/assemble_1/pallas_call | solution.py:176
  (42 shorter events, 0.2 us)
Async XLA Ops:
  0.0 5.0 %copy-start.6 = (s32[2]{0:T(128)S(1)}, s32[2]{0:T(128)}, u32[]{:S(2)}) copy-start(s32[2]{0:T(128)} %param.14) | copy-start | bytes 28
  0.0 5.0 %copy-start = (bf16[2,8,256,256]{3,2,1,0:T(8,128)(2,1)S(1)}, bf16[2,8,256,256]{3,2,1,0:T(8,128)(2,1)}, u32[]{:S(2)}) copy-start(bf16[2,8,256,256]{3,2,1,0:T(8,128)(2,1)} %param.13) | copy-start | bytes 6291460
  0.0 62.6 %all-to-all-start = ((bf16[32,256,256]{2,1,0:T(8,128)(2,1)}), bf16[32,256,256]{2,1,0:T(8,128)(2,1)}, u32[]{:S(2)}, u32[]{:S(2)}) async-start(bf16[32,256,256]{2,1,0:T(8,128)(2,1)} %param.8), calls=%async_computation | async-start | bytes 8388608 | tf_op jit(solution)/shard_map/all_to_all | solution.py:32
  5.0 5.1 %copy-start.1 = (bf16[2,8,256,256]{3,2,1,0:T(8,128)(2,1)S(1)}, bf16[2,8,256,256]{3,2,1,0:T(8,128)(2,1)}, u32[]{:S(2)}) copy-start(bf16[2,8,256,256]{3,2,1,0:T(8,128)(2,1)} %param.11) | copy-start | bytes 6291460
  5.0 5.1 %copy-start.7 = (s32[2]{0:T(128)S(1)}, s32[2]{0:T(128)}, u32[]{:S(2)}) copy-start(s32[2]{0:T(128)} %param.12) | copy-start | bytes 28
  5.8 5.2 %copy-start.2 = (bf16[2,8,256,256]{3,2,1,0:T(8,128)(2,1)}, bf16[2,8,256,256]{3,2,1,0:T(8,128)(2,1)S(1)}, u32[]{:S(2)}) copy-start(bf16[2,8,256,256]{3,2,1,0:T(8,128)(2,1)S(1)} %fusion) | copy-start | bytes 6291460
  5.8 8.1 %copy-start.11 = (s32[32]{0:T(128)S(1)}, s32[32]{0:T(128)}, u32[]{:S(2)}) copy-start(s32[32]{0:T(128)} %param.9) | copy-start | bytes 388
  5.8 8.0 %copy-start.12 = (s32[32]{0:T(128)S(1)}, s32[32]{0:T(128)}, u32[]{:S(2)}) copy-start(s32[32]{0:T(128)} %param.10) | copy-start | bytes 388
  5.9 8.1 %collective-permute-start.4 = (bf16[2,2048,256]{2,1,0:T(8,128)(2,1)S(1)}, bf16[2,2048,256]{2,1,0:T(8,128)(2,1)S(1)}, u32[]{:S(2)}, u32[]{:S(2)}) collective-permute-start(bf16[2,2048,256]{2,1,0:T(8,128)(2,1)S(1)} %bitcast.12), channel_id=1, source_target_pairs={{0,1},{1,0},{2,3},{3,2},{4,5},{5,4},{6,7},{7,6},{8,9},{9,8},{10,11... | collective-permute-start | bytes 6291464 | tf_op jit(solution)/shard_map/ppermute | solution.py:36
  6.0 49.7 %collective-permute-start.1 = (bf16[2,2048,256]{2,1,0:T(8,128)(2,1)S(1)}, bf16[2,2048,256]{2,1,0:T(8,128)(2,1)}, u32[]{:S(2)}, u32[]{:S(2)}) collective-permute-start(bf16[2,2048,256]{2,1,0:T(8,128)(2,1)S(1)} %bitcast.13), channel_id=1, source_target_pairs={{0,24},{8,0},{16,8},{24,16},{1,25},{9,1},{17,9},{25,17},{2,26},{10... | collective-permute-start | bytes 6291464 | tf_op jit(solution)/shard_map/ppermute | solution.py:36
  10.1 49.0 %collective-permute-start = (bf16[2,2048,256]{2,1,0:T(8,128)(2,1)S(1)}, bf16[2,2048,256]{2,1,0:T(8,128)(2,1)}, u32[]{:S(2)}, u32[]{:S(2)}) collective-permute-start(bf16[2,2048,256]{2,1,0:T(8,128)(2,1)S(1)} %bitcast.14), channel_id=1, source_target_pairs={{0,8},{8,16},{16,24},{24,0},{1,9},{9,17},{17,25},{25,1},{2,10},{10... | collective-permute-start | bytes 6291464 | tf_op jit(solution)/shard_map/ppermute | solution.py:36
  11.0 48.1 %copy-start.3 = (bf16[2,8,256,256]{3,2,1,0:T(8,128)(2,1)}, bf16[2,8,256,256]{3,2,1,0:T(8,128)(2,1)S(1)}, u32[]{:S(2)}) copy-start(bf16[2,8,256,256]{3,2,1,0:T(8,128)(2,1)S(1)} %fusion.1) | copy-start | bytes 6291460
  11.1 48.1 %collective-permute-start.3 = (bf16[2,2048,256]{2,1,0:T(8,128)(2,1)S(1)}, bf16[2,2048,256]{2,1,0:T(8,128)(2,1)S(1)}, u32[]{:S(2)}, u32[]{:S(2)}) collective-permute-start(bf16[2,2048,256]{2,1,0:T(8,128)(2,1)S(1)} %bitcast.19), channel_id=1, source_target_pairs={{0,6},{2,0},{4,2},{6,4},{1,7},{3,1},{5,3},{7,5},{8,14},{10,8},{12,... | collective-permute-start | bytes 6291464 | tf_op jit(solution)/shard_map/ppermute | solution.py:36
  13.9 48.7 %collective-permute-start.2 = (bf16[2,2048,256]{2,1,0:T(8,128)(2,1)S(1)}, bf16[2,2048,256]{2,1,0:T(8,128)(2,1)}, u32[]{:S(2)}, u32[]{:S(2)}) collective-permute-start(bf16[2,2048,256]{2,1,0:T(8,128)(2,1)S(1)} %bitcast.20), channel_id=1, source_target_pairs={{0,2},{2,4},{4,6},{6,0},{1,3},{3,5},{5,7},{7,1},{8,10},{10,12},{12... | collective-permute-start | bytes 6291464 | tf_op jit(solution)/shard_map/ppermute | solution.py:36
  13.9 45.2 %copy-start.8 = (bf16[2,2048,256]{2,1,0:T(8,128)(2,1)}, bf16[2,2048,256]{2,1,0:T(8,128)(2,1)S(1)}, u32[]{:S(2)}) copy-start(bf16[2,2048,256]{2,1,0:T(8,128)(2,1)S(1)} %collective-permute-done.4.refs_3_.refs_2_) | copy-start | bytes 6291460
  59.2 1.3 copy-start.4
  63.9 24.3 %collective-permute-start.10 = (bf16[2,1024,256]{2,1,0:T(8,128)(2,1)S(1)}, bf16[2,1024,256]{2,1,0:T(8,128)(2,1)S(1)}, u32[]{:S(2)}, u32[]{:S(2)}) collective-permute-start(bf16[2,1024,256]{2,1,0:T(8,128)(2,1)S(1)} %slice.13), channel_id=1, source_target_pairs={{0,24},{8,0},{16,8},{24,16},{1,25},{9,1},{17,9},{25,17},{2,26},{10... | collective-permute-start | bytes 3145736 | tf_op jit(solution)/shard_map/ppermute | solution.py:36
  70.5 41.1 %collective-permute-start.7 = (bf16[2,2048,256]{2,1,0:T(8,128)(2,1)}, bf16[2,2048,256]{2,1,0:T(8,128)(2,1)}, u32[]{:S(2)}, u32[]{:S(2)}) collective-permute-start(bf16[2,2048,256]{2,1,0:T(8,128)(2,1)} %collective-permute-done.refs_4_.refs_3_), channel_id=1, source_target_pairs={{0,1},{1,0},{2,3},{3,2},{4,5},{5,4},{6,7},{7,6},{8,9},{9,8},{10,11... | collective-permute-start | bytes 6291464 | tf_op jit(solution)/shard_map/ppermute | solution.py:36
  70.5 41.1 %collective-permute-start.8 = (bf16[2,2048,256]{2,1,0:T(8,128)(2,1)}, bf16[2,2048,256]{2,1,0:T(8,128)(2,1)}, u32[]{:S(2)}, u32[]{:S(2)}) collective-permute-start(bf16[2,2048,256]{2,1,0:T(8,128)(2,1)} %collective-permute-done.1.refs_6_.refs_5_), channel_id=1, source_target_pairs={{0,1},{1,0},{2,3},{3,2},{4,5},{5,4},{6,7},{7,6},{8,9},{9,8},{10,11... | collective-permute-start | bytes 6291464 | tf_op jit(solution)/shard_map/ppermute | solution.py:36
  71.7 22.8 %all-to-all-start.1 = ((s32[16,2,1]{1,2,0:T(1,128)}), s32[16,2,1]{1,2,0:T(1,128)}, u32[]{:S(2)}, u32[]{:S(2)}) async-start(s32[16,2,1]{1,2,0:T(1,128)} %bitcast.4), calls=%async_computation.1 | async-start | bytes 16384 | tf_op jit(solution)/shard_map/all_to_all | solution.py:32
  77.5 26.4 %collective-permute-start.9 = (bf16[2,1024,256]{2,1,0:T(8,128)(2,1)}, bf16[2,1024,256]{2,1,0:T(8,128)(2,1)}, u32[]{:S(2)}, u32[]{:S(2)}) collective-permute-start(bf16[2,1024,256]{2,1,0:T(8,128)(2,1)} %slice.12), channel_id=1, source_target_pairs={{0,8},{8,16},{16,24},{24,0},{1,9},{9,17},{17,25},{25,1},{2,10},{10... | collective-permute-start | bytes 3145736 | tf_op jit(solution)/shard_map/ppermute | solution.py:36
  82.1 26.3 %collective-permute-start.5 = (bf16[8,256,256]{2,1,0:T(8,128)(2,1)}, bf16[8,256,256]{2,1,0:T(8,128)(2,1)}, u32[]{:S(2)}, u32[]{:S(2)}) collective-permute-start(bf16[8,256,256]{2,1,0:T(8,128)(2,1)} %get-tuple-element.30), channel_id=1, source_target_pairs={{0,2},{2,4},{4,6},{6,0},{1,3},{3,5},{5,7},{7,1},{8,10},{10,12},{12... | collective-permute-start | bytes 3145736 | tf_op jit(solution)/shard_map/ppermute | solution.py:36
  88.2 1.8 copy-start.9
  88.2 23.4 %collective-permute-start.6 = (bf16[8,256,256]{2,1,0:T(8,128)(2,1)}, bf16[8,256,256]{2,1,0:T(8,128)(2,1)}, u32[]{:S(2)}, u32[]{:S(2)}) collective-permute-start(bf16[8,256,256]{2,1,0:T(8,128)(2,1)} %get-tuple-element.31), channel_id=1, source_target_pairs={{0,6},{2,0},{4,2},{6,4},{1,7},{3,1},{5,3},{7,5},{8,14},{10,8},{12,... | collective-permute-start | bytes 3145736 | tf_op jit(solution)/shard_map/ppermute | solution.py:36
  94.5 20.0 %copy-start.5 = (bf16[2,2048,256]{2,1,0:T(8,128)(2,1)S(1)}, bf16[2,2048,256]{2,1,0:T(8,128)(2,1)}, u32[]{:S(2)}) copy-start(bf16[2,2048,256]{2,1,0:T(8,128)(2,1)} %copy-done.4) | copy-start | bytes 6291460
  111.7 8.7 %collective-permute-start.14 = (bf16[2,1024,256]{2,1,0:T(8,128)(2,1)}, bf16[2,1024,256]{2,1,0:T(8,128)(2,1)S(1)}, u32[]{:S(2)}, u32[]{:S(2)}) collective-permute-start(bf16[2,1024,256]{2,1,0:T(8,128)(2,1)} %collective-permute-done.9.refs_8_.refs_7_), channel_id=1, source_target_pairs={{0,1},{1,0},{2,3},{3,2},{4,5},{5,4},{6,7},{7,6},{8,9},{9,8},{10,11... | collective-permute-start | bytes 3145736 | tf_op jit(solution)/shard_map/ppermute | solution.py:36
  111.7 8.7 %collective-permute-start.15 = (bf16[2,1024,256]{2,1,0:T(8,128)(2,1)}, bf16[2,1024,256]{2,1,0:T(8,128)(2,1)}, u32[]{:S(2)}, u32[]{:S(2)}) collective-permute-start(bf16[2,1024,256]{2,1,0:T(8,128)(2,1)} %copy-done.9), channel_id=1, source_target_pairs={{0,1},{1,0},{2,3},{3,2},{4,5},{5,4},{6,7},{7,6},{8,9},{9,8},{10,11... | collective-permute-start | bytes 3145736 | tf_op jit(solution)/shard_map/ppermute | solution.py:36
  115.5 61.7 %collective-permute-start.13 = (bf16[2,1024,256]{2,1,0:T(8,128)(2,1)}, bf16[2,1024,256]{2,1,0:T(8,128)(2,1)}, u32[]{:S(2)}, u32[]{:S(2)}) collective-permute-start(bf16[2,1024,256]{2,1,0:T(8,128)(2,1)} %slice.15), channel_id=1, source_target_pairs={{0,6},{2,0},{4,2},{6,4},{1,7},{3,1},{5,3},{7,5},{8,14},{10,8},{12,... | collective-permute-start | bytes 3145736 | tf_op jit(solution)/shard_map/ppermute | solution.py:36
  118.9 58.4 %collective-permute-start.12 = (bf16[2,1024,256]{2,1,0:T(8,128)(2,1)}, bf16[2,1024,256]{2,1,0:T(8,128)(2,1)}, u32[]{:S(2)}, u32[]{:S(2)}) collective-permute-start(bf16[2,1024,256]{2,1,0:T(8,128)(2,1)} %slice.14), channel_id=1, source_target_pairs={{0,2},{2,4},{4,6},{6,0},{1,3},{3,5},{5,7},{7,1},{8,10},{10,12},{12... | collective-permute-start | bytes 3145736 | tf_op jit(solution)/shard_map/ppermute | solution.py:36
  118.9 58.4 %collective-permute-start.11 = (bf16[8,256,256]{2,1,0:T(8,128)(2,1)}, bf16[8,256,256]{2,1,0:T(8,128)(2,1)}, u32[]{:S(2)}, u32[]{:S(2)}) collective-permute-start(bf16[8,256,256]{2,1,0:T(8,128)(2,1)} %get-tuple-element.36), channel_id=1, source_target_pairs={{0,4},{2,6},{4,0},{6,2},{1,5},{3,7},{5,1},{7,3},{8,12},{10,14},{12... | collective-permute-start | bytes 3145736 | tf_op jit(solution)/shard_map/ppermute | solution.py:36
  120.3 1.1 copy-start.10
  132.0 20.8 %all-to-all-start.3 = ((bf16[8,256,256]{2,1,0:T(8,128)(2,1)}), bf16[8,256,256]{2,1,0:T(8,128)(2,1)}, u32[]{:S(2)}, u32[]{:S(2)}) async-start(bf16[8,256,256]{2,1,0:T(8,128)(2,1)} %combine_0.1), calls=%async_computation.3 | async-start | bytes 2097152 | tf_op jit(solution)/shard_map/all_to_all | solution.py:32
  152.8 20.2 %all-to-all-start.4 = ((bf16[8,256,256]{2,1,0:T(8,128)(2,1)}), bf16[8,256,256]{2,1,0:T(8,128)(2,1)}, u32[]{:S(2)}, u32[]{:S(2)}) async-start(bf16[8,256,256]{2,1,0:T(8,128)(2,1)} %combine_1.1), calls=%async_computation.4 | async-start | bytes 2097152 | tf_op jit(solution)/shard_map/all_to_all | solution.py:32
  173.0 20.2 %all-to-all-start.5 = ((bf16[8,256,256]{2,1,0:T(8,128)(2,1)}), bf16[8,256,256]{2,1,0:T(8,128)(2,1)}, u32[]{:S(2)}, u32[]{:S(2)}) async-start(bf16[8,256,256]{2,1,0:T(8,128)(2,1)} %combine_2.1), calls=%async_computation.5 | async-start | bytes 2097152 | tf_op jit(solution)/shard_map/all_to_all | solution.py:32
  193.2 20.2 %all-to-all-start.2 = ((bf16[8,256,256]{2,1,0:T(8,128)(2,1)}), bf16[8,256,256]{2,1,0:T(8,128)(2,1)}, u32[]{:S(2)}, u32[]{:S(2)}) async-start(bf16[8,256,256]{2,1,0:T(8,128)(2,1)} %combine_3.1), calls=%async_computation.2 | async-start | bytes 2097152 | tf_op jit(solution)/shard_map/all_to_all | solution.py:32

commit v4 on v3

v4 whole, which is shorter than its diff:
```python
import jax
import jax.numpy as jnp
import numpy as np
from jax import lax
from jax.experimental import pallas as pl
from jax.experimental.pallas import tpu as pltpu
from jax.sharding import Mesh, PartitionSpec as P

AXES = ("y", "z", "x", "c")
OFFSETS = (0, 3, 1, 2)
STEPS = (0, 1, 3, 2)
SLOTS = 3
BF16 = jnp.bfloat16
BRIEF = pl.CostEstimate(flops=1, bytes_accessed=1, transcendentals=0)
LONG = pl.CostEstimate(flops=10**12, bytes_accessed=1, transcendentals=0)
VMEM = 60 * 2**20


def ring_positions():
    rows = []
    for y, z, x, c in np.ndindex(4, 4, 4, 2):
        rows.append(
            [(z + o) % 4 for o in OFFSETS]
            + [(x + o) % 4 for o in OFFSETS]
            + [c]
            + [(x + o) % 4 for o in STEPS]
        )
    return np.asarray(rows, np.int32)


def exchange(array, axis):
    return lax.all_to_all(array, axis, split_axis=0, concat_axis=0, tiled=True)


def shift(array, axis, step, size=4):
    return lax.ppermute(array, axis, [(i, (i + step) % size) for i in range(size)])


def both_ways(array, axis):
    return shift(array, axis, 1), shift(array, axis, 3)


def onward(from_low, from_high, axis):
    half = from_low.shape[1] // 2
    return shift(from_low[:, :half], axis, 1), shift(from_high[:, half:], axis, 3)


def combine(where, codes, psis, lefts, rights, first, z_first=0, kept=None):
    width = psis[0].shape[-1]
    depth = sum(a.shape[1] for a in lefts[0])
    terms = depth // width
    count = len(lefts)
    left_parts = [a for group in lefts for a in group]
    right_parts = [a for pair in rights for group in pair for a in group]
    steps = len(rights)
    slots = min(SLOTS, steps)
    each = [(core, k) for core in range(2) for k in range(count)]

    def code_of(step, core, k, where, codes):
        return codes[(where[z_first + step] * 4 + where[4 + first + k]) * 2 + (where[8] ^ core)]

    def kernel(where, codes, *refs):
        refs = list(refs)
        psi_refs = [refs.pop(0) for _ in psis]
        left_refs = [[refs.pop(0) for _ in group] for group in lefts]
        right_refs = [[[refs.pop(0) for _ in group] for group in pair] for pair in rights]
        out_ref, left_buf, right_buf, partial, left_sems, sems = refs[kept is not None :]
        step = pl.program_id(0)

        def copy_left(k, go):
            row = 0
            for n, ref in enumerate(left_refs[k]):
                size = ref.shape[1]
                copy = pltpu.make_async_copy(
                    ref, left_buf.at[k, :, pl.ds(row, size)], left_sems.at[k, n]
                )
                copy.start() if go else copy.wait()
                row += size

        def fetch(at, go):
            slot = lax.rem(at, slots)
            for n_step in range(steps):

                @pl.when(at == n_step)
                def _(n_step=n_step):
                    for n_block, (core, k) in enumerate(each):
                        right = code_of(n_step, core, k, where, codes) // 2
                        row = 0
                        for n, ref in enumerate(right_refs[n_step][core]):
                            size = ref.shape[1]
                            copy = pltpu.make_async_copy(
                                ref.at[right],
                                right_buf.at[slot, n_block, pl.ds(row, size)],
                                sems.at[slot, n_block, n],
                            )
                            copy.start() if go else copy.wait()
                            row += size

        @pl.when(step == 0)
        def _():
            for k in range(count):
                copy_left(k, True)
            for ahead in range(max(slots - 1, 1)):
                fetch(ahead, True)

        if slots > 1:

            @pl.when(step + slots - 1 < steps)
            def _():
                fetch(step + slots - 1, True)

        @pl.when(step == 0)
        def _():
            for k in range(count):
                copy_left(k, False)

        fetch(step, False)
        slot = lax.rem(step, slots)
        for n_block, (core, k) in enumerate(each):
            left = code_of(step, core, k, where, codes) % 2
            block = psi_refs[k][where[8] ^ core]
            for t in range(terms):
                product = jnp.dot(
                    left_buf[k, left, t * width : (t + 1) * width],
                    block,
                    preferred_element_type=jnp.float32,
                )
                partial[n_block, :, t * width : (t + 1) * width] = product.astype(BF16)
        for n_block, (core, k) in enumerate(each):
            total = jnp.dot(
                partial[n_block], right_buf[slot, n_block], preferred_element_type=jnp.float32
            )
            out_ref[(where[8] ^ core) * count + k] = total.astype(BF16)

    in_place = pl.BlockSpec(memory_space=pl.ANY)
    of_g = lambda step, where, codes: (where[z_first + step], 0, 0)
    parts = max(len(group) for pair in rights for group in pair)
    extra = [] if kept is None else [kept]
    operands = [*psis, *left_parts, *right_parts, *extra]
    return pl.pallas_call(
        kernel,
        out_shape=jax.ShapeDtypeStruct((8 * count, width, width), BF16),
        grid_spec=pltpu.PrefetchScalarGridSpec(
            num_scalar_prefetch=2,
            grid=(steps,),
            in_specs=[pl.BlockSpec((2, width, width), of_g)] * count
            + [in_place] * (len(operands) - count),
            out_specs=pl.BlockSpec((2 * count, width, width), of_g),
            scratch_shapes=[
                pltpu.VMEM((count, 2, depth, width), BF16),
                pltpu.VMEM((slots, len(each), depth, width), BF16),
                pltpu.VMEM((len(each), width, depth), BF16),
                pltpu.SemaphoreType.DMA((count, max(len(group) for group in lefts))),
                pltpu.SemaphoreType.DMA((slots, len(each), parts)),
            ],
        ),
        input_output_aliases={1 + len(operands): 0} if extra else {},
        compiler_params=pltpu.CompilerParams(
            dimension_semantics=("arbitrary",), vmem_limit_bytes=VMEM
        ),
        cost_estimate=LONG,
        name=f"combine_{first}_{z_first}",
    )(where, codes, *operands)


def assemble(where, pieces):
    width = pieces[0][1].shape[-1]
    counts = [piece.shape[0] // 8 for _, piece in pieces]

    def kernel(where, *refs):
        *piece_refs, out_ref = refs
        for (first, _), count, ref in zip(pieces, counts, piece_refs):
            for k in range(count):
                out_ref[0, where[4 + first + k]] = ref[0, :, k]

    at_z = lambda z_j, where: (z_j, 0, 0, 0, 0)
    return pl.pallas_call(
        kernel,
        out_shape=jax.ShapeDtypeStruct((4, 4, 2, width, width), BF16),
        grid_spec=pltpu.PrefetchScalarGridSpec(
            num_scalar_prefetch=1,
            grid=(4,),
            in_specs=[pl.BlockSpec((1, 2, count, width, width), at_z) for count in counts],
            out_specs=pl.BlockSpec((1, 4, 2, width, width), at_z),
        ),
        compiler_params=pltpu.CompilerParams(vmem_limit_bytes=VMEM),
        cost_estimate=BRIEF,
        name="assemble",
    )(where, *[p.reshape(4, 2, n, width, width) for (_, p), n in zip(pieces, counts)])


def pick(where, psi, columns, cost):
    width = psi.shape[-1]

    def kernel(where, *refs):
        for n in range(len(columns)):
            refs[len(columns) + n][...] = refs[n][0, 0]

    def column(n):
        return pl.BlockSpec((1, 1, 2, width, width), lambda g, where: (g, where[9 + n], 0, 0, 0))

    return pl.pallas_call(
        kernel,
        out_shape=[jax.ShapeDtypeStruct((8, width, width), BF16)] * len(columns),
        grid_spec=pltpu.PrefetchScalarGridSpec(
            num_scalar_prefetch=1,
            grid=(4,),
            in_specs=[column(n) for n in columns],
            out_specs=[pl.BlockSpec((2, width, width), lambda g, where: (g, 0, 0))] * len(columns),
        ),
        compiler_params=pltpu.CompilerParams(vmem_limit_bytes=VMEM),
        cost_estimate=cost,
        name=f"pick_{columns[0]}",
    )(where, *[psi] * len(columns))


def together(*arrays):
    return lax.optimization_barrier(arrays)


def body(where, wavefunction, pair_left, pair_right, left_env, left_dims, right_env, right_dims):
    width = wavefunction.shape[-1]
    sectors, terms = left_env.shape[:2]
    where = where.reshape(-1)

    index = lax.broadcasted_iota(jnp.int32, right_env.shape, 2)
    right_own = jnp.where(index < right_dims[:, None, None, None], right_env, jnp.zeros_like(right_env))
    index = lax.broadcasted_iota(jnp.int32, left_env.shape, 3)
    left_own = jnp.where(index < left_dims[:, None, None, None], left_env, jnp.zeros_like(left_env))
    left_own = left_own.reshape(sectors, terms * width, width)
    right_own = right_own.reshape(sectors, terms * width, width)

    psi = exchange(wavefunction, "y").reshape(4, 4, 2, width, width)
    right_low, right_high = both_ways(right_own, "z")
    left_low, left_high = both_ways(left_own, "x")
    other_own = shift(right_own, "c", 1, 2)
    picks = pair_left + 2 * pair_right
    psi, right_low, right_high, left_low, left_high, other_own, picks = together(
        psi, right_low, right_high, left_low, left_high, other_own, picks
    )

    for_low, for_high = pick(where, psi, (1, 2), BRIEF)
    far = onward(right_low, right_high, "z")
    for_low, for_high, psi, picks = together(for_low, for_high, psi, picks)
    psi_low, psi_high = shift(for_low, "x", 1), shift(for_high, "x", 3)
    codes = exchange(picks, ("y", "x"))
    psi_own, psi_rest = pick(where, psi, (0, 3), LONG)
    psi_rest, *to_core = together(psi_rest, right_low, right_high)
    other_low, other_high = [shift(a, "c", 1, 2) for a in to_core]
    rights = [
        ((right_own,), (other_own,)),
        ((right_low,), (other_low,)),
        ((right_high,), (other_high,)),
    ]
    left_own_ = (left_own,)
    own = combine(where, codes, [psi_own], [left_own_], rights, 0)
    halves = left_low[:, : terms * width // 2], left_high[:, terms * width // 2 :]
    psi_rest, psi_low, psi_high, own, *far_halves = together(
        psi_rest, psi_low, psi_high, own, *halves, *far
    )
    *halves, far_low, far_high = far_halves
    far = far_low, far_high

    left_far = shift(halves[0], "x", 1), shift(halves[1], "x", 3)
    psi_far = shift(psi_rest, "x", 2)
    rights.append((far, tuple(shift(a, "c", 1, 2) for a in far)))

    own = combine(where, codes, [psi_own], [left_own_], rights[3:], 0, 3, own)
    own = exchange(own, ("z", "c"))
    near = combine(where, codes, [psi_low, psi_high], [(left_low,), (left_high,)], rights, 1)
    near = exchange(near, ("z", "c"))
    rest = combine(where, codes, [psi_far], [left_far], rights, 3)
    rest = exchange(rest, ("z", "c"))
    applied = assemble(where, [(0, own), (1, near)])
    applied = lax.dynamic_update_slice(
        applied, rest.reshape(4, 1, 2, width, width), (0, where[7], 0, 0, 0)
    )
    return applied.reshape(wavefunction.shape)


def solution(mesh):
    fine = Mesh(mesh.devices.reshape(4, 4, 4, 2), AXES)
    mapped = jax.shard_map(
        body, mesh=fine, in_specs=P(AXES), out_specs=P(AXES), check_vma=False
    )

    def run(*arrays):
        return mapped(jnp.asarray(ring_positions()), *arrays)

    return run
```

time: 220 us -> 206 us (0.936)
  Pallas kernels: 64.9 us -> 55 us
  waiting for transfers between devices: 88.5 us -> 82.2 us
  local copies, waits for them, and re-layouts: 12.6 us -> 15.9 us
  starting transfers between devices: 48.1 us -> 45.3 us
    pallas_call x2 -> x1, Pallas kernels: 13.7 us -> 5.04 us  [assemble(): pl.pallas_call(kernel, out_shape=jax.ShapeDtypeStruct((4, 4, 2, width, wi...]
    all_to_all x6 -> x5, waiting for transfers between devices: 22.4 us -> 15.5 us  [exchange(): return lax.all_to_all(array, axis, split_axis=0, concat_axis=0, tiled=True)]
    slice x0 -> x3, local copies, waits for them, and re-layouts: none -> 5.18 us  [the longest x1 2.31 us: body(): left_low[:, :terms * width // 2]]
    all_to_all x6 -> x5, starting transfers between devices: 28.5 us -> 25.2 us  [exchange(): return lax.all_to_all(array, axis, split_axis=0, concat_axis=0, tiled=True)]
    slice x2 -> x1, local copies, waits for them, and re-layouts: 4.68 us -> 2.3 us  [onward(): from_low[:, :half]]
  transfers between devices with their start and end apart: 22 -> 21, of which waited for: 11 -> 8; matrix products, arithmetic and copies ran while one was open for 5% -> 8% of each run, Pallas kernels for 28% -> 23%
where the time goes in v4:
time: 206 us; the launch traced here: 205 us
  waiting for transfers between devices  82.2 us (40%)
  Pallas kernels  55 us (27%)
  starting transfers between devices  45.3 us (22%)
  local copies, waits for them, and re-layouts  15.9 us (8%)
  other arithmetic  4.25 us (2%)
  between operations  2.13 us (1%)
    ppermute x16, waiting for transfers between devices, shift(): lax.ppermute(array, axis, [(i, (i + step) % size) for i in range(size)])  66.7 us
    pallas_call x4, Pallas kernels, combine(): pl.pallas_call(kernel, out_shape=jax.ShapeDtypeStruct((8 * count, width,...  41 us
    all_to_all x5, starting transfers between devices, exchange(): return lax.all_to_all(array, axis, split_axis=0, concat_axis=0, tiled=True)  25.2 us
    ppermute x16, starting transfers between devices, shift(): lax.ppermute(array, axis, [(i, (i + step) % size) for i in range(size)])  20.1 us
    all_to_all x5, waiting for transfers between devices, exchange(): return lax.all_to_all(array, axis, split_axis=0, concat_axis=0, tiled=True)  15.5 us
    pallas_call x2, Pallas kernels, pick(): pl.pallas_call(kernel, out_shape=[jax.ShapeDtypeStruct((8, width, width),...  8.9 us
    pallas_call x1, Pallas kernels, assemble(): pl.pallas_call(kernel, out_shape=jax.ShapeDtypeStruct((4, 4, 2, width, wi...  5.04 us
  transfers between devices with their start and end apart: 21, of which 8 were waited for; matrix products, arithmetic and copies ran while one was open for 8% of the time, Pallas kernels for 23%

profile of v4, /device:TPU:0, one launch (start us, length us, event | category | flops | bytes accessed | tf_op | source)
XLA Modules:
  0.0 204.8 jit_solution(13328281896479182382)
XLA Ops:
  0.0 5.0 %all-to-all-start = ((bf16[32,256,256]{2,1,0:T(8,128)(2,1)}), bf16[32,256,256]{2,1,0:T(8,128)(2,1)}, u32[]{:S(2)}, u32[]{:S(2)}) async-start(bf16[32,256,256]{2,1,0:T(8,128)(2,1)} %param.8), calls=%async_computation | async-start | bytes 8388608 | tf_op jit(solution)/shard_map/all_to_all | solution.py:32
  5.0 2.2 %fusion = bf16[2,8,256,256]{3,2,1,0:T(8,128)(2,1)} fusion(bf16[2,8,256,256]{3,2,1,0:T(8,128)(2,1)S(1)} %copy-done, s32[2]{0:T(128)S(1)} %copy-done.3), kind=kLoop, calls=%fused_computation.2 | loop fusion | flops 2097152 | bytes 4194312 | tf_op jit(solution)/shard_map/jit(_where)/select_n | solution.py:227
  7.2 2.0 collective-permute-start
  9.2 2.1 %collective-permute-start.1 = (bf16[2,2048,256]{2,1,0:T(8,128)(2,1)}, bf16[2,2048,256]{2,1,0:T(8,128)(2,1)}, u32[]{:S(2)}, u32[]{:S(2)}) collective-permute-start(bf16[2,2048,256]{2,1,0:T(8,128)(2,1)} %bitcast.2.refs_2_.refs_4_.refs_3_), channel_id=1, source_target_pairs={{0,24},{8,0},{16,8},{24,16},{1,25},{9,1},{17,9},{25,17},{2,26},{10... | collective-permute-start | bytes 6291464 | tf_op jit(solution)/shard_map/ppermute | solution.py:36
  11.3 0.9 fusion.1
  12.2 1.6 collective-permute-start.2
  13.8 1.7 collective-permute-start.3
  15.5 1.2 constant_dynamic-slice_fusion
  16.8 0.5 multiply_add_fusion
  17.3 40.0 %collective-permute-done.refs_4_.refs_6_.refs_5_ = bf16[2,2048,256]{2,1,0:T(8,128)(2,1)} collective-permute-done((bf16[2,2048,256]{2,1,0:T(8,128)(2,1)}, bf16[2,2048,256]{2,1,0:T(8,128)(2,1)}, u32[]{:S(2)}, u32[]{:S(2)}) %collective-permute-start) | collective-permute-done | bytes 2097184 | tf_op jit(solution)/shard_map/ppermute | solution.py:36
  57.3 3.4 %collective-permute-done.2.refs_2_ = bf16[2,2048,256]{2,1,0:T(8,128)(2,1)} collective-permute-done((bf16[2,2048,256]{2,1,0:T(8,128)(2,1)S(1)}, bf16[2,2048,256]{2,1,0:T(8,128)(2,1)}, u32[]{:S(2)}, u32[]{:S(2)}) %collective-permute-start.2) | collective-permute-done | bytes 2097184 | tf_op jit(solution)/shard_map/ppermute | solution.py:36
  60.7 4.4 %pick_1.1 = (bf16[8,256,256]{2,1,0:T(8,128)(2,1)}, bf16[8,256,256]{2,1,0:T(8,128)(2,1)}) custom-call(s32[13]{0:T(128)} %get-tuple-element.58.where, bf16[4,4,2,256,256]{4,3,2,1,0:T(8,128)(2,1)} %bitcast.1.refs_0_.refs_1_, bf16[4,4,2,256,256]{4,3,2,1,0:T(8,128)(2,1)} %bitcast.1.refs_0_.refs_1_), custom_call_target="tpu_custom_call" | custom-call | flops 1 | bytes 1 | tf_op jit(solution)/shard_map/pick_1/pallas_call | solution.py:202
  65.2 4.5 %pick_0.1 = (bf16[8,256,256]{2,1,0:T(8,128)(2,1)}, bf16[8,256,256]{2,1,0:T(8,128)(2,1)}) custom-call(s32[13]{0:T(128)} %get-tuple-element.58.where, bf16[4,4,2,256,256]{4,3,2,1,0:T(8,128)(2,1)} %bitcast.1.refs_0_.refs_1_, bf16[4,4,2,256,256]{4,3,2,1,0:T(8,128)(2,1)} %bitcast.1.refs_0_.refs_1_), custom_call_target="tpu_custom_call" | custom-call | flops 999999995904 | bytes 1 | tf_op jit(solution)/shard_map/pick_0/pallas_call | solution.py:202
  69.6 0.5 collective-permute-start.8
  70.1 2.3 %slice.18 = bf16[2,1024,256]{2,1,0:T(8,128)(2,1)} slice(bf16[2,2048,256]{2,1,0:T(8,128)(2,1)} %collective-permute-done.refs_4_.refs_6_.refs_5_), slice={[0:2], [0:1024], [0:256]} | slice | bytes 2097152 | tf_op jit(solution)/shard_map/slice | solution.py:45
  72.4 2.3 %slice.19 = bf16[2,1024,256]{2,1,0:T(8,128)(2,1)} slice(bf16[2,2048,256]{2,1,0:T(8,128)(2,1)} %collective-permute-done.1.refs_6_.refs_8_.refs_7_), slice={[0:2], [1024:2048], [0:256]} | slice | bytes 2097152 | tf_op jit(solution)/shard_map/slice | solution.py:45
  74.7 0.7 all_to_all.20
  75.4 7.0 %all-to-all-start.1 = ((s32[16,2,1]{1,2,0:T(1,128)}), s32[16,2,1]{1,2,0:T(1,128)S(1)}, u32[]{:S(2)}, u32[]{:S(2)}) async-start(s32[16,2,1]{1,2,0:T(1,128)} %bitcast.4), calls=%async_computation.1 | async-start | bytes 16384 | tf_op jit(solution)/shard_map/all_to_all | solution.py:32
  82.4 1.9 collective-permute-start.5
  84.3 1.4 collective-permute-start.6
  85.7 2.3 %slice.16 = bf16[2,1024,256]{2,1,0:T(8,128)(2,1)} slice(bf16[2,2048,256]{2,1,0:T(8,128)(2,1)} %collective-permute-done.2.refs_2_), slice={[0:2], [0:1024], [0:256]} | slice | bytes 2097152 | tf_op jit(solution)/shard_map/slice | solution.py:257
  88.0 2.3 %slice.17 = bf16[2,1024,256]{2,1,0:T(8,128)(2,1)} slice(bf16[2,2048,256]{2,1,0:T(8,128)(2,1)} %collective-permute-done.3.refs_3_), slice={[0:2], [1024:2048], [0:256]} | slice | bytes 2097152 | tf_op jit(solution)/shard_map/slice | solution.py:257
  90.3 0.6 broadcast.11
  90.9 0.6 reduce.3
  91.5 0.6 all_to_all.22.codes
  92.1 3.2 %collective-permute-start.10 = (bf16[2,1024,256]{2,1,0:T(8,128)(2,1)}, bf16[2,1024,256]{2,1,0:T(8,128)(2,1)}, u32[]{:S(2)}, u32[]{:S(2)}) collective-permute-start(bf16[2,1024,256]{2,1,0:T(8,128)(2,1)} %slice.19), channel_id=1, source_target_pairs={{0,24},{8,0},{16,8},{24,16},{1,25},{9,1},{17,9},{25,17},{2,26},{10... | collective-permute-start | bytes 3145736 | tf_op jit(solution)/shard_map/ppermute | solution.py:36
  95.4 8.6 %combine_0_0.1.refs_6_ = bf16[8,256,256]{2,1,0:T(8,128)(2,1)} custom-call(s32[13]{0:T(128)} %get-tuple-element.58.where, s32[32]{0:T(128)} %all_to_all.22.codes, bf16[8,256,256]{2,1,0:T(8,128)(2,1)} %get-tuple-element.37.refs_0_, bf16[2,2048,256]{2,1,0:T(8,128)(2,1)} %bitcast.17, bf16[2,2048,256]{2,1,0:T(8,128)(2,1)} %bitcast.2.refs_2_.refs_4_.refs_3_, ...), custom_call_target="tpu_custom_call" | custom-call | flops 999999995904 | bytes 1 | tf_op jit(solution)/shard_map/combine_0_0/pallas_call | solution.py:140
  104.0 4.9 %collective-permute-done.5.refs_0_ = bf16[8,256,256]{2,1,0:T(8,128)(2,1)} collective-permute-done((bf16[8,256,256]{2,1,0:T(8,128)(2,1)}, bf16[8,256,256]{2,1,0:T(8,128)(2,1)}, u32[]{:S(2)}, u32[]{:S(2)}) %collective-permute-start.5) | collective-permute-done | bytes 1048608 | tf_op jit(solution)/shard_map/ppermute | solution.py:36
  108.9 7.2 %collective-permute-done.9.refs_2_.refs_10_.refs_9_ = bf16[2,1024,256]{2,1,0:T(8,128)(2,1)} collective-permute-done((bf16[2,1024,256]{2,1,0:T(8,128)(2,1)}, bf16[2,1024,256]{2,1,0:T(8,128)(2,1)}, u32[]{:S(2)}, u32[]{:S(2)}) %collective-permute-start.9) | collective-permute-done | bytes 1048608 | tf_op jit(solution)/shard_map/ppermute | solution.py:36
  116.1 1.1 collective-permute-done.10.refs_3_.refs_11_.refs_10_
  117.2 0.5 collective-permute-start.12
  117.7 1.9 collective-permute-start.13
  119.6 0.6 collective-permute-start.14
  120.2 2.7 %collective-permute-start.15 = (bf16[2,1024,256]{2,1,0:T(8,128)(2,1)}, bf16[2,1024,256]{2,1,0:T(8,128)(2,1)}, u32[]{:S(2)}, u32[]{:S(2)}) collective-permute-start(bf16[2,1024,256]{2,1,0:T(8,128)(2,1)} %slice.17), channel_id=1, source_target_pairs={{0,6},{2,0},{4,2},{6,4},{1,7},{3,1},{5,3},{7,5},{8,14},{10,8},{12,... | collective-permute-start | bytes 3145736 | tf_op jit(solution)/shard_map/ppermute | solution.py:36
  122.9 1.0 copy-done.8
  123.8 1.1 copy-done.9
  124.9 5.8 %combine_0_3.1 = bf16[8,256,256]{2,1,0:T(8,128)(2,1)} custom-call(s32[13]{0:T(128)} %get-tuple-element.58.where, s32[32]{0:T(128)} %all_to_all.22.codes, bf16[8,256,256]{2,1,0:T(8,128)(2,1)} %get-tuple-element.37.refs_0_, bf16[2,2048,256]{2,1,0:T(8,128)(2,1)} %bitcast.18, ...), custom_call_target="tpu_custom_call", output_to_operand_aliasing={{}: (8, {})} | custom-call | flops 999999995904 | bytes 1 | tf_op jit(solution)/shard_map/combine_0_3/pallas_call | solution.py:140
  130.7 4.9 %all-to-all-start.2 = ((bf16[8,256,256]{2,1,0:T(8,128)(2,1)}), bf16[8,256,256]{2,1,0:T(8,128)(2,1)}, u32[]{:S(2)}, u32[]{:S(2)}) async-start(bf16[8,256,256]{2,1,0:T(8,128)(2,1)} %combine_0_3.1), calls=%async_computation.2 | async-start | bytes 2097152 | tf_op jit(solution)/shard_map/all_to_all | solution.py:32
  135.6 16.6 %combine_1_0.1 = bf16[16,256,256]{2,1,0:T(8,128)(2,1)} custom-call(s32[13]{0:T(128)} %get-tuple-element.58.where, s32[32]{0:T(128)} %all_to_all.22.codes, bf16[8,256,256]{2,1,0:T(8,128)(2,1)} %collective-permute-done.5.refs_0_, bf16[8,256,256]{2,1,0:T(8,128)(2,1)} %collective-permute-done.6.refs_1_, bf16[2,2048,256]{2,1,0:T(8,128)(2,1)} %collective-permute-done.2.refs_2_, ...), custom_call_target="tpu_custom_call" | custom-call | flops 999999995904 | bytes 1 | tf_op jit(solution)/shard_map/combine_1_0/pallas_call | solution.py:140
  152.2 4.8 %all-to-all-start.3 = ((bf16[16,256,256]{2,1,0:T(8,128)(2,1)}), bf16[16,256,256]{2,1,0:T(8,128)(2,1)}, u32[]{:S(2)}, u32[]{:S(2)}) async-start(bf16[16,256,256]{2,1,0:T(8,128)(2,1)} %combine_1_0.1), calls=%async_computation.3 | async-start | bytes 4194304 | tf_op jit(solution)/shard_map/all_to_all | solution.py:32
  157.0 10.0 %collective-permute-done.14.refs_1_ = bf16[2,1024,256]{2,1,0:T(8,128)(2,1)} collective-permute-done((bf16[2,1024,256]{2,1,0:T(8,128)(2,1)}, bf16[2,1024,256]{2,1,0:T(8,128)(2,1)}, u32[]{:S(2)}, u32[]{:S(2)}) %collective-permute-start.14) | collective-permute-done | bytes 1048608 | tf_op jit(solution)/shard_map/ppermute | solution.py:36
  167.1 10.1 %combine_3_0.1 = bf16[8,256,256]{2,1,0:T(8,128)(2,1)} custom-call(s32[13]{0:T(128)} %get-tuple-element.58.where, s32[32]{0:T(128)} %all_to_all.22.codes, bf16[8,256,256]{2,1,0:T(8,128)(2,1)} %collective-permute-done.13.refs_0_, bf16[2,1024,256]{2,1,0:T(8,128)(2,1)} %collective-permute-done.14.refs_1_, bf16[2,1024,256]{2,1,0:T(8,128)(2,1)} %collective-permute-done.15.refs_2_, ...), custom_call_target="tpu_custom_call" | custom-call | flops 999999995904 | bytes 1 | tf_op jit(solution)/shard_map/combine_3_0/pallas_call | solution.py:140
  177.2 7.2 %all-to-all-done.3 = bf16[16,256,256]{2,1,0:T(8,128)(2,1)} async-done(((bf16[16,256,256]{2,1,0:T(8,128)(2,1)}), bf16[16,256,256]{2,1,0:T(8,128)(2,1)}, u32[]{:S(2)}, u32[]{:S(2)}) %all-to-all-start.3) | async-done | bytes 2097184 | tf_op jit(solution)/shard_map/all_to_all | solution.py:32
  184.3 3.6 %all-to-all-start.4 = ((bf16[8,256,256]{2,1,0:T(8,128)(2,1)}), bf16[8,256,256]{2,1,0:T(8,128)(2,1)S(1)}, u32[]{:S(2)}, u32[]{:S(2)}) async-start(bf16[8,256,256]{2,1,0:T(8,128)(2,1)} %combine_3_0.1), calls=%async_computation.4 | async-start | bytes 2097152 | tf_op jit(solution)/shard_map/all_to_all | solution.py:32
  187.9 0.6 slice.20
  190.4 5.0 %assemble.1 = bf16[4,4,2,256,256]{4,3,2,1,0:T(8,128)(2,1)} custom-call(s32[13]{0:T(128)} %get-tuple-element.58.where, bf16[4,2,1,256,256]{4,3,2,1,0:T(8,128)(2,1)} %bitcast.5.refs_0_, bf16[4,2,2,256,256]{4,3,2,1,0:T(8,128)(2,1)} %bitcast.6.refs_1_), custom_call_target="tpu_custom_call" | custom-call | flops 1 | bytes 1 | tf_op jit(solution)/shard_map/assemble/pallas_call | solution.py:177
  195.5 8.3 %all-to-all-done.4 = bf16[8,256,256]{2,1,0:T(8,128)(2,1)S(1)} async-done(((bf16[8,256,256]{2,1,0:T(8,128)(2,1)}), bf16[8,256,256]{2,1,0:T(8,128)(2,1)S(1)}, u32[]{:S(2)}, u32[]{:S(2)}) %all-to-all-start.4) | async-done | bytes 1048608 | tf_op jit(solution)/shard_map/all_to_all | solution.py:32
  203.8 1.0 constant_dynamic-update-slice_fusion
  (39 shorter events, 0.1 us)
Async XLA Ops:
  0.0 5.0 %copy-start = (bf16[2,8,256,256]{3,2,1,0:T(8,128)(2,1)S(1)}, bf16[2,8,256,256]{3,2,1,0:T(8,128)(2,1)}, u32[]{:S(2)}) copy-start(bf16[2,8,256,256]{3,2,1,0:T(8,128)(2,1)} %param.13) | copy-start | bytes 6291460
  0.0 5.0 %copy-start.3 = (s32[2]{0:T(128)S(1)}, s32[2]{0:T(128)}, u32[]{:S(2)}) copy-start(s32[2]{0:T(128)} %param.14) | copy-start | bytes 28
  0.0 60.7 %all-to-all-start = ((bf16[32,256,256]{2,1,0:T(8,128)(2,1)}), bf16[32,256,256]{2,1,0:T(8,128)(2,1)}, u32[]{:S(2)}, u32[]{:S(2)}) async-start(bf16[32,256,256]{2,1,0:T(8,128)(2,1)} %param.8), calls=%async_computation | async-start | bytes 8388608 | tf_op jit(solution)/shard_map/all_to_all | solution.py:32
  5.0 6.3 %copy-start.1 = (bf16[2,8,256,256]{3,2,1,0:T(8,128)(2,1)S(1)}, bf16[2,8,256,256]{3,2,1,0:T(8,128)(2,1)}, u32[]{:S(2)}) copy-start(bf16[2,8,256,256]{3,2,1,0:T(8,128)(2,1)} %param.11) | copy-start | bytes 6291460
  5.0 6.3 %copy-start.4 = (s32[2]{0:T(128)S(1)}, s32[2]{0:T(128)}, u32[]{:S(2)}) copy-start(s32[2]{0:T(128)} %param.12) | copy-start | bytes 28
  7.2 9.6 %copy-start.10 = (s32[32]{0:T(128)S(1)}, s32[32]{0:T(128)}, u32[]{:S(2)}) copy-start(s32[32]{0:T(128)} %param.9) | copy-start | bytes 388
  7.2 9.6 %copy-start.11 = (s32[32]{0:T(128)S(1)}, s32[32]{0:T(128)}, u32[]{:S(2)}) copy-start(s32[32]{0:T(128)} %param.10) | copy-start | bytes 388
  7.2 50.1 %collective-permute-start = (bf16[2,2048,256]{2,1,0:T(8,128)(2,1)}, bf16[2,2048,256]{2,1,0:T(8,128)(2,1)}, u32[]{:S(2)}, u32[]{:S(2)}) collective-permute-start(bf16[2,2048,256]{2,1,0:T(8,128)(2,1)} %bitcast.2.refs_2_.refs_4_.refs_3_), channel_id=1, source_target_pairs={{0,8},{8,16},{16,24},{24,0},{1,9},{9,17},{17,25},{25,1},{2,10},{10... | collective-permute-start | bytes 6291464 | tf_op jit(solution)/shard_map/ppermute | solution.py:36
  9.2 48.1 %collective-permute-start.1 = (bf16[2,2048,256]{2,1,0:T(8,128)(2,1)}, bf16[2,2048,256]{2,1,0:T(8,128)(2,1)}, u32[]{:S(2)}, u32[]{:S(2)}) collective-permute-start(bf16[2,2048,256]{2,1,0:T(8,128)(2,1)} %bitcast.2.refs_2_.refs_4_.refs_3_), channel_id=1, source_target_pairs={{0,24},{8,0},{16,8},{24,16},{1,25},{9,1},{17,9},{25,17},{2,26},{10... | collective-permute-start | bytes 6291464 | tf_op jit(solution)/shard_map/ppermute | solution.py:36
  12.2 52.9 %copy-start.2 = (bf16[2,8,256,256]{3,2,1,0:T(8,128)(2,1)}, bf16[2,8,256,256]{3,2,1,0:T(8,128)(2,1)S(1)}, u32[]{:S(2)}) copy-start(bf16[2,8,256,256]{3,2,1,0:T(8,128)(2,1)S(1)} %fusion.1) | copy-start | bytes 6291460
  12.2 48.5 %collective-permute-start.2 = (bf16[2,2048,256]{2,1,0:T(8,128)(2,1)S(1)}, bf16[2,2048,256]{2,1,0:T(8,128)(2,1)}, u32[]{:S(2)}, u32[]{:S(2)}) collective-permute-start(bf16[2,2048,256]{2,1,0:T(8,128)(2,1)S(1)} %bitcast.15), channel_id=1, source_target_pairs={{0,2},{2,4},{4,6},{6,0},{1,3},{3,5},{5,7},{7,1},{8,10},{10,12},{12... | collective-permute-start | bytes 6291464 | tf_op jit(solution)/shard_map/ppermute | solution.py:36
  13.8 46.9 %collective-permute-start.3 = (bf16[2,2048,256]{2,1,0:T(8,128)(2,1)S(1)}, bf16[2,2048,256]{2,1,0:T(8,128)(2,1)}, u32[]{:S(2)}, u32[]{:S(2)}) collective-permute-start(bf16[2,2048,256]{2,1,0:T(8,128)(2,1)S(1)} %bitcast.16), channel_id=1, source_target_pairs={{0,6},{2,0},{4,2},{6,4},{1,7},{3,1},{5,3},{7,5},{8,14},{10,8},{12,... | collective-permute-start | bytes 6291464 | tf_op jit(solution)/shard_map/ppermute | solution.py:36
  15.5 45.2 %collective-permute-start.4 = (bf16[2,2048,256]{2,1,0:T(8,128)(2,1)}, bf16[2,2048,256]{2,1,0:T(8,128)(2,1)}, u32[]{:S(2)}, u32[]{:S(2)}) collective-permute-start(bf16[2,2048,256]{2,1,0:T(8,128)(2,1)} %bitcast.2.refs_2_.refs_4_.refs_3_), channel_id=1, source_target_pairs={{0,1},{1,0},{2,3},{3,2},{4,5},{5,4},{6,7},{7,6},{8,9},{9,8},{10,11... | collective-permute-start | bytes 6291464 | tf_op jit(solution)/shard_map/ppermute | solution.py:36
  69.6 5.1 %copy-start.5 = (s32[32]{0:T(128)S(1)}, s32[32]{0:T(128)}, u32[]{:S(2)}) copy-start(s32[32]{0:T(128)} %multiply_add_fusion) | copy-start | bytes 388
  69.6 22.5 %collective-permute-start.7 = (bf16[2,2048,256]{2,1,0:T(8,128)(2,1)}, bf16[2,2048,256]{2,1,0:T(8,128)(2,1)S(1)}, u32[]{:S(2)}, u32[]{:S(2)}) collective-permute-start(bf16[2,2048,256]{2,1,0:T(8,128)(2,1)} %collective-permute-done.refs_4_.refs_6_.refs_5_), channel_id=1, source_target_pairs={{0,1},{1,0},{2,3},{3,2},{4,5},{5,4},{6,7},{7,6},{8,9},{9,8},{10,11... | collective-permute-start | bytes 6291464 | tf_op jit(solution)/shard_map/ppermute | solution.py:36
  69.6 25.7 %collective-permute-start.8 = (bf16[2,2048,256]{2,1,0:T(8,128)(2,1)}, bf16[2,2048,256]{2,1,0:T(8,128)(2,1)}, u32[]{:S(2)}, u32[]{:S(2)}) collective-permute-start(bf16[2,2048,256]{2,1,0:T(8,128)(2,1)} %collective-permute-done.1.refs_6_.refs_8_.refs_7_), channel_id=1, source_target_pairs={{0,1},{1,0},{2,3},{3,2},{4,5},{5,4},{6,7},{7,6},{8,9},{9,8},{10,11... | collective-permute-start | bytes 6291464 | tf_op jit(solution)/shard_map/ppermute | solution.py:36
  75.4 14.9 %all-to-all-start.1 = ((s32[16,2,1]{1,2,0:T(1,128)}), s32[16,2,1]{1,2,0:T(1,128)S(1)}, u32[]{:S(2)}, u32[]{:S(2)}) async-start(s32[16,2,1]{1,2,0:T(1,128)} %bitcast.4), calls=%async_computation.1 | async-start | bytes 16384 | tf_op jit(solution)/shard_map/all_to_all | solution.py:32
  82.4 26.5 %collective-permute-start.5 = (bf16[8,256,256]{2,1,0:T(8,128)(2,1)}, bf16[8,256,256]{2,1,0:T(8,128)(2,1)}, u32[]{:S(2)}, u32[]{:S(2)}) collective-permute-start(bf16[8,256,256]{2,1,0:T(8,128)(2,1)} %get-tuple-element.42), channel_id=1, source_target_pairs={{0,2},{2,4},{4,6},{6,0},{1,3},{3,5},{5,7},{7,1},{8,10},{10,12},{12... | collective-permute-start | bytes 3145736 | tf_op jit(solution)/shard_map/ppermute | solution.py:36
  84.3 24.6 %collective-permute-start.6 = (bf16[8,256,256]{2,1,0:T(8,128)(2,1)}, bf16[8,256,256]{2,1,0:T(8,128)(2,1)}, u32[]{:S(2)}, u32[]{:S(2)}) collective-permute-start(bf16[8,256,256]{2,1,0:T(8,128)(2,1)} %get-tuple-element.43), channel_id=1, source_target_pairs={{0,6},{2,0},{4,2},{6,4},{1,7},{3,1},{5,3},{7,5},{8,14},{10,8},{12,... | collective-permute-start | bytes 3145736 | tf_op jit(solution)/shard_map/ppermute | solution.py:36
  90.3 25.8 %collective-permute-start.9 = (bf16[2,1024,256]{2,1,0:T(8,128)(2,1)}, bf16[2,1024,256]{2,1,0:T(8,128)(2,1)}, u32[]{:S(2)}, u32[]{:S(2)}) collective-permute-start(bf16[2,1024,256]{2,1,0:T(8,128)(2,1)} %slice.18), channel_id=1, source_target_pairs={{0,8},{8,16},{16,24},{24,0},{1,9},{9,17},{17,25},{25,1},{2,10},{10... | collective-permute-start | bytes 3145736 | tf_op jit(solution)/shard_map/ppermute | solution.py:36
  92.1 3.2 %copy-start.7 = (bf16[2,2048,256]{2,1,0:T(8,128)(2,1)}, bf16[2,2048,256]{2,1,0:T(8,128)(2,1)S(1)}, u32[]{:S(2)}) copy-start(bf16[2,2048,256]{2,1,0:T(8,128)(2,1)S(1)} %collective-permute-done.7.refs_5_.refs_7_.refs_6_) | copy-start | bytes 6291460
  92.1 25.1 %collective-permute-start.10 = (bf16[2,1024,256]{2,1,0:T(8,128)(2,1)}, bf16[2,1024,256]{2,1,0:T(8,128)(2,1)}, u32[]{:S(2)}, u32[]{:S(2)}) collective-permute-start(bf16[2,1024,256]{2,1,0:T(8,128)(2,1)} %slice.19), channel_id=1, source_target_pairs={{0,24},{8,0},{16,8},{24,16},{1,25},{9,1},{17,9},{25,17},{2,26},{10... | collective-permute-start | bytes 3145736 | tf_op jit(solution)/shard_map/ppermute | solution.py:36
  117.2 5.6 %collective-permute-start.11 = (bf16[2,1024,256]{2,1,0:T(8,128)(2,1)}, bf16[2,1024,256]{2,1,0:T(8,128)(2,1)S(1)}, u32[]{:S(2)}, u32[]{:S(2)}) collective-permute-start(bf16[2,1024,256]{2,1,0:T(8,128)(2,1)} %collective-permute-done.9.refs_2_.refs_10_.refs_9_), channel_id=1, source_target_pairs={{0,1},{1,0},{2,3},{3,2},{4,5},{5,4},{6,7},{7,6},{8,9},{9,8},{10,11... | collective-permute-start | bytes 3145736 | tf_op jit(solution)/shard_map/ppermute | solution.py:36
  117.2 5.6 %collective-permute-start.12 = (bf16[2,1024,256]{2,1,0:T(8,128)(2,1)}, bf16[2,1024,256]{2,1,0:T(8,128)(2,1)S(1)}, u32[]{:S(2)}, u32[]{:S(2)}) collective-permute-start(bf16[2,1024,256]{2,1,0:T(8,128)(2,1)} %collective-permute-done.10.refs_3_.refs_11_.refs_10_), channel_id=1, source_target_pairs={{0,1},{1,0},{2,3},{3,2},{4,5},{5,4},{6,7},{7,6},{8,9},{9,8},{10,11... | collective-permute-start | bytes 3145736 | tf_op jit(solution)/shard_map/ppermute | solution.py:36
  117.7 39.3 %collective-permute-start.13 = (bf16[8,256,256]{2,1,0:T(8,128)(2,1)}, bf16[8,256,256]{2,1,0:T(8,128)(2,1)}, u32[]{:S(2)}, u32[]{:S(2)}) collective-permute-start(bf16[8,256,256]{2,1,0:T(8,128)(2,1)} %get-tuple-element.54), channel_id=1, source_target_pairs={{0,4},{2,6},{4,0},{6,2},{1,5},{3,7},{5,1},{7,3},{8,12},{10,14},{12... | collective-permute-start | bytes 3145736 | tf_op jit(solution)/shard_map/ppermute | solution.py:36
  119.6 47.5 %collective-permute-start.14 = (bf16[2,1024,256]{2,1,0:T(8,128)(2,1)}, bf16[2,1024,256]{2,1,0:T(8,128)(2,1)}, u32[]{:S(2)}, u32[]{:S(2)}) collective-permute-start(bf16[2,1024,256]{2,1,0:T(8,128)(2,1)} %slice.16), channel_id=1, source_target_pairs={{0,2},{2,4},{4,6},{6,0},{1,3},{3,5},{5,7},{7,1},{8,10},{10,12},{12... | collective-permute-start | bytes 3145736 | tf_op jit(solution)/shard_map/ppermute | solution.py:36
  120.2 46.9 %collective-permute-start.15 = (bf16[2,1024,256]{2,1,0:T(8,128)(2,1)}, bf16[2,1024,256]{2,1,0:T(8,128)(2,1)}, u32[]{:S(2)}, u32[]{:S(2)}) collective-permute-start(bf16[2,1024,256]{2,1,0:T(8,128)(2,1)} %slice.17), channel_id=1, source_target_pairs={{0,6},{2,0},{4,2},{6,4},{1,7},{3,1},{5,3},{7,5},{8,14},{10,8},{12,... | collective-permute-start | bytes 3145736 | tf_op jit(solution)/shard_map/ppermute | solution.py:36
  122.8 1.0 copy-start.8
  123.8 1.1 copy-start.9
  130.7 21.5 %all-to-all-start.2 = ((bf16[8,256,256]{2,1,0:T(8,128)(2,1)}), bf16[8,256,256]{2,1,0:T(8,128)(2,1)}, u32[]{:S(2)}, u32[]{:S(2)}) async-start(bf16[8,256,256]{2,1,0:T(8,128)(2,1)} %combine_0_3.1), calls=%async_computation.2 | async-start | bytes 2097152 | tf_op jit(solution)/shard_map/all_to_all | solution.py:32
  152.2 32.1 %all-to-all-start.3 = ((bf16[16,256,256]{2,1,0:T(8,128)(2,1)}), bf16[16,256,256]{2,1,0:T(8,128)(2,1)}, u32[]{:S(2)}, u32[]{:S(2)}) async-start(bf16[16,256,256]{2,1,0:T(8,128)(2,1)} %combine_1_0.1), calls=%async_computation.3 | async-start | bytes 4194304 | tf_op jit(solution)/shard_map/all_to_all | solution.py:32
  177.2 10.7 %copy-start.6 = (s32[1,13]{1,0:T(1,128)S(1)}, s32[1,13]{1,0:T(1,128)}, u32[]{:S(2)}) copy-start(s32[1,13]{1,0:T(1,128)} %get-tuple-element.57) | copy-start | bytes 160
  184.3 19.4 %all-to-all-start.4 = ((bf16[8,256,256]{2,1,0:T(8,128)(2,1)}), bf16[8,256,256]{2,1,0:T(8,128)(2,1)S(1)}, u32[]{:S(2)}, u32[]{:S(2)}) async-start(bf16[8,256,256]{2,1,0:T(8,128)(2,1)} %combine_3_0.1), calls=%async_computation.4 | async-start | bytes 2097152 | tf_op jit(solution)/shard_map/all_to_all | solution.py:32

commit v5 on v4

--- a/solution.py
+++ b/solution.py
@@ -47,11 +47,11 @@
 
 def combine(where, codes, psis, lefts, rights, first, z_first=0, kept=None):
     width = psis[0].shape[-1]
-    depth = sum(a.shape[1] for a in lefts[0])
+    depth = sum(a.shape[1] for a in lefts[0][0])
     terms = depth // width
     count = len(lefts)
-    left_parts = [a for group in lefts for a in group]
-    right_parts = [a for pair in rights for group in pair for a in group]
+    left_parts = [a for pair in lefts for group in pair for a in group]
+    right_parts = [a for group in rights for a in group]
     steps = len(rights)
     slots = min(SLOTS, steps)
     each = [(core, k) for core in range(2) for k in range(count)]
@@ -62,20 +62,21 @@
     def kernel(where, codes, *refs):
         refs = list(refs)
         psi_refs = [refs.pop(0) for _ in psis]
-        left_refs = [[refs.pop(0) for _ in group] for group in lefts]
-        right_refs = [[[refs.pop(0) for _ in group] for group in pair] for pair in rights]
+        left_refs = [[[refs.pop(0) for _ in group] for group in pair] for pair in lefts]
+        right_refs = [[refs.pop(0) for _ in group] for group in rights]
         out_ref, left_buf, right_buf, partial, left_sems, sems = refs[kept is not None :]
         step = pl.program_id(0)
 
         def copy_left(k, go):
-            row = 0
-            for n, ref in enumerate(left_refs[k]):
-                size = ref.shape[1]
-                copy = pltpu.make_async_copy(
-                    ref, left_buf.at[k, :, pl.ds(row, size)], left_sems.at[k, n]
-                )
-                copy.start() if go else copy.wait()
-                row += size
+            for core in range(2):
+                row = 0
+                for n, ref in enumerate(left_refs[k][core]):
+                    size = ref.shape[1]
+                    copy = pltpu.make_async_copy(
+                        ref, left_buf.at[k, core, :, pl.ds(row, size)], left_sems.at[k, core, n]
+                    )
+                    copy.start() if go else copy.wait()
+                    row += size
 
         def fetch(at, go):
             slot = lax.rem(at, slots)
@@ -86,7 +87,7 @@
                     for n_block, (core, k) in enumerate(each):
                         right = code_of(n_step, core, k, where, codes) // 2
                         row = 0
-                        for n, ref in enumerate(right_refs[n_step][core]):
+                        for n, ref in enumerate(right_refs[n_step]):
                             size = ref.shape[1]
                             copy = pltpu.make_async_copy(
                                 ref.at[right],
@@ -121,7 +122,7 @@
             block = psi_refs[k][where[8] ^ core]
             for t in range(terms):
                 product = jnp.dot(
-                    left_buf[k, left, t * width : (t + 1) * width],
+                    left_buf[k, core, left, t * width : (t + 1) * width],
                     block,
                     preferred_element_type=jnp.float32,
                 )
@@ -134,7 +135,7 @@
 
     in_place = pl.BlockSpec(memory_space=pl.ANY)
     of_g = lambda step, where, codes: (where[z_first + step], 0, 0)
-    parts = max(len(group) for pair in rights for group in pair)
+    parts = max(len(group) for group in rights)
     extra = [] if kept is None else [kept]
     operands = [*psis, *left_parts, *right_parts, *extra]
     return pl.pallas_call(
@@ -147,10 +148,10 @@
             + [in_place] * (len(operands) - count),
             out_specs=pl.BlockSpec((2 * count, width, width), of_g),
             scratch_shapes=[
-                pltpu.VMEM((count, 2, depth, width), BF16),
+                pltpu.VMEM((count, 2, 2, depth, width), BF16),
                 pltpu.VMEM((slots, len(each), depth, width), BF16),
                 pltpu.VMEM((len(each), width, depth), BF16),
-                pltpu.SemaphoreType.DMA((count, max(len(group) for group in lefts))),
+                pltpu.SemaphoreType.DMA((count, 2, max(len(pair[0]) for pair in lefts))),
                 pltpu.SemaphoreType.DMA((slots, len(each), parts)),
             ],
         ),
@@ -158,7 +159,7 @@
         compiler_params=pltpu.CompilerParams(
             dimension_semantics=("arbitrary",), vmem_limit_bytes=VMEM
         ),
-        cost_estimate=LONG,
+        cost_estimate=BRIEF if first == 3 else LONG,
         name=f"combine_{first}_{z_first}",
     )(where, codes, *operands)
 
@@ -189,29 +190,10 @@
     )(where, *[p.reshape(4, 2, n, width, width) for (_, p), n in zip(pieces, counts)])
 
 
-def pick(where, psi, columns, cost):
-    width = psi.shape[-1]
-
-    def kernel(where, *refs):
-        for n in range(len(columns)):
-            refs[len(columns) + n][...] = refs[n][0, 0]
-
-    def column(n):
-        return pl.BlockSpec((1, 1, 2, width, width), lambda g, where: (g, where[9 + n], 0, 0, 0))
-
-    return pl.pallas_call(
-        kernel,
-        out_shape=[jax.ShapeDtypeStruct((8, width, width), BF16)] * len(columns),
-        grid_spec=pltpu.PrefetchScalarGridSpec(
-            num_scalar_prefetch=1,
-            grid=(4,),
-            in_specs=[column(n) for n in columns],
-            out_specs=[pl.BlockSpec((2, width, width), lambda g, where: (g, 0, 0))] * len(columns),
-        ),
-        compiler_params=pltpu.CompilerParams(vmem_limit_bytes=VMEM),
-        cost_estimate=cost,
-        name=f"pick_{columns[0]}",
-    )(where, *[psi] * len(columns))
+def column(psi, position):
+    zero = jnp.uint32(0)
+    start = (zero, zero, position.astype(jnp.uint32), zero, zero)
+    return lax.dynamic_slice(psi, start, (4, 2, 1) + psi.shape[3:]).reshape((8,) + psi.shape[3:])
 
 
 def together(*arrays):
@@ -230,50 +212,49 @@
     left_own = left_own.reshape(sectors, terms * width, width)
     right_own = right_own.reshape(sectors, terms * width, width)
 
-    psi = exchange(wavefunction, "y").reshape(4, 4, 2, width, width)
+    codes = exchange(pair_left + 2 * pair_right, ("y", "x", "c"))
+    psi = wavefunction.reshape(4, 4, 2, width, width).swapaxes(1, 2).reshape(wavefunction.shape)
+    psi, codes = together(psi, codes)
+    psi = exchange(psi, ("y", "c")).reshape(4, 2, 4, width, width)
     right_low, right_high = both_ways(right_own, "z")
     left_low, left_high = both_ways(left_own, "x")
-    other_own = shift(right_own, "c", 1, 2)
-    picks = pair_left + 2 * pair_right
-    psi, right_low, right_high, left_low, left_high, other_own, picks = together(
-        psi, right_low, right_high, left_low, left_high, other_own, picks
-    )
-
-    for_low, for_high = pick(where, psi, (1, 2), BRIEF)
+    left_other = shift(left_own, "c", 1, 2)
+    psi, right_low, right_high, left_low, left_high, left_other = together(
+        psi, right_low, right_high, left_low, left_high, left_other
+    )
+
+    psi_low = shift(column(psi, where[10]), "x", 1)
+    psi_high = shift(column(psi, where[11]), "x", 3)
     far = onward(right_low, right_high, "z")
-    for_low, for_high, psi, picks = together(for_low, for_high, psi, picks)
-    psi_low, psi_high = shift(for_low, "x", 1), shift(for_high, "x", 3)
-    codes = exchange(picks, ("y", "x"))
-    psi_own, psi_rest = pick(where, psi, (0, 3), LONG)
-    psi_rest, *to_core = together(psi_rest, right_low, right_high)
-    other_low, other_high = [shift(a, "c", 1, 2) for a in to_core]
-    rights = [
-        ((right_own,), (other_own,)),
-        ((right_low,), (other_low,)),
-        ((right_high,), (other_high,)),
-    ]
-    left_own_ = (left_own,)
-    own = combine(where, codes, [psi_own], [left_own_], rights, 0)
+    psi_own, psi_rest = column(psi, where[9]), column(psi, where[12])
+    rights = [(right_own,), (right_low,), (right_high,)]
+    lefts_own = [((left_own,), (left_other,))]
+    own = combine(where, codes, [psi_own], lefts_own, rights, 0)
+    own, left_low, left_high = together(own, left_low, left_high)
     halves = left_low[:, : terms * width // 2], left_high[:, terms * width // 2 :]
-    psi_rest, psi_low, psi_high, own, *far_halves = together(
-        psi_rest, psi_low, psi_high, own, *halves, *far
-    )
-    *halves, far_low, far_high = far_halves
-    far = far_low, far_high
+    psi_rest, psi_low, psi_high, own, *arrived = together(
+        psi_rest, psi_low, psi_high, own, *halves, *far, left_low, left_high
+    )
+    *halves, far_low, far_high, left_low, left_high = arrived
 
     left_far = shift(halves[0], "x", 1), shift(halves[1], "x", 3)
     psi_far = shift(psi_rest, "x", 2)
-    rights.append((far, tuple(shift(a, "c", 1, 2) for a in far)))
-
-    own = combine(where, codes, [psi_own], [left_own_], rights[3:], 0, 3, own)
-    own = exchange(own, ("z", "c"))
-    near = combine(where, codes, [psi_low, psi_high], [(left_low,), (left_high,)], rights, 1)
-    near = exchange(near, ("z", "c"))
-    rest = combine(where, codes, [psi_far], [left_far], rights, 3)
-    rest = exchange(rest, ("z", "c"))
+    rights.append((far_low, far_high))
+    own = combine(where, codes, [psi_own], lefts_own, rights[3:], 0, 3, own)
+    own = exchange(own, "z")
+    lefts_near = [((a,), (shift(a, "c", 1, 2),)) for a in (left_low, left_high)]
+    near = combine(where, codes, [psi_low, psi_high], lefts_near, rights, 1)
+    psi_far, *left_far = together(psi_far, *left_far, near)[:-1]
+    near = exchange(near, "z")
+    left_far = [(tuple(left_far), tuple(shift(a, "c", 1, 2) for a in left_far))]
+    rest = combine(where, codes, [psi_far], left_far, rights, 3)
+    rest = exchange(rest, "z")
     applied = assemble(where, [(0, own), (1, near)])
+    zero = jnp.uint32(0)
     applied = lax.dynamic_update_slice(
-        applied, rest.reshape(4, 1, 2, width, width), (0, where[7], 0, 0, 0)
+        applied,
+        rest.reshape(4, 1, 2, width, width),
+        (zero, where[7].astype(jnp.uint32), zero, zero, zero),
     )
     return applied.reshape(wavefunction.shape)
 

time: 206 us -> 220 us (1.068)
  waiting for transfers between devices: 82.2 us -> 91.2 us
  local copies, waits for them, and re-layouts: 15.9 us -> 22.6 us
  Pallas kernels: 55 us -> 49.3 us
  other arithmetic: 4.25 us -> 6.65 us
    ppermute x16, waiting for transfers between devices: 66.7 us -> 79 us  [shift(): lax.ppermute(array, axis, [(i, (i + step) % size) for i in range(size)])]
    pallas_call x2 -> x0, Pallas kernels: 8.9 us -> none  [pick(): pl.pallas_call(kernel, out_shape=[jax.ShapeDtypeStruct((8, width, width),...]
    transpose x0 -> x1, local copies, waits for them, and re-layouts: none -> 4.64 us  [body(): wavefunction.reshape(4, 4, 2, width, width).swapaxes(1, 2)]
    dynamic_slice x0 -> x1, local copies, waits for them, and re-layouts: none -> 4.25 us  [column(): lax.dynamic_slice(psi, start, (4, 2, 1) + psi.shape[3:])]
    all_to_all x5, waiting for transfers between devices: 15.5 us -> 12.2 us  [exchange(): return lax.all_to_all(array, axis, split_axis=0, concat_axis=0, tiled=True)]
    pallas_call x4, Pallas kernels: 41 us -> 44.2 us  [combine(): pl.pallas_call(kernel, out_shape=jax.ShapeDtypeStruct((8 * count, width,...]
  transfers between devices with their start and end apart: 21 -> 21, of which waited for: 8 -> 14; matrix products, arithmetic and copies ran while one was open for 8% -> 9% of each run, Pallas kernels for 23% -> 23%
where the time goes in v5:
time: 220 us; the launch traced here: 218 us
  waiting for transfers between devices  91.2 us (41%)
  Pallas kernels  49.3 us (22%)
  starting transfers between devices  45.3 us (21%)
  local copies, waits for them, and re-layouts  22.6 us (10%)
  other arithmetic  6.65 us (3%)
  between operations  3.28 us (1%)
    ppermute x16, waiting for transfers between devices, shift(): lax.ppermute(array, axis, [(i, (i + step) % size) for i in range(size)])  79 us
    pallas_call x4, Pallas kernels, combine(): pl.pallas_call(kernel, out_shape=jax.ShapeDtypeStruct((8 * count, width,...  44.2 us
    all_to_all x5, starting transfers between devices, exchange(): return lax.all_to_all(array, axis, split_axis=0, concat_axis=0, tiled=True)  26.8 us
    ppermute x16, starting transfers between devices, shift(): lax.ppermute(array, axis, [(i, (i + step) % size) for i in range(size)])  18.5 us
    all_to_all x5, waiting for transfers between devices, exchange(): return lax.all_to_all(array, axis, split_axis=0, concat_axis=0, tiled=True)  12.2 us
    pallas_call x1, Pallas kernels, assemble(): pl.pallas_call(kernel, out_shape=jax.ShapeDtypeStruct((4, 4, 2, width, wi...  5.04 us
    transpose x1, local copies, waits for them, and re-layouts, body(): wavefunction.reshape(4, 4, 2, width, width).swapaxes(1, 2)  4.64 us
  transfers between devices with their start and end apart: 21, of which 14 were waited for; matrix products, arithmetic and copies ran while one was open for 9% of the time, Pallas kernels for 23%

profile of v5, /device:TPU:0, one launch (start us, length us, event | category | flops | bytes accessed | tf_op | source)
XLA Modules:
  0.0 218.4 jit_solution(10962082791213336790)
XLA Ops:
  0.0 0.7 add_bitcast_fusion
  0.7 0.7 copy.18
  1.4 7.4 %all-to-all-start = ((s32[32,1,1]{2,1,0:T(1,128)}), s32[32,1,1]{2,1,0:T(1,128)S(1)}, u32[]{:S(2)}, u32[]{:S(2)}) async-start(s32[32,1,1]{2,1,0:T(1,128)} %copy.18), calls=%async_computation | async-start | bytes 32768 | tf_op jit(solution)/shard_map/all_to_all | solution.py:32
  8.8 4.6 %copy.17 = bf16[4,2,4,256,256]{4,3,2,1,0:T(8,128)(2,1)} copy(bf16[4,2,4,256,256]{4,3,1,2,0:T(8,128)(2,1)} %bitcast.34) | data formatting | bytes 8388608 | tf_op jit(solution)/shard_map/transpose | solution.py:216
  13.4 2.7 %all-to-all-done = s32[32,1,1]{2,1,0:T(1,128)S(1)} async-done(((s32[32,1,1]{2,1,0:T(1,128)}), s32[32,1,1]{2,1,0:T(1,128)S(1)}, u32[]{:S(2)}, u32[]{:S(2)}) %all-to-all-start) | async-done | bytes 160 | tf_op jit(solution)/shard_map/all_to_all | solution.py:32
  16.1 1.2 reduce.codes
  17.4 4.7 %all-to-all-start.1 = ((bf16[32,256,256]{2,1,0:T(8,128)(2,1)}), bf16[32,256,256]{2,1,0:T(8,128)(2,1)}, u32[]{:S(2)}, u32[]{:S(2)}) async-start(bf16[32,256,256]{2,1,0:T(8,128)(2,1)} %bitcast.26), calls=%async_computation.1 | async-start | bytes 8388608 | tf_op jit(solution)/shard_map/all_to_all | solution.py:32
  22.1 2.5 %fusion = bf16[2,8,256,256]{3,2,1,0:T(8,128)(2,1)S(1)} fusion(bf16[2,8,256,256]{3,2,1,0:T(8,128)(2,1)} %param.13, s32[2]{0:T(128)S(1)} %copy-done.4), kind=kLoop, calls=%fused_computation.2 | loop fusion | flops 2097152 | bytes 4194312 | tf_op jit(solution)/shard_map/jit(_where)/select_n | solution.py:209
  24.6 4.1 %collective-permute-start.1 = (bf16[2,2048,256]{2,1,0:T(8,128)(2,1)S(1)}, bf16[2,2048,256]{2,1,0:T(8,128)(2,1)}, u32[]{:S(2)}, u32[]{:S(2)}) collective-permute-start(bf16[2,2048,256]{2,1,0:T(8,128)(2,1)S(1)} %bitcast.28), channel_id=1, source_target_pairs={{0,24},{8,0},{16,8},{24,16},{1,25},{9,1},{17,9},{25,17},{2,26},{10... | collective-permute-start | bytes 6291464 | tf_op jit(solution)/shard_map/ppermute | solution.py:36
  28.8 2.2 %fusion.1 = bf16[2,8,256,256]{3,2,1,0:T(8,128)(2,1)} fusion(bf16[2,8,256,256]{3,2,1,0:T(8,128)(2,1)S(1)} %copy-done.2, s32[2]{0:T(128)S(1)} %copy-done.5), kind=kLoop, calls=%fused_computation.3 | loop fusion | flops 2097152 | bytes 4194312 | tf_op jit(solution)/shard_map/jit(_where)/select_n | solution.py:211
  31.0 1.2 collective-permute-start.3
  32.2 0.8 collective-permute-start.2
  33.1 1.2 constant_dynamic-slice_fusion.4
  34.3 0.7 fusion.3
  37.4 36.7 %collective-permute-done.1.refs_5_.refs_8_.refs_7_ = bf16[2,2048,256]{2,1,0:T(8,128)(2,1)} collective-permute-done((bf16[2,2048,256]{2,1,0:T(8,128)(2,1)S(1)}, bf16[2,2048,256]{2,1,0:T(8,128)(2,1)}, u32[]{:S(2)}, u32[]{:S(2)}) %collective-permute-start.1) | collective-permute-done | bytes 2097184 | tf_op jit(solution)/shard_map/ppermute | solution.py:36
  74.2 3.5 %collective-permute-done.refs_4_.refs_7_.refs_6_ = bf16[2,2048,256]{2,1,0:T(8,128)(2,1)} collective-permute-done((bf16[2,2048,256]{2,1,0:T(8,128)(2,1)S(1)}, bf16[2,2048,256]{2,1,0:T(8,128)(2,1)}, u32[]{:S(2)}, u32[]{:S(2)}) %collective-permute-start) | collective-permute-done | bytes 2097184 | tf_op jit(solution)/shard_map/ppermute | solution.py:36
  77.7 1.7 collective-permute-done.3.refs_4_
  79.3 2.1 collective-permute-done.2.refs_2_
  81.4 2.4 %slice.38 = bf16[2,1024,256]{2,1,0:T(8,128)(2,1)} slice(bf16[2,2048,256]{2,1,0:T(8,128)(2,1)} %collective-permute-done.refs_4_.refs_7_.refs_6_), slice={[0:2], [0:1024], [0:256]} | slice | bytes 2097152 | tf_op jit(solution)/shard_map/slice | solution.py:45
  83.8 2.3 %slice.39 = bf16[2,1024,256]{2,1,0:T(8,128)(2,1)} slice(bf16[2,2048,256]{2,1,0:T(8,128)(2,1)} %collective-permute-done.1.refs_5_.refs_8_.refs_7_), slice={[0:2], [1024:2048], [0:256]} | slice | bytes 2097152 | tf_op jit(solution)/shard_map/slice | solution.py:45
  86.1 3.2 %collective-permute-start.8 = (bf16[2,1024,256]{2,1,0:T(8,128)(2,1)}, bf16[2,1024,256]{2,1,0:T(8,128)(2,1)}, u32[]{:S(2)}, u32[]{:S(2)}) collective-permute-start(bf16[2,1024,256]{2,1,0:T(8,128)(2,1)} %slice.39), channel_id=1, source_target_pairs={{0,24},{8,0},{16,8},{24,16},{1,25},{9,1},{17,9},{25,17},{2,26},{10... | collective-permute-start | bytes 3145736 | tf_op jit(solution)/shard_map/ppermute | solution.py:36
  89.4 4.2 %constant_dynamic-slice_fusion = (bf16[4,2,1,256,256]{4,3,2,1,0:T(8,128)(2,1)}, bf16[4,2,1,256,256]{4,3,2,1,0:T(8,128)(2,1)}, bf16[4,2,1,256,256]{4,3,2,1,0:T(8,128)(2,1)}, bf16[4,2,1,256,256]{4,3,2,1,0:T(8,128)(2,1)}) fusion(bf16[4,2,4,256,256]{4,3,2,1,0:T(8,128)(2,1)} %bitcast.5, u32[]{:T(128)} %bitcast.14, u32[]{:T(128)} %bitcast.12, u32[]{:T(128)} %bitcast.10, ...), kind=kLoop, calls=%fused_computation.5 | loop fusion | bytes 8388624 | tf_op jit(solution)/shard_map/dynamic_slice | solution.py:196
  93.6 3.2 %collective-permute-start.6 = (bf16[8,256,256]{2,1,0:T(8,128)(2,1)}, bf16[8,256,256]{2,1,0:T(8,128)(2,1)}, u32[]{:S(2)}, u32[]{:S(2)}) collective-permute-start(bf16[8,256,256]{2,1,0:T(8,128)(2,1)} %bitcast.15), channel_id=1, source_target_pairs={{0,6},{2,0},{4,2},{6,4},{1,7},{3,1},{5,3},{7,5},{8,14},{10,8},{12,... | collective-permute-start | bytes 3145736 | tf_op jit(solution)/shard_map/ppermute | solution.py:36
  96.9 9.3 %combine_0_0.1.refs_5_ = bf16[8,256,256]{2,1,0:T(8,128)(2,1)} custom-call(s32[13]{0:T(128)} %get-tuple-element.58.where, s32[32]{0:T(128)} %reduce.codes, bf16[8,256,256]{2,1,0:T(8,128)(2,1)} %bitcast.35, bf16[2,2048,256]{2,1,0:T(8,128)(2,1)} %bitcast.7.refs_1_, bf16[2,2048,256]{2,1,0:T(8,128)(2,1)} %collective-permute-done.4.refs_2_, ...), custom_call_target="tpu_custom_call" | custom-call | flops 999999995904 | bytes 1 | tf_op jit(solution)/shard_map/combine_0_0/pallas_call | solution.py:141
  106.1 2.3 %slice.36 = bf16[2,1024,256]{2,1,0:T(8,128)(2,1)} slice(bf16[2,2048,256]{2,1,0:T(8,128)(2,1)} %collective-permute-done.2.refs_2_), slice={[0:2], [0:1024], [0:256]} | slice | bytes 2097152 | tf_op jit(solution)/shard_map/slice | solution.py:234
  108.4 2.3 %slice.37 = bf16[2,1024,256]{2,1,0:T(8,128)(2,1)} slice(bf16[2,2048,256]{2,1,0:T(8,128)(2,1)} %collective-permute-done.3.refs_4_), slice={[0:2], [1024:2048], [0:256]} | slice | bytes 2097152 | tf_op jit(solution)/shard_map/slice | solution.py:234
  110.7 1.0 collective-permute-done.8.refs_4_.refs_10_.refs_9_
  111.7 3.4 %collective-permute-done.7.refs_3_.refs_9_.refs_8_ = bf16[2,1024,256]{2,1,0:T(8,128)(2,1)} collective-permute-done((bf16[2,1024,256]{2,1,0:T(8,128)(2,1)}, bf16[2,1024,256]{2,1,0:T(8,128)(2,1)}, u32[]{:S(2)}, u32[]{:S(2)}) %collective-permute-start.7) | collective-permute-done | bytes 1048608 | tf_op jit(solution)/shard_map/ppermute | solution.py:36
  115.1 4.2 %collective-permute-done.5.refs_0_ = bf16[8,256,256]{2,1,0:T(8,128)(2,1)} collective-permute-done((bf16[8,256,256]{2,1,0:T(8,128)(2,1)}, bf16[8,256,256]{2,1,0:T(8,128)(2,1)}, u32[]{:S(2)}, u32[]{:S(2)}) %collective-permute-start.5) | collective-permute-done | bytes 1048608 | tf_op jit(solution)/shard_map/ppermute | solution.py:36
  119.3 0.5 collective-permute-start.10
  119.9 6.4 %combine_0_3.1 = bf16[8,256,256]{2,1,0:T(8,128)(2,1)} custom-call(s32[13]{0:T(128)} %get-tuple-element.58.where, s32[32]{0:T(128)} %reduce.codes, bf16[8,256,256]{2,1,0:T(8,128)(2,1)} %bitcast.36, bf16[2,2048,256]{2,1,0:T(8,128)(2,1)} %bitcast.7.refs_1_, bf16[2,2048,256]{2,1,0:T(8,128)(2,1)} %collective-permute-done.4.refs_2_, ...), custom_call_target="tpu_custom_call", output_to_operand_aliasing={{}: (7, {})} | custom-call | flops 999999995904 | bytes 1 | tf_op jit(solution)/shard_map/combine_0_3/pallas_call | solution.py:141
  126.3 4.3 %all-to-all-start.2 = ((bf16[8,256,256]{2,1,0:T(8,128)(2,1)}), bf16[8,256,256]{2,1,0:T(8,128)(2,1)}, u32[]{:S(2)}, u32[]{:S(2)}) async-start(bf16[8,256,256]{2,1,0:T(8,128)(2,1)} %combine_0_3.1), calls=%async_computation.2 | async-start | bytes 2097152 | tf_op jit(solution)/shard_map/all_to_all | solution.py:32
  130.5 1.5 collective-permute-start.11
  132.1 2.3 %collective-permute-start.12 = (bf16[2,1024,256]{2,1,0:T(8,128)(2,1)}, bf16[2,1024,256]{2,1,0:T(8,128)(2,1)}, u32[]{:S(2)}, u32[]{:S(2)}) collective-permute-start(bf16[2,1024,256]{2,1,0:T(8,128)(2,1)} %slice.36), channel_id=1, source_target_pairs={{0,2},{2,4},{4,6},{6,0},{1,3},{3,5},{5,7},{7,1},{8,10},{10,12},{12... | collective-permute-start | bytes 3145736 | tf_op jit(solution)/shard_map/ppermute | solution.py:36
  134.4 0.9 collective-permute-start.13
  135.3 18.0 %combine_1_0.1 = bf16[16,256,256]{2,1,0:T(8,128)(2,1)} custom-call(s32[13]{0:T(128)} %get-tuple-element.58.where, s32[32]{0:T(128)} %reduce.codes, bf16[8,256,256]{2,1,0:T(8,128)(2,1)} %collective-permute-done.5.refs_0_, bf16[8,256,256]{2,1,0:T(8,128)(2,1)} %collective-permute-done.6.refs_1_, bf16[2,2048,256]{2,1,0:T(8,128)(2,1)} %collective-permute-done.2.refs_2_, ...), custom_call_target="tpu_custom_call" | custom-call | flops 999999995904 | bytes 1 | tf_op jit(solution)/shard_map/combine_1_0/pallas_call | solution.py:141
  153.3 4.7 %all-to-all-start.3 = ((bf16[16,256,256]{2,1,0:T(8,128)(2,1)}), bf16[16,256,256]{2,1,0:T(8,128)(2,1)S(1)}, u32[]{:S(2)}, u32[]{:S(2)}) async-start(bf16[16,256,256]{2,1,0:T(8,128)(2,1)} %combine_1_0.1), calls=%async_computation.3 | async-start | bytes 4194304 | tf_op jit(solution)/shard_map/all_to_all | solution.py:32
  158.0 0.5 collective-permute-done.11.refs_0_
  158.5 21.5 %collective-permute-done.12.refs_1_ = bf16[2,1024,256]{2,1,0:T(8,128)(2,1)} collective-permute-done((bf16[2,1024,256]{2,1,0:T(8,128)(2,1)}, bf16[2,1024,256]{2,1,0:T(8,128)(2,1)}, u32[]{:S(2)}, u32[]{:S(2)}) %collective-permute-start.12) | collective-permute-done | bytes 1048608 | tf_op jit(solution)/shard_map/ppermute | solution.py:36
  180.0 0.3 collective-permute-done.13.refs_2_
  180.3 0.5 collective-permute-start.15
  180.8 3.8 %collective-permute-done.14.refs_3_ = bf16[2,1024,256]{2,1,0:T(8,128)(2,1)S(1)} collective-permute-done((bf16[2,1024,256]{2,1,0:T(8,128)(2,1)}, bf16[2,1024,256]{2,1,0:T(8,128)(2,1)S(1)}, u32[]{:S(2)}, u32[]{:S(2)}) %collective-permute-start.14) | collective-permute-done | bytes 1048608 | tf_op jit(solution)/shard_map/ppermute | solution.py:36
  184.8 0.9 copy-done.3
  185.7 10.6 %combine_3_0.1 = bf16[8,256,256]{2,1,0:T(8,128)(2,1)} custom-call(s32[13]{0:T(128)} %get-tuple-element.58.where, s32[32]{0:T(128)} %reduce.codes, bf16[8,256,256]{2,1,0:T(8,128)(2,1)} %collective-permute-done.11.refs_0_, bf16[2,1024,256]{2,1,0:T(8,128)(2,1)} %collective-permute-done.12.refs_1_, bf16[2,1024,256]{2,1,0:T(8,128)(2,1)} %collective-permute-done.13.refs_2_, ...), custom_call_target="tpu_custom_call" | custom-call | flops 1 | bytes 1 | tf_op jit(solution)/shard_map/combine_3_0/pallas_call | solution.py:141
  196.4 5.8 %all-to-all-start.4 = ((bf16[8,256,256]{2,1,0:T(8,128)(2,1)}), bf16[8,256,256]{2,1,0:T(8,128)(2,1)S(1)}, u32[]{:S(2)}, u32[]{:S(2)}) async-start(bf16[8,256,256]{2,1,0:T(8,128)(2,1)} %combine_3_0.1), calls=%async_computation.4 | async-start | bytes 2097152 | tf_op jit(solution)/shard_map/all_to_all | solution.py:32
  202.8 5.0 %assemble.1 = bf16[4,4,2,256,256]{4,3,2,1,0:T(8,128)(2,1)} custom-call(s32[13]{0:T(128)} %get-tuple-element.58.where, bf16[4,2,1,256,256]{4,3,2,1,0:T(8,128)(2,1)} %bitcast.16.refs_0_, bf16[4,2,2,256,256]{4,3,2,1,0:T(8,128)(2,1)} %bitcast.27), custom_call_target="tpu_custom_call" | custom-call | flops 1 | bytes 1 | tf_op jit(solution)/shard_map/assemble/pallas_call | solution.py:178
  207.8 9.5 %all-to-all-done.4 = bf16[8,256,256]{2,1,0:T(8,128)(2,1)S(1)} async-done(((bf16[8,256,256]{2,1,0:T(8,128)(2,1)}), bf16[8,256,256]{2,1,0:T(8,128)(2,1)S(1)}, u32[]{:S(2)}, u32[]{:S(2)}) %all-to-all-start.4) | async-done | bytes 1048608 | tf_op jit(solution)/shard_map/all_to_all | solution.py:32
  217.3 1.0 constant_dynamic-update-slice_fusion
  (25 shorter events, 0.3 us)
Async XLA Ops:
  1.4 14.8 %all-to-all-start = ((s32[32,1,1]{2,1,0:T(1,128)}), s32[32,1,1]{2,1,0:T(1,128)S(1)}, u32[]{:S(2)}, u32[]{:S(2)}) async-start(s32[32,1,1]{2,1,0:T(1,128)} %copy.18), calls=%async_computation | async-start | bytes 32768 | tf_op jit(solution)/shard_map/all_to_all | solution.py:32
  17.4 4.7 %copy-start.4 = (s32[2]{0:T(128)S(1)}, s32[2]{0:T(128)}, u32[]{:S(2)}) copy-start(s32[2]{0:T(128)} %param.14) | copy-start | bytes 28
  17.4 64.1 %all-to-all-start.1 = ((bf16[32,256,256]{2,1,0:T(8,128)(2,1)}), bf16[32,256,256]{2,1,0:T(8,128)(2,1)}, u32[]{:S(2)}, u32[]{:S(2)}) async-start(bf16[32,256,256]{2,1,0:T(8,128)(2,1)} %bitcast.26), calls=%async_computation.1 | async-start | bytes 8388608 | tf_op jit(solution)/shard_map/all_to_all | solution.py:32
  22.1 6.7 %copy-start.2 = (bf16[2,8,256,256]{3,2,1,0:T(8,128)(2,1)S(1)}, bf16[2,8,256,256]{3,2,1,0:T(8,128)(2,1)}, u32[]{:S(2)}) copy-start(bf16[2,8,256,256]{3,2,1,0:T(8,128)(2,1)} %param.11) | copy-start | bytes 6291460
  22.1 6.7 %copy-start.5 = (s32[2]{0:T(128)S(1)}, s32[2]{0:T(128)}, u32[]{:S(2)}) copy-start(s32[2]{0:T(128)} %param.12) | copy-start | bytes 28
  24.6 6.3 %copy-start.1 = (bf16[2,8,256,256]{3,2,1,0:T(8,128)(2,1)}, bf16[2,8,256,256]{3,2,1,0:T(8,128)(2,1)S(1)}, u32[]{:S(2)}) copy-start(bf16[2,8,256,256]{3,2,1,0:T(8,128)(2,1)S(1)} %fusion) | copy-start | bytes 6291460
  24.6 49.5 %collective-permute-start.1 = (bf16[2,2048,256]{2,1,0:T(8,128)(2,1)S(1)}, bf16[2,2048,256]{2,1,0:T(8,128)(2,1)}, u32[]{:S(2)}, u32[]{:S(2)}) collective-permute-start(bf16[2,2048,256]{2,1,0:T(8,128)(2,1)S(1)} %bitcast.28), channel_id=1, source_target_pairs={{0,24},{8,0},{16,8},{24,16},{1,25},{9,1},{17,9},{25,17},{2,26},{10... | collective-permute-start | bytes 6291464 | tf_op jit(solution)/shard_map/ppermute | solution.py:36
  28.8 48.9 %collective-permute-start = (bf16[2,2048,256]{2,1,0:T(8,128)(2,1)S(1)}, bf16[2,2048,256]{2,1,0:T(8,128)(2,1)}, u32[]{:S(2)}, u32[]{:S(2)}) collective-permute-start(bf16[2,2048,256]{2,1,0:T(8,128)(2,1)S(1)} %bitcast.29), channel_id=1, source_target_pairs={{0,8},{8,16},{16,24},{24,0},{1,9},{9,17},{17,25},{25,1},{2,10},{10... | collective-permute-start | bytes 6291464 | tf_op jit(solution)/shard_map/ppermute | solution.py:36
  31.0 46.7 %collective-permute-start.4 = (bf16[2,2048,256]{2,1,0:T(8,128)(2,1)}, bf16[2,2048,256]{2,1,0:T(8,128)(2,1)}, u32[]{:S(2)}, u32[]{:S(2)}) collective-permute-start(bf16[2,2048,256]{2,1,0:T(8,128)(2,1)} %bitcast.7.refs_1_), channel_id=1, source_target_pairs={{0,1},{1,0},{2,3},{3,2},{4,5},{5,4},{6,7},{7,6},{8,9},{9,8},{10,11... | collective-permute-start | bytes 6291464 | tf_op jit(solution)/shard_map/ppermute | solution.py:36
  31.0 48.3 %collective-permute-start.3 = (bf16[2,2048,256]{2,1,0:T(8,128)(2,1)}, bf16[2,2048,256]{2,1,0:T(8,128)(2,1)}, u32[]{:S(2)}, u32[]{:S(2)}) collective-permute-start(bf16[2,2048,256]{2,1,0:T(8,128)(2,1)} %bitcast.7.refs_1_), channel_id=1, source_target_pairs={{0,6},{2,0},{4,2},{6,4},{1,7},{3,1},{5,3},{7,5},{8,14},{10,8},{12,... | collective-permute-start | bytes 6291464 | tf_op jit(solution)/shard_map/ppermute | solution.py:36
  32.2 49.2 %collective-permute-start.2 = (bf16[2,2048,256]{2,1,0:T(8,128)(2,1)}, bf16[2,2048,256]{2,1,0:T(8,128)(2,1)}, u32[]{:S(2)}, u32[]{:S(2)}) collective-permute-start(bf16[2,2048,256]{2,1,0:T(8,128)(2,1)} %bitcast.7.refs_1_), channel_id=1, source_target_pairs={{0,2},{2,4},{4,6},{6,0},{1,3},{3,5},{5,7},{7,1},{8,10},{10,12},{12... | collective-permute-start | bytes 6291464 | tf_op jit(solution)/shard_map/ppermute | solution.py:36
  86.1 25.5 %collective-permute-start.8 = (bf16[2,1024,256]{2,1,0:T(8,128)(2,1)}, bf16[2,1024,256]{2,1,0:T(8,128)(2,1)}, u32[]{:S(2)}, u32[]{:S(2)}) collective-permute-start(bf16[2,1024,256]{2,1,0:T(8,128)(2,1)} %slice.39), channel_id=1, source_target_pairs={{0,24},{8,0},{16,8},{24,16},{1,25},{9,1},{17,9},{25,17},{2,26},{10... | collective-permute-start | bytes 3145736 | tf_op jit(solution)/shard_map/ppermute | solution.py:36
  89.4 25.7 %collective-permute-start.7 = (bf16[2,1024,256]{2,1,0:T(8,128)(2,1)}, bf16[2,1024,256]{2,1,0:T(8,128)(2,1)}, u32[]{:S(2)}, u32[]{:S(2)}) collective-permute-start(bf16[2,1024,256]{2,1,0:T(8,128)(2,1)} %slice.38), channel_id=1, source_target_pairs={{0,8},{8,16},{16,24},{24,0},{1,9},{9,17},{17,25},{25,1},{2,10},{10... | collective-permute-start | bytes 3145736 | tf_op jit(solution)/shard_map/ppermute | solution.py:36
  93.6 25.7 %collective-permute-start.5 = (bf16[8,256,256]{2,1,0:T(8,128)(2,1)}, bf16[8,256,256]{2,1,0:T(8,128)(2,1)}, u32[]{:S(2)}, u32[]{:S(2)}) collective-permute-start(bf16[8,256,256]{2,1,0:T(8,128)(2,1)} %bitcast.13), channel_id=1, source_target_pairs={{0,2},{2,4},{4,6},{6,0},{1,3},{3,5},{5,7},{7,1},{8,10},{10,12},{12... | collective-permute-start | bytes 3145736 | tf_op jit(solution)/shard_map/ppermute | solution.py:36
  93.6 25.7 %collective-permute-start.6 = (bf16[8,256,256]{2,1,0:T(8,128)(2,1)}, bf16[8,256,256]{2,1,0:T(8,128)(2,1)}, u32[]{:S(2)}, u32[]{:S(2)}) collective-permute-start(bf16[8,256,256]{2,1,0:T(8,128)(2,1)} %bitcast.15), channel_id=1, source_target_pairs={{0,6},{2,0},{4,2},{6,4},{1,7},{3,1},{5,3},{7,5},{8,14},{10,8},{12,... | collective-permute-start | bytes 3145736 | tf_op jit(solution)/shard_map/ppermute | solution.py:36
  119.3 16.0 %collective-permute-start.9 = (bf16[2,2048,256]{2,1,0:T(8,128)(2,1)}, bf16[2,2048,256]{2,1,0:T(8,128)(2,1)}, u32[]{:S(2)}, u32[]{:S(2)}) collective-permute-start(bf16[2,2048,256]{2,1,0:T(8,128)(2,1)} %collective-permute-done.2.refs_2_), channel_id=1, source_target_pairs={{0,1},{1,0},{2,3},{3,2},{4,5},{5,4},{6,7},{7,6},{8,9},{9,8},{10,11... | collective-permute-start | bytes 6291464 | tf_op jit(solution)/shard_map/ppermute | solution.py:36
  119.3 16.0 %collective-permute-start.10 = (bf16[2,2048,256]{2,1,0:T(8,128)(2,1)}, bf16[2,2048,256]{2,1,0:T(8,128)(2,1)}, u32[]{:S(2)}, u32[]{:S(2)}) collective-permute-start(bf16[2,2048,256]{2,1,0:T(8,128)(2,1)} %collective-permute-done.3.refs_4_), channel_id=1, source_target_pairs={{0,1},{1,0},{2,3},{3,2},{4,5},{5,4},{6,7},{7,6},{8,9},{9,8},{10,11... | collective-permute-start | bytes 6291464 | tf_op jit(solution)/shard_map/ppermute | solution.py:36
  126.3 27.0 %all-to-all-start.2 = ((bf16[8,256,256]{2,1,0:T(8,128)(2,1)}), bf16[8,256,256]{2,1,0:T(8,128)(2,1)}, u32[]{:S(2)}, u32[]{:S(2)}) async-start(bf16[8,256,256]{2,1,0:T(8,128)(2,1)} %combine_0_3.1), calls=%async_computation.2 | async-start | bytes 2097152 | tf_op jit(solution)/shard_map/all_to_all | solution.py:32
  130.5 28.0 %collective-permute-start.11 = (bf16[8,256,256]{2,1,0:T(8,128)(2,1)}, bf16[8,256,256]{2,1,0:T(8,128)(2,1)}, u32[]{:S(2)}, u32[]{:S(2)}) collective-permute-start(bf16[8,256,256]{2,1,0:T(8,128)(2,1)} %bitcast.11), channel_id=1, source_target_pairs={{0,4},{2,6},{4,0},{6,2},{1,5},{3,7},{5,1},{7,3},{8,12},{10,14},{12... | collective-permute-start | bytes 3145736 | tf_op jit(solution)/shard_map/ppermute | solution.py:36
  132.1 47.9 %collective-permute-start.12 = (bf16[2,1024,256]{2,1,0:T(8,128)(2,1)}, bf16[2,1024,256]{2,1,0:T(8,128)(2,1)}, u32[]{:S(2)}, u32[]{:S(2)}) collective-permute-start(bf16[2,1024,256]{2,1,0:T(8,128)(2,1)} %slice.36), channel_id=1, source_target_pairs={{0,2},{2,4},{4,6},{6,0},{1,3},{3,5},{5,7},{7,1},{8,10},{10,12},{12... | collective-permute-start | bytes 3145736 | tf_op jit(solution)/shard_map/ppermute | solution.py:36
  134.4 45.9 %collective-permute-start.13 = (bf16[2,1024,256]{2,1,0:T(8,128)(2,1)}, bf16[2,1024,256]{2,1,0:T(8,128)(2,1)}, u32[]{:S(2)}, u32[]{:S(2)}) collective-permute-start(bf16[2,1024,256]{2,1,0:T(8,128)(2,1)} %slice.37), channel_id=1, source_target_pairs={{0,6},{2,0},{4,2},{6,4},{1,7},{3,1},{5,3},{7,5},{8,14},{10,8},{12,... | collective-permute-start | bytes 3145736 | tf_op jit(solution)/shard_map/ppermute | solution.py:36
  153.3 43.0 %all-to-all-start.3 = ((bf16[16,256,256]{2,1,0:T(8,128)(2,1)}), bf16[16,256,256]{2,1,0:T(8,128)(2,1)S(1)}, u32[]{:S(2)}, u32[]{:S(2)}) async-start(bf16[16,256,256]{2,1,0:T(8,128)(2,1)} %combine_1_0.1), calls=%async_computation.3 | async-start | bytes 4194304 | tf_op jit(solution)/shard_map/all_to_all | solution.py:32
  180.3 4.3 %collective-permute-start.14 = (bf16[2,1024,256]{2,1,0:T(8,128)(2,1)}, bf16[2,1024,256]{2,1,0:T(8,128)(2,1)S(1)}, u32[]{:S(2)}, u32[]{:S(2)}) collective-permute-start(bf16[2,1024,256]{2,1,0:T(8,128)(2,1)} %collective-permute-done.12.refs_1_), channel_id=1, source_target_pairs={{0,1},{1,0},{2,3},{3,2},{4,5},{5,4},{6,7},{7,6},{8,9},{9,8},{10,11... | collective-permute-start | bytes 3145736 | tf_op jit(solution)/shard_map/ppermute | solution.py:36
  180.3 4.5 %collective-permute-start.15 = (bf16[2,1024,256]{2,1,0:T(8,128)(2,1)}, bf16[2,1024,256]{2,1,0:T(8,128)(2,1)}, u32[]{:S(2)}, u32[]{:S(2)}) collective-permute-start(bf16[2,1024,256]{2,1,0:T(8,128)(2,1)} %collective-permute-done.13.refs_2_), channel_id=1, source_target_pairs={{0,1},{1,0},{2,3},{3,2},{4,5},{5,4},{6,7},{7,6},{8,9},{9,8},{10,11... | collective-permute-start | bytes 3145736 | tf_op jit(solution)/shard_map/ppermute | solution.py:36
  184.7 1.1 copy-start.3
  196.4 6.4 %copy-start = (bf16[16,256,256]{2,1,0:T(8,128)(2,1)}, bf16[16,256,256]{2,1,0:T(8,128)(2,1)S(1)}, u32[]{:S(2)}) copy-start(bf16[16,256,256]{2,1,0:T(8,128)(2,1)S(1)} %all-to-all-done.3) | copy-start | bytes 6291460
  196.4 21.0 %all-to-all-start.4 = ((bf16[8,256,256]{2,1,0:T(8,128)(2,1)}), bf16[8,256,256]{2,1,0:T(8,128)(2,1)S(1)}, u32[]{:S(2)}, u32[]{:S(2)}) async-start(bf16[8,256,256]{2,1,0:T(8,128)(2,1)} %combine_3_0.1), calls=%async_computation.4 | async-start | bytes 2097152 | tf_op jit(solution)/shard_map/all_to_all | solution.py:32

commit v6 on v5

--- a/solution.py
+++ b/solution.py
@@ -9,6 +9,7 @@
 AXES = ("y", "z", "x", "c")
 OFFSETS = (0, 3, 1, 2)
 STEPS = (0, 1, 3, 2)
+TAIL = 16
 SLOTS = 3
 BF16 = jnp.bfloat16
 BRIEF = pl.CostEstimate(flops=1, bytes_accessed=1, transcendentals=0)
@@ -45,8 +46,10 @@
     return shift(from_low[:, :half], axis, 1), shift(from_high[:, half:], axis, 3)
 
 
-def combine(where, codes, psis, lefts, rights, first, z_first=0, kept=None):
-    width = psis[0].shape[-1]
+def combine(where, psis, lefts, rights, first, z_first=0, kept=None):
+    codes = [codes for _, codes in psis]
+    psis = [psi for psi, _ in psis]
+    rows, width = psis[0].shape[1:]
     depth = sum(a.shape[1] for a in lefts[0][0])
     terms = depth // width
     count = len(lefts)
@@ -56,11 +59,11 @@
     slots = min(SLOTS, steps)
     each = [(core, k) for core in range(2) for k in range(count)]
 
-    def code_of(step, core, k, where, codes):
-        return codes[(where[z_first + step] * 4 + where[4 + first + k]) * 2 + (where[8] ^ core)]
-
-    def kernel(where, codes, *refs):
-        refs = list(refs)
+    def pick_of(step, core, k, side, where, codes):
+        return codes[k][(where[z_first + step] * 2 + (where[8] ^ core)) * 2 + side]
+
+    def kernel(where, *refs):
+        codes, refs = refs[:count], list(refs[count:])
         psi_refs = [refs.pop(0) for _ in psis]
         left_refs = [[[refs.pop(0) for _ in group] for group in pair] for pair in lefts]
         right_refs = [[refs.pop(0) for _ in group] for group in rights]
@@ -85,7 +88,7 @@
                 @pl.when(at == n_step)
                 def _(n_step=n_step):
                     for n_block, (core, k) in enumerate(each):
-                        right = code_of(n_step, core, k, where, codes) // 2
+                        right = pick_of(n_step, core, k, 1, where, codes)
                         row = 0
                         for n, ref in enumerate(right_refs[n_step]):
                             size = ref.shape[1]
@@ -118,8 +121,8 @@
         fetch(step, False)
         slot = lax.rem(step, slots)
         for n_block, (core, k) in enumerate(each):
-            left = code_of(step, core, k, where, codes) % 2
-            block = psi_refs[k][where[8] ^ core]
+            left = pick_of(step, core, k, 0, where, codes)
+            block = psi_refs[k][where[8] ^ core, :width]
             for t in range(terms):
                 product = jnp.dot(
                     left_buf[k, core, left, t * width : (t + 1) * width],
@@ -134,7 +137,7 @@
             out_ref[(where[8] ^ core) * count + k] = total.astype(BF16)
 
     in_place = pl.BlockSpec(memory_space=pl.ANY)
-    of_g = lambda step, where, codes: (where[z_first + step], 0, 0)
+    of_g = lambda step, where, *codes: (where[z_first + step], 0, 0)
     parts = max(len(group) for group in rights)
     extra = [] if kept is None else [kept]
     operands = [*psis, *left_parts, *right_parts, *extra]
@@ -142,9 +145,9 @@
         kernel,
         out_shape=jax.ShapeDtypeStruct((8 * count, width, width), BF16),
         grid_spec=pltpu.PrefetchScalarGridSpec(
-            num_scalar_prefetch=2,
+            num_scalar_prefetch=1 + count,
             grid=(steps,),
-            in_specs=[pl.BlockSpec((2, width, width), of_g)] * count
+            in_specs=[pl.BlockSpec((2, rows, width), of_g)] * count
             + [in_place] * (len(operands) - count),
             out_specs=pl.BlockSpec((2 * count, width, width), of_g),
             scratch_shapes=[
@@ -155,13 +158,13 @@
                 pltpu.SemaphoreType.DMA((slots, len(each), parts)),
             ],
         ),
-        input_output_aliases={1 + len(operands): 0} if extra else {},
+        input_output_aliases={count + len(operands): 0} if extra else {},
         compiler_params=pltpu.CompilerParams(
             dimension_semantics=("arbitrary",), vmem_limit_bytes=VMEM
         ),
-        cost_estimate=BRIEF if first == 3 else LONG,
+        cost_estimate=BRIEF if first == 3 or z_first else LONG,
         name=f"combine_{first}_{z_first}",
-    )(where, codes, *operands)
+    )(where, *codes, *operands)
 
 
 def assemble(where, pieces):
@@ -190,10 +193,41 @@
     )(where, *[p.reshape(4, 2, n, width, width) for (_, p), n in zip(pieces, counts)])
 
 
+def pack(wavefunction, pair_left, pair_right):
+    width = wavefunction.shape[-1]
+
+    def kernel(left, right, in_ref, out_ref):
+        lane = lax.broadcasted_iota(jnp.int32, (TAIL, width), 1)
+        for x_r, c_r in np.ndindex(4, 2):
+            slot = x_r * 2 + c_r
+            n = pl.program_id(0) * 8 + slot
+            picks = jnp.where(lane == 0, left[n], jnp.where(lane == 1, right[n], 0))
+            out_ref[c_r, x_r, :width] = in_ref[slot]
+            out_ref[c_r, x_r, width:] = picks.astype(jnp.float32).astype(BF16)
+
+    return pl.pallas_call(
+        kernel,
+        out_shape=jax.ShapeDtypeStruct((8, 4, width + TAIL, width), BF16),
+        grid_spec=pltpu.PrefetchScalarGridSpec(
+            num_scalar_prefetch=2,
+            grid=(4,),
+            in_specs=[pl.BlockSpec((8, width, width), lambda q, left, right: (q, 0, 0))],
+            out_specs=pl.BlockSpec((2, 4, width + TAIL, width), lambda q, left, right: (q, 0, 0, 0)),
+        ),
+        compiler_params=pltpu.CompilerParams(vmem_limit_bytes=VMEM),
+        cost_estimate=BRIEF,
+        name="pack",
+    )(pair_left, pair_right, wavefunction)
+
+
 def column(psi, position):
     zero = jnp.uint32(0)
-    start = (zero, zero, position.astype(jnp.uint32), zero, zero)
-    return lax.dynamic_slice(psi, start, (4, 2, 1) + psi.shape[3:]).reshape((8,) + psi.shape[3:])
+    start = (zero, position.astype(jnp.uint32), zero, zero)
+    return lax.dynamic_slice(psi, start, (8, 1) + psi.shape[2:]).reshape((8,) + psi.shape[2:])
+
+
+def split(piece):
+    return piece, piece[:, -TAIL, :2].astype(jnp.int32).reshape(-1)
 
 
 def together(*arrays):
@@ -212,10 +246,7 @@
     left_own = left_own.reshape(sectors, terms * width, width)
     right_own = right_own.reshape(sectors, terms * width, width)
 
-    codes = exchange(pair_left + 2 * pair_right, ("y", "x", "c"))
-    psi = wavefunction.reshape(4, 4, 2, width, width).swapaxes(1, 2).reshape(wavefunction.shape)
-    psi, codes = together(psi, codes)
-    psi = exchange(psi, ("y", "c")).reshape(4, 2, 4, width, width)
+    psi = exchange(pack(wavefunction, pair_left, pair_right), ("y", "c"))
     right_low, right_high = both_ways(right_own, "z")
     left_low, left_high = both_ways(left_own, "x")
     left_other = shift(left_own, "c", 1, 2)
@@ -223,31 +254,31 @@
         psi, right_low, right_high, left_low, left_high, left_other
     )
 
-    psi_low = shift(column(psi, where[10]), "x", 1)
-    psi_high = shift(column(psi, where[11]), "x", 3)
-    far = onward(right_low, right_high, "z")
-    psi_own, psi_rest = column(psi, where[9]), column(psi, where[12])
+    for_low, for_high = column(psi, where[10]), column(psi, where[11])
+    for_low, for_high, psi, *to_far = together(for_low, for_high, psi, right_low, right_high)
+    psi_low, psi_high = shift(for_low, "x", 1), shift(for_high, "x", 3)
+    far = onward(*to_far, "z")
+    psi_own, psi_rest = split(column(psi, where[9])), column(psi, where[12])
     rights = [(right_own,), (right_low,), (right_high,)]
     lefts_own = [((left_own,), (left_other,))]
-    own = combine(where, codes, [psi_own], lefts_own, rights, 0)
+    own = combine(where, [psi_own], lefts_own, rights, 0)
     own, left_low, left_high = together(own, left_low, left_high)
     halves = left_low[:, : terms * width // 2], left_high[:, terms * width // 2 :]
-    psi_rest, psi_low, psi_high, own, *arrived = together(
-        psi_rest, psi_low, psi_high, own, *halves, *far, left_low, left_high
+    rights.append(tuple(far))
+    own = combine(where, [psi_own], lefts_own, rights[3:], 0, 3, own)
+    psi_rest, psi_low, psi_high, own, left_low, left_high, *halves = together(
+        psi_rest, psi_low, psi_high, own, left_low, left_high, *halves
     )
-    *halves, far_low, far_high, left_low, left_high = arrived
 
     left_far = shift(halves[0], "x", 1), shift(halves[1], "x", 3)
     psi_far = shift(psi_rest, "x", 2)
-    rights.append((far_low, far_high))
-    own = combine(where, codes, [psi_own], lefts_own, rights[3:], 0, 3, own)
     own = exchange(own, "z")
     lefts_near = [((a,), (shift(a, "c", 1, 2),)) for a in (left_low, left_high)]
-    near = combine(where, codes, [psi_low, psi_high], lefts_near, rights, 1)
-    psi_far, *left_far = together(psi_far, *left_far, near)[:-1]
+    near = combine(where, [split(psi_low), split(psi_high)], lefts_near, rights, 1)
+    left_far = together(*left_far, near)[:-1]
     near = exchange(near, "z")
     left_far = [(tuple(left_far), tuple(shift(a, "c", 1, 2) for a in left_far))]
-    rest = combine(where, codes, [psi_far], left_far, rights, 3)
+    rest = combine(where, [split(psi_far)], left_far, rights, 3)
     rest = exchange(rest, "z")
     applied = assemble(where, [(0, own), (1, near)])
     zero = jnp.uint32(0)

time: 220 us -> 203 us (0.923)
  waiting for transfers between devices: 91.2 us -> 78.2 us
  Pallas kernels: 49.3 us -> 55.4 us
  starting transfers between devices: 45.3 us -> 39.3 us
  other arithmetic: 6.65 us -> 3.84 us
    ppermute x16, waiting for transfers between devices: 79 us -> 71.1 us  [shift(): lax.ppermute(array, axis, [(i, (i + step) % size) for i in range(size)])]
    all_to_all x5 -> x4, starting transfers between devices: 26.8 us -> 20.1 us  [exchange(): return lax.all_to_all(array, axis, split_axis=0, concat_axis=0, tiled=True)]
    reshape x0 -> x2, local copies, waits for them, and re-layouts: none -> 5.85 us  [column(): lax.dynamic_slice(psi, start, (8, 1) + psi.shape[2:])]
    pallas_call x0 -> x1, Pallas kernels: none -> 5.5 us  [pack(): pl.pallas_call(kernel, out_shape=jax.ShapeDtypeStruct((8, 4, width + TAIL...]
    all_to_all x5 -> x4, waiting for transfers between devices: 12.2 us -> 7.06 us  [exchange(): return lax.all_to_all(array, axis, split_axis=0, concat_axis=0, tiled=True)]
    transpose x1 -> x0, local copies, waits for them, and re-layouts: 4.64 us -> none  [body(): wavefunction.reshape(4, 4, 2, width, width).swapaxes(1, 2)]
    dynamic_slice x1 -> x0, local copies, waits for them, and re-layouts: 4.25 us -> none  [column(): lax.dynamic_slice(psi, start, (4, 2, 1) + psi.shape[3:])]
    convert_element_type x0 -> x4, local copies, waits for them, and re-layouts: none -> 2.78 us  [split(): return (piece, piece[:, -TAIL, :2].astype(jnp.int32).reshape(-1))]
  transfers between devices with their start and end apart: 21 -> 20, of which waited for: 14 -> 6; matrix products, arithmetic and copies ran while one was open for 9% -> 7% of each run, Pallas kernels for 23% -> 25%
where the time goes in v6:
time: 203 us; the launch traced here: 202 us
  waiting for transfers between devices  78.2 us (39%)
  Pallas kernels  55.4 us (27%)
  starting transfers between devices  39.3 us (19%)
  local copies, waits for them, and re-layouts  22.2 us (11%)
  other arithmetic  3.84 us (2%)
  between operations  3.25 us (2%)
    ppermute x16, waiting for transfers between devices, shift(): lax.ppermute(array, axis, [(i, (i + step) % size) for i in range(size)])  71.1 us
    pallas_call x4, Pallas kernels, combine(): pl.pallas_call(kernel, out_shape=jax.ShapeDtypeStruct((8 * count, width,...  44.9 us
    all_to_all x4, starting transfers between devices, exchange(): return lax.all_to_all(array, axis, split_axis=0, concat_axis=0, tiled=True)  20.1 us
    ppermute x16, starting transfers between devices, shift(): lax.ppermute(array, axis, [(i, (i + step) % size) for i in range(size)])  19.1 us
    all_to_all x4, waiting for transfers between devices, exchange(): return lax.all_to_all(array, axis, split_axis=0, concat_axis=0, tiled=True)  7.06 us
    reshape x2, local copies, waits for them, and re-layouts, column(): lax.dynamic_slice(psi, start, (8, 1) + psi.shape[2:])  5.85 us
    pallas_call x1, Pallas kernels, pack(): pl.pallas_call(kernel, out_shape=jax.ShapeDtypeStruct((8, 4, width + TAIL...  5.5 us
    pallas_call x1, Pallas kernels, assemble(): pl.pallas_call(kernel, out_shape=jax.ShapeDtypeStruct((4, 4, 2, width, wi...  5.04 us
  transfers between devices with their start and end apart: 20, of which 6 were waited for; matrix products, arithmetic and copies ran while one was open for 7% of the time, Pallas kernels for 25%

profile of v6, /device:TPU:0, one launch (start us, length us, event | category | flops | bytes accessed | tf_op | source)
XLA Modules:
  0.0 202.1 jit_solution(18417752271971224302)
XLA Ops:
  0.0 5.5 %pack.1 = bf16[8,4,272,256]{3,2,1,0:T(8,128)(2,1)} custom-call(s32[32]{0:T(128)} %left.1, s32[32]{0:T(128)} %right.1, bf16[32,256,256]{2,1,0:T(8,128)(2,1)} %in_ref.1), custom_call_target="tpu_custom_call" | custom-call | flops 1 | bytes 1 | tf_op jit(solution)/shard_map/pack/pallas_call | solution.py:208
  5.5 4.7 %all-to-all-start = ((bf16[8,4,272,256]{3,2,1,0:T(8,128)(2,1)}), bf16[8,4,272,256]{3,2,1,0:T(8,128)(2,1)}, u32[]{:S(2)}, u32[]{:S(2)}) async-start(bf16[8,4,272,256]{3,2,1,0:T(8,128)(2,1)} %pack.1), calls=%async_computation | async-start | bytes 8912896 | tf_op jit(solution)/shard_map/all_to_all | solution.py:33
  10.3 0.0 copy-start.4
  10.3 2.1 %fusion = bf16[2,8,256,256]{3,2,1,0:T(8,128)(2,1)} fusion(bf16[2,8,256,256]{3,2,1,0:T(8,128)(2,1)S(1)} %copy-done.3, s32[2]{0:T(128)S(1)} %copy-done.6), kind=kLoop, calls=%fused_computation.2 | loop fusion | flops 2097152 | bytes 4194312 | tf_op jit(solution)/shard_map/jit(_where)/select_n | solution.py:243
  12.4 2.0 collective-permute-start
  14.5 2.1 %collective-permute-start.1 = (bf16[2,2048,256]{2,1,0:T(8,128)(2,1)}, bf16[2,2048,256]{2,1,0:T(8,128)(2,1)}, u32[]{:S(2)}, u32[]{:S(2)}) collective-permute-start(bf16[2,2048,256]{2,1,0:T(8,128)(2,1)} %bitcast.1.refs_4_.refs_8_.refs_6_), channel_id=1, source_target_pairs={{0,24},{8,0},{16,8},{24,16},{1,25},{9,1},{17,9},{25,17},{2,26},{10... | collective-permute-start | bytes 6291464 | tf_op jit(solution)/shard_map/ppermute | solution.py:37
  16.6 0.9 fusion.1
  17.5 1.6 collective-permute-start.2
  19.0 1.7 collective-permute-start.3
  20.8 1.2 constant_dynamic-slice_fusion
  22.0 0.7 fusion.5
  25.0 38.0 %collective-permute-done.refs_5_.refs_9_.refs_7_ = bf16[2,2048,256]{2,1,0:T(8,128)(2,1)} collective-permute-done((bf16[2,2048,256]{2,1,0:T(8,128)(2,1)}, bf16[2,2048,256]{2,1,0:T(8,128)(2,1)}, u32[]{:S(2)}, u32[]{:S(2)}) %collective-permute-start) | collective-permute-done | bytes 2097184 | tf_op jit(solution)/shard_map/ppermute | solution.py:37
  63.0 3.4 %collective-permute-done.2.refs_4_ = bf16[2,2048,256]{2,1,0:T(8,128)(2,1)} collective-permute-done((bf16[2,2048,256]{2,1,0:T(8,128)(2,1)S(1)}, bf16[2,2048,256]{2,1,0:T(8,128)(2,1)}, u32[]{:S(2)}, u32[]{:S(2)}) %collective-permute-start.2) | collective-permute-done | bytes 2097184 | tf_op jit(solution)/shard_map/ppermute | solution.py:37
  66.5 3.1 %dynamic-slice_bitcast_fusion.2 = (bf16[8,272,256]{2,1,0:T(8,128)(2,1)}, bf16[8,272,256]{2,1,0:T(8,128)(2,1)}) fusion(bf16[8,4,272,256]{3,2,1,0:T(8,128)(2,1)} %all-to-all-done, u32[]{:T(128)} %bitcast.5, u32[]{:T(128)} %bitcast.3), kind=kLoop, calls=%fused_computation.6 | loop fusion | bytes 4456456 | tf_op jit(solution)/shard_map/reshape | solution.py:226
  69.6 2.7 %dynamic-slice_bitcast_fusion = (bf16[8,272,256]{2,1,0:T(8,128)(2,1)S(1)}, bf16[8,272,256]{2,1,0:T(8,128)(2,1)}) fusion(bf16[8,4,272,256]{3,2,1,0:T(8,128)(2,1)} %all-to-all-done, u32[]{:T(128)} %bitcast.9, u32[]{:T(128)} %bitcast.7), kind=kLoop, calls=%fused_computation.4 | loop fusion | bytes 4456456 | tf_op jit(solution)/shard_map/reshape | solution.py:226
  72.4 0.8 reshape.80.refs_0_
  73.2 2.3 %slice.49 = bf16[2,1024,256]{2,1,0:T(8,128)(2,1)} slice(bf16[2,2048,256]{2,1,0:T(8,128)(2,1)} %collective-permute-done.refs_5_.refs_9_.refs_7_), slice={[0:2], [0:1024], [0:256]} | slice | bytes 2097152 | tf_op jit(solution)/shard_map/slice | solution.py:46
  75.4 2.2 %slice.50 = bf16[2,1024,256]{2,1,0:T(8,128)(2,1)} slice(bf16[2,2048,256]{2,1,0:T(8,128)(2,1)} %collective-permute-done.1.refs_6_.refs_10_.refs_8_), slice={[0:2], [1024:2048], [0:256]} | slice | bytes 2097152 | tf_op jit(solution)/shard_map/slice | solution.py:46
  77.7 3.2 %collective-permute-start.8 = (bf16[2,1024,256]{2,1,0:T(8,128)(2,1)}, bf16[2,1024,256]{2,1,0:T(8,128)(2,1)}, u32[]{:S(2)}, u32[]{:S(2)}) collective-permute-start(bf16[2,1024,256]{2,1,0:T(8,128)(2,1)} %slice.50), channel_id=1, source_target_pairs={{0,24},{8,0},{16,8},{24,16},{1,25},{9,1},{17,9},{25,17},{2,26},{10... | collective-permute-start | bytes 3145736 | tf_op jit(solution)/shard_map/ppermute | solution.py:37
  80.9 1.5 collective-permute-start.5
  82.4 1.8 collective-permute-start.6
  84.1 9.9 %combine_0_0.1.refs_6_ = bf16[8,256,256]{2,1,0:T(8,128)(2,1)} custom-call(s32[13]{0:T(128)} %get-tuple-element.58.where, s32[16]{0:T(128)} %reshape.80.refs_0_, bf16[8,272,256]{2,1,0:T(8,128)(2,1)} %copy-done.2, bf16[2,2048,256]{2,1,0:T(8,128)(2,1)} %bitcast.26, bf16[2,2048,256]{2,1,0:T(8,128)(2,1)} %collective-permute-done.4.refs_3_, ...), custom_call_target="tpu_custom_call" | custom-call | flops 999999995904 | bytes 1 | tf_op jit(solution)/shard_map/combine_0_0/pallas_call | solution.py:144
  94.1 2.3 %slice.51 = bf16[2,1024,256]{2,1,0:T(8,128)(2,1)} slice(bf16[2,2048,256]{2,1,0:T(8,128)(2,1)} %collective-permute-done.2.refs_4_), slice={[0:2], [0:1024], [0:256]} | slice | bytes 2097152 | tf_op jit(solution)/shard_map/slice | solution.py:266
  96.3 2.3 %slice.52 = bf16[2,1024,256]{2,1,0:T(8,128)(2,1)} slice(bf16[2,2048,256]{2,1,0:T(8,128)(2,1)} %collective-permute-done.3.refs_6_), slice={[0:2], [1024:2048], [0:256]} | slice | bytes 2097152 | tf_op jit(solution)/shard_map/slice | solution.py:266
  98.6 2.6 %collective-permute-done.7.refs_4_.refs_11_.refs_9_ = bf16[2,1024,256]{2,1,0:T(8,128)(2,1)} collective-permute-done((bf16[2,1024,256]{2,1,0:T(8,128)(2,1)}, bf16[2,1024,256]{2,1,0:T(8,128)(2,1)}, u32[]{:S(2)}, u32[]{:S(2)}) %collective-permute-start.7) | collective-permute-done | bytes 1048608 | tf_op jit(solution)/shard_map/ppermute | solution.py:37
  101.3 1.5 collective-permute-done.8.refs_5_.refs_12_.refs_10_
  102.8 6.4 %combine_0_3.1 = bf16[8,256,256]{2,1,0:T(8,128)(2,1)} custom-call(s32[13]{0:T(128)} %get-tuple-element.58.where, s32[16]{0:T(128)} %reshape.80.refs_0_, bf16[8,272,256]{2,1,0:T(8,128)(2,1)} %copy-done.2, bf16[2,2048,256]{2,1,0:T(8,128)(2,1)} %bitcast.27, bf16[2,2048,256]{2,1,0:T(8,128)(2,1)} %collective-permute-done.4.refs_3_, ...), custom_call_target="tpu_custom_call", output_to_operand_aliasing={{}: (7, {})} | custom-call | flops 1 | bytes 1 | tf_op jit(solution)/shard_map/combine_0_3/pallas_call | solution.py:144
  109.2 0.1 collective-permute-start.10
  109.3 0.5 collective-permute-start.9
  109.8 0.8 convert_reduce_fusion
  110.6 0.7 reshape.81.refs_0_
  111.2 0.6 reshape.82.refs_1_
  111.8 1.2 collective-permute-start.12
  113.0 2.1 %collective-permute-start.13 = (bf16[2,1024,256]{2,1,0:T(8,128)(2,1)}, bf16[2,1024,256]{2,1,0:T(8,128)(2,1)}, u32[]{:S(2)}, u32[]{:S(2)}) collective-permute-start(bf16[2,1024,256]{2,1,0:T(8,128)(2,1)} %slice.52), channel_id=1, source_target_pairs={{0,6},{2,0},{4,2},{6,4},{1,7},{3,1},{5,3},{7,5},{8,14},{10,8},{12,... | collective-permute-start | bytes 3145736 | tf_op jit(solution)/shard_map/ppermute | solution.py:37
  115.1 4.9 %all-to-all-start.1 = ((bf16[8,256,256]{2,1,0:T(8,128)(2,1)}), bf16[8,256,256]{2,1,0:T(8,128)(2,1)}, u32[]{:S(2)}, u32[]{:S(2)}) async-start(bf16[8,256,256]{2,1,0:T(8,128)(2,1)} %combine_0_3.1), calls=%async_computation.1 | async-start | bytes 2097152 | tf_op jit(solution)/shard_map/all_to_all | solution.py:33
  120.0 1.3 copy-done.8
  121.3 17.9 %combine_1_0.1 = bf16[16,256,256]{2,1,0:T(8,128)(2,1)} custom-call(s32[13]{0:T(128)} %get-tuple-element.58.where, s32[16]{0:T(128)} %reshape.81.refs_0_, s32[16]{0:T(128)} %reshape.82.refs_1_, bf16[8,272,256]{2,1,0:T(8,128)(2,1)} %collective-permute-done.5.refs_2_, bf16[8,272,256]{2,1,0:T(8,128)(2,1)} %collective-permute-done.6.refs_3_, ...), custom_call_target="tpu_custom_call" | custom-call | flops 999999995904 | bytes 1 | tf_op jit(solution)/shard_map/combine_1_0/pallas_call | solution.py:144
  139.3 5.1 %all-to-all-start.2 = ((bf16[16,256,256]{2,1,0:T(8,128)(2,1)}), bf16[16,256,256]{2,1,0:T(8,128)(2,1)S(1)}, u32[]{:S(2)}, u32[]{:S(2)}) async-start(bf16[16,256,256]{2,1,0:T(8,128)(2,1)} %combine_1_0.1), calls=%async_computation.2 | async-start | bytes 4194304 | tf_op jit(solution)/shard_map/all_to_all | solution.py:33
  144.4 0.9 collective-permute-start.11
  145.3 0.5 collective-permute-start.15
  145.8 25.5 %collective-permute-done.11.refs_1_ = bf16[8,272,256]{2,1,0:T(8,128)(2,1)S(1)} collective-permute-done((bf16[8,272,256]{2,1,0:T(8,128)(2,1)}, bf16[8,272,256]{2,1,0:T(8,128)(2,1)S(1)}, u32[]{:S(2)}, u32[]{:S(2)}) %collective-permute-start.11) | collective-permute-done | bytes 1114144 | tf_op jit(solution)/shard_map/ppermute | solution.py:37
  171.3 0.7 reshape.83.refs_0_
  172.0 0.2 copy-done.5
  172.2 10.7 %combine_3_0.1 = bf16[8,256,256]{2,1,0:T(8,128)(2,1)} custom-call(s32[13]{0:T(128)} %get-tuple-element.58.where, s32[16]{0:T(128)} %reshape.83.refs_0_, bf16[8,272,256]{2,1,0:T(8,128)(2,1)} %copy-done.5, bf16[2,1024,256]{2,1,0:T(8,128)(2,1)} %collective-permute-done.12.refs_2_, bf16[2,1024,256]{2,1,0:T(8,128)(2,1)} %collective-permute-done.13.refs_3_, ...), custom_call_target="tpu_custom_call" | custom-call | flops 1 | bytes 1 | tf_op jit(solution)/shard_map/combine_3_0/pallas_call | solution.py:144
  182.9 5.3 %all-to-all-start.3 = ((bf16[8,256,256]{2,1,0:T(8,128)(2,1)}), bf16[8,256,256]{2,1,0:T(8,128)(2,1)S(1)}, u32[]{:S(2)}, u32[]{:S(2)}) async-start(bf16[8,256,256]{2,1,0:T(8,128)(2,1)} %combine_3_0.1), calls=%async_computation.3 | async-start | bytes 2097152 | tf_op jit(solution)/shard_map/all_to_all | solution.py:33
  188.9 5.0 %assemble.1 = bf16[4,4,2,256,256]{4,3,2,1,0:T(8,128)(2,1)} custom-call(s32[13]{0:T(128)} %get-tuple-element.58.where, bf16[4,2,1,256,256]{4,3,2,1,0:T(8,128)(2,1)} %bitcast.11.refs_0_, bf16[4,2,2,256,256]{4,3,2,1,0:T(8,128)(2,1)} %bitcast.28), custom_call_target="tpu_custom_call" | custom-call | flops 1 | bytes 1 | tf_op jit(solution)/shard_map/assemble/pallas_call | solution.py:181
  194.0 7.1 %all-to-all-done.3 = bf16[8,256,256]{2,1,0:T(8,128)(2,1)S(1)} async-done(((bf16[8,256,256]{2,1,0:T(8,128)(2,1)}), bf16[8,256,256]{2,1,0:T(8,128)(2,1)S(1)}, u32[]{:S(2)}, u32[]{:S(2)}) %all-to-all-start.3) | async-done | bytes 1048608 | tf_op jit(solution)/shard_map/all_to_all | solution.py:33
  201.0 1.0 constant_dynamic-update-slice_fusion
  (34 shorter events, 0.1 us)
Async XLA Ops:
  5.5 4.7 %copy-start.3 = (bf16[2,8,256,256]{3,2,1,0:T(8,128)(2,1)S(1)}, bf16[2,8,256,256]{3,2,1,0:T(8,128)(2,1)}, u32[]{:S(2)}) copy-start(bf16[2,8,256,256]{3,2,1,0:T(8,128)(2,1)} %param.13) | copy-start | bytes 6291460
  5.5 4.8 %copy-start.6 = (s32[2]{0:T(128)S(1)}, s32[2]{0:T(128)}, u32[]{:S(2)}) copy-start(s32[2]{0:T(128)} %param.14) | copy-start | bytes 28
  5.5 61.0 %all-to-all-start = ((bf16[8,4,272,256]{3,2,1,0:T(8,128)(2,1)}), bf16[8,4,272,256]{3,2,1,0:T(8,128)(2,1)}, u32[]{:S(2)}, u32[]{:S(2)}) async-start(bf16[8,4,272,256]{3,2,1,0:T(8,128)(2,1)} %pack.1), calls=%async_computation | async-start | bytes 8912896 | tf_op jit(solution)/shard_map/all_to_all | solution.py:33
  10.3 6.3 %copy-start.4 = (bf16[2,8,256,256]{3,2,1,0:T(8,128)(2,1)S(1)}, bf16[2,8,256,256]{3,2,1,0:T(8,128)(2,1)}, u32[]{:S(2)}) copy-start(bf16[2,8,256,256]{3,2,1,0:T(8,128)(2,1)} %param.11) | copy-start | bytes 6291460
  10.3 6.3 %copy-start.7 = (s32[2]{0:T(128)S(1)}, s32[2]{0:T(128)}, u32[]{:S(2)}) copy-start(s32[2]{0:T(128)} %param.12) | copy-start | bytes 28
  12.4 50.6 %collective-permute-start = (bf16[2,2048,256]{2,1,0:T(8,128)(2,1)}, bf16[2,2048,256]{2,1,0:T(8,128)(2,1)}, u32[]{:S(2)}, u32[]{:S(2)}) collective-permute-start(bf16[2,2048,256]{2,1,0:T(8,128)(2,1)} %bitcast.1.refs_4_.refs_8_.refs_6_), channel_id=1, source_target_pairs={{0,8},{8,16},{16,24},{24,0},{1,9},{9,17},{17,25},{25,1},{2,10},{10... | collective-permute-start | bytes 6291464 | tf_op jit(solution)/shard_map/ppermute | solution.py:37
  14.5 48.6 %collective-permute-start.1 = (bf16[2,2048,256]{2,1,0:T(8,128)(2,1)}, bf16[2,2048,256]{2,1,0:T(8,128)(2,1)}, u32[]{:S(2)}, u32[]{:S(2)}) collective-permute-start(bf16[2,2048,256]{2,1,0:T(8,128)(2,1)} %bitcast.1.refs_4_.refs_8_.refs_6_), channel_id=1, source_target_pairs={{0,24},{8,0},{16,8},{24,16},{1,25},{9,1},{17,9},{25,17},{2,26},{10... | collective-permute-start | bytes 6291464 | tf_op jit(solution)/shard_map/ppermute | solution.py:37
  17.5 52.1 %copy-start = (bf16[2,8,256,256]{3,2,1,0:T(8,128)(2,1)}, bf16[2,8,256,256]{3,2,1,0:T(8,128)(2,1)S(1)}, u32[]{:S(2)}) copy-start(bf16[2,8,256,256]{3,2,1,0:T(8,128)(2,1)S(1)} %fusion.1) | copy-start | bytes 6291460
  17.5 49.0 %collective-permute-start.2 = (bf16[2,2048,256]{2,1,0:T(8,128)(2,1)S(1)}, bf16[2,2048,256]{2,1,0:T(8,128)(2,1)}, u32[]{:S(2)}, u32[]{:S(2)}) collective-permute-start(bf16[2,2048,256]{2,1,0:T(8,128)(2,1)S(1)} %bitcast.23), channel_id=1, source_target_pairs={{0,2},{2,4},{4,6},{6,0},{1,3},{3,5},{5,7},{7,1},{8,10},{10,12},{12... | collective-permute-start | bytes 6291464 | tf_op jit(solution)/shard_map/ppermute | solution.py:37
  19.0 47.4 %collective-permute-start.3 = (bf16[2,2048,256]{2,1,0:T(8,128)(2,1)S(1)}, bf16[2,2048,256]{2,1,0:T(8,128)(2,1)}, u32[]{:S(2)}, u32[]{:S(2)}) collective-permute-start(bf16[2,2048,256]{2,1,0:T(8,128)(2,1)S(1)} %bitcast.24), channel_id=1, source_target_pairs={{0,6},{2,0},{4,2},{6,4},{1,7},{3,1},{5,3},{7,5},{8,14},{10,8},{12,... | collective-permute-start | bytes 6291464 | tf_op jit(solution)/shard_map/ppermute | solution.py:37
  20.8 45.7 %collective-permute-start.4 = (bf16[2,2048,256]{2,1,0:T(8,128)(2,1)S(1)}, bf16[2,2048,256]{2,1,0:T(8,128)(2,1)}, u32[]{:S(2)}, u32[]{:S(2)}) collective-permute-start(bf16[2,2048,256]{2,1,0:T(8,128)(2,1)S(1)} %bitcast.25), channel_id=1, source_target_pairs={{0,1},{1,0},{2,3},{3,2},{4,5},{5,4},{6,7},{7,6},{8,9},{9,8},{10,11... | collective-permute-start | bytes 6291464 | tf_op jit(solution)/shard_map/ppermute | solution.py:37
  72.3 5.3 %copy-start.2 = (bf16[8,272,256]{2,1,0:T(8,128)(2,1)}, bf16[8,272,256]{2,1,0:T(8,128)(2,1)S(1)}, u32[]{:S(2)}) copy-start(bf16[8,272,256]{2,1,0:T(8,128)(2,1)S(1)} %get-tuple-element.53.refs_1_) | copy-start | bytes 3342340
  75.4 25.8 %collective-permute-start.7 = (bf16[2,1024,256]{2,1,0:T(8,128)(2,1)}, bf16[2,1024,256]{2,1,0:T(8,128)(2,1)}, u32[]{:S(2)}, u32[]{:S(2)}) collective-permute-start(bf16[2,1024,256]{2,1,0:T(8,128)(2,1)} %slice.49), channel_id=1, source_target_pairs={{0,8},{8,16},{16,24},{24,0},{1,9},{9,17},{17,25},{25,1},{2,10},{10... | collective-permute-start | bytes 3145736 | tf_op jit(solution)/shard_map/ppermute | solution.py:37
  77.7 25.1 %collective-permute-start.8 = (bf16[2,1024,256]{2,1,0:T(8,128)(2,1)}, bf16[2,1024,256]{2,1,0:T(8,128)(2,1)}, u32[]{:S(2)}, u32[]{:S(2)}) collective-permute-start(bf16[2,1024,256]{2,1,0:T(8,128)(2,1)} %slice.50), channel_id=1, source_target_pairs={{0,24},{8,0},{16,8},{24,16},{1,25},{9,1},{17,9},{25,17},{2,26},{10... | collective-permute-start | bytes 3145736 | tf_op jit(solution)/shard_map/ppermute | solution.py:37
  80.9 28.3 %collective-permute-start.5 = (bf16[8,272,256]{2,1,0:T(8,128)(2,1)}, bf16[8,272,256]{2,1,0:T(8,128)(2,1)}, u32[]{:S(2)}, u32[]{:S(2)}) collective-permute-start(bf16[8,272,256]{2,1,0:T(8,128)(2,1)} %get-tuple-element.33), channel_id=1, source_target_pairs={{0,2},{2,4},{4,6},{6,0},{1,3},{3,5},{5,7},{7,1},{8,10},{10,12},{12... | collective-permute-start | bytes 3342344 | tf_op jit(solution)/shard_map/ppermute | solution.py:37
  82.4 26.8 %collective-permute-start.6 = (bf16[8,272,256]{2,1,0:T(8,128)(2,1)}, bf16[8,272,256]{2,1,0:T(8,128)(2,1)}, u32[]{:S(2)}, u32[]{:S(2)}) collective-permute-start(bf16[8,272,256]{2,1,0:T(8,128)(2,1)} %get-tuple-element.34), channel_id=1, source_target_pairs={{0,6},{2,0},{4,2},{6,4},{1,7},{3,1},{5,3},{7,5},{8,14},{10,8},{12,... | collective-permute-start | bytes 3342344 | tf_op jit(solution)/shard_map/ppermute | solution.py:37
  109.2 10.8 %collective-permute-start.10 = (bf16[2,2048,256]{2,1,0:T(8,128)(2,1)}, bf16[2,2048,256]{2,1,0:T(8,128)(2,1)S(1)}, u32[]{:S(2)}, u32[]{:S(2)}) collective-permute-start(bf16[2,2048,256]{2,1,0:T(8,128)(2,1)} %collective-permute-done.3.refs_6_), channel_id=1, source_target_pairs={{0,1},{1,0},{2,3},{3,2},{4,5},{5,4},{6,7},{7,6},{8,9},{9,8},{10,11... | collective-permute-start | bytes 6291464 | tf_op jit(solution)/shard_map/ppermute | solution.py:37
  109.3 10.7 %collective-permute-start.9 = (bf16[2,2048,256]{2,1,0:T(8,128)(2,1)}, bf16[2,2048,256]{2,1,0:T(8,128)(2,1)}, u32[]{:S(2)}, u32[]{:S(2)}) collective-permute-start(bf16[2,2048,256]{2,1,0:T(8,128)(2,1)} %collective-permute-done.2.refs_4_), channel_id=1, source_target_pairs={{0,1},{1,0},{2,3},{3,2},{4,5},{5,4},{6,7},{7,6},{8,9},{9,8},{10,11... | collective-permute-start | bytes 6291464 | tf_op jit(solution)/shard_map/ppermute | solution.py:37
  111.8 33.5 %collective-permute-start.12 = (bf16[2,1024,256]{2,1,0:T(8,128)(2,1)}, bf16[2,1024,256]{2,1,0:T(8,128)(2,1)}, u32[]{:S(2)}, u32[]{:S(2)}) collective-permute-start(bf16[2,1024,256]{2,1,0:T(8,128)(2,1)} %slice.51), channel_id=1, source_target_pairs={{0,2},{2,4},{4,6},{6,0},{1,3},{3,5},{5,7},{7,1},{8,10},{10,12},{12... | collective-permute-start | bytes 3145736 | tf_op jit(solution)/shard_map/ppermute | solution.py:37
  113.0 32.3 %collective-permute-start.13 = (bf16[2,1024,256]{2,1,0:T(8,128)(2,1)}, bf16[2,1024,256]{2,1,0:T(8,128)(2,1)}, u32[]{:S(2)}, u32[]{:S(2)}) collective-permute-start(bf16[2,1024,256]{2,1,0:T(8,128)(2,1)} %slice.52), channel_id=1, source_target_pairs={{0,6},{2,0},{4,2},{6,4},{1,7},{3,1},{5,3},{7,5},{8,14},{10,8},{12,... | collective-permute-start | bytes 3145736 | tf_op jit(solution)/shard_map/ppermute | solution.py:37
  115.1 24.2 %all-to-all-start.1 = ((bf16[8,256,256]{2,1,0:T(8,128)(2,1)}), bf16[8,256,256]{2,1,0:T(8,128)(2,1)}, u32[]{:S(2)}, u32[]{:S(2)}) async-start(bf16[8,256,256]{2,1,0:T(8,128)(2,1)} %combine_0_3.1), calls=%async_computation.1 | async-start | bytes 2097152 | tf_op jit(solution)/shard_map/all_to_all | solution.py:33
  120.0 1.3 copy-start.8
  139.3 43.7 %all-to-all-start.2 = ((bf16[16,256,256]{2,1,0:T(8,128)(2,1)}), bf16[16,256,256]{2,1,0:T(8,128)(2,1)S(1)}, u32[]{:S(2)}, u32[]{:S(2)}) async-start(bf16[16,256,256]{2,1,0:T(8,128)(2,1)} %combine_1_0.1), calls=%async_computation.2 | async-start | bytes 4194304 | tf_op jit(solution)/shard_map/all_to_all | solution.py:33
  144.4 26.9 %collective-permute-start.11 = (bf16[8,272,256]{2,1,0:T(8,128)(2,1)}, bf16[8,272,256]{2,1,0:T(8,128)(2,1)S(1)}, u32[]{:S(2)}, u32[]{:S(2)}) collective-permute-start(bf16[8,272,256]{2,1,0:T(8,128)(2,1)} %get-tuple-element.48), channel_id=1, source_target_pairs={{0,4},{2,6},{4,0},{6,2},{1,5},{3,7},{5,1},{7,3},{8,12},{10,14},{12... | collective-permute-start | bytes 3342344 | tf_op jit(solution)/shard_map/ppermute | solution.py:37
  145.3 26.7 %collective-permute-start.14 = (bf16[2,1024,256]{2,1,0:T(8,128)(2,1)}, bf16[2,1024,256]{2,1,0:T(8,128)(2,1)}, u32[]{:S(2)}, u32[]{:S(2)}) collective-permute-start(bf16[2,1024,256]{2,1,0:T(8,128)(2,1)} %collective-permute-done.12.refs_2_), channel_id=1, source_target_pairs={{0,1},{1,0},{2,3},{3,2},{4,5},{5,4},{6,7},{7,6},{8,9},{9,8},{10,11... | collective-permute-start | bytes 3145736 | tf_op jit(solution)/shard_map/ppermute | solution.py:37
  145.3 26.7 %collective-permute-start.15 = (bf16[2,1024,256]{2,1,0:T(8,128)(2,1)}, bf16[2,1024,256]{2,1,0:T(8,128)(2,1)}, u32[]{:S(2)}, u32[]{:S(2)}) collective-permute-start(bf16[2,1024,256]{2,1,0:T(8,128)(2,1)} %collective-permute-done.13.refs_3_), channel_id=1, source_target_pairs={{0,1},{1,0},{2,3},{3,2},{4,5},{5,4},{6,7},{7,6},{8,9},{9,8},{10,11... | collective-permute-start | bytes 3145736 | tf_op jit(solution)/shard_map/ppermute | solution.py:37
  171.3 1.0 copy-start.5
  182.9 6.0 %copy-start.1 = (bf16[16,256,256]{2,1,0:T(8,128)(2,1)}, bf16[16,256,256]{2,1,0:T(8,128)(2,1)S(1)}, u32[]{:S(2)}) copy-start(bf16[16,256,256]{2,1,0:T(8,128)(2,1)S(1)} %all-to-all-done.2) | copy-start | bytes 6291460
  182.9 18.1 %all-to-all-start.3 = ((bf16[8,256,256]{2,1,0:T(8,128)(2,1)}), bf16[8,256,256]{2,1,0:T(8,128)(2,1)S(1)}, u32[]{:S(2)}, u32[]{:S(2)}) async-start(bf16[8,256,256]{2,1,0:T(8,128)(2,1)} %combine_3_0.1), calls=%async_computation.3 | async-start | bytes 2097152 | tf_op jit(solution)/shard_map/all_to_all | solution.py:33

commit v7 on v6

--- a/solution.py
+++ b/solution.py
@@ -49,7 +49,8 @@
 def combine(where, psis, lefts, rights, first, z_first=0, kept=None):
     codes = [codes for _, codes in psis]
     psis = [psi for psi, _ in psis]
-    rows, width = psis[0].shape[1:]
+    rows, width = psis[0].shape[2:]
+    columns = psis[0].shape[1]
     depth = sum(a.shape[1] for a in lefts[0][0])
     terms = depth // width
     count = len(lefts)
@@ -59,8 +60,12 @@
     slots = min(SLOTS, steps)
     each = [(core, k) for core in range(2) for k in range(count)]
 
+    def mine(where):
+        return where[9] if columns > 1 else 0
+
     def pick_of(step, core, k, side, where, codes):
-        return codes[k][(where[z_first + step] * 2 + (where[8] ^ core)) * 2 + side]
+        block = where[z_first + step] * 2 + (where[8] ^ core)
+        return codes[k][(block * columns + mine(where)) * 2 + side]
 
     def kernel(where, *refs):
         codes, refs = refs[:count], list(refs[count:])
@@ -122,7 +127,7 @@
         slot = lax.rem(step, slots)
         for n_block, (core, k) in enumerate(each):
             left = pick_of(step, core, k, 0, where, codes)
-            block = psi_refs[k][where[8] ^ core, :width]
+            block = psi_refs[k][where[8] ^ core, 0, :width]
             for t in range(terms):
                 product = jnp.dot(
                     left_buf[k, core, left, t * width : (t + 1) * width],
@@ -138,6 +143,7 @@
 
     in_place = pl.BlockSpec(memory_space=pl.ANY)
     of_g = lambda step, where, *codes: (where[z_first + step], 0, 0)
+    psi_of_g = lambda step, where, *codes: (where[z_first + step], mine(where), 0, 0)
     parts = max(len(group) for group in rights)
     extra = [] if kept is None else [kept]
     operands = [*psis, *left_parts, *right_parts, *extra]
@@ -147,7 +153,7 @@
         grid_spec=pltpu.PrefetchScalarGridSpec(
             num_scalar_prefetch=1 + count,
             grid=(steps,),
-            in_specs=[pl.BlockSpec((2, rows, width), of_g)] * count
+            in_specs=[pl.BlockSpec((2, 1, rows, width), psi_of_g)] * count
             + [in_place] * (len(operands) - count),
             out_specs=pl.BlockSpec((2 * count, width, width), of_g),
             scratch_shapes=[
@@ -223,11 +229,11 @@
 def column(psi, position):
     zero = jnp.uint32(0)
     start = (zero, position.astype(jnp.uint32), zero, zero)
-    return lax.dynamic_slice(psi, start, (8, 1) + psi.shape[2:]).reshape((8,) + psi.shape[2:])
+    return lax.dynamic_slice(psi, start, (8, 1) + psi.shape[2:])
 
 
 def split(piece):
-    return piece, piece[:, -TAIL, :2].astype(jnp.int32).reshape(-1)
+    return piece, piece[:, :, -TAIL, :2].astype(jnp.int32).reshape(-1)
 
 
 def together(*arrays):
@@ -258,24 +264,26 @@
     for_low, for_high, psi, *to_far = together(for_low, for_high, psi, right_low, right_high)
     psi_low, psi_high = shift(for_low, "x", 1), shift(for_high, "x", 3)
     far = onward(*to_far, "z")
-    psi_own, psi_rest = split(column(psi, where[9])), column(psi, where[12])
+    psi_own = split(psi)
     rights = [(right_own,), (right_low,), (right_high,)]
     lefts_own = [((left_own,), (left_other,))]
     own = combine(where, [psi_own], lefts_own, rights, 0)
-    own, left_low, left_high = together(own, left_low, left_high)
+    own, psi, left_low, left_high = together(own, psi, left_low, left_high)
     halves = left_low[:, : terms * width // 2], left_high[:, terms * width // 2 :]
     rights.append(tuple(far))
     own = combine(where, [psi_own], lefts_own, rights[3:], 0, 3, own)
     psi_rest, psi_low, psi_high, own, left_low, left_high, *halves = together(
-        psi_rest, psi_low, psi_high, own, left_low, left_high, *halves
+        column(psi, where[12]), psi_low, psi_high, own, left_low, left_high, *halves
     )
 
     left_far = shift(halves[0], "x", 1), shift(halves[1], "x", 3)
     psi_far = shift(psi_rest, "x", 2)
     own = exchange(own, "z")
-    lefts_near = [((a,), (shift(a, "c", 1, 2),)) for a in (left_low, left_high)]
+    others = [shift(a, "c", 1, 2) for a in (left_low, left_high)]
+    psi_low, psi_high, *others = together(psi_low, psi_high, *others)
+    lefts_near = [((left_low,), (others[0],)), ((left_high,), (others[1],))]
     near = combine(where, [split(psi_low), split(psi_high)], lefts_near, rights, 1)
-    left_far = together(*left_far, near)[:-1]
+    psi_far, *left_far = together(psi_far, *left_far, near)[:-1]
     near = exchange(near, "z")
     left_far = [(tuple(left_far), tuple(shift(a, "c", 1, 2) for a in left_far))]
     rest = combine(where, [split(psi_far)], left_far, rights, 3)

time: 203 us -> 196 us (0.966)
  waiting for transfers between devices: 78.2 us -> 70.6 us
    ppermute x16, waiting for transfers between devices: 71.1 us -> 60.8 us  [shift(): lax.ppermute(array, axis, [(i, (i + step) % size) for i in range(size)])]
    reshape x2 -> x0, local copies, waits for them, and re-layouts: 5.85 us -> none  [column(): lax.dynamic_slice(psi, start, (8, 1) + psi.shape[2:])]
    dynamic_slice x0 -> x2, local copies, waits for them, and re-layouts: none -> 5.52 us  [column(): return lax.dynamic_slice(psi, start, (8, 1) + psi.shape[2:])]
    all_to_all x4, waiting for transfers between devices: 7.06 us -> 9.77 us  [exchange(): return lax.all_to_all(array, axis, split_axis=0, concat_axis=0, tiled=True)]
  transfers between devices with their start and end apart: 20 -> 20, of which waited for: 6 -> 8; matrix products, arithmetic and copies ran while one was open for 7% -> 10% of each run, Pallas kernels for 25% -> 25%
where the time goes in v7:
time: 196 us; the launch traced here: 195 us
  waiting for transfers between devices  70.6 us (36%)
  Pallas kernels  54.8 us (28%)
  starting transfers between devices  40.6 us (21%)
  local copies, waits for them, and re-layouts  20.6 us (11%)
  other arithmetic  5.49 us (3%)
  between operations  2.67 us (1%)
    ppermute x16, waiting for transfers between devices, shift(): lax.ppermute(array, axis, [(i, (i + step) % size) for i in range(size)])  60.8 us
    pallas_call x4, Pallas kernels, combine(): pl.pallas_call(kernel, out_shape=jax.ShapeDtypeStruct((8 * count, width,...  44.2 us
    ppermute x16, starting transfers between devices, shift(): lax.ppermute(array, axis, [(i, (i + step) % size) for i in range(size)])  20.7 us
    all_to_all x4, starting transfers between devices, exchange(): return lax.all_to_all(array, axis, split_axis=0, concat_axis=0, tiled=True)  19.9 us
    all_to_all x4, waiting for transfers between devices, exchange(): return lax.all_to_all(array, axis, split_axis=0, concat_axis=0, tiled=True)  9.77 us
    pallas_call x1, Pallas kernels, pack(): pl.pallas_call(kernel, out_shape=jax.ShapeDtypeStruct((8, 4, width + TAIL...  5.54 us
    dynamic_slice x2, local copies, waits for them, and re-layouts, column(): return lax.dynamic_slice(psi, start, (8, 1) + psi.shape[2:])  5.52 us
    pallas_call x1, Pallas kernels, assemble(): pl.pallas_call(kernel, out_shape=jax.ShapeDtypeStruct((4, 4, 2, width, wi...  5.04 us
  transfers between devices with their start and end apart: 20, of which 8 were waited for; matrix products, arithmetic and copies ran while one was open for 10% of the time, Pallas kernels for 25%

profile of v7, /device:TPU:0, one launch (start us, length us, event | category | flops | bytes accessed | tf_op | source)
XLA Modules:
  0.0 194.7 jit_solution(12554046505640024445)
XLA Ops:
  0.0 5.5 %pack.1 = bf16[8,4,272,256]{3,2,1,0:T(8,128)(2,1)} custom-call(s32[32]{0:T(128)} %left.1, s32[32]{0:T(128)} %right.1, bf16[32,256,256]{2,1,0:T(8,128)(2,1)} %in_ref.1), custom_call_target="tpu_custom_call" | custom-call | flops 1 | bytes 1 | tf_op jit(solution)/shard_map/pack/pallas_call | solution.py:214
  5.5 4.7 %all-to-all-start = ((bf16[8,4,272,256]{3,2,1,0:T(8,128)(2,1)}), bf16[8,4,272,256]{3,2,1,0:T(8,128)(2,1)}, u32[]{:S(2)}, u32[]{:S(2)}) async-start(bf16[8,4,272,256]{3,2,1,0:T(8,128)(2,1)} %pack.1), calls=%async_computation | async-start | bytes 8912896 | tf_op jit(solution)/shard_map/all_to_all | solution.py:33
  10.3 2.1 %fusion = bf16[2,8,256,256]{3,2,1,0:T(8,128)(2,1)} fusion(bf16[2,8,256,256]{3,2,1,0:T(8,128)(2,1)S(1)} %copy-done.2, s32[2]{0:T(128)S(1)} %copy-done.5), kind=kLoop, calls=%fused_computation.2 | loop fusion | flops 2097152 | bytes 4194312 | tf_op jit(solution)/shard_map/jit(_where)/select_n | solution.py:249
  12.4 2.0 %collective-permute-start = (bf16[2,2048,256]{2,1,0:T(8,128)(2,1)}, bf16[2,2048,256]{2,1,0:T(8,128)(2,1)}, u32[]{:S(2)}, u32[]{:S(2)}) collective-permute-start(bf16[2,2048,256]{2,1,0:T(8,128)(2,1)} %bitcast.1.refs_4_.refs_8_.refs_6_), channel_id=1, source_target_pairs={{0,8},{8,16},{16,24},{24,0},{1,9},{9,17},{17,25},{25,1},{2,10},{10... | collective-permute-start | bytes 6291464 | tf_op jit(solution)/shard_map/ppermute | solution.py:37
  14.5 2.1 %collective-permute-start.1 = (bf16[2,2048,256]{2,1,0:T(8,128)(2,1)}, bf16[2,2048,256]{2,1,0:T(8,128)(2,1)}, u32[]{:S(2)}, u32[]{:S(2)}) collective-permute-start(bf16[2,2048,256]{2,1,0:T(8,128)(2,1)} %bitcast.1.refs_4_.refs_8_.refs_6_), channel_id=1, source_target_pairs={{0,24},{8,0},{16,8},{24,16},{1,25},{9,1},{17,9},{25,17},{2,26},{10... | collective-permute-start | bytes 6291464 | tf_op jit(solution)/shard_map/ppermute | solution.py:37
  16.6 0.9 fusion.1
  17.5 1.6 collective-permute-start.2
  19.1 1.7 collective-permute-start.3
  20.8 1.2 constant_dynamic-slice_fusion.3
  22.0 0.6 fusion.3
  24.6 38.5 %collective-permute-done.refs_5_.refs_9_.refs_7_ = bf16[2,2048,256]{2,1,0:T(8,128)(2,1)} collective-permute-done((bf16[2,2048,256]{2,1,0:T(8,128)(2,1)}, bf16[2,2048,256]{2,1,0:T(8,128)(2,1)}, u32[]{:S(2)}, u32[]{:S(2)}) %collective-permute-start) | collective-permute-done | bytes 2097184 | tf_op jit(solution)/shard_map/ppermute | solution.py:37
  63.0 3.4 %collective-permute-done.2.refs_4_ = bf16[2,2048,256]{2,1,0:T(8,128)(2,1)} collective-permute-done((bf16[2,2048,256]{2,1,0:T(8,128)(2,1)S(1)}, bf16[2,2048,256]{2,1,0:T(8,128)(2,1)}, u32[]{:S(2)}, u32[]{:S(2)}) %collective-permute-start.2) | collective-permute-done | bytes 2097184 | tf_op jit(solution)/shard_map/ppermute | solution.py:37
  66.5 3.2 %constant_dynamic-slice_fusion.1 = (bf16[8,1,272,256]{3,2,1,0:T(8,128)(2,1)}, bf16[8,1,272,256]{3,2,1,0:T(8,128)(2,1)}) fusion(bf16[8,4,272,256]{3,2,1,0:T(8,128)(2,1)} %all-to-all-done.refs_1_, u32[]{:T(128)} %bitcast.4, u32[]{:T(128)} %bitcast.3), kind=kLoop, calls=%fused_computation.10 | loop fusion | bytes 4456456 | tf_op jit(solution)/shard_map/dynamic_slice | solution.py:232
  69.7 2.3 %slice.44 = bf16[2,1024,256]{2,1,0:T(8,128)(2,1)} slice(bf16[2,2048,256]{2,1,0:T(8,128)(2,1)} %collective-permute-done.refs_5_.refs_9_.refs_7_), slice={[0:2], [0:1024], [0:256]} | slice | bytes 2097152 | tf_op jit(solution)/shard_map/slice | solution.py:46
  71.9 2.3 %slice.45 = bf16[2,1024,256]{2,1,0:T(8,128)(2,1)} slice(bf16[2,2048,256]{2,1,0:T(8,128)(2,1)} %collective-permute-done.1.refs_6_.refs_10_.refs_8_), slice={[0:2], [1024:2048], [0:256]} | slice | bytes 2097152 | tf_op jit(solution)/shard_map/slice | solution.py:46
  74.2 3.2 %collective-permute-start.8 = (bf16[2,1024,256]{2,1,0:T(8,128)(2,1)}, bf16[2,1024,256]{2,1,0:T(8,128)(2,1)}, u32[]{:S(2)}, u32[]{:S(2)}) collective-permute-start(bf16[2,1024,256]{2,1,0:T(8,128)(2,1)} %slice.45), channel_id=1, source_target_pairs={{0,24},{8,0},{16,8},{24,16},{1,25},{9,1},{17,9},{25,17},{2,26},{10... | collective-permute-start | bytes 3145736 | tf_op jit(solution)/shard_map/ppermute | solution.py:37
  77.4 0.9 convert_reduce_fusion
  78.3 0.7 reshape.70.refs_0_
  79.0 1.5 collective-permute-start.5
  80.5 1.8 collective-permute-start.6
  82.2 9.2 %combine_0_0.1.refs_6_ = bf16[8,256,256]{2,1,0:T(8,128)(2,1)} custom-call(s32[13]{0:T(128)} %get-tuple-element.68.where, s32[64]{0:T(128)} %reshape.70.refs_0_, bf16[8,4,272,256]{3,2,1,0:T(8,128)(2,1)} %all-to-all-done.refs_1_, bf16[2,2048,256]{2,1,0:T(8,128)(2,1)} %bitcast.17, bf16[2,2048,256]{2,1,0:T(8,128)(2,1)} %collective-permute-done.4.refs_3_, ...), custom_call_target="tpu_custom_call" | custom-call | flops 999999995904 | bytes 1 | tf_op jit(solution)/shard_map/combine_0_0/pallas_call | solution.py:150
  91.5 2.3 %slice.46 = bf16[2,1024,256]{2,1,0:T(8,128)(2,1)} slice(bf16[2,2048,256]{2,1,0:T(8,128)(2,1)} %collective-permute-done.2.refs_4_), slice={[0:2], [0:1024], [0:256]} | slice | bytes 2097152 | tf_op jit(solution)/shard_map/slice | solution.py:272
  93.8 2.2 %slice.47 = bf16[2,1024,256]{2,1,0:T(8,128)(2,1)} slice(bf16[2,2048,256]{2,1,0:T(8,128)(2,1)} %collective-permute-done.3.refs_6_), slice={[0:2], [1024:2048], [0:256]} | slice | bytes 2097152 | tf_op jit(solution)/shard_map/slice | solution.py:272
  96.1 2.4 %constant_dynamic-slice_fusion = bf16[8,1,272,256]{3,2,1,0:T(8,128)(2,1)} fusion(bf16[8,4,272,256]{3,2,1,0:T(8,128)(2,1)} %all-to-all-done.refs_1_, u32[]{:T(128)} %bitcast.5), kind=kLoop, calls=%fused_computation.9 | loop fusion | bytes 2228228 | tf_op jit(solution)/shard_map/dynamic_slice | solution.py:232
  98.4 0.9 collective-permute-done.8.refs_5_.refs_12_.refs_10_
  99.3 6.4 %combine_0_3.1 = bf16[8,256,256]{2,1,0:T(8,128)(2,1)} custom-call(s32[13]{0:T(128)} %get-tuple-element.68.where, s32[64]{0:T(128)} %reshape.70.refs_0_, bf16[8,4,272,256]{3,2,1,0:T(8,128)(2,1)} %all-to-all-done.refs_1_, bf16[2,2048,256]{2,1,0:T(8,128)(2,1)} %bitcast.18, ...), custom_call_target="tpu_custom_call", output_to_operand_aliasing={{}: (7, {})} | custom-call | flops 1 | bytes 1 | tf_op jit(solution)/shard_map/combine_0_3/pallas_call | solution.py:150
  105.8 0.5 collective-permute-start.9
  106.3 2.4 %collective-permute-start.11 = (bf16[8,1,272,256]{3,2,1,0:T(8,128)(2,1)}, bf16[8,1,272,256]{3,2,1,0:T(8,128)(2,1)}, u32[]{:S(2)}, u32[]{:S(2)}) collective-permute-start(bf16[8,1,272,256]{3,2,1,0:T(8,128)(2,1)} %constant_dynamic-slice_fusion), channel_id=1, source_target_pairs={{0,4},{2,6},{4,0},{6,2},{1,5},{3,7},{5,1},{7,3},{8,12},{10,14},{12... | collective-permute-start | bytes 3342344 | tf_op jit(solution)/shard_map/ppermute | solution.py:37
  108.8 1.2 collective-permute-start.12
  110.0 2.0 %collective-permute-start.13 = (bf16[2,1024,256]{2,1,0:T(8,128)(2,1)}, bf16[2,1024,256]{2,1,0:T(8,128)(2,1)}, u32[]{:S(2)}, u32[]{:S(2)}) collective-permute-start(bf16[2,1024,256]{2,1,0:T(8,128)(2,1)} %slice.47), channel_id=1, source_target_pairs={{0,6},{2,0},{4,2},{6,4},{1,7},{3,1},{5,3},{7,5},{8,14},{10,8},{12,... | collective-permute-start | bytes 3145736 | tf_op jit(solution)/shard_map/ppermute | solution.py:37
  112.0 4.9 %all-to-all-start.1 = ((bf16[8,256,256]{2,1,0:T(8,128)(2,1)}), bf16[8,256,256]{2,1,0:T(8,128)(2,1)}, u32[]{:S(2)}, u32[]{:S(2)}) async-start(bf16[8,256,256]{2,1,0:T(8,128)(2,1)} %combine_0_3.1), calls=%async_computation.1 | async-start | bytes 2097152 | tf_op jit(solution)/shard_map/all_to_all | solution.py:33
  117.0 0.8 convert_reduce_fusion.2
  117.8 0.7 reshape.71.refs_0_
  118.5 0.7 reshape.72.refs_1_
  119.1 17.9 %combine_1_0.1 = bf16[16,256,256]{2,1,0:T(8,128)(2,1)} custom-call(s32[13]{0:T(128)} %get-tuple-element.68.where, s32[16]{0:T(128)} %reshape.71.refs_0_, s32[16]{0:T(128)} %reshape.72.refs_1_, bf16[8,1,272,256]{3,2,1,0:T(8,128)(2,1)} %collective-permute-done.5.refs_2_, bf16[8,1,272,256]{3,2,1,0:T(8,128)(2,1)} %collective-permute-done.6.refs_3_, ...), custom_call_target="tpu_custom_call" | custom-call | flops 999999995904 | bytes 1 | tf_op jit(solution)/shard_map/combine_1_0/pallas_call | solution.py:150
  137.0 4.8 %all-to-all-start.2 = ((bf16[16,256,256]{2,1,0:T(8,128)(2,1)}), bf16[16,256,256]{2,1,0:T(8,128)(2,1)S(1)}, u32[]{:S(2)}, u32[]{:S(2)}) async-start(bf16[16,256,256]{2,1,0:T(8,128)(2,1)} %combine_1_0.1), calls=%async_computation.2 | async-start | bytes 4194304 | tf_op jit(solution)/shard_map/all_to_all | solution.py:33
  141.8 15.3 %collective-permute-done.12.refs_2_ = bf16[2,1024,256]{2,1,0:T(8,128)(2,1)} collective-permute-done((bf16[2,1024,256]{2,1,0:T(8,128)(2,1)}, bf16[2,1024,256]{2,1,0:T(8,128)(2,1)}, u32[]{:S(2)}, u32[]{:S(2)}) %collective-permute-start.12) | collective-permute-done | bytes 1048608 | tf_op jit(solution)/shard_map/ppermute | solution.py:37
  157.3 0.5 collective-permute-start.15
  157.8 0.7 convert_reduce_fusion.1
  158.5 0.7 reshape.73.refs_0_
  159.2 2.0 %collective-permute-done.14.refs_4_ = bf16[2,1024,256]{2,1,0:T(8,128)(2,1)S(1)} collective-permute-done((bf16[2,1024,256]{2,1,0:T(8,128)(2,1)}, bf16[2,1024,256]{2,1,0:T(8,128)(2,1)S(1)}, u32[]{:S(2)}, u32[]{:S(2)}) %collective-permute-start.14) | collective-permute-done | bytes 1048608 | tf_op jit(solution)/shard_map/ppermute | solution.py:37
  161.2 0.6 collective-permute-done.15.refs_5_
  161.8 0.4 copy-done.4
  162.2 10.6 %combine_3_0.1 = bf16[8,256,256]{2,1,0:T(8,128)(2,1)} custom-call(s32[13]{0:T(128)} %get-tuple-element.68.where, s32[16]{0:T(128)} %reshape.73.refs_0_, bf16[8,1,272,256]{3,2,1,0:T(8,128)(2,1)} %collective-permute-done.11.refs_1_, bf16[2,1024,256]{2,1,0:T(8,128)(2,1)} %collective-permute-done.12.refs_2_, ...), custom_call_target="tpu_custom_call" | custom-call | flops 1 | bytes 1 | tf_op jit(solution)/shard_map/combine_3_0/pallas_call | solution.py:150
  172.8 5.5 %all-to-all-start.3 = ((bf16[8,256,256]{2,1,0:T(8,128)(2,1)}), bf16[8,256,256]{2,1,0:T(8,128)(2,1)S(1)}, u32[]{:S(2)}, u32[]{:S(2)}) async-start(bf16[8,256,256]{2,1,0:T(8,128)(2,1)} %combine_3_0.1), calls=%async_computation.3 | async-start | bytes 2097152 | tf_op jit(solution)/shard_map/all_to_all | solution.py:33
  178.9 5.0 %assemble.1 = bf16[4,4,2,256,256]{4,3,2,1,0:T(8,128)(2,1)} custom-call(s32[13]{0:T(128)} %get-tuple-element.68.where, bf16[4,2,1,256,256]{4,3,2,1,0:T(8,128)(2,1)} %bitcast.6.refs_0_, bf16[4,2,2,256,256]{4,3,2,1,0:T(8,128)(2,1)} %bitcast.19), custom_call_target="tpu_custom_call" | custom-call | flops 1 | bytes 1 | tf_op jit(solution)/shard_map/assemble/pallas_call | solution.py:187
  183.9 9.8 %all-to-all-done.3 = bf16[8,256,256]{2,1,0:T(8,128)(2,1)S(1)} async-done(((bf16[8,256,256]{2,1,0:T(8,128)(2,1)}), bf16[8,256,256]{2,1,0:T(8,128)(2,1)S(1)}, u32[]{:S(2)}, u32[]{:S(2)}) %all-to-all-start.3) | async-done | bytes 1048608 | tf_op jit(solution)/shard_map/all_to_all | solution.py:33
  193.7 1.0 constant_dynamic-update-slice_fusion
  (32 shorter events, 0.2 us)
Async XLA Ops:
  5.5 4.7 %copy-start.2 = (bf16[2,8,256,256]{3,2,1,0:T(8,128)(2,1)S(1)}, bf16[2,8,256,256]{3,2,1,0:T(8,128)(2,1)}, u32[]{:S(2)}) copy-start(bf16[2,8,256,256]{3,2,1,0:T(8,128)(2,1)} %param.13) | copy-start | bytes 6291460
  5.5 4.7 %copy-start.5 = (s32[2]{0:T(128)S(1)}, s32[2]{0:T(128)}, u32[]{:S(2)}) copy-start(s32[2]{0:T(128)} %param.14) | copy-start | bytes 28
  5.5 61.0 %all-to-all-start = ((bf16[8,4,272,256]{3,2,1,0:T(8,128)(2,1)}), bf16[8,4,272,256]{3,2,1,0:T(8,128)(2,1)}, u32[]{:S(2)}, u32[]{:S(2)}) async-start(bf16[8,4,272,256]{3,2,1,0:T(8,128)(2,1)} %pack.1), calls=%async_computation | async-start | bytes 8912896 | tf_op jit(solution)/shard_map/all_to_all | solution.py:33
  10.3 6.3 %copy-start.3 = (bf16[2,8,256,256]{3,2,1,0:T(8,128)(2,1)S(1)}, bf16[2,8,256,256]{3,2,1,0:T(8,128)(2,1)}, u32[]{:S(2)}) copy-start(bf16[2,8,256,256]{3,2,1,0:T(8,128)(2,1)} %param.11) | copy-start | bytes 6291460
  10.3 6.3 %copy-start.6 = (s32[2]{0:T(128)S(1)}, s32[2]{0:T(128)}, u32[]{:S(2)}) copy-start(s32[2]{0:T(128)} %param.12) | copy-start | bytes 28
  12.4 50.6 %collective-permute-start = (bf16[2,2048,256]{2,1,0:T(8,128)(2,1)}, bf16[2,2048,256]{2,1,0:T(8,128)(2,1)}, u32[]{:S(2)}, u32[]{:S(2)}) collective-permute-start(bf16[2,2048,256]{2,1,0:T(8,128)(2,1)} %bitcast.1.refs_4_.refs_8_.refs_6_), channel_id=1, source_target_pairs={{0,8},{8,16},{16,24},{24,0},{1,9},{9,17},{17,25},{25,1},{2,10},{10... | collective-permute-start | bytes 6291464 | tf_op jit(solution)/shard_map/ppermute | solution.py:37
  14.5 48.6 %collective-permute-start.1 = (bf16[2,2048,256]{2,1,0:T(8,128)(2,1)}, bf16[2,2048,256]{2,1,0:T(8,128)(2,1)}, u32[]{:S(2)}, u32[]{:S(2)}) collective-permute-start(bf16[2,2048,256]{2,1,0:T(8,128)(2,1)} %bitcast.1.refs_4_.refs_8_.refs_6_), channel_id=1, source_target_pairs={{0,24},{8,0},{16,8},{24,16},{1,25},{9,1},{17,9},{25,17},{2,26},{10... | collective-permute-start | bytes 6291464 | tf_op jit(solution)/shard_map/ppermute | solution.py:37
  17.5 52.2 %copy-start = (bf16[2,8,256,256]{3,2,1,0:T(8,128)(2,1)}, bf16[2,8,256,256]{3,2,1,0:T(8,128)(2,1)S(1)}, u32[]{:S(2)}) copy-start(bf16[2,8,256,256]{3,2,1,0:T(8,128)(2,1)S(1)} %fusion.1) | copy-start | bytes 6291460
  17.5 49.0 %collective-permute-start.2 = (bf16[2,2048,256]{2,1,0:T(8,128)(2,1)S(1)}, bf16[2,2048,256]{2,1,0:T(8,128)(2,1)}, u32[]{:S(2)}, u32[]{:S(2)}) collective-permute-start(bf16[2,2048,256]{2,1,0:T(8,128)(2,1)S(1)} %bitcast.14), channel_id=1, source_target_pairs={{0,2},{2,4},{4,6},{6,0},{1,3},{3,5},{5,7},{7,1},{8,10},{10,12},{12... | collective-permute-start | bytes 6291464 | tf_op jit(solution)/shard_map/ppermute | solution.py:37
  19.1 47.4 %collective-permute-start.3 = (bf16[2,2048,256]{2,1,0:T(8,128)(2,1)S(1)}, bf16[2,2048,256]{2,1,0:T(8,128)(2,1)}, u32[]{:S(2)}, u32[]{:S(2)}) collective-permute-start(bf16[2,2048,256]{2,1,0:T(8,128)(2,1)S(1)} %bitcast.15), channel_id=1, source_target_pairs={{0,6},{2,0},{4,2},{6,4},{1,7},{3,1},{5,3},{7,5},{8,14},{10,8},{12,... | collective-permute-start | bytes 6291464 | tf_op jit(solution)/shard_map/ppermute | solution.py:37
  20.8 45.7 %collective-permute-start.4 = (bf16[2,2048,256]{2,1,0:T(8,128)(2,1)S(1)}, bf16[2,2048,256]{2,1,0:T(8,128)(2,1)}, u32[]{:S(2)}, u32[]{:S(2)}) collective-permute-start(bf16[2,2048,256]{2,1,0:T(8,128)(2,1)S(1)} %bitcast.16), channel_id=1, source_target_pairs={{0,1},{1,0},{2,3},{3,2},{4,5},{5,4},{6,7},{7,6},{8,9},{9,8},{10,11... | collective-permute-start | bytes 6291464 | tf_op jit(solution)/shard_map/ppermute | solution.py:37
  71.9 26.5 %collective-permute-start.7 = (bf16[2,1024,256]{2,1,0:T(8,128)(2,1)}, bf16[2,1024,256]{2,1,0:T(8,128)(2,1)}, u32[]{:S(2)}, u32[]{:S(2)}) collective-permute-start(bf16[2,1024,256]{2,1,0:T(8,128)(2,1)} %slice.44), channel_id=1, source_target_pairs={{0,8},{8,16},{16,24},{24,0},{1,9},{9,17},{17,25},{25,1},{2,10},{10... | collective-permute-start | bytes 3145736 | tf_op jit(solution)/shard_map/ppermute | solution.py:37
  74.2 25.1 %collective-permute-start.8 = (bf16[2,1024,256]{2,1,0:T(8,128)(2,1)}, bf16[2,1024,256]{2,1,0:T(8,128)(2,1)}, u32[]{:S(2)}, u32[]{:S(2)}) collective-permute-start(bf16[2,1024,256]{2,1,0:T(8,128)(2,1)} %slice.45), channel_id=1, source_target_pairs={{0,24},{8,0},{16,8},{24,16},{1,25},{9,1},{17,9},{25,17},{2,26},{10... | collective-permute-start | bytes 3145736 | tf_op jit(solution)/shard_map/ppermute | solution.py:37
  79.0 26.7 %collective-permute-start.5 = (bf16[8,1,272,256]{3,2,1,0:T(8,128)(2,1)}, bf16[8,1,272,256]{3,2,1,0:T(8,128)(2,1)}, u32[]{:S(2)}, u32[]{:S(2)}) collective-permute-start(bf16[8,1,272,256]{3,2,1,0:T(8,128)(2,1)} %get-tuple-element.43), channel_id=1, source_target_pairs={{0,2},{2,4},{4,6},{6,0},{1,3},{3,5},{5,7},{7,1},{8,10},{10,12},{12... | collective-permute-start | bytes 3342344 | tf_op jit(solution)/shard_map/ppermute | solution.py:37
  80.5 25.3 %collective-permute-start.6 = (bf16[8,1,272,256]{3,2,1,0:T(8,128)(2,1)}, bf16[8,1,272,256]{3,2,1,0:T(8,128)(2,1)}, u32[]{:S(2)}, u32[]{:S(2)}) collective-permute-start(bf16[8,1,272,256]{3,2,1,0:T(8,128)(2,1)} %get-tuple-element.44), channel_id=1, source_target_pairs={{0,6},{2,0},{4,2},{6,4},{1,7},{3,1},{5,3},{7,5},{8,14},{10,8},{12,... | collective-permute-start | bytes 3342344 | tf_op jit(solution)/shard_map/ppermute | solution.py:37
  105.7 11.2 %collective-permute-start.10 = (bf16[2,2048,256]{2,1,0:T(8,128)(2,1)}, bf16[2,2048,256]{2,1,0:T(8,128)(2,1)S(1)}, u32[]{:S(2)}, u32[]{:S(2)}) collective-permute-start(bf16[2,2048,256]{2,1,0:T(8,128)(2,1)} %collective-permute-done.3.refs_6_), channel_id=1, source_target_pairs={{0,1},{1,0},{2,3},{3,2},{4,5},{5,4},{6,7},{7,6},{8,9},{9,8},{10,11... | collective-permute-start | bytes 6291464 | tf_op jit(solution)/shard_map/ppermute | solution.py:37
  105.8 11.1 %collective-permute-start.9 = (bf16[2,2048,256]{2,1,0:T(8,128)(2,1)}, bf16[2,2048,256]{2,1,0:T(8,128)(2,1)}, u32[]{:S(2)}, u32[]{:S(2)}) collective-permute-start(bf16[2,2048,256]{2,1,0:T(8,128)(2,1)} %collective-permute-done.2.refs_4_), channel_id=1, source_target_pairs={{0,1},{1,0},{2,3},{3,2},{4,5},{5,4},{6,7},{7,6},{8,9},{9,8},{10,11... | collective-permute-start | bytes 6291464 | tf_op jit(solution)/shard_map/ppermute | solution.py:37
  106.3 50.9 %collective-permute-start.11 = (bf16[8,1,272,256]{3,2,1,0:T(8,128)(2,1)}, bf16[8,1,272,256]{3,2,1,0:T(8,128)(2,1)}, u32[]{:S(2)}, u32[]{:S(2)}) collective-permute-start(bf16[8,1,272,256]{3,2,1,0:T(8,128)(2,1)} %constant_dynamic-slice_fusion), channel_id=1, source_target_pairs={{0,4},{2,6},{4,0},{6,2},{1,5},{3,7},{5,1},{7,3},{8,12},{10,14},{12... | collective-permute-start | bytes 3342344 | tf_op jit(solution)/shard_map/ppermute | solution.py:37
  108.8 48.4 %collective-permute-start.12 = (bf16[2,1024,256]{2,1,0:T(8,128)(2,1)}, bf16[2,1024,256]{2,1,0:T(8,128)(2,1)}, u32[]{:S(2)}, u32[]{:S(2)}) collective-permute-start(bf16[2,1024,256]{2,1,0:T(8,128)(2,1)} %slice.46), channel_id=1, source_target_pairs={{0,2},{2,4},{4,6},{6,0},{1,3},{3,5},{5,7},{7,1},{8,10},{10,12},{12... | collective-permute-start | bytes 3145736 | tf_op jit(solution)/shard_map/ppermute | solution.py:37
  110.0 47.3 %collective-permute-start.13 = (bf16[2,1024,256]{2,1,0:T(8,128)(2,1)}, bf16[2,1024,256]{2,1,0:T(8,128)(2,1)}, u32[]{:S(2)}, u32[]{:S(2)}) collective-permute-start(bf16[2,1024,256]{2,1,0:T(8,128)(2,1)} %slice.47), channel_id=1, source_target_pairs={{0,6},{2,0},{4,2},{6,4},{1,7},{3,1},{5,3},{7,5},{8,14},{10,8},{12,... | collective-permute-start | bytes 3145736 | tf_op jit(solution)/shard_map/ppermute | solution.py:37
  112.0 25.0 %all-to-all-start.1 = ((bf16[8,256,256]{2,1,0:T(8,128)(2,1)}), bf16[8,256,256]{2,1,0:T(8,128)(2,1)}, u32[]{:S(2)}, u32[]{:S(2)}) async-start(bf16[8,256,256]{2,1,0:T(8,128)(2,1)} %combine_0_3.1), calls=%async_computation.1 | async-start | bytes 2097152 | tf_op jit(solution)/shard_map/all_to_all | solution.py:33
  116.9 2.2 %copy-start.7 = (bf16[2,2048,256]{2,1,0:T(8,128)(2,1)}, bf16[2,2048,256]{2,1,0:T(8,128)(2,1)S(1)}, u32[]{:S(2)}) copy-start(bf16[2,2048,256]{2,1,0:T(8,128)(2,1)S(1)} %collective-permute-done.10.refs_7_) | copy-start | bytes 6291460
  137.0 35.8 %all-to-all-start.2 = ((bf16[16,256,256]{2,1,0:T(8,128)(2,1)}), bf16[16,256,256]{2,1,0:T(8,128)(2,1)S(1)}, u32[]{:S(2)}, u32[]{:S(2)}) async-start(bf16[16,256,256]{2,1,0:T(8,128)(2,1)} %combine_1_0.1), calls=%async_computation.2 | async-start | bytes 4194304 | tf_op jit(solution)/shard_map/all_to_all | solution.py:33
  157.3 3.9 %collective-permute-start.14 = (bf16[2,1024,256]{2,1,0:T(8,128)(2,1)}, bf16[2,1024,256]{2,1,0:T(8,128)(2,1)S(1)}, u32[]{:S(2)}, u32[]{:S(2)}) collective-permute-start(bf16[2,1024,256]{2,1,0:T(8,128)(2,1)} %collective-permute-done.12.refs_2_), channel_id=1, source_target_pairs={{0,1},{1,0},{2,3},{3,2},{4,5},{5,4},{6,7},{7,6},{8,9},{9,8},{10,11... | collective-permute-start | bytes 3145736 | tf_op jit(solution)/shard_map/ppermute | solution.py:37
  157.3 4.5 %collective-permute-start.15 = (bf16[2,1024,256]{2,1,0:T(8,128)(2,1)}, bf16[2,1024,256]{2,1,0:T(8,128)(2,1)}, u32[]{:S(2)}, u32[]{:S(2)}) collective-permute-start(bf16[2,1024,256]{2,1,0:T(8,128)(2,1)} %collective-permute-done.13.refs_3_), channel_id=1, source_target_pairs={{0,1},{1,0},{2,3},{3,2},{4,5},{5,4},{6,7},{7,6},{8,9},{9,8},{10,11... | collective-permute-start | bytes 3145736 | tf_op jit(solution)/shard_map/ppermute | solution.py:37
  161.2 1.0 copy-start.4
  172.8 6.0 %copy-start.1 = (bf16[16,256,256]{2,1,0:T(8,128)(2,1)}, bf16[16,256,256]{2,1,0:T(8,128)(2,1)S(1)}, u32[]{:S(2)}) copy-start(bf16[16,256,256]{2,1,0:T(8,128)(2,1)S(1)} %all-to-all-done.2) | copy-start | bytes 6291460
  172.8 20.8 %all-to-all-start.3 = ((bf16[8,256,256]{2,1,0:T(8,128)(2,1)}), bf16[8,256,256]{2,1,0:T(8,128)(2,1)S(1)}, u32[]{:S(2)}, u32[]{:S(2)}) async-start(bf16[8,256,256]{2,1,0:T(8,128)(2,1)} %combine_3_0.1), calls=%async_computation.3 | async-start | bytes 2097152 | tf_op jit(solution)/shard_map/all_to_all | solution.py:33

commit v8 on v7

--- a/solution.py
+++ b/solution.py
@@ -46,7 +46,7 @@
     return shift(from_low[:, :half], axis, 1), shift(from_high[:, half:], axis, 3)
 
 
-def combine(where, psis, lefts, rights, first, z_first=0, kept=None):
+def combine(where, psis, lefts, rights, first, z_first=0, kept=None, cores=(0, 1)):
     codes = [codes for _, codes in psis]
     psis = [psi for psi, _ in psis]
     rows, width = psis[0].shape[2:]
@@ -58,7 +58,7 @@
     right_parts = [a for group in rights for a in group]
     steps = len(rights)
     slots = min(SLOTS, steps)
-    each = [(core, k) for core in range(2) for k in range(count)]
+    each = [(core, k) for core in cores for k in range(count)]
 
     def mine(where):
         return where[9] if columns > 1 else 0
@@ -75,13 +75,18 @@
         out_ref, left_buf, right_buf, partial, left_sems, sems = refs[kept is not None :]
         step = pl.program_id(0)
 
-        def copy_left(k, go):
-            for core in range(2):
+        def copy_lefts(needed, go):
+            for core, k in each:
+                at = core - cores[0]
+                pick = pick_of(0, core, k, 0, where, codes)
+                pick = pick if needed else 1 - pick
                 row = 0
-                for n, ref in enumerate(left_refs[k][core]):
+                for n, ref in enumerate(left_refs[k][at]):
                     size = ref.shape[1]
                     copy = pltpu.make_async_copy(
-                        ref, left_buf.at[k, core, :, pl.ds(row, size)], left_sems.at[k, core, n]
+                        ref.at[pick],
+                        left_buf.at[k, at, pick, pl.ds(row, size)],
+                        left_sems.at[k, at, n, 0 if needed else 1],
                     )
                     copy.start() if go else copy.wait()
                     row += size
@@ -107,9 +112,11 @@
 
         @pl.when(step == 0)
         def _():
-            for k in range(count):
-                copy_left(k, True)
-            for ahead in range(max(slots - 1, 1)):
+            copy_lefts(True, True)
+            fetch(0, True)
+            if steps > 1:
+                copy_lefts(False, True)
+            for ahead in range(1, slots - 1):
                 fetch(ahead, True)
 
         if slots > 1:
@@ -120,8 +127,13 @@
 
         @pl.when(step == 0)
         def _():
-            for k in range(count):
-                copy_left(k, False)
+            copy_lefts(True, False)
+
+        if steps > 1:
+
+            @pl.when(step == 1)
+            def _():
+                copy_lefts(False, False)
 
         fetch(step, False)
         slot = lax.rem(step, slots)
@@ -130,7 +142,7 @@
             block = psi_refs[k][where[8] ^ core, 0, :width]
             for t in range(terms):
                 product = jnp.dot(
-                    left_buf[k, core, left, t * width : (t + 1) * width],
+                    left_buf[k, core - cores[0], left, t * width : (t + 1) * width],
                     block,
                     preferred_element_type=jnp.float32,
                 )
@@ -139,10 +151,15 @@
             total = jnp.dot(
                 partial[n_block], right_buf[slot, n_block], preferred_element_type=jnp.float32
             )
-            out_ref[(where[8] ^ core) * count + k] = total.astype(BF16)
+            row = (where[8] ^ core) * count if len(cores) > 1 else 0
+            out_ref[row + k] = total.astype(BF16)
 
     in_place = pl.BlockSpec(memory_space=pl.ANY)
-    of_g = lambda step, where, *codes: (where[z_first + step], 0, 0)
+
+    def of_g(step, where, *codes):
+        g = where[z_first + step]
+        return (g if len(cores) > 1 else g * 2 + (where[8] ^ cores[0])), 0, 0
+
     psi_of_g = lambda step, where, *codes: (where[z_first + step], mine(where), 0, 0)
     parts = max(len(group) for group in rights)
     extra = [] if kept is None else [kept]
@@ -155,12 +172,12 @@
             grid=(steps,),
             in_specs=[pl.BlockSpec((2, 1, rows, width), psi_of_g)] * count
             + [in_place] * (len(operands) - count),
-            out_specs=pl.BlockSpec((2 * count, width, width), of_g),
+            out_specs=pl.BlockSpec((len(cores) * count, width, width), of_g),
             scratch_shapes=[
-                pltpu.VMEM((count, 2, 2, depth, width), BF16),
+                pltpu.VMEM((count, len(cores), 2, depth, width), BF16),
                 pltpu.VMEM((slots, len(each), depth, width), BF16),
                 pltpu.VMEM((len(each), width, depth), BF16),
-                pltpu.SemaphoreType.DMA((count, 2, max(len(pair[0]) for pair in lefts))),
+                pltpu.SemaphoreType.DMA((count, len(cores), max(len(pair[0]) for pair in lefts), 2)),
                 pltpu.SemaphoreType.DMA((slots, len(each), parts)),
             ],
         ),
@@ -169,7 +186,7 @@
             dimension_semantics=("arbitrary",), vmem_limit_bytes=VMEM
         ),
         cost_estimate=BRIEF if first == 3 or z_first else LONG,
-        name=f"combine_{first}_{z_first}",
+        name=f"combine_{first}_{z_first}_{cores[0]}",
     )(where, *codes, *operands)
 
 
@@ -201,29 +218,49 @@
 
 def pack(wavefunction, pair_left, pair_right):
     width = wavefunction.shape[-1]
-
-    def kernel(left, right, in_ref, out_ref):
+    blocks = wavefunction.reshape(4, 4, 2, width, width)
+
+    def kernel(left, right, in_ref, out_ref, buf, in_sems, out_sems):
+        copies = []
+        for n in range(8):
+            copies.append(
+                pltpu.make_async_copy(
+                    in_ref.at[n // 2, :, n % 2], buf.at[n, :, pl.ds(0, width)], in_sems.at[n]
+                )
+            )
+            copies[n].start()
         lane = lax.broadcasted_iota(jnp.int32, (TAIL, width), 1)
-        for x_r, c_r in np.ndindex(4, 2):
-            slot = x_r * 2 + c_r
-            n = pl.program_id(0) * 8 + slot
-            picks = jnp.where(lane == 0, left[n], jnp.where(lane == 1, right[n], 0))
-            out_ref[c_r, x_r, :width] = in_ref[slot]
-            out_ref[c_r, x_r, width:] = picks.astype(jnp.float32).astype(BF16)
-
+        for n in range(8):
+            for x_r in range(4):
+                slot = (n // 2 * 4 + x_r) * 2 + n % 2
+                picks = jnp.where(lane == 0, left[slot], jnp.where(lane == 1, right[slot], 0))
+                buf[n, x_r, width:] = picks.astype(jnp.float32).astype(BF16)
+        for n in range(8):
+            copies[n].wait()
+            copies[n] = pltpu.make_async_copy(buf.at[n], out_ref.at[n], out_sems.at[n])
+            copies[n].start()
+        for copy in copies:
+            copy.wait()
+
+    shape = (8, 4, width + TAIL, width)
     return pl.pallas_call(
         kernel,
-        out_shape=jax.ShapeDtypeStruct((8, 4, width + TAIL, width), BF16),
+        out_shape=jax.ShapeDtypeStruct(shape, BF16),
         grid_spec=pltpu.PrefetchScalarGridSpec(
             num_scalar_prefetch=2,
-            grid=(4,),
-            in_specs=[pl.BlockSpec((8, width, width), lambda q, left, right: (q, 0, 0))],
-            out_specs=pl.BlockSpec((2, 4, width + TAIL, width), lambda q, left, right: (q, 0, 0, 0)),
+            grid=(1,),
+            in_specs=[pl.BlockSpec(memory_space=pl.ANY)],
+            out_specs=pl.BlockSpec(memory_space=pl.ANY),
+            scratch_shapes=[
+                pltpu.VMEM(shape, BF16),
+                pltpu.SemaphoreType.DMA((8,)),
+                pltpu.SemaphoreType.DMA((8,)),
+            ],
         ),
         compiler_params=pltpu.CompilerParams(vmem_limit_bytes=VMEM),
         cost_estimate=BRIEF,
         name="pack",
-    )(pair_left, pair_right, wavefunction)
+    )(pair_left, pair_right, blocks)
 
 
 def column(psi, position):
@@ -285,8 +322,10 @@
     near = combine(where, [split(psi_low), split(psi_high)], lefts_near, rights, 1)
     psi_far, *left_far = together(psi_far, *left_far, near)[:-1]
     near = exchange(near, "z")
-    left_far = [(tuple(left_far), tuple(shift(a, "c", 1, 2) for a in left_far))]
-    rest = combine(where, [split(psi_far)], left_far, rights, 3)
+    other_far = [shift(a, "c", 1, 2) for a in left_far]
+    psi_far = split(psi_far)
+    rest = combine(where, [psi_far], [(tuple(left_far),)], rights, 3, cores=(0,))
+    rest = combine(where, [psi_far], [(tuple(other_far),)], rights, 3, kept=rest, cores=(1,))
     rest = exchange(rest, "z")
     applied = assemble(where, [(0, own), (1, near)])
     zero = jnp.uint32(0)

time: 196 us -> 199 us (1.015)
  Pallas kernels: 54.8 us -> 58.9 us
  waiting for transfers between devices: 70.6 us -> 68.6 us
    pallas_call x4 -> x5, Pallas kernels: 44.2 us -> 49.5 us  [combine(): pl.pallas_call(kernel, out_shape=jax.ShapeDtypeStruct((8 * count, width,...]
  transfers between devices with their start and end apart: 20 -> 20, of which waited for: 8 -> 7; matrix products, arithmetic and copies ran while one was open for 10% -> 11% of each run, Pallas kernels for 25% -> 28%
where the time goes in v8:
time: 199 us; the launch traced here: 197 us
  waiting for transfers between devices  68.6 us (34%)
  Pallas kernels  58.9 us (30%)
  starting transfers between devices  38.8 us (19%)
  local copies, waits for them, and re-layouts  21.1 us (11%)
  other arithmetic  7.24 us (4%)
  between operations  2.67 us (1%)
    ppermute x16, waiting for transfers between devices, shift(): lax.ppermute(array, axis, [(i, (i + step) % size) for i in range(size)])  58.8 us
    pallas_call x5, Pallas kernels, combine(): pl.pallas_call(kernel, out_shape=jax.ShapeDtypeStruct((8 * count, width,...  49.5 us
    ppermute x16, starting transfers between devices, shift(): lax.ppermute(array, axis, [(i, (i + step) % size) for i in range(size)])  20.9 us
    all_to_all x4, starting transfers between devices, exchange(): return lax.all_to_all(array, axis, split_axis=0, concat_axis=0, tiled=True)  18 us
    all_to_all x4, waiting for transfers between devices, exchange(): return lax.all_to_all(array, axis, split_axis=0, concat_axis=0, tiled=True)  9.72 us
    dynamic_slice x2, local copies, waits for them, and re-layouts, column(): return lax.dynamic_slice(psi, start, (8, 1) + psi.shape[2:])  5.51 us
    pallas_call x1, Pallas kernels, assemble(): pl.pallas_call(kernel, out_shape=jax.ShapeDtypeStruct((4, 4, 2, width, wi...  5.04 us
    pallas_call x1, Pallas kernels, pack(): pl.pallas_call(kernel, out_shape=jax.ShapeDtypeStruct(shape, BF16), grid_...  4.32 us
  transfers between devices with their start and end apart: 20, of which 7 were waited for; matrix products, arithmetic and copies ran while one was open for 11% of the time, Pallas kernels for 28%

profile of v8, /device:TPU:0, one launch (start us, length us, event | category | flops | bytes accessed | tf_op | source)
XLA Modules:
  0.0 197.3 jit_solution(16273878481226334006)
XLA Ops:
  0.0 4.3 %pack.1 = bf16[8,4,272,256]{3,2,1,0:T(8,128)(2,1)} custom-call(s32[32]{0:T(128)} %left.1, s32[32]{0:T(128)} %right.1, bf16[4,4,2,256,256]{4,3,2,1,0:T(8,128)(2,1)} %bitcast.23), custom_call_target="tpu_custom_call" | custom-call | flops 1 | bytes 1 | tf_op jit(solution)/shard_map/pack/pallas_call | solution.py:246
  4.3 4.6 %all-to-all-start = ((bf16[8,4,272,256]{3,2,1,0:T(8,128)(2,1)}), bf16[8,4,272,256]{3,2,1,0:T(8,128)(2,1)}, u32[]{:S(2)}, u32[]{:S(2)}) async-start(bf16[8,4,272,256]{3,2,1,0:T(8,128)(2,1)} %pack.1), calls=%async_computation | async-start | bytes 8912896 | tf_op jit(solution)/shard_map/all_to_all | solution.py:33
  9.0 2.5 %fusion = bf16[2,8,256,256]{3,2,1,0:T(8,128)(2,1)S(1)} fusion(bf16[2,8,256,256]{3,2,1,0:T(8,128)(2,1)} %param.13, s32[2]{0:T(128)S(1)} %copy-done.4), kind=kLoop, calls=%fused_computation.2 | loop fusion | flops 2097152 | bytes 4194312 | tf_op jit(solution)/shard_map/jit(_where)/select_n | solution.py:286
  11.5 2.1 %collective-permute-start = (bf16[2,2048,256]{2,1,0:T(8,128)(2,1)S(1)}, bf16[2,2048,256]{2,1,0:T(8,128)(2,1)}, u32[]{:S(2)}, u32[]{:S(2)}) collective-permute-start(bf16[2,2048,256]{2,1,0:T(8,128)(2,1)S(1)} %bitcast.15), channel_id=1, source_target_pairs={{0,8},{8,16},{16,24},{24,0},{1,9},{9,17},{17,25},{25,1},{2,10},{10... | collective-permute-start | bytes 6291464 | tf_op jit(solution)/shard_map/ppermute | solution.py:37
  13.6 2.2 %collective-permute-start.1 = (bf16[2,2048,256]{2,1,0:T(8,128)(2,1)S(1)}, bf16[2,2048,256]{2,1,0:T(8,128)(2,1)}, u32[]{:S(2)}, u32[]{:S(2)}) collective-permute-start(bf16[2,2048,256]{2,1,0:T(8,128)(2,1)S(1)} %bitcast.16), channel_id=1, source_target_pairs={{0,24},{8,0},{16,8},{24,16},{1,25},{9,1},{17,9},{25,17},{2,26},{10... | collective-permute-start | bytes 6291464 | tf_op jit(solution)/shard_map/ppermute | solution.py:37
  15.8 2.2 %fusion.1 = bf16[2,8,256,256]{3,2,1,0:T(8,128)(2,1)} fusion(bf16[2,8,256,256]{3,2,1,0:T(8,128)(2,1)S(1)} %copy-done.2, s32[2]{0:T(128)S(1)} %copy-done.5), kind=kLoop, calls=%fused_computation.3 | loop fusion | flops 2097152 | bytes 4194312 | tf_op jit(solution)/shard_map/jit(_where)/select_n | solution.py:288
  18.0 1.5 collective-permute-start.2
  19.5 1.7 collective-permute-start.3
  21.3 1.3 constant_dynamic-slice_fusion.3
  22.6 0.7 fusion.3
  25.1 36.9 %collective-permute-done.refs_5_.refs_9_ = bf16[2,2048,256]{2,1,0:T(8,128)(2,1)} collective-permute-done((bf16[2,2048,256]{2,1,0:T(8,128)(2,1)S(1)}, bf16[2,2048,256]{2,1,0:T(8,128)(2,1)}, u32[]{:S(2)}, u32[]{:S(2)}) %collective-permute-start) | collective-permute-done | bytes 2097184 | tf_op jit(solution)/shard_map/ppermute | solution.py:37
  62.0 5.2 %collective-permute-done.2.refs_4_ = bf16[2,2048,256]{2,1,0:T(8,128)(2,1)} collective-permute-done((bf16[2,2048,256]{2,1,0:T(8,128)(2,1)}, bf16[2,2048,256]{2,1,0:T(8,128)(2,1)}, u32[]{:S(2)}, u32[]{:S(2)}) %collective-permute-start.2) | collective-permute-done | bytes 2097184 | tf_op jit(solution)/shard_map/ppermute | solution.py:37
  67.2 3.2 %constant_dynamic-slice_fusion.1 = (bf16[8,1,272,256]{3,2,1,0:T(8,128)(2,1)}, bf16[8,1,272,256]{3,2,1,0:T(8,128)(2,1)}) fusion(bf16[8,4,272,256]{3,2,1,0:T(8,128)(2,1)} %all-to-all-done.refs_1_, u32[]{:T(128)} %bitcast.5, u32[]{:T(128)} %bitcast.4), kind=kLoop, calls=%fused_computation.10 | loop fusion | bytes 4456456 | tf_op jit(solution)/shard_map/dynamic_slice | solution.py:269
  70.3 2.3 %slice.44 = bf16[2,1024,256]{2,1,0:T(8,128)(2,1)} slice(bf16[2,2048,256]{2,1,0:T(8,128)(2,1)} %collective-permute-done.refs_5_.refs_9_), slice={[0:2], [0:1024], [0:256]} | slice | bytes 2097152 | tf_op jit(solution)/shard_map/slice | solution.py:46
  72.6 2.3 %slice.45 = bf16[2,1024,256]{2,1,0:T(8,128)(2,1)} slice(bf16[2,2048,256]{2,1,0:T(8,128)(2,1)} %collective-permute-done.1.refs_6_.refs_10_), slice={[0:2], [1024:2048], [0:256]} | slice | bytes 2097152 | tf_op jit(solution)/shard_map/slice | solution.py:46
  74.9 3.2 %collective-permute-start.8 = (bf16[2,1024,256]{2,1,0:T(8,128)(2,1)}, bf16[2,1024,256]{2,1,0:T(8,128)(2,1)}, u32[]{:S(2)}, u32[]{:S(2)}) collective-permute-start(bf16[2,1024,256]{2,1,0:T(8,128)(2,1)} %slice.45), channel_id=1, source_target_pairs={{0,24},{8,0},{16,8},{24,16},{1,25},{9,1},{17,9},{25,17},{2,26},{10... | collective-permute-start | bytes 3145736 | tf_op jit(solution)/shard_map/ppermute | solution.py:37
  78.1 0.9 convert_reduce_fusion
  79.0 0.6 reshape.74.refs_0_
  79.7 1.5 collective-permute-start.5
  81.1 1.8 collective-permute-start.6
  82.9 9.7 %combine_0_0_0.1.refs_6_ = bf16[8,256,256]{2,1,0:T(8,128)(2,1)} custom-call(s32[13]{0:T(128)} %get-tuple-element.68.where, s32[64]{0:T(128)} %reshape.74.refs_0_, bf16[8,4,272,256]{3,2,1,0:T(8,128)(2,1)} %all-to-all-done.refs_1_, bf16[2,2048,256]{2,1,0:T(8,128)(2,1)} %bitcast.3.refs_2_, bf16[2,2048,256]{2,1,0:T(8,128)(2,1)} %collective-permute-done.4.refs_3_, ...), custom_call_target="tpu_custom_call" | custom-call | flops 999999995904 | bytes 1 | tf_op jit(solution)/shard_map/combine_0_0_0/pallas_call | solution.py:167
  92.6 2.4 %slice.46 = bf16[2,1024,256]{2,1,0:T(8,128)(2,1)} slice(bf16[2,2048,256]{2,1,0:T(8,128)(2,1)} %collective-permute-done.2.refs_4_), slice={[0:2], [0:1024], [0:256]} | slice | bytes 2097152 | tf_op jit(solution)/shard_map/slice | solution.py:309
  94.9 2.3 %slice.47 = bf16[2,1024,256]{2,1,0:T(8,128)(2,1)} slice(bf16[2,2048,256]{2,1,0:T(8,128)(2,1)} %collective-permute-done.3.refs_6_), slice={[0:2], [1024:2048], [0:256]} | slice | bytes 2097152 | tf_op jit(solution)/shard_map/slice | solution.py:309
  97.2 2.4 %constant_dynamic-slice_fusion = bf16[8,1,272,256]{3,2,1,0:T(8,128)(2,1)} fusion(bf16[8,4,272,256]{3,2,1,0:T(8,128)(2,1)} %all-to-all-done.refs_1_, u32[]{:T(128)} %bitcast.6), kind=kLoop, calls=%fused_computation.9 | loop fusion | bytes 2228228 | tf_op jit(solution)/shard_map/dynamic_slice | solution.py:269
  99.5 0.4 collective-permute-done.8.refs_5_.refs_12_.refs_8_
  100.0 5.8 %combine_0_3_0.1 = bf16[8,256,256]{2,1,0:T(8,128)(2,1)} custom-call(s32[13]{0:T(128)} %get-tuple-element.68.where, s32[64]{0:T(128)} %reshape.74.refs_0_, bf16[8,4,272,256]{3,2,1,0:T(8,128)(2,1)} %all-to-all-done.refs_1_, bf16[2,2048,256]{2,1,0:T(8,128)(2,1)} %bitcast.3.refs_2_, ...), custom_call_target="tpu_custom_call", output_to_operand_aliasing={{}: (7, {})} | custom-call | flops 1 | bytes 1 | tf_op jit(solution)/shard_map/combine_0_3_0/pallas_call | solution.py:167
  105.8 0.5 collective-permute-done.5.refs_2_
  106.3 0.5 collective-permute-start.9
  106.8 2.6 %collective-permute-start.11 = (bf16[8,1,272,256]{3,2,1,0:T(8,128)(2,1)}, bf16[8,1,272,256]{3,2,1,0:T(8,128)(2,1)}, u32[]{:S(2)}, u32[]{:S(2)}) collective-permute-start(bf16[8,1,272,256]{3,2,1,0:T(8,128)(2,1)} %constant_dynamic-slice_fusion), channel_id=1, source_target_pairs={{0,4},{2,6},{4,0},{6,2},{1,5},{3,7},{5,1},{7,3},{8,12},{10,14},{12... | collective-permute-start | bytes 3342344 | tf_op jit(solution)/shard_map/ppermute | solution.py:37
  109.4 1.2 collective-permute-start.12
  110.6 2.0 %collective-permute-start.13 = (bf16[2,1024,256]{2,1,0:T(8,128)(2,1)}, bf16[2,1024,256]{2,1,0:T(8,128)(2,1)}, u32[]{:S(2)}, u32[]{:S(2)}) collective-permute-start(bf16[2,1024,256]{2,1,0:T(8,128)(2,1)} %slice.47), channel_id=1, source_target_pairs={{0,6},{2,0},{4,2},{6,4},{1,7},{3,1},{5,3},{7,5},{8,14},{10,8},{12,... | collective-permute-start | bytes 3145736 | tf_op jit(solution)/shard_map/ppermute | solution.py:37
  112.7 4.4 %all-to-all-start.1 = ((bf16[8,256,256]{2,1,0:T(8,128)(2,1)}), bf16[8,256,256]{2,1,0:T(8,128)(2,1)}, u32[]{:S(2)}, u32[]{:S(2)}) async-start(bf16[8,256,256]{2,1,0:T(8,128)(2,1)} %combine_0_3_0.1), calls=%async_computation.1 | async-start | bytes 2097152 | tf_op jit(solution)/shard_map/all_to_all | solution.py:33
  117.1 0.9 convert_reduce_fusion.2
  118.0 0.6 reshape.75.refs_0_
  118.6 0.7 reshape.76.refs_1_
  119.3 18.2 %combine_1_0_0.1 = bf16[16,256,256]{2,1,0:T(8,128)(2,1)} custom-call(s32[13]{0:T(128)} %get-tuple-element.68.where, s32[16]{0:T(128)} %reshape.75.refs_0_, s32[16]{0:T(128)} %reshape.76.refs_1_, bf16[8,1,272,256]{3,2,1,0:T(8,128)(2,1)} %collective-permute-done.5.refs_2_, bf16[8,1,272,256]{3,2,1,0:T(8,128)(2,1)} %collective-permute-done.6.refs_3_, ...), custom_call_target="tpu_custom_call" | custom-call | flops 999999995904 | bytes 1 | tf_op jit(solution)/shard_map/combine_1_0_0/pallas_call | solution.py:167
  137.5 4.6 %all-to-all-start.2 = ((bf16[16,256,256]{2,1,0:T(8,128)(2,1)}), bf16[16,256,256]{2,1,0:T(8,128)(2,1)S(1)}, u32[]{:S(2)}, u32[]{:S(2)}) async-start(bf16[16,256,256]{2,1,0:T(8,128)(2,1)} %combine_1_0_0.1), calls=%async_computation.2 | async-start | bytes 4194304 | tf_op jit(solution)/shard_map/all_to_all | solution.py:33
  142.1 15.5 %collective-permute-done.12.refs_2_ = bf16[2,1024,256]{2,1,0:T(8,128)(2,1)} collective-permute-done((bf16[2,1024,256]{2,1,0:T(8,128)(2,1)}, bf16[2,1024,256]{2,1,0:T(8,128)(2,1)}, u32[]{:S(2)}, u32[]{:S(2)}) %collective-permute-start.12) | collective-permute-done | bytes 1048608 | tf_op jit(solution)/shard_map/ppermute | solution.py:37
  157.9 0.5 collective-permute-start.15
  158.4 0.7 convert_reduce_fusion.1
  159.2 0.6 reshape.77.refs_0_
  159.8 7.9 %combine_3_0_0.1.refs_9_ = bf16[8,256,256]{2,1,0:T(8,128)(2,1)} custom-call(s32[13]{0:T(128)} %get-tuple-element.68.where, s32[16]{0:T(128)} %reshape.77.refs_0_, bf16[8,1,272,256]{3,2,1,0:T(8,128)(2,1)} %collective-permute-done.11.refs_1_, bf16[2,1024,256]{2,1,0:T(8,128)(2,1)} %collective-permute-done.12.refs_2_, ...), custom_call_target="tpu_custom_call" | custom-call | flops 1 | bytes 1 | tf_op jit(solution)/shard_map/combine_3_0_0/pallas_call | solution.py:167
  167.7 0.9 copy-done.3
  168.7 7.9 %combine_3_0_1.1 = bf16[8,256,256]{2,1,0:T(8,128)(2,1)} custom-call(s32[13]{0:T(128)} %get-tuple-element.68.where, s32[16]{0:T(128)} %reshape.77.refs_0_, bf16[8,1,272,256]{3,2,1,0:T(8,128)(2,1)} %collective-permute-done.11.refs_1_, bf16[2,1024,256]{2,1,0:T(8,128)(2,1)} %copy-done.3, ...), custom_call_target="tpu_custom_call", output_to_operand_aliasing={{}: (10, {})} | custom-call | flops 1 | bytes 1 | tf_op jit(solution)/shard_map/combine_3_0_1/pallas_call | solution.py:167
  176.6 4.3 %all-to-all-start.3 = ((bf16[8,256,256]{2,1,0:T(8,128)(2,1)}), bf16[8,256,256]{2,1,0:T(8,128)(2,1)S(1)}, u32[]{:S(2)}, u32[]{:S(2)}) async-start(bf16[8,256,256]{2,1,0:T(8,128)(2,1)} %combine_3_0_1.1), calls=%async_computation.3 | async-start | bytes 2097152 | tf_op jit(solution)/shard_map/all_to_all | solution.py:33
  181.5 5.0 %assemble.1 = bf16[4,4,2,256,256]{4,3,2,1,0:T(8,128)(2,1)} custom-call(s32[13]{0:T(128)} %get-tuple-element.68.where, bf16[4,2,1,256,256]{4,3,2,1,0:T(8,128)(2,1)} %bitcast.7.refs_0_, bf16[4,2,2,256,256]{4,3,2,1,0:T(8,128)(2,1)} %bitcast.21), custom_call_target="tpu_custom_call" | custom-call | flops 1 | bytes 1 | tf_op jit(solution)/shard_map/assemble/pallas_call | solution.py:204
  186.5 9.7 %all-to-all-done.3 = bf16[8,256,256]{2,1,0:T(8,128)(2,1)S(1)} async-done(((bf16[8,256,256]{2,1,0:T(8,128)(2,1)}), bf16[8,256,256]{2,1,0:T(8,128)(2,1)S(1)}, u32[]{:S(2)}, u32[]{:S(2)}) %all-to-all-start.3) | async-done | bytes 1048608 | tf_op jit(solution)/shard_map/all_to_all | solution.py:33
  196.2 1.0 constant_dynamic-update-slice_fusion
  (31 shorter events, 0.4 us)
Async XLA Ops:
  4.3 4.6 %copy-start.4 = (s32[2]{0:T(128)S(1)}, s32[2]{0:T(128)}, u32[]{:S(2)}) copy-start(s32[2]{0:T(128)} %param.14) | copy-start | bytes 28
  4.3 62.8 %all-to-all-start = ((bf16[8,4,272,256]{3,2,1,0:T(8,128)(2,1)}), bf16[8,4,272,256]{3,2,1,0:T(8,128)(2,1)}, u32[]{:S(2)}, u32[]{:S(2)}) async-start(bf16[8,4,272,256]{3,2,1,0:T(8,128)(2,1)} %pack.1), calls=%async_computation | async-start | bytes 8912896 | tf_op jit(solution)/shard_map/all_to_all | solution.py:33
  9.0 6.9 %copy-start.2 = (bf16[2,8,256,256]{3,2,1,0:T(8,128)(2,1)S(1)}, bf16[2,8,256,256]{3,2,1,0:T(8,128)(2,1)}, u32[]{:S(2)}) copy-start(bf16[2,8,256,256]{3,2,1,0:T(8,128)(2,1)} %param.11) | copy-start | bytes 6291460
  9.0 6.8 %copy-start.5 = (s32[2]{0:T(128)S(1)}, s32[2]{0:T(128)}, u32[]{:S(2)}) copy-start(s32[2]{0:T(128)} %param.12) | copy-start | bytes 28
  11.5 6.5 %copy-start = (bf16[2,8,256,256]{3,2,1,0:T(8,128)(2,1)}, bf16[2,8,256,256]{3,2,1,0:T(8,128)(2,1)S(1)}, u32[]{:S(2)}) copy-start(bf16[2,8,256,256]{3,2,1,0:T(8,128)(2,1)S(1)} %fusion) | copy-start | bytes 6291460
  11.5 50.5 %collective-permute-start = (bf16[2,2048,256]{2,1,0:T(8,128)(2,1)S(1)}, bf16[2,2048,256]{2,1,0:T(8,128)(2,1)}, u32[]{:S(2)}, u32[]{:S(2)}) collective-permute-start(bf16[2,2048,256]{2,1,0:T(8,128)(2,1)S(1)} %bitcast.15), channel_id=1, source_target_pairs={{0,8},{8,16},{16,24},{24,0},{1,9},{9,17},{17,25},{25,1},{2,10},{10... | collective-permute-start | bytes 6291464 | tf_op jit(solution)/shard_map/ppermute | solution.py:37
  13.6 48.4 %collective-permute-start.1 = (bf16[2,2048,256]{2,1,0:T(8,128)(2,1)S(1)}, bf16[2,2048,256]{2,1,0:T(8,128)(2,1)}, u32[]{:S(2)}, u32[]{:S(2)}) collective-permute-start(bf16[2,2048,256]{2,1,0:T(8,128)(2,1)S(1)} %bitcast.16), channel_id=1, source_target_pairs={{0,24},{8,0},{16,8},{24,16},{1,25},{9,1},{17,9},{25,17},{2,26},{10... | collective-permute-start | bytes 6291464 | tf_op jit(solution)/shard_map/ppermute | solution.py:37
  18.0 49.1 %collective-permute-start.2 = (bf16[2,2048,256]{2,1,0:T(8,128)(2,1)}, bf16[2,2048,256]{2,1,0:T(8,128)(2,1)}, u32[]{:S(2)}, u32[]{:S(2)}) collective-permute-start(bf16[2,2048,256]{2,1,0:T(8,128)(2,1)} %bitcast.3.refs_2_), channel_id=1, source_target_pairs={{0,2},{2,4},{4,6},{6,0},{1,3},{3,5},{5,7},{7,1},{8,10},{10,12},{12... | collective-permute-start | bytes 6291464 | tf_op jit(solution)/shard_map/ppermute | solution.py:37
  19.5 47.6 %collective-permute-start.3 = (bf16[2,2048,256]{2,1,0:T(8,128)(2,1)}, bf16[2,2048,256]{2,1,0:T(8,128)(2,1)}, u32[]{:S(2)}, u32[]{:S(2)}) collective-permute-start(bf16[2,2048,256]{2,1,0:T(8,128)(2,1)} %bitcast.3.refs_2_), channel_id=1, source_target_pairs={{0,6},{2,0},{4,2},{6,4},{1,7},{3,1},{5,3},{7,5},{8,14},{10,8},{12,... | collective-permute-start | bytes 6291464 | tf_op jit(solution)/shard_map/ppermute | solution.py:37
  21.3 45.9 %collective-permute-start.4 = (bf16[2,2048,256]{2,1,0:T(8,128)(2,1)}, bf16[2,2048,256]{2,1,0:T(8,128)(2,1)}, u32[]{:S(2)}, u32[]{:S(2)}) collective-permute-start(bf16[2,2048,256]{2,1,0:T(8,128)(2,1)} %bitcast.3.refs_2_), channel_id=1, source_target_pairs={{0,1},{1,0},{2,3},{3,2},{4,5},{5,4},{6,7},{7,6},{8,9},{9,8},{10,11... | collective-permute-start | bytes 6291464 | tf_op jit(solution)/shard_map/ppermute | solution.py:37
  72.6 26.9 %collective-permute-start.7 = (bf16[2,1024,256]{2,1,0:T(8,128)(2,1)}, bf16[2,1024,256]{2,1,0:T(8,128)(2,1)}, u32[]{:S(2)}, u32[]{:S(2)}) collective-permute-start(bf16[2,1024,256]{2,1,0:T(8,128)(2,1)} %slice.44), channel_id=1, source_target_pairs={{0,8},{8,16},{16,24},{24,0},{1,9},{9,17},{17,25},{25,1},{2,10},{10... | collective-permute-start | bytes 3145736 | tf_op jit(solution)/shard_map/ppermute | solution.py:37
  74.9 25.1 %collective-permute-start.8 = (bf16[2,1024,256]{2,1,0:T(8,128)(2,1)}, bf16[2,1024,256]{2,1,0:T(8,128)(2,1)}, u32[]{:S(2)}, u32[]{:S(2)}) collective-permute-start(bf16[2,1024,256]{2,1,0:T(8,128)(2,1)} %slice.45), channel_id=1, source_target_pairs={{0,24},{8,0},{16,8},{24,16},{1,25},{9,1},{17,9},{25,17},{2,26},{10... | collective-permute-start | bytes 3145736 | tf_op jit(solution)/shard_map/ppermute | solution.py:37
  79.7 26.7 %collective-permute-start.5 = (bf16[8,1,272,256]{3,2,1,0:T(8,128)(2,1)}, bf16[8,1,272,256]{3,2,1,0:T(8,128)(2,1)}, u32[]{:S(2)}, u32[]{:S(2)}) collective-permute-start(bf16[8,1,272,256]{3,2,1,0:T(8,128)(2,1)} %get-tuple-element.43), channel_id=1, source_target_pairs={{0,2},{2,4},{4,6},{6,0},{1,3},{3,5},{5,7},{7,1},{8,10},{10,12},{12... | collective-permute-start | bytes 3342344 | tf_op jit(solution)/shard_map/ppermute | solution.py:37
  81.1 25.2 %collective-permute-start.6 = (bf16[8,1,272,256]{3,2,1,0:T(8,128)(2,1)}, bf16[8,1,272,256]{3,2,1,0:T(8,128)(2,1)}, u32[]{:S(2)}, u32[]{:S(2)}) collective-permute-start(bf16[8,1,272,256]{3,2,1,0:T(8,128)(2,1)} %get-tuple-element.44), channel_id=1, source_target_pairs={{0,6},{2,0},{4,2},{6,4},{1,7},{3,1},{5,3},{7,5},{8,14},{10,8},{12,... | collective-permute-start | bytes 3342344 | tf_op jit(solution)/shard_map/ppermute | solution.py:37
  106.3 10.8 %collective-permute-start.10 = (bf16[2,2048,256]{2,1,0:T(8,128)(2,1)}, bf16[2,2048,256]{2,1,0:T(8,128)(2,1)S(1)}, u32[]{:S(2)}, u32[]{:S(2)}) collective-permute-start(bf16[2,2048,256]{2,1,0:T(8,128)(2,1)} %collective-permute-done.3.refs_6_), channel_id=1, source_target_pairs={{0,1},{1,0},{2,3},{3,2},{4,5},{5,4},{6,7},{7,6},{8,9},{9,8},{10,11... | collective-permute-start | bytes 6291464 | tf_op jit(solution)/shard_map/ppermute | solution.py:37
  106.3 10.8 %collective-permute-start.9 = (bf16[2,2048,256]{2,1,0:T(8,128)(2,1)}, bf16[2,2048,256]{2,1,0:T(8,128)(2,1)}, u32[]{:S(2)}, u32[]{:S(2)}) collective-permute-start(bf16[2,2048,256]{2,1,0:T(8,128)(2,1)} %collective-permute-done.2.refs_4_), channel_id=1, source_target_pairs={{0,1},{1,0},{2,3},{3,2},{4,5},{5,4},{6,7},{7,6},{8,9},{9,8},{10,11... | collective-permute-start | bytes 6291464 | tf_op jit(solution)/shard_map/ppermute | solution.py:37
  106.8 51.1 %collective-permute-start.11 = (bf16[8,1,272,256]{3,2,1,0:T(8,128)(2,1)}, bf16[8,1,272,256]{3,2,1,0:T(8,128)(2,1)}, u32[]{:S(2)}, u32[]{:S(2)}) collective-permute-start(bf16[8,1,272,256]{3,2,1,0:T(8,128)(2,1)} %constant_dynamic-slice_fusion), channel_id=1, source_target_pairs={{0,4},{2,6},{4,0},{6,2},{1,5},{3,7},{5,1},{7,3},{8,12},{10,14},{12... | collective-permute-start | bytes 3342344 | tf_op jit(solution)/shard_map/ppermute | solution.py:37
  109.4 48.2 %collective-permute-start.12 = (bf16[2,1024,256]{2,1,0:T(8,128)(2,1)}, bf16[2,1024,256]{2,1,0:T(8,128)(2,1)}, u32[]{:S(2)}, u32[]{:S(2)}) collective-permute-start(bf16[2,1024,256]{2,1,0:T(8,128)(2,1)} %slice.46), channel_id=1, source_target_pairs={{0,2},{2,4},{4,6},{6,0},{1,3},{3,5},{5,7},{7,1},{8,10},{10,12},{12... | collective-permute-start | bytes 3145736 | tf_op jit(solution)/shard_map/ppermute | solution.py:37
  110.6 47.3 %collective-permute-start.13 = (bf16[2,1024,256]{2,1,0:T(8,128)(2,1)}, bf16[2,1024,256]{2,1,0:T(8,128)(2,1)}, u32[]{:S(2)}, u32[]{:S(2)}) collective-permute-start(bf16[2,1024,256]{2,1,0:T(8,128)(2,1)} %slice.47), channel_id=1, source_target_pairs={{0,6},{2,0},{4,2},{6,4},{1,7},{3,1},{5,3},{7,5},{8,14},{10,8},{12,... | collective-permute-start | bytes 3145736 | tf_op jit(solution)/shard_map/ppermute | solution.py:37
  112.7 24.8 %all-to-all-start.1 = ((bf16[8,256,256]{2,1,0:T(8,128)(2,1)}), bf16[8,256,256]{2,1,0:T(8,128)(2,1)}, u32[]{:S(2)}, u32[]{:S(2)}) async-start(bf16[8,256,256]{2,1,0:T(8,128)(2,1)} %combine_0_3_0.1), calls=%async_computation.1 | async-start | bytes 2097152 | tf_op jit(solution)/shard_map/all_to_all | solution.py:33
  117.1 2.2 %copy-start.6 = (bf16[2,2048,256]{2,1,0:T(8,128)(2,1)}, bf16[2,2048,256]{2,1,0:T(8,128)(2,1)S(1)}, u32[]{:S(2)}) copy-start(bf16[2,2048,256]{2,1,0:T(8,128)(2,1)S(1)} %collective-permute-done.10.refs_7_) | copy-start | bytes 6291460
  137.5 39.1 %all-to-all-start.2 = ((bf16[16,256,256]{2,1,0:T(8,128)(2,1)}), bf16[16,256,256]{2,1,0:T(8,128)(2,1)S(1)}, u32[]{:S(2)}, u32[]{:S(2)}) async-start(bf16[16,256,256]{2,1,0:T(8,128)(2,1)} %combine_1_0_0.1), calls=%async_computation.2 | async-start | bytes 4194304 | tf_op jit(solution)/shard_map/all_to_all | solution.py:33
  157.9 9.8 %collective-permute-start.14 = (bf16[2,1024,256]{2,1,0:T(8,128)(2,1)}, bf16[2,1024,256]{2,1,0:T(8,128)(2,1)S(1)}, u32[]{:S(2)}, u32[]{:S(2)}) collective-permute-start(bf16[2,1024,256]{2,1,0:T(8,128)(2,1)} %collective-permute-done.12.refs_2_), channel_id=1, source_target_pairs={{0,1},{1,0},{2,3},{3,2},{4,5},{5,4},{6,7},{7,6},{8,9},{9,8},{10,11... | collective-permute-start | bytes 3145736 | tf_op jit(solution)/shard_map/ppermute | solution.py:37
  157.9 9.8 %collective-permute-start.15 = (bf16[2,1024,256]{2,1,0:T(8,128)(2,1)}, bf16[2,1024,256]{2,1,0:T(8,128)(2,1)}, u32[]{:S(2)}, u32[]{:S(2)}) collective-permute-start(bf16[2,1024,256]{2,1,0:T(8,128)(2,1)} %collective-permute-done.13.refs_3_), channel_id=1, source_target_pairs={{0,1},{1,0},{2,3},{3,2},{4,5},{5,4},{6,7},{7,6},{8,9},{9,8},{10,11... | collective-permute-start | bytes 3145736 | tf_op jit(solution)/shard_map/ppermute | solution.py:37
  167.7 1.0 copy-start.3
  176.6 4.9 %copy-start.1 = (bf16[16,256,256]{2,1,0:T(8,128)(2,1)}, bf16[16,256,256]{2,1,0:T(8,128)(2,1)S(1)}, u32[]{:S(2)}) copy-start(bf16[16,256,256]{2,1,0:T(8,128)(2,1)S(1)} %all-to-all-done.2) | copy-start | bytes 6291460
  176.6 19.6 %all-to-all-start.3 = ((bf16[8,256,256]{2,1,0:T(8,128)(2,1)}), bf16[8,256,256]{2,1,0:T(8,128)(2,1)S(1)}, u32[]{:S(2)}, u32[]{:S(2)}) async-start(bf16[8,256,256]{2,1,0:T(8,128)(2,1)} %combine_3_0_1.1), calls=%async_computation.3 | async-start | bytes 2097152 | tf_op jit(solution)/shard_map/all_to_all | solution.py:33

commit v9 on v8

--- a/solution.py
+++ b/solution.py
@@ -10,7 +10,6 @@
 OFFSETS = (0, 3, 1, 2)
 STEPS = (0, 1, 3, 2)
 TAIL = 16
-SLOTS = 3
 BF16 = jnp.bfloat16
 BRIEF = pl.CostEstimate(flops=1, bytes_accessed=1, transcendentals=0)
 LONG = pl.CostEstimate(flops=10**12, bytes_accessed=1, transcendentals=0)
@@ -41,15 +40,19 @@
     return shift(array, axis, 1), shift(array, axis, 3)
 
 
-def onward(from_low, from_high, axis):
+def halves_of(from_low, from_high):
     half = from_low.shape[1] // 2
-    return shift(from_low[:, :half], axis, 1), shift(from_high[:, half:], axis, 3)
+    return from_low[:, :half], from_high[:, half:]
+
+
+def onward(halves, axis):
+    return shift(halves[0], axis, 1), shift(halves[1], axis, 3)
 
 
 def combine(where, psis, lefts, rights, first, z_first=0, kept=None, cores=(0, 1)):
     codes = [codes for _, codes in psis]
     psis = [psi for psi, _ in psis]
-    rows, width = psis[0].shape[2:]
+    width = psis[0].shape[-1]
     columns = psis[0].shape[1]
     depth = sum(a.shape[1] for a in lefts[0][0])
     terms = depth // width
@@ -57,7 +60,8 @@
     left_parts = [a for pair in lefts for group in pair for a in group]
     right_parts = [a for group in rights for a in group]
     steps = len(rights)
-    slots = min(SLOTS, steps)
+    last = steps - 1
+    size_out = len(cores) * count
     each = [(core, k) for core in cores for k in range(count)]
 
     def mine(where):
@@ -72,7 +76,9 @@
         psi_refs = [refs.pop(0) for _ in psis]
         left_refs = [[[refs.pop(0) for _ in group] for group in pair] for pair in lefts]
         right_refs = [[refs.pop(0) for _ in group] for group in rights]
-        out_ref, left_buf, right_buf, partial, left_sems, sems = refs[kept is not None :]
+        (out_ref, psi_buf, left_buf, right_buf, partial, out_buf, psi_sems, left_sems, sems, out_sems) = refs[
+            kept is not None :
+        ]
         step = pl.program_id(0)
 
         def copy_lefts(needed, go):
@@ -91,24 +97,34 @@
                     copy.start() if go else copy.wait()
                     row += size
 
-        def fetch(at, go):
-            slot = lax.rem(at, slots)
-            for n_step in range(steps):
-
-                @pl.when(at == n_step)
-                def _(n_step=n_step):
-                    for n_block, (core, k) in enumerate(each):
-                        right = pick_of(n_step, core, k, 1, where, codes)
-                        row = 0
-                        for n, ref in enumerate(right_refs[n_step]):
-                            size = ref.shape[1]
-                            copy = pltpu.make_async_copy(
-                                ref.at[right],
-                                right_buf.at[slot, n_block, pl.ds(row, size)],
-                                sems.at[slot, n_block, n],
-                            )
-                            copy.start() if go else copy.wait()
-                            row += size
+        def fetch(n_step, go):
+            g = where[z_first + n_step]
+            for k in range(count):
+                copy = pltpu.make_async_copy(
+                    psi_refs[k].at[pl.ds(g * 2, 2), mine(where), pl.ds(0, width)],
+                    psi_buf.at[n_step, k],
+                    psi_sems.at[n_step, k],
+                )
+                copy.start() if go else copy.wait()
+            for n_block, (core, k) in enumerate(each):
+                right = pick_of(n_step, core, k, 1, where, codes)
+                row = 0
+                for n, ref in enumerate(right_refs[n_step]):
+                    size = ref.shape[1]
+                    copy = pltpu.make_async_copy(
+                        ref.at[right],
+                        right_buf.at[n_step, n_block, pl.ds(row, size)],
+                        sems.at[n_step, n_block, n],
+                    )
+                    copy.start() if go else copy.wait()
+                    row += size
+
+        def leave(n_step):
+            g = where[z_first + n_step]
+            to = g * size_out if len(cores) > 1 else (g * 2 + (where[8] ^ cores[0])) * count
+            return pltpu.make_async_copy(
+                out_buf.at[n_step], out_ref.at[pl.ds(to, size_out)], out_sems.at[n_step]
+            )
 
         @pl.when(step == 0)
         def _():
@@ -116,17 +132,8 @@
             fetch(0, True)
             if steps > 1:
                 copy_lefts(False, True)
-            for ahead in range(1, slots - 1):
-                fetch(ahead, True)
-
-        if slots > 1:
-
-            @pl.when(step + slots - 1 < steps)
-            def _():
-                fetch(step + slots - 1, True)
-
-        @pl.when(step == 0)
-        def _():
+            for n_step in range(1, steps):
+                fetch(n_step, True)
             copy_lefts(True, False)
 
         if steps > 1:
@@ -135,11 +142,15 @@
             def _():
                 copy_lefts(False, False)
 
-        fetch(step, False)
-        slot = lax.rem(step, slots)
+        for n_step in range(steps):
+
+            @pl.when(step == n_step)
+            def _(n_step=n_step):
+                fetch(n_step, False)
+
         for n_block, (core, k) in enumerate(each):
             left = pick_of(step, core, k, 0, where, codes)
-            block = psi_refs[k][where[8] ^ core, 0, :width]
+            block = psi_buf[step, k, where[8] ^ core]
             for t in range(terms):
                 product = jnp.dot(
                     left_buf[k, core - cores[0], left, t * width : (t + 1) * width],
@@ -149,18 +160,22 @@
                 partial[n_block, :, t * width : (t + 1) * width] = product.astype(BF16)
         for n_block, (core, k) in enumerate(each):
             total = jnp.dot(
-                partial[n_block], right_buf[slot, n_block], preferred_element_type=jnp.float32
+                partial[n_block], right_buf[step, n_block], preferred_element_type=jnp.float32
             )
             row = (where[8] ^ core) * count if len(cores) > 1 else 0
-            out_ref[row + k] = total.astype(BF16)
+            out_buf[step, row + k] = total.astype(BF16)
+        for n_step in range(steps):
+
+            @pl.when(step == n_step)
+            def _(n_step=n_step):
+                leave(n_step).start()
+
+        @pl.when(step == last)
+        def _():
+            for n_step in range(steps):
+                leave(n_step).wait()
 
     in_place = pl.BlockSpec(memory_space=pl.ANY)
-
-    def of_g(step, where, *codes):
-        g = where[z_first + step]
-        return (g if len(cores) > 1 else g * 2 + (where[8] ^ cores[0])), 0, 0
-
-    psi_of_g = lambda step, where, *codes: (where[z_first + step], mine(where), 0, 0)
     parts = max(len(group) for group in rights)
     extra = [] if kept is None else [kept]
     operands = [*psis, *left_parts, *right_parts, *extra]
@@ -170,15 +185,18 @@
         grid_spec=pltpu.PrefetchScalarGridSpec(
             num_scalar_prefetch=1 + count,
             grid=(steps,),
-            in_specs=[pl.BlockSpec((2, 1, rows, width), psi_of_g)] * count
-            + [in_place] * (len(operands) - count),
-            out_specs=pl.BlockSpec((len(cores) * count, width, width), of_g),
+            in_specs=[in_place] * len(operands),
+            out_specs=in_place,
             scratch_shapes=[
+                pltpu.VMEM((steps, count, 2, width, width), BF16),
                 pltpu.VMEM((count, len(cores), 2, depth, width), BF16),
-                pltpu.VMEM((slots, len(each), depth, width), BF16),
+                pltpu.VMEM((steps, len(each), depth, width), BF16),
                 pltpu.VMEM((len(each), width, depth), BF16),
+                pltpu.VMEM((steps, size_out, width, width), BF16),
+                pltpu.SemaphoreType.DMA((steps, count)),
                 pltpu.SemaphoreType.DMA((count, len(cores), max(len(pair[0]) for pair in lefts), 2)),
-                pltpu.SemaphoreType.DMA((slots, len(each), parts)),
+                pltpu.SemaphoreType.DMA((steps, len(each), parts)),
+                pltpu.SemaphoreType.DMA((steps,)),
             ],
         ),
         input_output_aliases={count + len(operands): 0} if extra else {},
@@ -293,27 +311,27 @@
     right_low, right_high = both_ways(right_own, "z")
     left_low, left_high = both_ways(left_own, "x")
     left_other = shift(left_own, "c", 1, 2)
-    psi, right_low, right_high, left_low, left_high, left_other = together(
-        psi, right_low, right_high, left_low, left_high, left_other
+    psi, right_low, right_high, left_low, left_high, left_other, *to_far = together(
+        psi, right_low, right_high, left_low, left_high, left_other, *halves_of(right_low, right_high)
     )
 
     for_low, for_high = column(psi, where[10]), column(psi, where[11])
-    for_low, for_high, psi, *to_far = together(for_low, for_high, psi, right_low, right_high)
+    for_low, for_high, psi, *to_far = together(for_low, for_high, psi, *to_far)
     psi_low, psi_high = shift(for_low, "x", 1), shift(for_high, "x", 3)
-    far = onward(*to_far, "z")
+    far = onward(to_far, "z")
     psi_own = split(psi)
     rights = [(right_own,), (right_low,), (right_high,)]
     lefts_own = [((left_own,), (left_other,))]
     own = combine(where, [psi_own], lefts_own, rights, 0)
     own, psi, left_low, left_high = together(own, psi, left_low, left_high)
-    halves = left_low[:, : terms * width // 2], left_high[:, terms * width // 2 :]
+    halves = halves_of(left_low, left_high)
     rights.append(tuple(far))
     own = combine(where, [psi_own], lefts_own, rights[3:], 0, 3, own)
     psi_rest, psi_low, psi_high, own, left_low, left_high, *halves = together(
         column(psi, where[12]), psi_low, psi_high, own, left_low, left_high, *halves
     )
 
-    left_far = shift(halves[0], "x", 1), shift(halves[1], "x", 3)
+    left_far = onward(halves, "x")
     psi_far = shift(psi_rest, "x", 2)
     own = exchange(own, "z")
     others = [shift(a, "c", 1, 2) for a in (left_low, left_high)]
@@ -324,8 +342,7 @@
     near = exchange(near, "z")
     other_far = [shift(a, "c", 1, 2) for a in left_far]
     psi_far = split(psi_far)
-    rest = combine(where, [psi_far], [(tuple(left_far),)], rights, 3, cores=(0,))
-    rest = combine(where, [psi_far], [(tuple(other_far),)], rights, 3, kept=rest, cores=(1,))
+    rest = combine(where, [psi_far], [(tuple(left_far), tuple(other_far))], rights, 3)
     rest = exchange(rest, "z")
     applied = assemble(where, [(0, own), (1, near)])
     zero = jnp.uint32(0)

time: 199 us -> 191 us (0.960)
  Pallas kernels: 58.9 us -> 50.9 us
  waiting for transfers between devices: 68.6 us -> 70.9 us
    pallas_call x5 -> x4, Pallas kernels: 49.5 us -> 41.5 us  [combine(): pl.pallas_call(kernel, out_shape=jax.ShapeDtypeStruct((8 * count, width,...]
    ppermute x16, waiting for transfers between devices: 58.8 us -> 61.1 us  [shift(): lax.ppermute(array, axis, [(i, (i + step) % size) for i in range(size)])]
  transfers between devices with their start and end apart: 20 -> 20, of which waited for: 7 -> 7; matrix products, arithmetic and copies ran while one was open for 11% -> 10% of each run, Pallas kernels for 28% -> 24%
where the time goes in v9:
time: 191 us; the launch traced here: 190 us
  waiting for transfers between devices  70.9 us (37%)
  Pallas kernels  50.9 us (27%)
  starting transfers between devices  39.4 us (21%)
  local copies, waits for them, and re-layouts  20.9 us (11%)
  other arithmetic  5.51 us (3%)
  between operations  2.81 us (1%)
    ppermute x16, waiting for transfers between devices, shift(): lax.ppermute(array, axis, [(i, (i + step) % size) for i in range(size)])  61.1 us
    pallas_call x4, Pallas kernels, combine(): pl.pallas_call(kernel, out_shape=jax.ShapeDtypeStruct((8 * count, width,...  41.5 us
    ppermute x16, starting transfers between devices, shift(): lax.ppermute(array, axis, [(i, (i + step) % size) for i in range(size)])  21.3 us
    all_to_all x4, starting transfers between devices, exchange(): return lax.all_to_all(array, axis, split_axis=0, concat_axis=0, tiled=True)  18.1 us
    all_to_all x4, waiting for transfers between devices, exchange(): return lax.all_to_all(array, axis, split_axis=0, concat_axis=0, tiled=True)  9.81 us
    slice x4, local copies, waits for them, and re-layouts, halves_of(): return (from_low[:, :half], from_high[:, half:])  9.11 us
    dynamic_slice x2, local copies, waits for them, and re-layouts, column(): return lax.dynamic_slice(psi, start, (8, 1) + psi.shape[2:])  5.52 us
    pallas_call x1, Pallas kernels, assemble(): pl.pallas_call(kernel, out_shape=jax.ShapeDtypeStruct((4, 4, 2, width, wi...  5.04 us
  transfers between devices with their start and end apart: 20, of which 7 were waited for; matrix products, arithmetic and copies ran while one was open for 10% of the time, Pallas kernels for 24%

profile of v9, /device:TPU:0, one launch (start us, length us, event | category | flops | bytes accessed | tf_op | source)
XLA Modules:
  0.0 190.3 jit_solution(8818553831843652359)
XLA Ops:
  0.0 4.3 %pack.1 = bf16[8,4,272,256]{3,2,1,0:T(8,128)(2,1)} custom-call(s32[32]{0:T(128)} %left.1, s32[32]{0:T(128)} %right.1, bf16[4,4,2,256,256]{4,3,2,1,0:T(8,128)(2,1)} %bitcast.22), custom_call_target="tpu_custom_call" | custom-call | flops 1 | bytes 1 | tf_op jit(solution)/shard_map/pack/pallas_call | solution.py:264
  4.4 4.7 %all-to-all-start = ((bf16[8,4,272,256]{3,2,1,0:T(8,128)(2,1)}), bf16[8,4,272,256]{3,2,1,0:T(8,128)(2,1)}, u32[]{:S(2)}, u32[]{:S(2)}) async-start(bf16[8,4,272,256]{3,2,1,0:T(8,128)(2,1)} %pack.1), calls=%async_computation | async-start | bytes 8912896 | tf_op jit(solution)/shard_map/all_to_all | solution.py:32
  9.1 2.1 %fusion = bf16[2,8,256,256]{3,2,1,0:T(8,128)(2,1)} fusion(bf16[2,8,256,256]{3,2,1,0:T(8,128)(2,1)S(1)} %copy-done.2, s32[2]{0:T(128)S(1)} %copy-done.5), kind=kLoop, calls=%fused_computation.2 | loop fusion | flops 2097152 | bytes 4194312 | tf_op jit(solution)/shard_map/jit(_where)/select_n | solution.py:304
  11.3 2.0 %collective-permute-start = (bf16[2,2048,256]{2,1,0:T(8,128)(2,1)}, bf16[2,2048,256]{2,1,0:T(8,128)(2,1)}, u32[]{:S(2)}, u32[]{:S(2)}) collective-permute-start(bf16[2,2048,256]{2,1,0:T(8,128)(2,1)} %bitcast.2.refs_4_.refs_8_.refs_6_), channel_id=1, source_target_pairs={{0,8},{8,16},{16,24},{24,0},{1,9},{9,17},{17,25},{25,1},{2,10},{10... | collective-permute-start | bytes 6291464 | tf_op jit(solution)/shard_map/ppermute | solution.py:36
  13.3 2.1 %collective-permute-start.1 = (bf16[2,2048,256]{2,1,0:T(8,128)(2,1)}, bf16[2,2048,256]{2,1,0:T(8,128)(2,1)}, u32[]{:S(2)}, u32[]{:S(2)}) collective-permute-start(bf16[2,2048,256]{2,1,0:T(8,128)(2,1)} %bitcast.2.refs_4_.refs_8_.refs_6_), channel_id=1, source_target_pairs={{0,24},{8,0},{16,8},{24,16},{1,25},{9,1},{17,9},{25,17},{2,26},{10... | collective-permute-start | bytes 6291464 | tf_op jit(solution)/shard_map/ppermute | solution.py:36
  15.4 0.9 fusion.1
  16.3 1.6 collective-permute-start.2
  17.9 1.7 collective-permute-start.3
  19.6 1.2 constant_dynamic-slice_fusion.3
  20.8 0.7 fusion.3
  23.5 38.4 %collective-permute-done.refs_5_.refs_9_.refs_7_ = bf16[2,2048,256]{2,1,0:T(8,128)(2,1)} collective-permute-done((bf16[2,2048,256]{2,1,0:T(8,128)(2,1)}, bf16[2,2048,256]{2,1,0:T(8,128)(2,1)}, u32[]{:S(2)}, u32[]{:S(2)}) %collective-permute-start) | collective-permute-done | bytes 2097184 | tf_op jit(solution)/shard_map/ppermute | solution.py:36
  61.9 2.3 %slice.52 = bf16[2,1024,256]{2,1,0:T(8,128)(2,1)} slice(bf16[2,2048,256]{2,1,0:T(8,128)(2,1)} %collective-permute-done.refs_5_.refs_9_.refs_7_), slice={[0:2], [0:1024], [0:256]} | slice | bytes 2097152 | tf_op jit(solution)/shard_map/slice | solution.py:45
  64.1 2.3 %slice.53 = bf16[2,1024,256]{2,1,0:T(8,128)(2,1)} slice(bf16[2,2048,256]{2,1,0:T(8,128)(2,1)} %collective-permute-done.1.refs_6_.refs_10_.refs_8_), slice={[0:2], [1024:2048], [0:256]} | slice | bytes 2097152 | tf_op jit(solution)/shard_map/slice | solution.py:45
  66.4 3.2 %constant_dynamic-slice_fusion.1 = (bf16[8,1,272,256]{3,2,1,0:T(8,128)(2,1)}, bf16[8,1,272,256]{3,2,1,0:T(8,128)(2,1)}) fusion(bf16[8,4,272,256]{3,2,1,0:T(8,128)(2,1)} %all-to-all-done.refs_1_, u32[]{:T(128)} %bitcast.5, u32[]{:T(128)} %bitcast.4), kind=kLoop, calls=%fused_computation.10 | loop fusion | bytes 4456456 | tf_op jit(solution)/shard_map/dynamic_slice | solution.py:287
  69.6 0.9 convert_reduce_fusion
  70.5 0.7 reshape.74.refs_0_
  71.2 3.2 %collective-permute-start.8 = (bf16[2,1024,256]{2,1,0:T(8,128)(2,1)}, bf16[2,1024,256]{2,1,0:T(8,128)(2,1)}, u32[]{:S(2)}, u32[]{:S(2)}) collective-permute-start(bf16[2,1024,256]{2,1,0:T(8,128)(2,1)} %slice.53), channel_id=1, source_target_pairs={{0,24},{8,0},{16,8},{24,16},{1,25},{9,1},{17,9},{25,17},{2,26},{10... | collective-permute-start | bytes 3145736 | tf_op jit(solution)/shard_map/ppermute | solution.py:36
  74.4 1.5 collective-permute-start.5
  75.9 1.7 collective-permute-start.6
  77.6 7.9 %combine_0_0_0.1.refs_6_ = bf16[8,256,256]{2,1,0:T(8,128)(2,1)} custom-call(s32[13]{0:T(128)} %get-tuple-element.72.where, s32[64]{0:T(128)} %reshape.74.refs_0_, bf16[8,4,272,256]{3,2,1,0:T(8,128)(2,1)} %all-to-all-done.refs_1_, bf16[2,2048,256]{2,1,0:T(8,128)(2,1)} %bitcast.18, bf16[2,2048,256]{2,1,0:T(8,128)(2,1)} %collective-permute-done.4.refs_3_, ...), custom_call_target="tpu_custom_call" | custom-call | flops 999999995904 | bytes 1 | tf_op jit(solution)/shard_map/combine_0_0_0/pallas_call | solution.py:182
  85.5 2.3 %slice.46 = bf16[2,1024,256]{2,1,0:T(8,128)(2,1)} slice(bf16[2,2048,256]{2,1,0:T(8,128)(2,1)} %collective-permute-done.2.refs_4_), slice={[0:2], [0:1024], [0:256]} | slice | bytes 2097152 | tf_op jit(solution)/shard_map/slice | solution.py:45
  87.9 2.2 %slice.47 = bf16[2,1024,256]{2,1,0:T(8,128)(2,1)} slice(bf16[2,2048,256]{2,1,0:T(8,128)(2,1)} %collective-permute-done.3.refs_6_), slice={[0:2], [1024:2048], [0:256]} | slice | bytes 2097152 | tf_op jit(solution)/shard_map/slice | solution.py:45
  90.1 2.4 %constant_dynamic-slice_fusion = bf16[8,1,272,256]{3,2,1,0:T(8,128)(2,1)} fusion(bf16[8,4,272,256]{3,2,1,0:T(8,128)(2,1)} %all-to-all-done.refs_1_, u32[]{:T(128)} %bitcast.6), kind=kLoop, calls=%fused_computation.9 | loop fusion | bytes 2228228 | tf_op jit(solution)/shard_map/dynamic_slice | solution.py:287
  92.5 5.0 %collective-permute-done.7.refs_4_.refs_11_.refs_9_ = bf16[2,1024,256]{2,1,0:T(8,128)(2,1)} collective-permute-done((bf16[2,1024,256]{2,1,0:T(8,128)(2,1)}, bf16[2,1024,256]{2,1,0:T(8,128)(2,1)}, u32[]{:S(2)}, u32[]{:S(2)}) %collective-permute-start.7) | collective-permute-done | bytes 1048608 | tf_op jit(solution)/shard_map/ppermute | solution.py:36
  97.5 5.0 %combine_0_3_0.1 = bf16[8,256,256]{2,1,0:T(8,128)(2,1)} custom-call(s32[13]{0:T(128)} %get-tuple-element.72.where, s32[64]{0:T(128)} %reshape.74.refs_0_, bf16[8,4,272,256]{3,2,1,0:T(8,128)(2,1)} %all-to-all-done.refs_1_, bf16[2,2048,256]{2,1,0:T(8,128)(2,1)} %bitcast.19, ...), custom_call_target="tpu_custom_call", output_to_operand_aliasing={{}: (7, {})} | custom-call | flops 1 | bytes 1 | tf_op jit(solution)/shard_map/combine_0_3_0/pallas_call | solution.py:182
  102.6 0.5 collective-permute-start.9
  103.1 3.0 %collective-permute-start.11 = (bf16[8,1,272,256]{3,2,1,0:T(8,128)(2,1)}, bf16[8,1,272,256]{3,2,1,0:T(8,128)(2,1)}, u32[]{:S(2)}, u32[]{:S(2)}) collective-permute-start(bf16[8,1,272,256]{3,2,1,0:T(8,128)(2,1)} %constant_dynamic-slice_fusion), channel_id=1, source_target_pairs={{0,4},{2,6},{4,0},{6,2},{1,5},{3,7},{5,1},{7,3},{8,12},{10,14},{12... | collective-permute-start | bytes 3342344 | tf_op jit(solution)/shard_map/ppermute | solution.py:36
  106.2 0.6 collective-permute-start.12
  106.7 2.6 %collective-permute-start.13 = (bf16[2,1024,256]{2,1,0:T(8,128)(2,1)}, bf16[2,1024,256]{2,1,0:T(8,128)(2,1)}, u32[]{:S(2)}, u32[]{:S(2)}) collective-permute-start(bf16[2,1024,256]{2,1,0:T(8,128)(2,1)} %slice.47), channel_id=1, source_target_pairs={{0,6},{2,0},{4,2},{6,4},{1,7},{3,1},{5,3},{7,5},{8,14},{10,8},{12,... | collective-permute-start | bytes 3145736 | tf_op jit(solution)/shard_map/ppermute | solution.py:36
  109.4 4.4 %all-to-all-start.1 = ((bf16[8,256,256]{2,1,0:T(8,128)(2,1)}), bf16[8,256,256]{2,1,0:T(8,128)(2,1)}, u32[]{:S(2)}, u32[]{:S(2)}) async-start(bf16[8,256,256]{2,1,0:T(8,128)(2,1)} %combine_0_3_0.1), calls=%async_computation.1 | async-start | bytes 2097152 | tf_op jit(solution)/shard_map/all_to_all | solution.py:32
  113.9 0.9 convert_reduce_fusion.2
  114.7 0.7 reshape.75.refs_0_
  115.4 0.7 reshape.76.refs_1_
  116.1 18.4 %combine_1_0_0.1 = bf16[16,256,256]{2,1,0:T(8,128)(2,1)} custom-call(s32[13]{0:T(128)} %get-tuple-element.72.where, s32[16]{0:T(128)} %reshape.75.refs_0_, s32[16]{0:T(128)} %reshape.76.refs_1_, bf16[8,1,272,256]{3,2,1,0:T(8,128)(2,1)} %collective-permute-done.5.refs_2_, bf16[8,1,272,256]{3,2,1,0:T(8,128)(2,1)} %collective-permute-done.6.refs_3_, ...), custom_call_target="tpu_custom_call" | custom-call | flops 999999995904 | bytes 1 | tf_op jit(solution)/shard_map/combine_1_0_0/pallas_call | solution.py:182
  134.4 4.6 %all-to-all-start.2 = ((bf16[16,256,256]{2,1,0:T(8,128)(2,1)}), bf16[16,256,256]{2,1,0:T(8,128)(2,1)S(1)}, u32[]{:S(2)}, u32[]{:S(2)}) async-start(bf16[16,256,256]{2,1,0:T(8,128)(2,1)} %combine_1_0_0.1), calls=%async_computation.2 | async-start | bytes 4194304 | tf_op jit(solution)/shard_map/all_to_all | solution.py:32
  139.1 14.9 %collective-permute-done.12.refs_2_ = bf16[2,1024,256]{2,1,0:T(8,128)(2,1)} collective-permute-done((bf16[2,1024,256]{2,1,0:T(8,128)(2,1)}, bf16[2,1024,256]{2,1,0:T(8,128)(2,1)}, u32[]{:S(2)}, u32[]{:S(2)}) %collective-permute-start.12) | collective-permute-done | bytes 1048608 | tf_op jit(solution)/shard_map/ppermute | solution.py:36
  154.0 0.1 collective-permute-done.13.refs_3_
  154.1 0.5 collective-permute-start.15
  154.6 0.7 convert_reduce_fusion.1
  155.4 0.7 reshape.77.refs_0_
  156.0 2.3 %collective-permute-done.14.refs_4_ = bf16[2,1024,256]{2,1,0:T(8,128)(2,1)S(1)} collective-permute-done((bf16[2,1024,256]{2,1,0:T(8,128)(2,1)}, bf16[2,1024,256]{2,1,0:T(8,128)(2,1)S(1)}, u32[]{:S(2)}, u32[]{:S(2)}) %collective-permute-start.14) | collective-permute-done | bytes 1048608 | tf_op jit(solution)/shard_map/ppermute | solution.py:36
  158.3 0.3 collective-permute-done.15.refs_5_
  158.6 0.7 copy-done.4
  159.3 10.3 %combine_3_0_0.1 = bf16[8,256,256]{2,1,0:T(8,128)(2,1)} custom-call(s32[13]{0:T(128)} %get-tuple-element.72.where, s32[16]{0:T(128)} %reshape.77.refs_0_, bf16[8,1,272,256]{3,2,1,0:T(8,128)(2,1)} %collective-permute-done.11.refs_1_, bf16[2,1024,256]{2,1,0:T(8,128)(2,1)} %collective-permute-done.12.refs_2_, ...), custom_call_target="tpu_custom_call" | custom-call | flops 1 | bytes 1 | tf_op jit(solution)/shard_map/combine_3_0_0/pallas_call | solution.py:182
  169.6 4.3 %all-to-all-start.3 = ((bf16[8,256,256]{2,1,0:T(8,128)(2,1)}), bf16[8,256,256]{2,1,0:T(8,128)(2,1)S(1)}, u32[]{:S(2)}, u32[]{:S(2)}) async-start(bf16[8,256,256]{2,1,0:T(8,128)(2,1)} %combine_3_0_0.1), calls=%async_computation.3 | async-start | bytes 2097152 | tf_op jit(solution)/shard_map/all_to_all | solution.py:32
  174.4 5.0 %assemble.1 = bf16[4,4,2,256,256]{4,3,2,1,0:T(8,128)(2,1)} custom-call(s32[13]{0:T(128)} %get-tuple-element.72.where, bf16[4,2,1,256,256]{4,3,2,1,0:T(8,128)(2,1)} %bitcast.7.refs_0_, bf16[4,2,2,256,256]{4,3,2,1,0:T(8,128)(2,1)} %bitcast.20), custom_call_target="tpu_custom_call" | custom-call | flops 1 | bytes 1 | tf_op jit(solution)/shard_map/assemble/pallas_call | solution.py:222
  179.5 9.8 %all-to-all-done.3 = bf16[8,256,256]{2,1,0:T(8,128)(2,1)S(1)} async-done(((bf16[8,256,256]{2,1,0:T(8,128)(2,1)}), bf16[8,256,256]{2,1,0:T(8,128)(2,1)S(1)}, u32[]{:S(2)}, u32[]{:S(2)}) %all-to-all-start.3) | async-done | bytes 1048608 | tf_op jit(solution)/shard_map/all_to_all | solution.py:32
  189.3 1.0 constant_dynamic-update-slice_fusion
  (32 shorter events, 0.2 us)
Async XLA Ops:
  4.3 4.8 %copy-start.2 = (bf16[2,8,256,256]{3,2,1,0:T(8,128)(2,1)S(1)}, bf16[2,8,256,256]{3,2,1,0:T(8,128)(2,1)}, u32[]{:S(2)}) copy-start(bf16[2,8,256,256]{3,2,1,0:T(8,128)(2,1)} %param.13) | copy-start | bytes 6291460
  4.3 4.8 %copy-start.5 = (s32[2]{0:T(128)S(1)}, s32[2]{0:T(128)}, u32[]{:S(2)}) copy-start(s32[2]{0:T(128)} %param.14) | copy-start | bytes 28
  4.4 62.1 %all-to-all-start = ((bf16[8,4,272,256]{3,2,1,0:T(8,128)(2,1)}), bf16[8,4,272,256]{3,2,1,0:T(8,128)(2,1)}, u32[]{:S(2)}, u32[]{:S(2)}) async-start(bf16[8,4,272,256]{3,2,1,0:T(8,128)(2,1)} %pack.1), calls=%async_computation | async-start | bytes 8912896 | tf_op jit(solution)/shard_map/all_to_all | solution.py:32
  9.1 6.3 %copy-start.3 = (bf16[2,8,256,256]{3,2,1,0:T(8,128)(2,1)S(1)}, bf16[2,8,256,256]{3,2,1,0:T(8,128)(2,1)}, u32[]{:S(2)}) copy-start(bf16[2,8,256,256]{3,2,1,0:T(8,128)(2,1)} %param.11) | copy-start | bytes 6291460
  9.1 6.3 %copy-start.6 = (s32[2]{0:T(128)S(1)}, s32[2]{0:T(128)}, u32[]{:S(2)}) copy-start(s32[2]{0:T(128)} %param.12) | copy-start | bytes 28
  11.3 50.6 %collective-permute-start = (bf16[2,2048,256]{2,1,0:T(8,128)(2,1)}, bf16[2,2048,256]{2,1,0:T(8,128)(2,1)}, u32[]{:S(2)}, u32[]{:S(2)}) collective-permute-start(bf16[2,2048,256]{2,1,0:T(8,128)(2,1)} %bitcast.2.refs_4_.refs_8_.refs_6_), channel_id=1, source_target_pairs={{0,8},{8,16},{16,24},{24,0},{1,9},{9,17},{17,25},{25,1},{2,10},{10... | collective-permute-start | bytes 6291464 | tf_op jit(solution)/shard_map/ppermute | solution.py:36
  13.3 50.8 %collective-permute-start.1 = (bf16[2,2048,256]{2,1,0:T(8,128)(2,1)}, bf16[2,2048,256]{2,1,0:T(8,128)(2,1)}, u32[]{:S(2)}, u32[]{:S(2)}) collective-permute-start(bf16[2,2048,256]{2,1,0:T(8,128)(2,1)} %bitcast.2.refs_4_.refs_8_.refs_6_), channel_id=1, source_target_pairs={{0,24},{8,0},{16,8},{24,16},{1,25},{9,1},{17,9},{25,17},{2,26},{10... | collective-permute-start | bytes 6291464 | tf_op jit(solution)/shard_map/ppermute | solution.py:36
  16.3 50.1 %copy-start = (bf16[2,8,256,256]{3,2,1,0:T(8,128)(2,1)}, bf16[2,8,256,256]{3,2,1,0:T(8,128)(2,1)S(1)}, u32[]{:S(2)}) copy-start(bf16[2,8,256,256]{3,2,1,0:T(8,128)(2,1)S(1)} %fusion.1) | copy-start | bytes 6291460
  16.3 50.1 %collective-permute-start.2 = (bf16[2,2048,256]{2,1,0:T(8,128)(2,1)S(1)}, bf16[2,2048,256]{2,1,0:T(8,128)(2,1)}, u32[]{:S(2)}, u32[]{:S(2)}) collective-permute-start(bf16[2,2048,256]{2,1,0:T(8,128)(2,1)S(1)} %bitcast.15), channel_id=1, source_target_pairs={{0,2},{2,4},{4,6},{6,0},{1,3},{3,5},{5,7},{7,1},{8,10},{10,12},{12... | collective-permute-start | bytes 6291464 | tf_op jit(solution)/shard_map/ppermute | solution.py:36
  17.9 48.5 %collective-permute-start.3 = (bf16[2,2048,256]{2,1,0:T(8,128)(2,1)S(1)}, bf16[2,2048,256]{2,1,0:T(8,128)(2,1)}, u32[]{:S(2)}, u32[]{:S(2)}) collective-permute-start(bf16[2,2048,256]{2,1,0:T(8,128)(2,1)S(1)} %bitcast.16), channel_id=1, source_target_pairs={{0,6},{2,0},{4,2},{6,4},{1,7},{3,1},{5,3},{7,5},{8,14},{10,8},{12,... | collective-permute-start | bytes 6291464 | tf_op jit(solution)/shard_map/ppermute | solution.py:36
  19.6 46.8 %collective-permute-start.4 = (bf16[2,2048,256]{2,1,0:T(8,128)(2,1)S(1)}, bf16[2,2048,256]{2,1,0:T(8,128)(2,1)}, u32[]{:S(2)}, u32[]{:S(2)}) collective-permute-start(bf16[2,2048,256]{2,1,0:T(8,128)(2,1)S(1)} %bitcast.17), channel_id=1, source_target_pairs={{0,1},{1,0},{2,3},{3,2},{4,5},{5,4},{6,7},{7,6},{8,9},{9,8},{10,11... | collective-permute-start | bytes 6291464 | tf_op jit(solution)/shard_map/ppermute | solution.py:36
  71.1 26.4 %collective-permute-start.7 = (bf16[2,1024,256]{2,1,0:T(8,128)(2,1)}, bf16[2,1024,256]{2,1,0:T(8,128)(2,1)}, u32[]{:S(2)}, u32[]{:S(2)}) collective-permute-start(bf16[2,1024,256]{2,1,0:T(8,128)(2,1)} %slice.52), channel_id=1, source_target_pairs={{0,8},{8,16},{16,24},{24,0},{1,9},{9,17},{17,25},{25,1},{2,10},{10... | collective-permute-start | bytes 3145736 | tf_op jit(solution)/shard_map/ppermute | solution.py:36
  71.2 26.4 %collective-permute-start.8 = (bf16[2,1024,256]{2,1,0:T(8,128)(2,1)}, bf16[2,1024,256]{2,1,0:T(8,128)(2,1)}, u32[]{:S(2)}, u32[]{:S(2)}) collective-permute-start(bf16[2,1024,256]{2,1,0:T(8,128)(2,1)} %slice.53), channel_id=1, source_target_pairs={{0,24},{8,0},{16,8},{24,16},{1,25},{9,1},{17,9},{25,17},{2,26},{10... | collective-permute-start | bytes 3145736 | tf_op jit(solution)/shard_map/ppermute | solution.py:36
  74.4 28.1 %collective-permute-start.5 = (bf16[8,1,272,256]{3,2,1,0:T(8,128)(2,1)}, bf16[8,1,272,256]{3,2,1,0:T(8,128)(2,1)}, u32[]{:S(2)}, u32[]{:S(2)}) collective-permute-start(bf16[8,1,272,256]{3,2,1,0:T(8,128)(2,1)} %get-tuple-element.47), channel_id=1, source_target_pairs={{0,2},{2,4},{4,6},{6,0},{1,3},{3,5},{5,7},{7,1},{8,10},{10,12},{12... | collective-permute-start | bytes 3342344 | tf_op jit(solution)/shard_map/ppermute | solution.py:36
  75.9 26.7 %collective-permute-start.6 = (bf16[8,1,272,256]{3,2,1,0:T(8,128)(2,1)}, bf16[8,1,272,256]{3,2,1,0:T(8,128)(2,1)}, u32[]{:S(2)}, u32[]{:S(2)}) collective-permute-start(bf16[8,1,272,256]{3,2,1,0:T(8,128)(2,1)} %get-tuple-element.48), channel_id=1, source_target_pairs={{0,6},{2,0},{4,2},{6,4},{1,7},{3,1},{5,3},{7,5},{8,14},{10,8},{12,... | collective-permute-start | bytes 3342344 | tf_op jit(solution)/shard_map/ppermute | solution.py:36
  102.5 11.3 %collective-permute-start.10 = (bf16[2,2048,256]{2,1,0:T(8,128)(2,1)}, bf16[2,2048,256]{2,1,0:T(8,128)(2,1)S(1)}, u32[]{:S(2)}, u32[]{:S(2)}) collective-permute-start(bf16[2,2048,256]{2,1,0:T(8,128)(2,1)} %collective-permute-done.3.refs_6_), channel_id=1, source_target_pairs={{0,1},{1,0},{2,3},{3,2},{4,5},{5,4},{6,7},{7,6},{8,9},{9,8},{10,11... | collective-permute-start | bytes 6291464 | tf_op jit(solution)/shard_map/ppermute | solution.py:36
  102.6 11.2 %collective-permute-start.9 = (bf16[2,2048,256]{2,1,0:T(8,128)(2,1)}, bf16[2,2048,256]{2,1,0:T(8,128)(2,1)}, u32[]{:S(2)}, u32[]{:S(2)}) collective-permute-start(bf16[2,2048,256]{2,1,0:T(8,128)(2,1)} %collective-permute-done.2.refs_4_), channel_id=1, source_target_pairs={{0,1},{1,0},{2,3},{3,2},{4,5},{5,4},{6,7},{7,6},{8,9},{9,8},{10,11... | collective-permute-start | bytes 6291464 | tf_op jit(solution)/shard_map/ppermute | solution.py:36
  103.1 51.0 %collective-permute-start.11 = (bf16[8,1,272,256]{3,2,1,0:T(8,128)(2,1)}, bf16[8,1,272,256]{3,2,1,0:T(8,128)(2,1)}, u32[]{:S(2)}, u32[]{:S(2)}) collective-permute-start(bf16[8,1,272,256]{3,2,1,0:T(8,128)(2,1)} %constant_dynamic-slice_fusion), channel_id=1, source_target_pairs={{0,4},{2,6},{4,0},{6,2},{1,5},{3,7},{5,1},{7,3},{8,12},{10,14},{12... | collective-permute-start | bytes 3342344 | tf_op jit(solution)/shard_map/ppermute | solution.py:36
  106.2 47.8 %collective-permute-start.12 = (bf16[2,1024,256]{2,1,0:T(8,128)(2,1)}, bf16[2,1024,256]{2,1,0:T(8,128)(2,1)}, u32[]{:S(2)}, u32[]{:S(2)}) collective-permute-start(bf16[2,1024,256]{2,1,0:T(8,128)(2,1)} %slice.46), channel_id=1, source_target_pairs={{0,2},{2,4},{4,6},{6,0},{1,3},{3,5},{5,7},{7,1},{8,10},{10,12},{12... | collective-permute-start | bytes 3145736 | tf_op jit(solution)/shard_map/ppermute | solution.py:36
  106.7 47.4 %collective-permute-start.13 = (bf16[2,1024,256]{2,1,0:T(8,128)(2,1)}, bf16[2,1024,256]{2,1,0:T(8,128)(2,1)}, u32[]{:S(2)}, u32[]{:S(2)}) collective-permute-start(bf16[2,1024,256]{2,1,0:T(8,128)(2,1)} %slice.47), channel_id=1, source_target_pairs={{0,6},{2,0},{4,2},{6,4},{1,7},{3,1},{5,3},{7,5},{8,14},{10,8},{12,... | collective-permute-start | bytes 3145736 | tf_op jit(solution)/shard_map/ppermute | solution.py:36
  109.4 25.0 %all-to-all-start.1 = ((bf16[8,256,256]{2,1,0:T(8,128)(2,1)}), bf16[8,256,256]{2,1,0:T(8,128)(2,1)}, u32[]{:S(2)}, u32[]{:S(2)}) async-start(bf16[8,256,256]{2,1,0:T(8,128)(2,1)} %combine_0_3_0.1), calls=%async_computation.1 | async-start | bytes 2097152 | tf_op jit(solution)/shard_map/all_to_all | solution.py:32
  113.8 2.2 %copy-start.7 = (bf16[2,2048,256]{2,1,0:T(8,128)(2,1)}, bf16[2,2048,256]{2,1,0:T(8,128)(2,1)S(1)}, u32[]{:S(2)}) copy-start(bf16[2,2048,256]{2,1,0:T(8,128)(2,1)S(1)} %collective-permute-done.10.refs_7_) | copy-start | bytes 6291460
  134.4 35.1 %all-to-all-start.2 = ((bf16[16,256,256]{2,1,0:T(8,128)(2,1)}), bf16[16,256,256]{2,1,0:T(8,128)(2,1)S(1)}, u32[]{:S(2)}, u32[]{:S(2)}) async-start(bf16[16,256,256]{2,1,0:T(8,128)(2,1)} %combine_1_0_0.1), calls=%async_computation.2 | async-start | bytes 4194304 | tf_op jit(solution)/shard_map/all_to_all | solution.py:32
  154.1 4.2 %collective-permute-start.14 = (bf16[2,1024,256]{2,1,0:T(8,128)(2,1)}, bf16[2,1024,256]{2,1,0:T(8,128)(2,1)S(1)}, u32[]{:S(2)}, u32[]{:S(2)}) collective-permute-start(bf16[2,1024,256]{2,1,0:T(8,128)(2,1)} %collective-permute-done.12.refs_2_), channel_id=1, source_target_pairs={{0,1},{1,0},{2,3},{3,2},{4,5},{5,4},{6,7},{7,6},{8,9},{9,8},{10,11... | collective-permute-start | bytes 3145736 | tf_op jit(solution)/shard_map/ppermute | solution.py:36
  154.1 4.5 %collective-permute-start.15 = (bf16[2,1024,256]{2,1,0:T(8,128)(2,1)}, bf16[2,1024,256]{2,1,0:T(8,128)(2,1)}, u32[]{:S(2)}, u32[]{:S(2)}) collective-permute-start(bf16[2,1024,256]{2,1,0:T(8,128)(2,1)} %collective-permute-done.13.refs_3_), channel_id=1, source_target_pairs={{0,1},{1,0},{2,3},{3,2},{4,5},{5,4},{6,7},{7,6},{8,9},{9,8},{10,11... | collective-permute-start | bytes 3145736 | tf_op jit(solution)/shard_map/ppermute | solution.py:36
  158.3 1.0 copy-start.4
  169.5 4.9 %copy-start.1 = (bf16[16,256,256]{2,1,0:T(8,128)(2,1)}, bf16[16,256,256]{2,1,0:T(8,128)(2,1)S(1)}, u32[]{:S(2)}) copy-start(bf16[16,256,256]{2,1,0:T(8,128)(2,1)S(1)} %all-to-all-done.2) | copy-start | bytes 6291460
  169.6 19.7 %all-to-all-start.3 = ((bf16[8,256,256]{2,1,0:T(8,128)(2,1)}), bf16[8,256,256]{2,1,0:T(8,128)(2,1)S(1)}, u32[]{:S(2)}, u32[]{:S(2)}) async-start(bf16[8,256,256]{2,1,0:T(8,128)(2,1)} %combine_3_0_0.1), calls=%async_computation.3 | async-start | bytes 2097152 | tf_op jit(solution)/shard_map/all_to_all | solution.py:32

commit v10 on v9

--- a/solution.py
+++ b/solution.py
@@ -47,6 +47,12 @@
 
 def onward(halves, axis):
     return shift(halves[0], axis, 1), shift(halves[1], axis, 3)
+
+
+def when(condition):
+    if isinstance(condition, bool):
+        return (lambda then: then()) if condition else (lambda then: None)
+    return pl.when(condition)
 
 
 def combine(where, psis, lefts, rights, first, z_first=0, kept=None, cores=(0, 1)):
@@ -61,6 +67,7 @@
     right_parts = [a for group in rights for a in group]
     steps = len(rights)
     last = steps - 1
+    unrolled = count == 1
     size_out = len(cores) * count
     each = [(core, k) for core in cores for k in range(count)]
 
@@ -79,8 +86,6 @@
         (out_ref, psi_buf, left_buf, right_buf, partial, out_buf, psi_sems, left_sems, sems, out_sems) = refs[
             kept is not None :
         ]
-        step = pl.program_id(0)
-
         def copy_lefts(needed, go):
             for core, k in each:
                 at = core - cores[0]
@@ -126,54 +131,58 @@
                 out_buf.at[n_step], out_ref.at[pl.ds(to, size_out)], out_sems.at[n_step]
             )
 
-        @pl.when(step == 0)
-        def _():
-            copy_lefts(True, True)
-            fetch(0, True)
+        def run(step):
+            @when(step == 0)
+            def _():
+                copy_lefts(True, True)
+                fetch(0, True)
+                if steps > 1:
+                    copy_lefts(False, True)
+                for n_step in range(1, steps):
+                    fetch(n_step, True)
+                copy_lefts(True, False)
+
             if steps > 1:
-                copy_lefts(False, True)
-            for n_step in range(1, steps):
-                fetch(n_step, True)
-            copy_lefts(True, False)
-
-        if steps > 1:
-
-            @pl.when(step == 1)
+
+                @when(step == 1)
+                def _():
+                    copy_lefts(False, False)
+
+            for n_step in range(steps):
+
+                @when(step == n_step)
+                def _(n_step=n_step):
+                    fetch(n_step, False)
+
+            for n_block, (core, k) in enumerate(each):
+                left = pick_of(step, core, k, 0, where, codes)
+                block = psi_buf[step, k, where[8] ^ core]
+                for t in range(terms):
+                    product = jnp.dot(
+                        left_buf[k, core - cores[0], left, t * width : (t + 1) * width],
+                        block,
+                        preferred_element_type=jnp.float32,
+                    )
+                    partial[n_block, :, t * width : (t + 1) * width] = product.astype(BF16)
+            for n_block, (core, k) in enumerate(each):
+                total = jnp.dot(
+                    partial[n_block], right_buf[step, n_block], preferred_element_type=jnp.float32
+                )
+                row = (where[8] ^ core) * count if len(cores) > 1 else 0
+                out_buf[step, row + k] = total.astype(BF16)
+            for n_step in range(steps):
+
+                @when(step == n_step)
+                def _(n_step=n_step):
+                    leave(n_step).start()
+
+            @when(step == last)
             def _():
-                copy_lefts(False, False)
-
-        for n_step in range(steps):
-
-            @pl.when(step == n_step)
-            def _(n_step=n_step):
-                fetch(n_step, False)
-
-        for n_block, (core, k) in enumerate(each):
-            left = pick_of(step, core, k, 0, where, codes)
-            block = psi_buf[step, k, where[8] ^ core]
-            for t in range(terms):
-                product = jnp.dot(
-                    left_buf[k, core - cores[0], left, t * width : (t + 1) * width],
-                    block,
-                    preferred_element_type=jnp.float32,
-                )
-                partial[n_block, :, t * width : (t + 1) * width] = product.astype(BF16)
-        for n_block, (core, k) in enumerate(each):
-            total = jnp.dot(
-                partial[n_block], right_buf[step, n_block], preferred_element_type=jnp.float32
-            )
-            row = (where[8] ^ core) * count if len(cores) > 1 else 0
-            out_buf[step, row + k] = total.astype(BF16)
-        for n_step in range(steps):
-
-            @pl.when(step == n_step)
-            def _(n_step=n_step):
-                leave(n_step).start()
-
-        @pl.when(step == last)
-        def _():
-            for n_step in range(steps):
-                leave(n_step).wait()
+                for n_step in range(steps):
+                    leave(n_step).wait()
+
+        for step in range(steps) if unrolled else [pl.program_id(0)]:
+            run(step)
 
     in_place = pl.BlockSpec(memory_space=pl.ANY)
     parts = max(len(group) for group in rights)
@@ -184,7 +193,7 @@
         out_shape=jax.ShapeDtypeStruct((8 * count, width, width), BF16),
         grid_spec=pltpu.PrefetchScalarGridSpec(
             num_scalar_prefetch=1 + count,
-            grid=(steps,),
+            grid=(1 if unrolled else steps,),
             in_specs=[in_place] * len(operands),
             out_specs=in_place,
             scratch_shapes=[

time: 191 us -> 191 us (level)
  no operation moved by 1% of the time
where the time goes in v10:
time: 191 us; the launch traced here: 190 us
  waiting for transfers between devices  71.1 us (37%)
  Pallas kernels  50.7 us (27%)
  starting transfers between devices  39.2 us (21%)
  local copies, waits for them, and re-layouts  20.9 us (11%)
  other arithmetic  5.51 us (3%)
  between operations  2.81 us (1%)
    ppermute x16, waiting for transfers between devices, shift(): lax.ppermute(array, axis, [(i, (i + step) % size) for i in range(size)])  61.2 us
    pallas_call x4, Pallas kernels, combine(): pl.pallas_call(kernel, out_shape=jax.ShapeDtypeStruct((8 * count, width,...  41.3 us
    ppermute x16, starting transfers between devices, shift(): lax.ppermute(array, axis, [(i, (i + step) % size) for i in range(size)])  21.3 us
    all_to_all x4, starting transfers between devices, exchange(): return lax.all_to_all(array, axis, split_axis=0, concat_axis=0, tiled=True)  17.9 us
    all_to_all x4, waiting for transfers between devices, exchange(): return lax.all_to_all(array, axis, split_axis=0, concat_axis=0, tiled=True)  9.83 us
    slice x4, local copies, waits for them, and re-layouts, halves_of(): return (from_low[:, :half], from_high[:, half:])  9.11 us
    dynamic_slice x2, local copies, waits for them, and re-layouts, column(): return lax.dynamic_slice(psi, start, (8, 1) + psi.shape[2:])  5.52 us
    pallas_call x1, Pallas kernels, assemble(): pl.pallas_call(kernel, out_shape=jax.ShapeDtypeStruct((4, 4, 2, width, wi...  5.04 us
  transfers between devices with their start and end apart: 20, of which 7 were waited for; matrix products, arithmetic and copies ran while one was open for 10% of the time, Pallas kernels for 24%

profile of v10, /device:TPU:0, one launch (start us, length us, event | category | flops | bytes accessed | tf_op | source)
XLA Modules:
  0.0 190.2 jit_solution(8527017259209468312)
XLA Ops:
  0.0 4.3 %pack.1 = bf16[8,4,272,256]{3,2,1,0:T(8,128)(2,1)} custom-call(s32[32]{0:T(128)} %left.1, s32[32]{0:T(128)} %right.1, bf16[4,4,2,256,256]{4,3,2,1,0:T(8,128)(2,1)} %bitcast.22), custom_call_target="tpu_custom_call" | custom-call | flops 1 | bytes 1 | tf_op jit(solution)/shard_map/pack/pallas_call | solution.py:273
  4.4 4.7 %all-to-all-start = ((bf16[8,4,272,256]{3,2,1,0:T(8,128)(2,1)}), bf16[8,4,272,256]{3,2,1,0:T(8,128)(2,1)}, u32[]{:S(2)}, u32[]{:S(2)}) async-start(bf16[8,4,272,256]{3,2,1,0:T(8,128)(2,1)} %pack.1), calls=%async_computation | async-start | bytes 8912896 | tf_op jit(solution)/shard_map/all_to_all | solution.py:32
  9.1 2.1 %fusion = bf16[2,8,256,256]{3,2,1,0:T(8,128)(2,1)} fusion(bf16[2,8,256,256]{3,2,1,0:T(8,128)(2,1)S(1)} %copy-done.2, s32[2]{0:T(128)S(1)} %copy-done.5), kind=kLoop, calls=%fused_computation.2 | loop fusion | flops 2097152 | bytes 4194312 | tf_op jit(solution)/shard_map/jit(_where)/select_n | solution.py:313
  11.3 2.0 %collective-permute-start = (bf16[2,2048,256]{2,1,0:T(8,128)(2,1)}, bf16[2,2048,256]{2,1,0:T(8,128)(2,1)}, u32[]{:S(2)}, u32[]{:S(2)}) collective-permute-start(bf16[2,2048,256]{2,1,0:T(8,128)(2,1)} %bitcast.2.refs_4_.refs_8_.refs_6_), channel_id=1, source_target_pairs={{0,8},{8,16},{16,24},{24,0},{1,9},{9,17},{17,25},{25,1},{2,10},{10... | collective-permute-start | bytes 6291464 | tf_op jit(solution)/shard_map/ppermute | solution.py:36
  13.3 2.1 %collective-permute-start.1 = (bf16[2,2048,256]{2,1,0:T(8,128)(2,1)}, bf16[2,2048,256]{2,1,0:T(8,128)(2,1)}, u32[]{:S(2)}, u32[]{:S(2)}) collective-permute-start(bf16[2,2048,256]{2,1,0:T(8,128)(2,1)} %bitcast.2.refs_4_.refs_8_.refs_6_), channel_id=1, source_target_pairs={{0,24},{8,0},{16,8},{24,16},{1,25},{9,1},{17,9},{25,17},{2,26},{10... | collective-permute-start | bytes 6291464 | tf_op jit(solution)/shard_map/ppermute | solution.py:36
  15.4 0.9 fusion.1
  16.3 1.6 collective-permute-start.2
  17.9 1.7 collective-permute-start.3
  19.6 1.2 constant_dynamic-slice_fusion.3
  20.8 0.7 fusion.3
  23.5 38.4 %collective-permute-done.refs_5_.refs_9_.refs_7_ = bf16[2,2048,256]{2,1,0:T(8,128)(2,1)} collective-permute-done((bf16[2,2048,256]{2,1,0:T(8,128)(2,1)}, bf16[2,2048,256]{2,1,0:T(8,128)(2,1)}, u32[]{:S(2)}, u32[]{:S(2)}) %collective-permute-start) | collective-permute-done | bytes 2097184 | tf_op jit(solution)/shard_map/ppermute | solution.py:36
  61.9 2.3 %slice.52 = bf16[2,1024,256]{2,1,0:T(8,128)(2,1)} slice(bf16[2,2048,256]{2,1,0:T(8,128)(2,1)} %collective-permute-done.refs_5_.refs_9_.refs_7_), slice={[0:2], [0:1024], [0:256]} | slice | bytes 2097152 | tf_op jit(solution)/shard_map/slice | solution.py:45
  64.1 2.3 %slice.53 = bf16[2,1024,256]{2,1,0:T(8,128)(2,1)} slice(bf16[2,2048,256]{2,1,0:T(8,128)(2,1)} %collective-permute-done.1.refs_6_.refs_10_.refs_8_), slice={[0:2], [1024:2048], [0:256]} | slice | bytes 2097152 | tf_op jit(solution)/shard_map/slice | solution.py:45
  66.4 3.2 %constant_dynamic-slice_fusion.1 = (bf16[8,1,272,256]{3,2,1,0:T(8,128)(2,1)}, bf16[8,1,272,256]{3,2,1,0:T(8,128)(2,1)}) fusion(bf16[8,4,272,256]{3,2,1,0:T(8,128)(2,1)} %all-to-all-done.refs_1_, u32[]{:T(128)} %bitcast.5, u32[]{:T(128)} %bitcast.4), kind=kLoop, calls=%fused_computation.10 | loop fusion | bytes 4456456 | tf_op jit(solution)/shard_map/dynamic_slice | solution.py:296
  69.6 0.9 convert_reduce_fusion
  70.5 0.7 reshape.74.refs_0_
  71.2 3.2 %collective-permute-start.8 = (bf16[2,1024,256]{2,1,0:T(8,128)(2,1)}, bf16[2,1024,256]{2,1,0:T(8,128)(2,1)}, u32[]{:S(2)}, u32[]{:S(2)}) collective-permute-start(bf16[2,1024,256]{2,1,0:T(8,128)(2,1)} %slice.53), channel_id=1, source_target_pairs={{0,24},{8,0},{16,8},{24,16},{1,25},{9,1},{17,9},{25,17},{2,26},{10... | collective-permute-start | bytes 3145736 | tf_op jit(solution)/shard_map/ppermute | solution.py:36
  74.4 1.5 collective-permute-start.5
  75.9 1.7 collective-permute-start.6
  77.6 7.9 %combine_0_0_0.1.refs_6_ = bf16[8,256,256]{2,1,0:T(8,128)(2,1)} custom-call(s32[13]{0:T(128)} %get-tuple-element.72.where, s32[64]{0:T(128)} %reshape.74.refs_0_, bf16[8,4,272,256]{3,2,1,0:T(8,128)(2,1)} %all-to-all-done.refs_1_, bf16[2,2048,256]{2,1,0:T(8,128)(2,1)} %bitcast.18, bf16[2,2048,256]{2,1,0:T(8,128)(2,1)} %collective-permute-done.4.refs_3_, ...), custom_call_target="tpu_custom_call" | custom-call | flops 999999995904 | bytes 1 | tf_op jit(solution)/shard_map/combine_0_0_0/pallas_call | solution.py:191
  85.5 2.3 %slice.46 = bf16[2,1024,256]{2,1,0:T(8,128)(2,1)} slice(bf16[2,2048,256]{2,1,0:T(8,128)(2,1)} %collective-permute-done.2.refs_4_), slice={[0:2], [0:1024], [0:256]} | slice | bytes 2097152 | tf_op jit(solution)/shard_map/slice | solution.py:45
  87.8 2.2 %slice.47 = bf16[2,1024,256]{2,1,0:T(8,128)(2,1)} slice(bf16[2,2048,256]{2,1,0:T(8,128)(2,1)} %collective-permute-done.3.refs_6_), slice={[0:2], [1024:2048], [0:256]} | slice | bytes 2097152 | tf_op jit(solution)/shard_map/slice | solution.py:45
  90.1 2.4 %constant_dynamic-slice_fusion = bf16[8,1,272,256]{3,2,1,0:T(8,128)(2,1)} fusion(bf16[8,4,272,256]{3,2,1,0:T(8,128)(2,1)} %all-to-all-done.refs_1_, u32[]{:T(128)} %bitcast.6), kind=kLoop, calls=%fused_computation.9 | loop fusion | bytes 2228228 | tf_op jit(solution)/shard_map/dynamic_slice | solution.py:296
  92.4 5.1 %collective-permute-done.7.refs_4_.refs_11_.refs_9_ = bf16[2,1024,256]{2,1,0:T(8,128)(2,1)} collective-permute-done((bf16[2,1024,256]{2,1,0:T(8,128)(2,1)}, bf16[2,1024,256]{2,1,0:T(8,128)(2,1)}, u32[]{:S(2)}, u32[]{:S(2)}) %collective-permute-start.7) | collective-permute-done | bytes 1048608 | tf_op jit(solution)/shard_map/ppermute | solution.py:36
  97.5 5.0 %combine_0_3_0.1 = bf16[8,256,256]{2,1,0:T(8,128)(2,1)} custom-call(s32[13]{0:T(128)} %get-tuple-element.72.where, s32[64]{0:T(128)} %reshape.74.refs_0_, bf16[8,4,272,256]{3,2,1,0:T(8,128)(2,1)} %all-to-all-done.refs_1_, bf16[2,2048,256]{2,1,0:T(8,128)(2,1)} %bitcast.19, ...), custom_call_target="tpu_custom_call", output_to_operand_aliasing={{}: (7, {})} | custom-call | flops 1 | bytes 1 | tf_op jit(solution)/shard_map/combine_0_3_0/pallas_call | solution.py:191
  102.6 0.5 collective-permute-start.9
  103.1 3.0 %collective-permute-start.11 = (bf16[8,1,272,256]{3,2,1,0:T(8,128)(2,1)}, bf16[8,1,272,256]{3,2,1,0:T(8,128)(2,1)}, u32[]{:S(2)}, u32[]{:S(2)}) collective-permute-start(bf16[8,1,272,256]{3,2,1,0:T(8,128)(2,1)} %constant_dynamic-slice_fusion), channel_id=1, source_target_pairs={{0,4},{2,6},{4,0},{6,2},{1,5},{3,7},{5,1},{7,3},{8,12},{10,14},{12... | collective-permute-start | bytes 3342344 | tf_op jit(solution)/shard_map/ppermute | solution.py:36
  106.2 0.6 collective-permute-start.12
  106.7 2.6 %collective-permute-start.13 = (bf16[2,1024,256]{2,1,0:T(8,128)(2,1)}, bf16[2,1024,256]{2,1,0:T(8,128)(2,1)}, u32[]{:S(2)}, u32[]{:S(2)}) collective-permute-start(bf16[2,1024,256]{2,1,0:T(8,128)(2,1)} %slice.47), channel_id=1, source_target_pairs={{0,6},{2,0},{4,2},{6,4},{1,7},{3,1},{5,3},{7,5},{8,14},{10,8},{12,... | collective-permute-start | bytes 3145736 | tf_op jit(solution)/shard_map/ppermute | solution.py:36
  109.4 4.4 %all-to-all-start.1 = ((bf16[8,256,256]{2,1,0:T(8,128)(2,1)}), bf16[8,256,256]{2,1,0:T(8,128)(2,1)}, u32[]{:S(2)}, u32[]{:S(2)}) async-start(bf16[8,256,256]{2,1,0:T(8,128)(2,1)} %combine_0_3_0.1), calls=%async_computation.1 | async-start | bytes 2097152 | tf_op jit(solution)/shard_map/all_to_all | solution.py:32
  113.9 0.9 convert_reduce_fusion.2
  114.7 0.7 reshape.75.refs_0_
  115.4 0.7 reshape.76.refs_1_
  116.1 18.2 %combine_1_0_0.1 = bf16[16,256,256]{2,1,0:T(8,128)(2,1)} custom-call(s32[13]{0:T(128)} %get-tuple-element.72.where, s32[16]{0:T(128)} %reshape.75.refs_0_, s32[16]{0:T(128)} %reshape.76.refs_1_, bf16[8,1,272,256]{3,2,1,0:T(8,128)(2,1)} %collective-permute-done.5.refs_2_, bf16[8,1,272,256]{3,2,1,0:T(8,128)(2,1)} %collective-permute-done.6.refs_3_, ...), custom_call_target="tpu_custom_call" | custom-call | flops 999999995904 | bytes 1 | tf_op jit(solution)/shard_map/combine_1_0_0/pallas_call | solution.py:191
  134.3 4.7 %all-to-all-start.2 = ((bf16[16,256,256]{2,1,0:T(8,128)(2,1)}), bf16[16,256,256]{2,1,0:T(8,128)(2,1)S(1)}, u32[]{:S(2)}, u32[]{:S(2)}) async-start(bf16[16,256,256]{2,1,0:T(8,128)(2,1)} %combine_1_0_0.1), calls=%async_computation.2 | async-start | bytes 4194304 | tf_op jit(solution)/shard_map/all_to_all | solution.py:32
  139.0 15.0 %collective-permute-done.12.refs_2_ = bf16[2,1024,256]{2,1,0:T(8,128)(2,1)} collective-permute-done((bf16[2,1024,256]{2,1,0:T(8,128)(2,1)}, bf16[2,1024,256]{2,1,0:T(8,128)(2,1)}, u32[]{:S(2)}, u32[]{:S(2)}) %collective-permute-start.12) | collective-permute-done | bytes 1048608 | tf_op jit(solution)/shard_map/ppermute | solution.py:36
  154.0 0.1 collective-permute-done.13.refs_3_
  154.1 0.5 collective-permute-start.15
  154.6 0.7 convert_reduce_fusion.1
  155.4 0.7 reshape.77.refs_0_
  156.0 2.3 %collective-permute-done.14.refs_4_ = bf16[2,1024,256]{2,1,0:T(8,128)(2,1)S(1)} collective-permute-done((bf16[2,1024,256]{2,1,0:T(8,128)(2,1)}, bf16[2,1024,256]{2,1,0:T(8,128)(2,1)S(1)}, u32[]{:S(2)}, u32[]{:S(2)}) %collective-permute-start.14) | collective-permute-done | bytes 1048608 | tf_op jit(solution)/shard_map/ppermute | solution.py:36
  158.3 0.3 collective-permute-done.15.refs_5_
  158.6 0.7 copy-done.4
  159.3 10.3 %combine_3_0_0.1 = bf16[8,256,256]{2,1,0:T(8,128)(2,1)} custom-call(s32[13]{0:T(128)} %get-tuple-element.72.where, s32[16]{0:T(128)} %reshape.77.refs_0_, bf16[8,1,272,256]{3,2,1,0:T(8,128)(2,1)} %collective-permute-done.11.refs_1_, bf16[2,1024,256]{2,1,0:T(8,128)(2,1)} %collective-permute-done.12.refs_2_, ...), custom_call_target="tpu_custom_call" | custom-call | flops 1 | bytes 1 | tf_op jit(solution)/shard_map/combine_3_0_0/pallas_call | solution.py:191
  169.6 4.1 %all-to-all-start.3 = ((bf16[8,256,256]{2,1,0:T(8,128)(2,1)}), bf16[8,256,256]{2,1,0:T(8,128)(2,1)S(1)}, u32[]{:S(2)}, u32[]{:S(2)}) async-start(bf16[8,256,256]{2,1,0:T(8,128)(2,1)} %combine_3_0_0.1), calls=%async_computation.3 | async-start | bytes 2097152 | tf_op jit(solution)/shard_map/all_to_all | solution.py:32
  174.3 5.0 %assemble.1 = bf16[4,4,2,256,256]{4,3,2,1,0:T(8,128)(2,1)} custom-call(s32[13]{0:T(128)} %get-tuple-element.72.where, bf16[4,2,1,256,256]{4,3,2,1,0:T(8,128)(2,1)} %bitcast.7.refs_0_, bf16[4,2,2,256,256]{4,3,2,1,0:T(8,128)(2,1)} %bitcast.20), custom_call_target="tpu_custom_call" | custom-call | flops 1 | bytes 1 | tf_op jit(solution)/shard_map/assemble/pallas_call | solution.py:231
  179.4 9.8 %all-to-all-done.3 = bf16[8,256,256]{2,1,0:T(8,128)(2,1)S(1)} async-done(((bf16[8,256,256]{2,1,0:T(8,128)(2,1)}), bf16[8,256,256]{2,1,0:T(8,128)(2,1)S(1)}, u32[]{:S(2)}, u32[]{:S(2)}) %all-to-all-start.3) | async-done | bytes 1048608 | tf_op jit(solution)/shard_map/all_to_all | solution.py:32
  189.2 1.0 constant_dynamic-update-slice_fusion
  (32 shorter events, 0.2 us)
Async XLA Ops:
  4.3 4.8 %copy-start.2 = (bf16[2,8,256,256]{3,2,1,0:T(8,128)(2,1)S(1)}, bf16[2,8,256,256]{3,2,1,0:T(8,128)(2,1)}, u32[]{:S(2)}) copy-start(bf16[2,8,256,256]{3,2,1,0:T(8,128)(2,1)} %param.13) | copy-start | bytes 6291460
  4.3 4.8 %copy-start.5 = (s32[2]{0:T(128)S(1)}, s32[2]{0:T(128)}, u32[]{:S(2)}) copy-start(s32[2]{0:T(128)} %param.14) | copy-start | bytes 28
  4.4 62.1 %all-to-all-start = ((bf16[8,4,272,256]{3,2,1,0:T(8,128)(2,1)}), bf16[8,4,272,256]{3,2,1,0:T(8,128)(2,1)}, u32[]{:S(2)}, u32[]{:S(2)}) async-start(bf16[8,4,272,256]{3,2,1,0:T(8,128)(2,1)} %pack.1), calls=%async_computation | async-start | bytes 8912896 | tf_op jit(solution)/shard_map/all_to_all | solution.py:32
  9.1 6.3 %copy-start.3 = (bf16[2,8,256,256]{3,2,1,0:T(8,128)(2,1)S(1)}, bf16[2,8,256,256]{3,2,1,0:T(8,128)(2,1)}, u32[]{:S(2)}) copy-start(bf16[2,8,256,256]{3,2,1,0:T(8,128)(2,1)} %param.11) | copy-start | bytes 6291460
  9.1 6.3 %copy-start.6 = (s32[2]{0:T(128)S(1)}, s32[2]{0:T(128)}, u32[]{:S(2)}) copy-start(s32[2]{0:T(128)} %param.12) | copy-start | bytes 28
  11.3 50.6 %collective-permute-start = (bf16[2,2048,256]{2,1,0:T(8,128)(2,1)}, bf16[2,2048,256]{2,1,0:T(8,128)(2,1)}, u32[]{:S(2)}, u32[]{:S(2)}) collective-permute-start(bf16[2,2048,256]{2,1,0:T(8,128)(2,1)} %bitcast.2.refs_4_.refs_8_.refs_6_), channel_id=1, source_target_pairs={{0,8},{8,16},{16,24},{24,0},{1,9},{9,17},{17,25},{25,1},{2,10},{10... | collective-permute-start | bytes 6291464 | tf_op jit(solution)/shard_map/ppermute | solution.py:36
  13.3 50.8 %collective-permute-start.1 = (bf16[2,2048,256]{2,1,0:T(8,128)(2,1)}, bf16[2,2048,256]{2,1,0:T(8,128)(2,1)}, u32[]{:S(2)}, u32[]{:S(2)}) collective-permute-start(bf16[2,2048,256]{2,1,0:T(8,128)(2,1)} %bitcast.2.refs_4_.refs_8_.refs_6_), channel_id=1, source_target_pairs={{0,24},{8,0},{16,8},{24,16},{1,25},{9,1},{17,9},{25,17},{2,26},{10... | collective-permute-start | bytes 6291464 | tf_op jit(solution)/shard_map/ppermute | solution.py:36
  16.3 50.1 %copy-start = (bf16[2,8,256,256]{3,2,1,0:T(8,128)(2,1)}, bf16[2,8,256,256]{3,2,1,0:T(8,128)(2,1)S(1)}, u32[]{:S(2)}) copy-start(bf16[2,8,256,256]{3,2,1,0:T(8,128)(2,1)S(1)} %fusion.1) | copy-start | bytes 6291460
  16.3 50.1 %collective-permute-start.2 = (bf16[2,2048,256]{2,1,0:T(8,128)(2,1)S(1)}, bf16[2,2048,256]{2,1,0:T(8,128)(2,1)}, u32[]{:S(2)}, u32[]{:S(2)}) collective-permute-start(bf16[2,2048,256]{2,1,0:T(8,128)(2,1)S(1)} %bitcast.15), channel_id=1, source_target_pairs={{0,2},{2,4},{4,6},{6,0},{1,3},{3,5},{5,7},{7,1},{8,10},{10,12},{12... | collective-permute-start | bytes 6291464 | tf_op jit(solution)/shard_map/ppermute | solution.py:36
  17.9 48.5 %collective-permute-start.3 = (bf16[2,2048,256]{2,1,0:T(8,128)(2,1)S(1)}, bf16[2,2048,256]{2,1,0:T(8,128)(2,1)}, u32[]{:S(2)}, u32[]{:S(2)}) collective-permute-start(bf16[2,2048,256]{2,1,0:T(8,128)(2,1)S(1)} %bitcast.16), channel_id=1, source_target_pairs={{0,6},{2,0},{4,2},{6,4},{1,7},{3,1},{5,3},{7,5},{8,14},{10,8},{12,... | collective-permute-start | bytes 6291464 | tf_op jit(solution)/shard_map/ppermute | solution.py:36
  19.6 46.8 %collective-permute-start.4 = (bf16[2,2048,256]{2,1,0:T(8,128)(2,1)S(1)}, bf16[2,2048,256]{2,1,0:T(8,128)(2,1)}, u32[]{:S(2)}, u32[]{:S(2)}) collective-permute-start(bf16[2,2048,256]{2,1,0:T(8,128)(2,1)S(1)} %bitcast.17), channel_id=1, source_target_pairs={{0,1},{1,0},{2,3},{3,2},{4,5},{5,4},{6,7},{7,6},{8,9},{9,8},{10,11... | collective-permute-start | bytes 6291464 | tf_op jit(solution)/shard_map/ppermute | solution.py:36
  71.1 26.4 %collective-permute-start.7 = (bf16[2,1024,256]{2,1,0:T(8,128)(2,1)}, bf16[2,1024,256]{2,1,0:T(8,128)(2,1)}, u32[]{:S(2)}, u32[]{:S(2)}) collective-permute-start(bf16[2,1024,256]{2,1,0:T(8,128)(2,1)} %slice.52), channel_id=1, source_target_pairs={{0,8},{8,16},{16,24},{24,0},{1,9},{9,17},{17,25},{25,1},{2,10},{10... | collective-permute-start | bytes 3145736 | tf_op jit(solution)/shard_map/ppermute | solution.py:36
  71.2 26.4 %collective-permute-start.8 = (bf16[2,1024,256]{2,1,0:T(8,128)(2,1)}, bf16[2,1024,256]{2,1,0:T(8,128)(2,1)}, u32[]{:S(2)}, u32[]{:S(2)}) collective-permute-start(bf16[2,1024,256]{2,1,0:T(8,128)(2,1)} %slice.53), channel_id=1, source_target_pairs={{0,24},{8,0},{16,8},{24,16},{1,25},{9,1},{17,9},{25,17},{2,26},{10... | collective-permute-start | bytes 3145736 | tf_op jit(solution)/shard_map/ppermute | solution.py:36
  74.4 28.1 %collective-permute-start.5 = (bf16[8,1,272,256]{3,2,1,0:T(8,128)(2,1)}, bf16[8,1,272,256]{3,2,1,0:T(8,128)(2,1)}, u32[]{:S(2)}, u32[]{:S(2)}) collective-permute-start(bf16[8,1,272,256]{3,2,1,0:T(8,128)(2,1)} %get-tuple-element.47), channel_id=1, source_target_pairs={{0,2},{2,4},{4,6},{6,0},{1,3},{3,5},{5,7},{7,1},{8,10},{10,12},{12... | collective-permute-start | bytes 3342344 | tf_op jit(solution)/shard_map/ppermute | solution.py:36
  75.9 26.7 %collective-permute-start.6 = (bf16[8,1,272,256]{3,2,1,0:T(8,128)(2,1)}, bf16[8,1,272,256]{3,2,1,0:T(8,128)(2,1)}, u32[]{:S(2)}, u32[]{:S(2)}) collective-permute-start(bf16[8,1,272,256]{3,2,1,0:T(8,128)(2,1)} %get-tuple-element.48), channel_id=1, source_target_pairs={{0,6},{2,0},{4,2},{6,4},{1,7},{3,1},{5,3},{7,5},{8,14},{10,8},{12,... | collective-permute-start | bytes 3342344 | tf_op jit(solution)/shard_map/ppermute | solution.py:36
  102.5 11.3 %collective-permute-start.10 = (bf16[2,2048,256]{2,1,0:T(8,128)(2,1)}, bf16[2,2048,256]{2,1,0:T(8,128)(2,1)S(1)}, u32[]{:S(2)}, u32[]{:S(2)}) collective-permute-start(bf16[2,2048,256]{2,1,0:T(8,128)(2,1)} %collective-permute-done.3.refs_6_), channel_id=1, source_target_pairs={{0,1},{1,0},{2,3},{3,2},{4,5},{5,4},{6,7},{7,6},{8,9},{9,8},{10,11... | collective-permute-start | bytes 6291464 | tf_op jit(solution)/shard_map/ppermute | solution.py:36
  102.6 11.2 %collective-permute-start.9 = (bf16[2,2048,256]{2,1,0:T(8,128)(2,1)}, bf16[2,2048,256]{2,1,0:T(8,128)(2,1)}, u32[]{:S(2)}, u32[]{:S(2)}) collective-permute-start(bf16[2,2048,256]{2,1,0:T(8,128)(2,1)} %collective-permute-done.2.refs_4_), channel_id=1, source_target_pairs={{0,1},{1,0},{2,3},{3,2},{4,5},{5,4},{6,7},{7,6},{8,9},{9,8},{10,11... | collective-permute-start | bytes 6291464 | tf_op jit(solution)/shard_map/ppermute | solution.py:36
  103.1 51.0 %collective-permute-start.11 = (bf16[8,1,272,256]{3,2,1,0:T(8,128)(2,1)}, bf16[8,1,272,256]{3,2,1,0:T(8,128)(2,1)}, u32[]{:S(2)}, u32[]{:S(2)}) collective-permute-start(bf16[8,1,272,256]{3,2,1,0:T(8,128)(2,1)} %constant_dynamic-slice_fusion), channel_id=1, source_target_pairs={{0,4},{2,6},{4,0},{6,2},{1,5},{3,7},{5,1},{7,3},{8,12},{10,14},{12... | collective-permute-start | bytes 3342344 | tf_op jit(solution)/shard_map/ppermute | solution.py:36
  106.2 47.8 %collective-permute-start.12 = (bf16[2,1024,256]{2,1,0:T(8,128)(2,1)}, bf16[2,1024,256]{2,1,0:T(8,128)(2,1)}, u32[]{:S(2)}, u32[]{:S(2)}) collective-permute-start(bf16[2,1024,256]{2,1,0:T(8,128)(2,1)} %slice.46), channel_id=1, source_target_pairs={{0,2},{2,4},{4,6},{6,0},{1,3},{3,5},{5,7},{7,1},{8,10},{10,12},{12... | collective-permute-start | bytes 3145736 | tf_op jit(solution)/shard_map/ppermute | solution.py:36
  106.7 47.4 %collective-permute-start.13 = (bf16[2,1024,256]{2,1,0:T(8,128)(2,1)}, bf16[2,1024,256]{2,1,0:T(8,128)(2,1)}, u32[]{:S(2)}, u32[]{:S(2)}) collective-permute-start(bf16[2,1024,256]{2,1,0:T(8,128)(2,1)} %slice.47), channel_id=1, source_target_pairs={{0,6},{2,0},{4,2},{6,4},{1,7},{3,1},{5,3},{7,5},{8,14},{10,8},{12,... | collective-permute-start | bytes 3145736 | tf_op jit(solution)/shard_map/ppermute | solution.py:36
  109.4 24.9 %all-to-all-start.1 = ((bf16[8,256,256]{2,1,0:T(8,128)(2,1)}), bf16[8,256,256]{2,1,0:T(8,128)(2,1)}, u32[]{:S(2)}, u32[]{:S(2)}) async-start(bf16[8,256,256]{2,1,0:T(8,128)(2,1)} %combine_0_3_0.1), calls=%async_computation.1 | async-start | bytes 2097152 | tf_op jit(solution)/shard_map/all_to_all | solution.py:32
  113.8 2.2 %copy-start.7 = (bf16[2,2048,256]{2,1,0:T(8,128)(2,1)}, bf16[2,2048,256]{2,1,0:T(8,128)(2,1)S(1)}, u32[]{:S(2)}) copy-start(bf16[2,2048,256]{2,1,0:T(8,128)(2,1)S(1)} %collective-permute-done.10.refs_7_) | copy-start | bytes 6291460
  134.3 35.3 %all-to-all-start.2 = ((bf16[16,256,256]{2,1,0:T(8,128)(2,1)}), bf16[16,256,256]{2,1,0:T(8,128)(2,1)S(1)}, u32[]{:S(2)}, u32[]{:S(2)}) async-start(bf16[16,256,256]{2,1,0:T(8,128)(2,1)} %combine_1_0_0.1), calls=%async_computation.2 | async-start | bytes 4194304 | tf_op jit(solution)/shard_map/all_to_all | solution.py:32
  154.1 4.2 %collective-permute-start.14 = (bf16[2,1024,256]{2,1,0:T(8,128)(2,1)}, bf16[2,1024,256]{2,1,0:T(8,128)(2,1)S(1)}, u32[]{:S(2)}, u32[]{:S(2)}) collective-permute-start(bf16[2,1024,256]{2,1,0:T(8,128)(2,1)} %collective-permute-done.12.refs_2_), channel_id=1, source_target_pairs={{0,1},{1,0},{2,3},{3,2},{4,5},{5,4},{6,7},{7,6},{8,9},{9,8},{10,11... | collective-permute-start | bytes 3145736 | tf_op jit(solution)/shard_map/ppermute | solution.py:36
  154.1 4.5 %collective-permute-start.15 = (bf16[2,1024,256]{2,1,0:T(8,128)(2,1)}, bf16[2,1024,256]{2,1,0:T(8,128)(2,1)}, u32[]{:S(2)}, u32[]{:S(2)}) collective-permute-start(bf16[2,1024,256]{2,1,0:T(8,128)(2,1)} %collective-permute-done.13.refs_3_), channel_id=1, source_target_pairs={{0,1},{1,0},{2,3},{3,2},{4,5},{5,4},{6,7},{7,6},{8,9},{9,8},{10,11... | collective-permute-start | bytes 3145736 | tf_op jit(solution)/shard_map/ppermute | solution.py:36
  158.3 1.0 copy-start.4
  169.6 4.7 %copy-start.1 = (bf16[16,256,256]{2,1,0:T(8,128)(2,1)}, bf16[16,256,256]{2,1,0:T(8,128)(2,1)S(1)}, u32[]{:S(2)}) copy-start(bf16[16,256,256]{2,1,0:T(8,128)(2,1)S(1)} %all-to-all-done.2) | copy-start | bytes 6291460
  169.6 19.6 %all-to-all-start.3 = ((bf16[8,256,256]{2,1,0:T(8,128)(2,1)}), bf16[8,256,256]{2,1,0:T(8,128)(2,1)S(1)}, u32[]{:S(2)}, u32[]{:S(2)}) async-start(bf16[8,256,256]{2,1,0:T(8,128)(2,1)} %combine_3_0_0.1), calls=%async_computation.3 | async-start | bytes 2097152 | tf_op jit(solution)/shard_map/all_to_all | solution.py:32

commit v11 on v9

--- a/solution.py
+++ b/solution.py
@@ -13,7 +13,7 @@
 BF16 = jnp.bfloat16
 BRIEF = pl.CostEstimate(flops=1, bytes_accessed=1, transcendentals=0)
 LONG = pl.CostEstimate(flops=10**12, bytes_accessed=1, transcendentals=0)
-VMEM = 60 * 2**20
+VMEM = 62 * 2**20
 
 
 def ring_positions():
@@ -311,15 +311,17 @@
     right_low, right_high = both_ways(right_own, "z")
     left_low, left_high = both_ways(left_own, "x")
     left_other = shift(left_own, "c", 1, 2)
-    psi, right_low, right_high, left_low, left_high, left_other, *to_far = together(
-        psi, right_low, right_high, left_low, left_high, left_other, *halves_of(right_low, right_high)
+    columns = column(psi, where[10]), column(psi, where[11])
+    psi, picks = split(psi)
+    psi, picks, for_low, for_high, right_low, right_high = together(psi, picks, *columns, right_low, right_high)
+    to_far = halves_of(right_low, right_high)
+    left_low, left_high, left_other, for_low, for_high, *to_far = together(
+        left_low, left_high, left_other, for_low, for_high, *to_far
     )
 
-    for_low, for_high = column(psi, where[10]), column(psi, where[11])
-    for_low, for_high, psi, *to_far = together(for_low, for_high, psi, *to_far)
     psi_low, psi_high = shift(for_low, "x", 1), shift(for_high, "x", 3)
     far = onward(to_far, "z")
-    psi_own = split(psi)
+    psi_own = psi, picks
     rights = [(right_own,), (right_low,), (right_high,)]
     lefts_own = [((left_own,), (left_other,))]
     own = combine(where, [psi_own], lefts_own, rights, 0)

time: 191 us -> 192 us (level)
    ppermute x16, waiting for transfers between devices: 61.1 us -> 21.4 us  [shift(): lax.ppermute(array, axis, [(i, (i + step) % size) for i in range(size)])]
    all_to_all x4, waiting for transfers between devices: 9.81 us -> 48.2 us  [exchange(): return lax.all_to_all(array, axis, split_axis=0, concat_axis=0, tiled=True)]
  transfers between devices with their start and end apart: 20 -> 20, of which waited for: 7 -> 7; matrix products, arithmetic and copies ran while one was open for 10% -> 13% of each run, Pallas kernels for 24% -> 25%
where the time goes in v11:
time: 192 us; the launch traced here: 191 us
  waiting for transfers between devices  69.6 us (36%)
  Pallas kernels  51.2 us (27%)
  starting transfers between devices  40.2 us (21%)
  local copies, waits for them, and re-layouts  22.1 us (12%)
  other arithmetic  5.4 us (3%)
  between operations  2.62 us (1%)
    all_to_all x4, waiting for transfers between devices, exchange(): return lax.all_to_all(array, axis, split_axis=0, concat_axis=0, tiled=True)  48.2 us
    pallas_call x4, Pallas kernels, combine(): pl.pallas_call(kernel, out_shape=jax.ShapeDtypeStruct((8 * count, width,...  41.9 us
    ppermute x16, starting transfers between devices, shift(): lax.ppermute(array, axis, [(i, (i + step) % size) for i in range(size)])  22.2 us
    ppermute x16, waiting for transfers between devices, shift(): lax.ppermute(array, axis, [(i, (i + step) % size) for i in range(size)])  21.4 us
    all_to_all x4, starting transfers between devices, exchange(): return lax.all_to_all(array, axis, split_axis=0, concat_axis=0, tiled=True)  18 us
    slice x4, local copies, waits for them, and re-layouts, halves_of(): return (from_low[:, :half], from_high[:, half:])  9.14 us
    dynamic_slice x2, local copies, waits for them, and re-layouts, column(): return lax.dynamic_slice(psi, start, (8, 1) + psi.shape[2:])  5.5 us
    pallas_call x1, Pallas kernels, assemble(): pl.pallas_call(kernel, out_shape=jax.ShapeDtypeStruct((4, 4, 2, width, wi...  5.04 us
  transfers between devices with their start and end apart: 20, of which 7 were waited for; matrix products, arithmetic and copies ran while one was open for 13% of the time, Pallas kernels for 25%

profile of v11, /device:TPU:0, one launch (start us, length us, event | category | flops | bytes accessed | tf_op | source)
XLA Modules:
  0.0 191.1 jit_solution(14742085847372052387)
XLA Ops:
  0.0 4.3 %pack.1 = bf16[8,4,272,256]{3,2,1,0:T(8,128)(2,1)} custom-call(s32[32]{0:T(128)} %left.1, s32[32]{0:T(128)} %right.1, bf16[4,4,2,256,256]{4,3,2,1,0:T(8,128)(2,1)} %bitcast.21), custom_call_target="tpu_custom_call" | custom-call | flops 1 | bytes 1 | tf_op jit(solution)/shard_map/pack/pallas_call | solution.py:264
  4.4 4.7 %all-to-all-start = ((bf16[8,4,272,256]{3,2,1,0:T(8,128)(2,1)}), bf16[8,4,272,256]{3,2,1,0:T(8,128)(2,1)}, u32[]{:S(2)}, u32[]{:S(2)}) async-start(bf16[8,4,272,256]{3,2,1,0:T(8,128)(2,1)} %pack.1), calls=%async_computation | async-start | bytes 8912896 | tf_op jit(solution)/shard_map/all_to_all | solution.py:32
  9.1 2.1 %fusion = bf16[2,8,256,256]{3,2,1,0:T(8,128)(2,1)} fusion(bf16[2,8,256,256]{3,2,1,0:T(8,128)(2,1)S(1)} %copy-done.1, s32[2]{0:T(128)S(1)} %copy-done.4), kind=kLoop, calls=%fused_computation.2 | loop fusion | flops 2097152 | bytes 4194312 | tf_op jit(solution)/shard_map/jit(_where)/select_n | solution.py:304
  11.2 2.0 %collective-permute-start = (bf16[2,2048,256]{2,1,0:T(8,128)(2,1)}, bf16[2,2048,256]{2,1,0:T(8,128)(2,1)}, u32[]{:S(2)}, u32[]{:S(2)}) collective-permute-start(bf16[2,2048,256]{2,1,0:T(8,128)(2,1)} %bitcast.4.refs_4_.refs_8_.refs_6_), channel_id=1, source_target_pairs={{0,8},{8,16},{16,24},{24,0},{1,9},{9,17},{17,25},{25,1},{2,10},{10... | collective-permute-start | bytes 6291464 | tf_op jit(solution)/shard_map/ppermute | solution.py:36
  13.3 2.1 %collective-permute-start.1 = (bf16[2,2048,256]{2,1,0:T(8,128)(2,1)}, bf16[2,2048,256]{2,1,0:T(8,128)(2,1)}, u32[]{:S(2)}, u32[]{:S(2)}) collective-permute-start(bf16[2,2048,256]{2,1,0:T(8,128)(2,1)} %bitcast.4.refs_4_.refs_8_.refs_6_), channel_id=1, source_target_pairs={{0,24},{8,0},{16,8},{24,16},{1,25},{9,1},{17,9},{25,17},{2,26},{10... | collective-permute-start | bytes 6291464 | tf_op jit(solution)/shard_map/ppermute | solution.py:36
  15.4 0.9 fusion.1
  16.3 1.6 collective-permute-start.2
  17.9 1.7 collective-permute-start.3
  19.6 1.3 constant_dynamic-slice_fusion.3
  20.9 0.7 fusion.4
  23.4 38.3 %all-to-all-done.refs_1_ = bf16[8,4,272,256]{3,2,1,0:T(8,128)(2,1)} async-done(((bf16[8,4,272,256]{3,2,1,0:T(8,128)(2,1)}), bf16[8,4,272,256]{3,2,1,0:T(8,128)(2,1)}, u32[]{:S(2)}, u32[]{:S(2)}) %all-to-all-start) | async-done | bytes 4456480 | tf_op jit(solution)/shard_map/all_to_all | solution.py:32
  61.6 0.9 fusion.2
  62.5 0.6 reshape.74.refs_0_
  63.1 3.1 %constant_dynamic-slice_fusion.1 = (bf16[8,1,272,256]{3,2,1,0:T(8,128)(2,1)}, bf16[8,1,272,256]{3,2,1,0:T(8,128)(2,1)}) fusion(bf16[8,4,272,256]{3,2,1,0:T(8,128)(2,1)} %all-to-all-done.refs_1_, u32[]{:T(128)} %bitcast.3, u32[]{:T(128)} %bitcast.2), kind=kLoop, calls=%fused_computation.11 | loop fusion | bytes 4456456 | tf_op jit(solution)/shard_map/dynamic_slice | solution.py:287
  66.3 2.3 %slice.43 = bf16[2,1024,256]{2,1,0:T(8,128)(2,1)} slice(bf16[2,2048,256]{2,1,0:T(8,128)(2,1)} %collective-permute-done.refs_5_.refs_9_.refs_7_), slice={[0:2], [0:1024], [0:256]} | slice | bytes 2097152 | tf_op jit(solution)/shard_map/slice | solution.py:45
  68.6 2.3 %slice.44 = bf16[2,1024,256]{2,1,0:T(8,128)(2,1)} slice(bf16[2,2048,256]{2,1,0:T(8,128)(2,1)} %collective-permute-done.1.refs_6_.refs_10_.refs_8_), slice={[0:2], [1024:2048], [0:256]} | slice | bytes 2097152 | tf_op jit(solution)/shard_map/slice | solution.py:45
  70.8 2.0 %collective-permute-start.7 = (bf16[2,1024,256]{2,1,0:T(8,128)(2,1)}, bf16[2,1024,256]{2,1,0:T(8,128)(2,1)}, u32[]{:S(2)}, u32[]{:S(2)}) collective-permute-start(bf16[2,1024,256]{2,1,0:T(8,128)(2,1)} %slice.43), channel_id=1, source_target_pairs={{0,8},{8,16},{16,24},{24,0},{1,9},{9,17},{17,25},{25,1},{2,10},{10... | collective-permute-start | bytes 3145736 | tf_op jit(solution)/shard_map/ppermute | solution.py:36
  72.8 2.2 %collective-permute-start.8 = (bf16[2,1024,256]{2,1,0:T(8,128)(2,1)}, bf16[2,1024,256]{2,1,0:T(8,128)(2,1)}, u32[]{:S(2)}, u32[]{:S(2)}) collective-permute-start(bf16[2,1024,256]{2,1,0:T(8,128)(2,1)} %slice.44), channel_id=1, source_target_pairs={{0,24},{8,0},{16,8},{24,16},{1,25},{9,1},{17,9},{25,17},{2,26},{10... | collective-permute-start | bytes 3145736 | tf_op jit(solution)/shard_map/ppermute | solution.py:36
  75.0 1.5 collective-permute-start.5
  76.5 1.7 collective-permute-start.6
  78.3 7.9 %combine_0_0_0.1.refs_6_ = bf16[8,256,256]{2,1,0:T(8,128)(2,1)} custom-call(s32[13]{0:T(128)} %get-tuple-element.72.where, s32[64]{0:T(128)} %reshape.74.refs_0_, bf16[8,4,272,256]{3,2,1,0:T(8,128)(2,1)} %all-to-all-done.refs_1_, bf16[2,2048,256]{2,1,0:T(8,128)(2,1)} %bitcast.18, bf16[2,2048,256]{2,1,0:T(8,128)(2,1)} %collective-permute-done.4.refs_3_, ...), custom_call_target="tpu_custom_call" | custom-call | flops 999999995904 | bytes 1 | tf_op jit(solution)/shard_map/combine_0_0_0/pallas_call | solution.py:182
  86.2 2.4 %slice.46 = bf16[2,1024,256]{2,1,0:T(8,128)(2,1)} slice(bf16[2,2048,256]{2,1,0:T(8,128)(2,1)} %collective-permute-done.2.refs_4_), slice={[0:2], [0:1024], [0:256]} | slice | bytes 2097152 | tf_op jit(solution)/shard_map/slice | solution.py:45
  88.5 2.3 %slice.47 = bf16[2,1024,256]{2,1,0:T(8,128)(2,1)} slice(bf16[2,2048,256]{2,1,0:T(8,128)(2,1)} %collective-permute-done.3.refs_6_), slice={[0:2], [1024:2048], [0:256]} | slice | bytes 2097152 | tf_op jit(solution)/shard_map/slice | solution.py:45
  90.8 2.4 %constant_dynamic-slice_fusion = bf16[8,1,272,256]{3,2,1,0:T(8,128)(2,1)} fusion(bf16[8,4,272,256]{3,2,1,0:T(8,128)(2,1)} %all-to-all-done.refs_1_, u32[]{:T(128)} %bitcast.6), kind=kLoop, calls=%fused_computation.10 | loop fusion | bytes 2228228 | tf_op jit(solution)/shard_map/dynamic_slice | solution.py:287
  93.1 5.1 %collective-permute-done.7.refs_4_.refs_11_.refs_9_ = bf16[2,1024,256]{2,1,0:T(8,128)(2,1)} collective-permute-done((bf16[2,1024,256]{2,1,0:T(8,128)(2,1)}, bf16[2,1024,256]{2,1,0:T(8,128)(2,1)}, u32[]{:S(2)}, u32[]{:S(2)}) %collective-permute-start.7) | collective-permute-done | bytes 1048608 | tf_op jit(solution)/shard_map/ppermute | solution.py:36
  98.2 5.0 %combine_0_3_0.1 = bf16[8,256,256]{2,1,0:T(8,128)(2,1)} custom-call(s32[13]{0:T(128)} %get-tuple-element.72.where, s32[64]{0:T(128)} %reshape.74.refs_0_, bf16[8,4,272,256]{3,2,1,0:T(8,128)(2,1)} %all-to-all-done.refs_1_, bf16[2,2048,256]{2,1,0:T(8,128)(2,1)} %bitcast.19, ...), custom_call_target="tpu_custom_call", output_to_operand_aliasing={{}: (7, {})} | custom-call | flops 1 | bytes 1 | tf_op jit(solution)/shard_map/combine_0_3_0/pallas_call | solution.py:182
  103.3 0.5 collective-permute-start.9
  103.8 3.0 %collective-permute-start.11 = (bf16[8,1,272,256]{3,2,1,0:T(8,128)(2,1)}, bf16[8,1,272,256]{3,2,1,0:T(8,128)(2,1)}, u32[]{:S(2)}, u32[]{:S(2)}) collective-permute-start(bf16[8,1,272,256]{3,2,1,0:T(8,128)(2,1)} %constant_dynamic-slice_fusion), channel_id=1, source_target_pairs={{0,4},{2,6},{4,0},{6,2},{1,5},{3,7},{5,1},{7,3},{8,12},{10,14},{12... | collective-permute-start | bytes 3342344 | tf_op jit(solution)/shard_map/ppermute | solution.py:36
  106.9 0.6 collective-permute-start.12
  107.4 2.6 %collective-permute-start.13 = (bf16[2,1024,256]{2,1,0:T(8,128)(2,1)}, bf16[2,1024,256]{2,1,0:T(8,128)(2,1)}, u32[]{:S(2)}, u32[]{:S(2)}) collective-permute-start(bf16[2,1024,256]{2,1,0:T(8,128)(2,1)} %slice.47), channel_id=1, source_target_pairs={{0,6},{2,0},{4,2},{6,4},{1,7},{3,1},{5,3},{7,5},{8,14},{10,8},{12,... | collective-permute-start | bytes 3145736 | tf_op jit(solution)/shard_map/ppermute | solution.py:36
  110.1 4.4 %all-to-all-start.1 = ((bf16[8,256,256]{2,1,0:T(8,128)(2,1)}), bf16[8,256,256]{2,1,0:T(8,128)(2,1)}, u32[]{:S(2)}, u32[]{:S(2)}) async-start(bf16[8,256,256]{2,1,0:T(8,128)(2,1)} %combine_0_3_0.1), calls=%async_computation.1 | async-start | bytes 2097152 | tf_op jit(solution)/shard_map/all_to_all | solution.py:32
  114.6 1.3 copy-done.6
  115.9 0.8 convert_reduce_fusion.1
  116.6 0.6 reshape.75.refs_0_
  117.3 0.7 reshape.76.refs_1_
  117.9 18.5 %combine_1_0_0.1 = bf16[16,256,256]{2,1,0:T(8,128)(2,1)} custom-call(s32[13]{0:T(128)} %get-tuple-element.72.where, s32[16]{0:T(128)} %reshape.75.refs_0_, s32[16]{0:T(128)} %reshape.76.refs_1_, bf16[8,1,272,256]{3,2,1,0:T(8,128)(2,1)} %collective-permute-done.5.refs_2_, bf16[8,1,272,256]{3,2,1,0:T(8,128)(2,1)} %collective-permute-done.6.refs_3_, ...), custom_call_target="tpu_custom_call" | custom-call | flops 999999995904 | bytes 1 | tf_op jit(solution)/shard_map/combine_1_0_0/pallas_call | solution.py:182
  136.5 4.7 %all-to-all-start.2 = ((bf16[16,256,256]{2,1,0:T(8,128)(2,1)}), bf16[16,256,256]{2,1,0:T(8,128)(2,1)}, u32[]{:S(2)}, u32[]{:S(2)}) async-start(bf16[16,256,256]{2,1,0:T(8,128)(2,1)} %combine_1_0_0.1), calls=%async_computation.2 | async-start | bytes 4194304 | tf_op jit(solution)/shard_map/all_to_all | solution.py:32
  141.2 13.5 %collective-permute-done.12.refs_2_ = bf16[2,1024,256]{2,1,0:T(8,128)(2,1)} collective-permute-done((bf16[2,1024,256]{2,1,0:T(8,128)(2,1)}, bf16[2,1024,256]{2,1,0:T(8,128)(2,1)}, u32[]{:S(2)}, u32[]{:S(2)}) %collective-permute-start.12) | collective-permute-done | bytes 1048608 | tf_op jit(solution)/shard_map/ppermute | solution.py:36
  154.8 0.5 collective-permute-start.15
  155.3 0.7 convert_reduce_fusion
  156.1 0.6 reshape.77.refs_0_
  156.7 2.3 %collective-permute-done.14.refs_4_ = bf16[2,1024,256]{2,1,0:T(8,128)(2,1)S(1)} collective-permute-done((bf16[2,1024,256]{2,1,0:T(8,128)(2,1)}, bf16[2,1024,256]{2,1,0:T(8,128)(2,1)S(1)}, u32[]{:S(2)}, u32[]{:S(2)}) %collective-permute-start.14) | collective-permute-done | bytes 1048608 | tf_op jit(solution)/shard_map/ppermute | solution.py:36
  159.3 0.7 copy-done.3
  160.0 10.4 %combine_3_0_0.1 = bf16[8,256,256]{2,1,0:T(8,128)(2,1)} custom-call(s32[13]{0:T(128)} %get-tuple-element.72.where, s32[16]{0:T(128)} %reshape.77.refs_0_, bf16[8,1,272,256]{3,2,1,0:T(8,128)(2,1)} %collective-permute-done.11.refs_1_, bf16[2,1024,256]{2,1,0:T(8,128)(2,1)} %collective-permute-done.12.refs_2_, ...), custom_call_target="tpu_custom_call" | custom-call | flops 1 | bytes 1 | tf_op jit(solution)/shard_map/combine_3_0_0/pallas_call | solution.py:182
  170.4 4.1 %all-to-all-start.3 = ((bf16[8,256,256]{2,1,0:T(8,128)(2,1)}), bf16[8,256,256]{2,1,0:T(8,128)(2,1)S(1)}, u32[]{:S(2)}, u32[]{:S(2)}) async-start(bf16[8,256,256]{2,1,0:T(8,128)(2,1)} %combine_3_0_0.1), calls=%async_computation.3 | async-start | bytes 2097152 | tf_op jit(solution)/shard_map/all_to_all | solution.py:32
  175.2 5.0 %assemble.1 = bf16[4,4,2,256,256]{4,3,2,1,0:T(8,128)(2,1)} custom-call(s32[13]{0:T(128)} %get-tuple-element.72.where, bf16[4,2,1,256,256]{4,3,2,1,0:T(8,128)(2,1)} %bitcast.7.refs_0_, bf16[4,2,2,256,256]{4,3,2,1,0:T(8,128)(2,1)} %bitcast.8.refs_1_), custom_call_target="tpu_custom_call" | custom-call | flops 1 | bytes 1 | tf_op jit(solution)/shard_map/assemble/pallas_call | solution.py:222
  180.2 9.9 %all-to-all-done.3 = bf16[8,256,256]{2,1,0:T(8,128)(2,1)S(1)} async-done(((bf16[8,256,256]{2,1,0:T(8,128)(2,1)}), bf16[8,256,256]{2,1,0:T(8,128)(2,1)S(1)}, u32[]{:S(2)}, u32[]{:S(2)}) %all-to-all-start.3) | async-done | bytes 1048608 | tf_op jit(solution)/shard_map/all_to_all | solution.py:32
  190.1 1.0 constant_dynamic-update-slice_fusion
  (30 shorter events, 0.6 us)
Async XLA Ops:
  4.3 4.8 %copy-start.1 = (bf16[2,8,256,256]{3,2,1,0:T(8,128)(2,1)S(1)}, bf16[2,8,256,256]{3,2,1,0:T(8,128)(2,1)}, u32[]{:S(2)}) copy-start(bf16[2,8,256,256]{3,2,1,0:T(8,128)(2,1)} %param.13) | copy-start | bytes 6291460
  4.3 4.8 %copy-start.4 = (s32[2]{0:T(128)S(1)}, s32[2]{0:T(128)}, u32[]{:S(2)}) copy-start(s32[2]{0:T(128)} %param.14) | copy-start | bytes 28
  4.4 57.3 %all-to-all-start = ((bf16[8,4,272,256]{3,2,1,0:T(8,128)(2,1)}), bf16[8,4,272,256]{3,2,1,0:T(8,128)(2,1)}, u32[]{:S(2)}, u32[]{:S(2)}) async-start(bf16[8,4,272,256]{3,2,1,0:T(8,128)(2,1)} %pack.1), calls=%async_computation | async-start | bytes 8912896 | tf_op jit(solution)/shard_map/all_to_all | solution.py:32
  9.1 6.3 %copy-start.2 = (bf16[2,8,256,256]{3,2,1,0:T(8,128)(2,1)S(1)}, bf16[2,8,256,256]{3,2,1,0:T(8,128)(2,1)}, u32[]{:S(2)}) copy-start(bf16[2,8,256,256]{3,2,1,0:T(8,128)(2,1)} %param.11) | copy-start | bytes 6291460
  9.1 6.3 %copy-start.5 = (s32[2]{0:T(128)S(1)}, s32[2]{0:T(128)}, u32[]{:S(2)}) copy-start(s32[2]{0:T(128)} %param.12) | copy-start | bytes 28
  11.2 55.0 %collective-permute-start = (bf16[2,2048,256]{2,1,0:T(8,128)(2,1)}, bf16[2,2048,256]{2,1,0:T(8,128)(2,1)}, u32[]{:S(2)}, u32[]{:S(2)}) collective-permute-start(bf16[2,2048,256]{2,1,0:T(8,128)(2,1)} %bitcast.4.refs_4_.refs_8_.refs_6_), channel_id=1, source_target_pairs={{0,8},{8,16},{16,24},{24,0},{1,9},{9,17},{17,25},{25,1},{2,10},{10... | collective-permute-start | bytes 6291464 | tf_op jit(solution)/shard_map/ppermute | solution.py:36
  13.3 53.0 %collective-permute-start.1 = (bf16[2,2048,256]{2,1,0:T(8,128)(2,1)}, bf16[2,2048,256]{2,1,0:T(8,128)(2,1)}, u32[]{:S(2)}, u32[]{:S(2)}) collective-permute-start(bf16[2,2048,256]{2,1,0:T(8,128)(2,1)} %bitcast.4.refs_4_.refs_8_.refs_6_), channel_id=1, source_target_pairs={{0,24},{8,0},{16,8},{24,16},{1,25},{9,1},{17,9},{25,17},{2,26},{10... | collective-permute-start | bytes 6291464 | tf_op jit(solution)/shard_map/ppermute | solution.py:36
  16.3 50.0 %copy-start = (bf16[2,8,256,256]{3,2,1,0:T(8,128)(2,1)}, bf16[2,8,256,256]{3,2,1,0:T(8,128)(2,1)S(1)}, u32[]{:S(2)}) copy-start(bf16[2,8,256,256]{3,2,1,0:T(8,128)(2,1)S(1)} %fusion.1) | copy-start | bytes 6291460
  16.3 54.5 %collective-permute-start.2 = (bf16[2,2048,256]{2,1,0:T(8,128)(2,1)S(1)}, bf16[2,2048,256]{2,1,0:T(8,128)(2,1)}, u32[]{:S(2)}, u32[]{:S(2)}) collective-permute-start(bf16[2,2048,256]{2,1,0:T(8,128)(2,1)S(1)} %bitcast.15), channel_id=1, source_target_pairs={{0,2},{2,4},{4,6},{6,0},{1,3},{3,5},{5,7},{7,1},{8,10},{10,12},{12... | collective-permute-start | bytes 6291464 | tf_op jit(solution)/shard_map/ppermute | solution.py:36
  17.9 53.0 %collective-permute-start.3 = (bf16[2,2048,256]{2,1,0:T(8,128)(2,1)S(1)}, bf16[2,2048,256]{2,1,0:T(8,128)(2,1)}, u32[]{:S(2)}, u32[]{:S(2)}) collective-permute-start(bf16[2,2048,256]{2,1,0:T(8,128)(2,1)S(1)} %bitcast.16), channel_id=1, source_target_pairs={{0,6},{2,0},{4,2},{6,4},{1,7},{3,1},{5,3},{7,5},{8,14},{10,8},{12,... | collective-permute-start | bytes 6291464 | tf_op jit(solution)/shard_map/ppermute | solution.py:36
  19.6 51.2 %collective-permute-start.4 = (bf16[2,2048,256]{2,1,0:T(8,128)(2,1)S(1)}, bf16[2,2048,256]{2,1,0:T(8,128)(2,1)}, u32[]{:S(2)}, u32[]{:S(2)}) collective-permute-start(bf16[2,2048,256]{2,1,0:T(8,128)(2,1)S(1)} %bitcast.17), channel_id=1, source_target_pairs={{0,1},{1,0},{2,3},{3,2},{4,5},{5,4},{6,7},{7,6},{8,9},{9,8},{10,11... | collective-permute-start | bytes 6291464 | tf_op jit(solution)/shard_map/ppermute | solution.py:36
  70.8 27.4 %collective-permute-start.7 = (bf16[2,1024,256]{2,1,0:T(8,128)(2,1)}, bf16[2,1024,256]{2,1,0:T(8,128)(2,1)}, u32[]{:S(2)}, u32[]{:S(2)}) collective-permute-start(bf16[2,1024,256]{2,1,0:T(8,128)(2,1)} %slice.43), channel_id=1, source_target_pairs={{0,8},{8,16},{16,24},{24,0},{1,9},{9,17},{17,25},{25,1},{2,10},{10... | collective-permute-start | bytes 3145736 | tf_op jit(solution)/shard_map/ppermute | solution.py:36
  72.8 25.4 %collective-permute-start.8 = (bf16[2,1024,256]{2,1,0:T(8,128)(2,1)}, bf16[2,1024,256]{2,1,0:T(8,128)(2,1)}, u32[]{:S(2)}, u32[]{:S(2)}) collective-permute-start(bf16[2,1024,256]{2,1,0:T(8,128)(2,1)} %slice.44), channel_id=1, source_target_pairs={{0,24},{8,0},{16,8},{24,16},{1,25},{9,1},{17,9},{25,17},{2,26},{10... | collective-permute-start | bytes 3145736 | tf_op jit(solution)/shard_map/ppermute | solution.py:36
  75.0 28.2 %collective-permute-start.5 = (bf16[8,1,272,256]{3,2,1,0:T(8,128)(2,1)}, bf16[8,1,272,256]{3,2,1,0:T(8,128)(2,1)}, u32[]{:S(2)}, u32[]{:S(2)}) collective-permute-start(bf16[8,1,272,256]{3,2,1,0:T(8,128)(2,1)} %get-tuple-element.47), channel_id=1, source_target_pairs={{0,2},{2,4},{4,6},{6,0},{1,3},{3,5},{5,7},{7,1},{8,10},{10,12},{12... | collective-permute-start | bytes 3342344 | tf_op jit(solution)/shard_map/ppermute | solution.py:36
  76.5 26.7 %collective-permute-start.6 = (bf16[8,1,272,256]{3,2,1,0:T(8,128)(2,1)}, bf16[8,1,272,256]{3,2,1,0:T(8,128)(2,1)}, u32[]{:S(2)}, u32[]{:S(2)}) collective-permute-start(bf16[8,1,272,256]{3,2,1,0:T(8,128)(2,1)} %get-tuple-element.48), channel_id=1, source_target_pairs={{0,6},{2,0},{4,2},{6,4},{1,7},{3,1},{5,3},{7,5},{8,14},{10,8},{12,... | collective-permute-start | bytes 3342344 | tf_op jit(solution)/shard_map/ppermute | solution.py:36
  103.2 11.3 %collective-permute-start.10 = (bf16[2,2048,256]{2,1,0:T(8,128)(2,1)}, bf16[2,2048,256]{2,1,0:T(8,128)(2,1)S(1)}, u32[]{:S(2)}, u32[]{:S(2)}) collective-permute-start(bf16[2,2048,256]{2,1,0:T(8,128)(2,1)} %collective-permute-done.3.refs_6_), channel_id=1, source_target_pairs={{0,1},{1,0},{2,3},{3,2},{4,5},{5,4},{6,7},{7,6},{8,9},{9,8},{10,11... | collective-permute-start | bytes 6291464 | tf_op jit(solution)/shard_map/ppermute | solution.py:36
  103.3 12.5 %collective-permute-start.9 = (bf16[2,2048,256]{2,1,0:T(8,128)(2,1)}, bf16[2,2048,256]{2,1,0:T(8,128)(2,1)}, u32[]{:S(2)}, u32[]{:S(2)}) collective-permute-start(bf16[2,2048,256]{2,1,0:T(8,128)(2,1)} %collective-permute-done.2.refs_4_), channel_id=1, source_target_pairs={{0,1},{1,0},{2,3},{3,2},{4,5},{5,4},{6,7},{7,6},{8,9},{9,8},{10,11... | collective-permute-start | bytes 6291464 | tf_op jit(solution)/shard_map/ppermute | solution.py:36
  103.8 51.0 %collective-permute-start.11 = (bf16[8,1,272,256]{3,2,1,0:T(8,128)(2,1)}, bf16[8,1,272,256]{3,2,1,0:T(8,128)(2,1)}, u32[]{:S(2)}, u32[]{:S(2)}) collective-permute-start(bf16[8,1,272,256]{3,2,1,0:T(8,128)(2,1)} %constant_dynamic-slice_fusion), channel_id=1, source_target_pairs={{0,4},{2,6},{4,0},{6,2},{1,5},{3,7},{5,1},{7,3},{8,12},{10,14},{12... | collective-permute-start | bytes 3342344 | tf_op jit(solution)/shard_map/ppermute | solution.py:36
  106.9 47.8 %collective-permute-start.12 = (bf16[2,1024,256]{2,1,0:T(8,128)(2,1)}, bf16[2,1024,256]{2,1,0:T(8,128)(2,1)}, u32[]{:S(2)}, u32[]{:S(2)}) collective-permute-start(bf16[2,1024,256]{2,1,0:T(8,128)(2,1)} %slice.46), channel_id=1, source_target_pairs={{0,2},{2,4},{4,6},{6,0},{1,3},{3,5},{5,7},{7,1},{8,10},{10,12},{12... | collective-permute-start | bytes 3145736 | tf_op jit(solution)/shard_map/ppermute | solution.py:36
  107.4 47.4 %collective-permute-start.13 = (bf16[2,1024,256]{2,1,0:T(8,128)(2,1)}, bf16[2,1024,256]{2,1,0:T(8,128)(2,1)}, u32[]{:S(2)}, u32[]{:S(2)}) collective-permute-start(bf16[2,1024,256]{2,1,0:T(8,128)(2,1)} %slice.47), channel_id=1, source_target_pairs={{0,6},{2,0},{4,2},{6,4},{1,7},{3,1},{5,3},{7,5},{8,14},{10,8},{12,... | collective-permute-start | bytes 3145736 | tf_op jit(solution)/shard_map/ppermute | solution.py:36
  110.1 26.4 %all-to-all-start.1 = ((bf16[8,256,256]{2,1,0:T(8,128)(2,1)}), bf16[8,256,256]{2,1,0:T(8,128)(2,1)}, u32[]{:S(2)}, u32[]{:S(2)}) async-start(bf16[8,256,256]{2,1,0:T(8,128)(2,1)} %combine_0_3_0.1), calls=%async_computation.1 | async-start | bytes 2097152 | tf_op jit(solution)/shard_map/all_to_all | solution.py:32
  114.5 1.3 copy-start.6
  136.5 33.9 %all-to-all-start.2 = ((bf16[16,256,256]{2,1,0:T(8,128)(2,1)}), bf16[16,256,256]{2,1,0:T(8,128)(2,1)}, u32[]{:S(2)}, u32[]{:S(2)}) async-start(bf16[16,256,256]{2,1,0:T(8,128)(2,1)} %combine_1_0_0.1), calls=%async_computation.2 | async-start | bytes 4194304 | tf_op jit(solution)/shard_map/all_to_all | solution.py:32
  154.8 4.2 %collective-permute-start.14 = (bf16[2,1024,256]{2,1,0:T(8,128)(2,1)}, bf16[2,1024,256]{2,1,0:T(8,128)(2,1)S(1)}, u32[]{:S(2)}, u32[]{:S(2)}) collective-permute-start(bf16[2,1024,256]{2,1,0:T(8,128)(2,1)} %collective-permute-done.12.refs_2_), channel_id=1, source_target_pairs={{0,1},{1,0},{2,3},{3,2},{4,5},{5,4},{6,7},{7,6},{8,9},{9,8},{10,11... | collective-permute-start | bytes 3145736 | tf_op jit(solution)/shard_map/ppermute | solution.py:36
  154.8 4.5 %collective-permute-start.15 = (bf16[2,1024,256]{2,1,0:T(8,128)(2,1)}, bf16[2,1024,256]{2,1,0:T(8,128)(2,1)}, u32[]{:S(2)}, u32[]{:S(2)}) collective-permute-start(bf16[2,1024,256]{2,1,0:T(8,128)(2,1)} %collective-permute-done.13.refs_3_), channel_id=1, source_target_pairs={{0,1},{1,0},{2,3},{3,2},{4,5},{5,4},{6,7},{7,6},{8,9},{9,8},{10,11... | collective-permute-start | bytes 3145736 | tf_op jit(solution)/shard_map/ppermute | solution.py:36
  159.0 1.0 copy-start.3
  170.4 19.7 %all-to-all-start.3 = ((bf16[8,256,256]{2,1,0:T(8,128)(2,1)}), bf16[8,256,256]{2,1,0:T(8,128)(2,1)S(1)}, u32[]{:S(2)}, u32[]{:S(2)}) async-start(bf16[8,256,256]{2,1,0:T(8,128)(2,1)} %combine_3_0_0.1), calls=%async_computation.3 | async-start | bytes 2097152 | tf_op jit(solution)/shard_map/all_to_all | solution.py:32

commit v12 on v9

--- a/solution.py
+++ b/solution.py
@@ -13,7 +13,6 @@
 BF16 = jnp.bfloat16
 BRIEF = pl.CostEstimate(flops=1, bytes_accessed=1, transcendentals=0)
 LONG = pl.CostEstimate(flops=10**12, bytes_accessed=1, transcendentals=0)
-VMEM = 60 * 2**20
 
 
 def ring_positions():
@@ -201,7 +200,7 @@
         ),
         input_output_aliases={count + len(operands): 0} if extra else {},
         compiler_params=pltpu.CompilerParams(
-            dimension_semantics=("arbitrary",), vmem_limit_bytes=VMEM
+            dimension_semantics=("arbitrary",), vmem_limit_bytes=(26 if count == 1 else 46) * 2**20
         ),
         cost_estimate=BRIEF if first == 3 or z_first else LONG,
         name=f"combine_{first}_{z_first}_{cores[0]}",
@@ -228,7 +227,7 @@
             in_specs=[pl.BlockSpec((1, 2, count, width, width), at_z) for count in counts],
             out_specs=pl.BlockSpec((1, 4, 2, width, width), at_z),
         ),
-        compiler_params=pltpu.CompilerParams(vmem_limit_bytes=VMEM),
+        compiler_params=pltpu.CompilerParams(vmem_limit_bytes=12 * 2**20),
         cost_estimate=BRIEF,
         name="assemble",
     )(where, *[p.reshape(4, 2, n, width, width) for (_, p), n in zip(pieces, counts)])
@@ -275,7 +274,7 @@
                 pltpu.SemaphoreType.DMA((8,)),
             ],
         ),
-        compiler_params=pltpu.CompilerParams(vmem_limit_bytes=VMEM),
+        compiler_params=pltpu.CompilerParams(vmem_limit_bytes=12 * 2**20),
         cost_estimate=BRIEF,
         name="pack",
     )(pair_left, pair_right, blocks)

time: 191 us -> 193 us (1.010)
  Pallas kernels: 50.9 us -> 46.3 us
  local copies, waits for them, and re-layouts: 20.9 us -> 24.7 us
  waiting for transfers between devices: 70.9 us -> 73.2 us
    unnamed x16 -> x20, local copies, waits for them, and re-layouts: 0.7 us -> 7.17 us
    pallas_call x1, Pallas kernels: 4.33 us -> 1.65 us  [pack(): pl.pallas_call(kernel, out_shape=jax.ShapeDtypeStruct(shape, BF16), grid_...]
    convert_element_type x4, local copies, waits for them, and re-layouts: 2.64 us -> 0.34 us  [split(): return (piece, piece[:, :, -TAIL, :2].astype(jnp.int32).reshape(-1))]
  transfers between devices with their start and end apart: 20 -> 20, of which waited for: 7 -> 7; matrix products, arithmetic and copies ran while one was open for 10% -> 9% of each run, Pallas kernels for 24% -> 23%
where the time goes in v12:
time: 193 us; the launch traced here: 192 us
  waiting for transfers between devices  73.2 us (38%)
  Pallas kernels  46.3 us (24%)
  starting transfers between devices  39.4 us (20%)
  local copies, waits for them, and re-layouts  24.7 us (13%)
  other arithmetic  5.53 us (3%)
  between operations  2.69 us (1%)
    ppermute x16, waiting for transfers between devices, shift(): lax.ppermute(array, axis, [(i, (i + step) % size) for i in range(size)])  62.9 us
    pallas_call x4, Pallas kernels, combine(): pl.pallas_call(kernel, out_shape=jax.ShapeDtypeStruct((8 * count, width,...  40.1 us
    ppermute x16, starting transfers between devices, shift(): lax.ppermute(array, axis, [(i, (i + step) % size) for i in range(size)])  21.3 us
    all_to_all x4, starting transfers between devices, exchange(): return lax.all_to_all(array, axis, split_axis=0, concat_axis=0, tiled=True)  18 us
    all_to_all x4, waiting for transfers between devices, exchange(): return lax.all_to_all(array, axis, split_axis=0, concat_axis=0, tiled=True)  10.3 us
    slice x4, local copies, waits for them, and re-layouts, halves_of(): return (from_low[:, :half], from_high[:, half:])  9.18 us
    unnamed x20, local copies, waits for them, and re-layouts  7.17 us
    dynamic_slice x2, local copies, waits for them, and re-layouts, column(): return lax.dynamic_slice(psi, start, (8, 1) + psi.shape[2:])  5.58 us
  transfers between devices with their start and end apart: 20, of which 7 were waited for; matrix products, arithmetic and copies ran while one was open for 9% of the time, Pallas kernels for 23%

profile of v12, /device:TPU:0, one launch (start us, length us, event | category | flops | bytes accessed | tf_op | source)
XLA Modules:
  0.0 191.8 jit_solution(14598451805064329220)
XLA Ops:
  0.0 2.2 %copy-done.1 = bf16[32,256,256]{2,1,0:T(8,128)(2,1)S(1)} copy-done((bf16[32,256,256]{2,1,0:T(8,128)(2,1)S(1)}, bf16[32,256,256]{2,1,0:T(8,128)(2,1)}, u32[]{:S(2)}) %copy-start.1) | copy-done | bytes 4194328
  2.2 0.7 copy-done.3
  2.8 0.7 copy-done.4
  3.5 1.7 pack.1
  5.2 2.1 %copy-done = bf16[8,4,272,256]{3,2,1,0:T(8,128)(2,1)} copy-done((bf16[8,4,272,256]{3,2,1,0:T(8,128)(2,1)}, bf16[8,4,272,256]{3,2,1,0:T(8,128)(2,1)S(1)}, u32[]{:S(2)}) %copy-start) | copy-done | bytes 4456472
  7.2 4.7 %all-to-all-start = ((bf16[8,4,272,256]{3,2,1,0:T(8,128)(2,1)}), bf16[8,4,272,256]{3,2,1,0:T(8,128)(2,1)}, u32[]{:S(2)}, u32[]{:S(2)}) async-start(bf16[8,4,272,256]{3,2,1,0:T(8,128)(2,1)} %copy-done), calls=%async_computation | async-start | bytes 8912896 | tf_op jit(solution)/shard_map/all_to_all | solution.py:31
  12.0 2.2 %fusion = bf16[2,8,256,256]{3,2,1,0:T(8,128)(2,1)} fusion(bf16[2,8,256,256]{3,2,1,0:T(8,128)(2,1)S(1)} %copy-done.5, s32[2]{0:T(128)S(1)} %copy-done.7), kind=kLoop, calls=%fused_computation.2 | loop fusion | flops 2097152 | bytes 4194312 | tf_op jit(solution)/shard_map/jit(_where)/select_n | solution.py:303
  14.2 2.0 %collective-permute-start = (bf16[2,2048,256]{2,1,0:T(8,128)(2,1)}, bf16[2,2048,256]{2,1,0:T(8,128)(2,1)}, u32[]{:S(2)}, u32[]{:S(2)}) collective-permute-start(bf16[2,2048,256]{2,1,0:T(8,128)(2,1)} %bitcast.2.refs_4_.refs_8_.refs_6_), channel_id=1, source_target_pairs={{0,8},{8,16},{16,24},{24,0},{1,9},{9,17},{17,25},{25,1},{2,10},{10... | collective-permute-start | bytes 6291464 | tf_op jit(solution)/shard_map/ppermute | solution.py:35
  16.2 2.1 %collective-permute-start.1 = (bf16[2,2048,256]{2,1,0:T(8,128)(2,1)}, bf16[2,2048,256]{2,1,0:T(8,128)(2,1)}, u32[]{:S(2)}, u32[]{:S(2)}) collective-permute-start(bf16[2,2048,256]{2,1,0:T(8,128)(2,1)} %bitcast.2.refs_4_.refs_8_.refs_6_), channel_id=1, source_target_pairs={{0,24},{8,0},{16,8},{24,16},{1,25},{9,1},{17,9},{25,17},{2,26},{10... | collective-permute-start | bytes 6291464 | tf_op jit(solution)/shard_map/ppermute | solution.py:35
  18.3 0.9 fusion.1
  19.2 1.6 collective-permute-start.2
  20.8 1.7 collective-permute-start.3
  22.5 0.7 constant_dynamic-slice_fusion.3
  23.2 0.7 fusion.3
  25.7 39.1 %collective-permute-done.refs_5_.refs_9_.refs_7_ = bf16[2,2048,256]{2,1,0:T(8,128)(2,1)} collective-permute-done((bf16[2,2048,256]{2,1,0:T(8,128)(2,1)}, bf16[2,2048,256]{2,1,0:T(8,128)(2,1)}, u32[]{:S(2)}, u32[]{:S(2)}) %collective-permute-start) | collective-permute-done | bytes 2097184 | tf_op jit(solution)/shard_map/ppermute | solution.py:35
  64.8 2.4 %slice.52 = bf16[2,1024,256]{2,1,0:T(8,128)(2,1)} slice(bf16[2,2048,256]{2,1,0:T(8,128)(2,1)} %collective-permute-done.refs_5_.refs_9_.refs_7_), slice={[0:2], [0:1024], [0:256]} | slice | bytes 2097152 | tf_op jit(solution)/shard_map/slice | solution.py:44
  67.1 2.3 %slice.53 = bf16[2,1024,256]{2,1,0:T(8,128)(2,1)} slice(bf16[2,2048,256]{2,1,0:T(8,128)(2,1)} %collective-permute-done.1.refs_6_.refs_10_.refs_8_), slice={[0:2], [1024:2048], [0:256]} | slice | bytes 2097152 | tf_op jit(solution)/shard_map/slice | solution.py:44
  69.4 3.2 %constant_dynamic-slice_fusion.1 = (bf16[8,1,272,256]{3,2,1,0:T(8,128)(2,1)}, bf16[8,1,272,256]{3,2,1,0:T(8,128)(2,1)}) fusion(bf16[8,4,272,256]{3,2,1,0:T(8,128)(2,1)} %all-to-all-done.refs_1_, u32[]{:T(128)} %bitcast.5, u32[]{:T(128)} %bitcast.4), kind=kLoop, calls=%fused_computation.10 | loop fusion | bytes 4456456 | tf_op jit(solution)/shard_map/dynamic_slice | solution.py:286
  72.6 0.9 convert_reduce_fusion
  73.7 3.2 %collective-permute-start.8 = (bf16[2,1024,256]{2,1,0:T(8,128)(2,1)}, bf16[2,1024,256]{2,1,0:T(8,128)(2,1)}, u32[]{:S(2)}, u32[]{:S(2)}) collective-permute-start(bf16[2,1024,256]{2,1,0:T(8,128)(2,1)} %slice.53), channel_id=1, source_target_pairs={{0,24},{8,0},{16,8},{24,16},{1,25},{9,1},{17,9},{25,17},{2,26},{10... | collective-permute-start | bytes 3145736 | tf_op jit(solution)/shard_map/ppermute | solution.py:35
  77.0 1.5 collective-permute-start.5
  78.5 1.7 collective-permute-start.6
  80.2 7.8 %combine_0_0_0.1.refs_6_ = bf16[8,256,256]{2,1,0:T(8,128)(2,1)} custom-call(s32[13]{0:T(128)S(1)} %get-tuple-element.72.where, s32[64]{0:T(128)S(1)} %reshape.74.refs_0_, bf16[8,4,272,256]{3,2,1,0:T(8,128)(2,1)} %all-to-all-done.refs_1_, bf16[2,2048,256]{2,1,0:T(8,128)(2,1)S(1)} %bitcast.18, bf16[2,2048,256]{2,1,0:T(8,128)(2,1)} %collective-permute-done.4.refs_3_, ...), custom_call_target="tpu_custom_call" | custom-call | flops 999999995904 | bytes 1 | tf_op jit(solution)/shard_map/combine_0_0_0/pallas_call | solution.py:181
  88.0 2.3 %slice.46 = bf16[2,1024,256]{2,1,0:T(8,128)(2,1)} slice(bf16[2,2048,256]{2,1,0:T(8,128)(2,1)} %collective-permute-done.2.refs_4_), slice={[0:2], [0:1024], [0:256]} | slice | bytes 2097152 | tf_op jit(solution)/shard_map/slice | solution.py:44
  90.2 2.3 %slice.47 = bf16[2,1024,256]{2,1,0:T(8,128)(2,1)} slice(bf16[2,2048,256]{2,1,0:T(8,128)(2,1)} %collective-permute-done.3.refs_6_), slice={[0:2], [1024:2048], [0:256]} | slice | bytes 2097152 | tf_op jit(solution)/shard_map/slice | solution.py:44
  92.5 2.4 %constant_dynamic-slice_fusion = bf16[8,1,272,256]{3,2,1,0:T(8,128)(2,1)} fusion(bf16[8,4,272,256]{3,2,1,0:T(8,128)(2,1)} %all-to-all-done.refs_1_, u32[]{:T(128)} %bitcast.6), kind=kLoop, calls=%fused_computation.9 | loop fusion | bytes 2228228 | tf_op jit(solution)/shard_map/dynamic_slice | solution.py:286
  94.9 5.2 %collective-permute-done.7.refs_4_.refs_11_.refs_9_ = bf16[2,1024,256]{2,1,0:T(8,128)(2,1)} collective-permute-done((bf16[2,1024,256]{2,1,0:T(8,128)(2,1)}, bf16[2,1024,256]{2,1,0:T(8,128)(2,1)}, u32[]{:S(2)}, u32[]{:S(2)}) %collective-permute-start.7) | collective-permute-done | bytes 1048608 | tf_op jit(solution)/shard_map/ppermute | solution.py:35
  100.1 4.6 %combine_0_3_0.1 = bf16[8,256,256]{2,1,0:T(8,128)(2,1)} custom-call(s32[13]{0:T(128)S(1)} %get-tuple-element.72.where, s32[64]{0:T(128)S(1)} %reshape.74.refs_0_, bf16[8,4,272,256]{3,2,1,0:T(8,128)(2,1)} %all-to-all-done.refs_1_, bf16[2,2048,256]{2,1,0:T(8,128)(2,1)S(1)} %bitcast.19, ...), custom_call_target="tpu_custom_call", output_to_operand_aliasing={{}: (7, {})} | custom-call | flops 1 | bytes 1 | tf_op jit(solution)/shard_map/combine_0_3_0/pallas_call | solution.py:181
  104.8 0.5 collective-permute-start.9
  105.3 3.0 %collective-permute-start.11 = (bf16[8,1,272,256]{3,2,1,0:T(8,128)(2,1)}, bf16[8,1,272,256]{3,2,1,0:T(8,128)(2,1)}, u32[]{:S(2)}, u32[]{:S(2)}) collective-permute-start(bf16[8,1,272,256]{3,2,1,0:T(8,128)(2,1)} %constant_dynamic-slice_fusion), channel_id=1, source_target_pairs={{0,4},{2,6},{4,0},{6,2},{1,5},{3,7},{5,1},{7,3},{8,12},{10,14},{12... | collective-permute-start | bytes 3342344 | tf_op jit(solution)/shard_map/ppermute | solution.py:35
  108.4 0.7 collective-permute-start.12
  109.0 2.6 %collective-permute-start.13 = (bf16[2,1024,256]{2,1,0:T(8,128)(2,1)}, bf16[2,1024,256]{2,1,0:T(8,128)(2,1)}, u32[]{:S(2)}, u32[]{:S(2)}) collective-permute-start(bf16[2,1024,256]{2,1,0:T(8,128)(2,1)} %slice.47), channel_id=1, source_target_pairs={{0,6},{2,0},{4,2},{6,4},{1,7},{3,1},{5,3},{7,5},{8,14},{10,8},{12,... | collective-permute-start | bytes 3145736 | tf_op jit(solution)/shard_map/ppermute | solution.py:35
  111.6 4.4 %all-to-all-start.1 = ((bf16[8,256,256]{2,1,0:T(8,128)(2,1)}), bf16[8,256,256]{2,1,0:T(8,128)(2,1)}, u32[]{:S(2)}, u32[]{:S(2)}) async-start(bf16[8,256,256]{2,1,0:T(8,128)(2,1)} %combine_0_3_0.1), calls=%async_computation.1 | async-start | bytes 2097152 | tf_op jit(solution)/shard_map/all_to_all | solution.py:31
  116.1 0.9 convert_reduce_fusion.2
  117.1 0.3 copy-done.9
  117.3 17.9 %combine_1_0_0.1 = bf16[16,256,256]{2,1,0:T(8,128)(2,1)S(1)} custom-call(s32[13]{0:T(128)S(1)} %get-tuple-element.72.where, s32[16]{0:T(128)S(1)} %reshape.75.refs_0_, s32[16]{0:T(128)S(1)} %reshape.76.refs_1_, bf16[8,1,272,256]{3,2,1,0:T(8,128)(2,1)} %collective-permute-done.5.refs_2_, bf16[8,1,272,256]{3,2,1,0:T(8,128)(2,1)} %collective-permute-done.6.refs_3_, ...), custom_call_target="tpu_custom_call" | custom-call | flops 999999995904 | bytes 1 | tf_op jit(solution)/shard_map/combine_1_0_0/pallas_call | solution.py:181
  135.3 1.3 copy-done.2
  136.6 4.4 %all-to-all-start.2 = ((bf16[16,256,256]{2,1,0:T(8,128)(2,1)}), bf16[16,256,256]{2,1,0:T(8,128)(2,1)S(1)}, u32[]{:S(2)}, u32[]{:S(2)}) async-start(bf16[16,256,256]{2,1,0:T(8,128)(2,1)} %copy-done.2), calls=%async_computation.2 | async-start | bytes 4194304 | tf_op jit(solution)/shard_map/all_to_all | solution.py:31
  141.0 15.2 %collective-permute-done.12.refs_2_ = bf16[2,1024,256]{2,1,0:T(8,128)(2,1)} collective-permute-done((bf16[2,1024,256]{2,1,0:T(8,128)(2,1)}, bf16[2,1024,256]{2,1,0:T(8,128)(2,1)}, u32[]{:S(2)}, u32[]{:S(2)}) %collective-permute-start.12) | collective-permute-done | bytes 1048608 | tf_op jit(solution)/shard_map/ppermute | solution.py:35
  156.2 0.2 collective-permute-done.13.refs_3_
  156.4 0.5 collective-permute-start.15
  156.9 0.7 convert_reduce_fusion.1
  157.7 3.0 %collective-permute-done.14.refs_4_ = bf16[2,1024,256]{2,1,0:T(8,128)(2,1)S(1)} collective-permute-done((bf16[2,1024,256]{2,1,0:T(8,128)(2,1)}, bf16[2,1024,256]{2,1,0:T(8,128)(2,1)S(1)}, u32[]{:S(2)}, u32[]{:S(2)}) %collective-permute-start.14) | collective-permute-done | bytes 1048608 | tf_op jit(solution)/shard_map/ppermute | solution.py:35
  160.9 9.9 %combine_3_0_0.1 = bf16[8,256,256]{2,1,0:T(8,128)(2,1)} custom-call(s32[13]{0:T(128)S(1)} %get-tuple-element.72.where, s32[16]{0:T(128)S(1)} %reshape.77.refs_0_, bf16[8,1,272,256]{3,2,1,0:T(8,128)(2,1)} %collective-permute-done.11.refs_1_, bf16[2,1024,256]{2,1,0:T(8,128)(2,1)} %collective-permute-done.12.refs_2_, ...), custom_call_target="tpu_custom_call" | custom-call | flops 1 | bytes 1 | tf_op jit(solution)/shard_map/combine_3_0_0/pallas_call | solution.py:181
  170.8 4.5 %all-to-all-start.3 = ((bf16[8,256,256]{2,1,0:T(8,128)(2,1)}), bf16[8,256,256]{2,1,0:T(8,128)(2,1)S(1)}, u32[]{:S(2)}, u32[]{:S(2)}) async-start(bf16[8,256,256]{2,1,0:T(8,128)(2,1)} %combine_3_0_0.1), calls=%async_computation.3 | async-start | bytes 2097152 | tf_op jit(solution)/shard_map/all_to_all | solution.py:31
  176.0 4.5 %assemble.1 = bf16[4,4,2,256,256]{4,3,2,1,0:T(8,128)(2,1)} custom-call(s32[13]{0:T(128)S(1)} %get-tuple-element.72.where, bf16[4,2,1,256,256]{4,3,2,1,0:T(8,128)(2,1)} %bitcast.7.refs_0_, bf16[4,2,2,256,256]{4,3,2,1,0:T(8,128)(2,1)S(1)} %bitcast.20), custom_call_target="tpu_custom_call" | custom-call | flops 1 | bytes 1 | tf_op jit(solution)/shard_map/assemble/pallas_call | solution.py:221
  180.5 10.2 %all-to-all-done.3 = bf16[8,256,256]{2,1,0:T(8,128)(2,1)S(1)} async-done(((bf16[8,256,256]{2,1,0:T(8,128)(2,1)}), bf16[8,256,256]{2,1,0:T(8,128)(2,1)S(1)}, u32[]{:S(2)}, u32[]{:S(2)}) %all-to-all-start.3) | async-done | bytes 1048608 | tf_op jit(solution)/shard_map/all_to_all | solution.py:31
  190.7 1.0 constant_dynamic-update-slice_fusion
  (36 shorter events, 0.7 us)
Async XLA Ops:
  0.0 2.2 %copy-start.1 = (bf16[32,256,256]{2,1,0:T(8,128)(2,1)S(1)}, bf16[32,256,256]{2,1,0:T(8,128)(2,1)}, u32[]{:S(2)}) copy-start(bf16[32,256,256]{2,1,0:T(8,128)(2,1)} %param.8) | copy-start | bytes 12582916
  2.2 0.7 copy-start.3
  2.8 0.7 copy-start.4
  5.2 2.1 %copy-start = (bf16[8,4,272,256]{3,2,1,0:T(8,128)(2,1)}, bf16[8,4,272,256]{3,2,1,0:T(8,128)(2,1)S(1)}, u32[]{:S(2)}) copy-start(bf16[8,4,272,256]{3,2,1,0:T(8,128)(2,1)S(1)} %pack.1) | copy-start | bytes 13369348
  7.2 4.7 %copy-start.5 = (bf16[2,8,256,256]{3,2,1,0:T(8,128)(2,1)S(1)}, bf16[2,8,256,256]{3,2,1,0:T(8,128)(2,1)}, u32[]{:S(2)}) copy-start(bf16[2,8,256,256]{3,2,1,0:T(8,128)(2,1)} %param.13) | copy-start | bytes 6291460
  7.2 4.7 %copy-start.7 = (s32[2]{0:T(128)S(1)}, s32[2]{0:T(128)}, u32[]{:S(2)}) copy-start(s32[2]{0:T(128)} %param.14) | copy-start | bytes 28
  7.2 62.2 %all-to-all-start = ((bf16[8,4,272,256]{3,2,1,0:T(8,128)(2,1)}), bf16[8,4,272,256]{3,2,1,0:T(8,128)(2,1)}, u32[]{:S(2)}, u32[]{:S(2)}) async-start(bf16[8,4,272,256]{3,2,1,0:T(8,128)(2,1)} %copy-done), calls=%async_computation | async-start | bytes 8912896 | tf_op jit(solution)/shard_map/all_to_all | solution.py:31
  12.0 6.3 %copy-start.6 = (bf16[2,8,256,256]{3,2,1,0:T(8,128)(2,1)S(1)}, bf16[2,8,256,256]{3,2,1,0:T(8,128)(2,1)}, u32[]{:S(2)}) copy-start(bf16[2,8,256,256]{3,2,1,0:T(8,128)(2,1)} %param.11) | copy-start | bytes 6291460
  12.0 6.3 %copy-start.8 = (s32[2]{0:T(128)S(1)}, s32[2]{0:T(128)}, u32[]{:S(2)}) copy-start(s32[2]{0:T(128)} %param.12) | copy-start | bytes 28
  14.2 50.6 %collective-permute-start = (bf16[2,2048,256]{2,1,0:T(8,128)(2,1)}, bf16[2,2048,256]{2,1,0:T(8,128)(2,1)}, u32[]{:S(2)}, u32[]{:S(2)}) collective-permute-start(bf16[2,2048,256]{2,1,0:T(8,128)(2,1)} %bitcast.2.refs_4_.refs_8_.refs_6_), channel_id=1, source_target_pairs={{0,8},{8,16},{16,24},{24,0},{1,9},{9,17},{17,25},{25,1},{2,10},{10... | collective-permute-start | bytes 6291464 | tf_op jit(solution)/shard_map/ppermute | solution.py:35
  16.2 51.0 %collective-permute-start.1 = (bf16[2,2048,256]{2,1,0:T(8,128)(2,1)}, bf16[2,2048,256]{2,1,0:T(8,128)(2,1)}, u32[]{:S(2)}, u32[]{:S(2)}) collective-permute-start(bf16[2,2048,256]{2,1,0:T(8,128)(2,1)} %bitcast.2.refs_4_.refs_8_.refs_6_), channel_id=1, source_target_pairs={{0,24},{8,0},{16,8},{24,16},{1,25},{9,1},{17,9},{25,17},{2,26},{10... | collective-permute-start | bytes 6291464 | tf_op jit(solution)/shard_map/ppermute | solution.py:35
  19.2 50.2 %collective-permute-start.2 = (bf16[2,2048,256]{2,1,0:T(8,128)(2,1)S(1)}, bf16[2,2048,256]{2,1,0:T(8,128)(2,1)}, u32[]{:S(2)}, u32[]{:S(2)}) collective-permute-start(bf16[2,2048,256]{2,1,0:T(8,128)(2,1)S(1)} %bitcast.15), channel_id=1, source_target_pairs={{0,2},{2,4},{4,6},{6,0},{1,3},{3,5},{5,7},{7,1},{8,10},{10,12},{12... | collective-permute-start | bytes 6291464 | tf_op jit(solution)/shard_map/ppermute | solution.py:35
  20.8 48.7 %collective-permute-start.3 = (bf16[2,2048,256]{2,1,0:T(8,128)(2,1)S(1)}, bf16[2,2048,256]{2,1,0:T(8,128)(2,1)}, u32[]{:S(2)}, u32[]{:S(2)}) collective-permute-start(bf16[2,2048,256]{2,1,0:T(8,128)(2,1)S(1)} %bitcast.16), channel_id=1, source_target_pairs={{0,6},{2,0},{4,2},{6,4},{1,7},{3,1},{5,3},{7,5},{8,14},{10,8},{12,... | collective-permute-start | bytes 6291464 | tf_op jit(solution)/shard_map/ppermute | solution.py:35
  22.5 46.9 %collective-permute-start.4 = (bf16[2,2048,256]{2,1,0:T(8,128)(2,1)S(1)}, bf16[2,2048,256]{2,1,0:T(8,128)(2,1)}, u32[]{:S(2)}, u32[]{:S(2)}) collective-permute-start(bf16[2,2048,256]{2,1,0:T(8,128)(2,1)S(1)} %bitcast.17), channel_id=1, source_target_pairs={{0,1},{1,0},{2,3},{3,2},{4,5},{5,4},{6,7},{7,6},{8,9},{9,8},{10,11... | collective-permute-start | bytes 6291464 | tf_op jit(solution)/shard_map/ppermute | solution.py:35
  73.7 26.5 %collective-permute-start.7 = (bf16[2,1024,256]{2,1,0:T(8,128)(2,1)}, bf16[2,1024,256]{2,1,0:T(8,128)(2,1)}, u32[]{:S(2)}, u32[]{:S(2)}) collective-permute-start(bf16[2,1024,256]{2,1,0:T(8,128)(2,1)} %slice.52), channel_id=1, source_target_pairs={{0,8},{8,16},{16,24},{24,0},{1,9},{9,17},{17,25},{25,1},{2,10},{10... | collective-permute-start | bytes 3145736 | tf_op jit(solution)/shard_map/ppermute | solution.py:35
  73.7 26.4 %collective-permute-start.8 = (bf16[2,1024,256]{2,1,0:T(8,128)(2,1)}, bf16[2,1024,256]{2,1,0:T(8,128)(2,1)}, u32[]{:S(2)}, u32[]{:S(2)}) collective-permute-start(bf16[2,1024,256]{2,1,0:T(8,128)(2,1)} %slice.53), channel_id=1, source_target_pairs={{0,24},{8,0},{16,8},{24,16},{1,25},{9,1},{17,9},{25,17},{2,26},{10... | collective-permute-start | bytes 3145736 | tf_op jit(solution)/shard_map/ppermute | solution.py:35
  77.0 27.8 %collective-permute-start.5 = (bf16[8,1,272,256]{3,2,1,0:T(8,128)(2,1)}, bf16[8,1,272,256]{3,2,1,0:T(8,128)(2,1)}, u32[]{:S(2)}, u32[]{:S(2)}) collective-permute-start(bf16[8,1,272,256]{3,2,1,0:T(8,128)(2,1)} %get-tuple-element.47), channel_id=1, source_target_pairs={{0,2},{2,4},{4,6},{6,0},{1,3},{3,5},{5,7},{7,1},{8,10},{10,12},{12... | collective-permute-start | bytes 3342344 | tf_op jit(solution)/shard_map/ppermute | solution.py:35
  78.5 26.3 %collective-permute-start.6 = (bf16[8,1,272,256]{3,2,1,0:T(8,128)(2,1)}, bf16[8,1,272,256]{3,2,1,0:T(8,128)(2,1)}, u32[]{:S(2)}, u32[]{:S(2)}) collective-permute-start(bf16[8,1,272,256]{3,2,1,0:T(8,128)(2,1)} %get-tuple-element.48), channel_id=1, source_target_pairs={{0,6},{2,0},{4,2},{6,4},{1,7},{3,1},{5,3},{7,5},{8,14},{10,8},{12,... | collective-permute-start | bytes 3342344 | tf_op jit(solution)/shard_map/ppermute | solution.py:35
  104.8 11.3 %collective-permute-start.10 = (bf16[2,2048,256]{2,1,0:T(8,128)(2,1)}, bf16[2,2048,256]{2,1,0:T(8,128)(2,1)S(1)}, u32[]{:S(2)}, u32[]{:S(2)}) collective-permute-start(bf16[2,2048,256]{2,1,0:T(8,128)(2,1)} %collective-permute-done.3.refs_6_), channel_id=1, source_target_pairs={{0,1},{1,0},{2,3},{3,2},{4,5},{5,4},{6,7},{7,6},{8,9},{9,8},{10,11... | collective-permute-start | bytes 6291464 | tf_op jit(solution)/shard_map/ppermute | solution.py:35
  104.8 11.2 %collective-permute-start.9 = (bf16[2,2048,256]{2,1,0:T(8,128)(2,1)}, bf16[2,2048,256]{2,1,0:T(8,128)(2,1)}, u32[]{:S(2)}, u32[]{:S(2)}) collective-permute-start(bf16[2,2048,256]{2,1,0:T(8,128)(2,1)} %collective-permute-done.2.refs_4_), channel_id=1, source_target_pairs={{0,1},{1,0},{2,3},{3,2},{4,5},{5,4},{6,7},{7,6},{8,9},{9,8},{10,11... | collective-permute-start | bytes 6291464 | tf_op jit(solution)/shard_map/ppermute | solution.py:35
  105.3 51.1 %collective-permute-start.11 = (bf16[8,1,272,256]{3,2,1,0:T(8,128)(2,1)}, bf16[8,1,272,256]{3,2,1,0:T(8,128)(2,1)}, u32[]{:S(2)}, u32[]{:S(2)}) collective-permute-start(bf16[8,1,272,256]{3,2,1,0:T(8,128)(2,1)} %constant_dynamic-slice_fusion), channel_id=1, source_target_pairs={{0,4},{2,6},{4,0},{6,2},{1,5},{3,7},{5,1},{7,3},{8,12},{10,14},{12... | collective-permute-start | bytes 3342344 | tf_op jit(solution)/shard_map/ppermute | solution.py:35
  108.4 47.8 %collective-permute-start.12 = (bf16[2,1024,256]{2,1,0:T(8,128)(2,1)}, bf16[2,1024,256]{2,1,0:T(8,128)(2,1)}, u32[]{:S(2)}, u32[]{:S(2)}) collective-permute-start(bf16[2,1024,256]{2,1,0:T(8,128)(2,1)} %slice.46), channel_id=1, source_target_pairs={{0,2},{2,4},{4,6},{6,0},{1,3},{3,5},{5,7},{7,1},{8,10},{10,12},{12... | collective-permute-start | bytes 3145736 | tf_op jit(solution)/shard_map/ppermute | solution.py:35
  109.0 47.4 %collective-permute-start.13 = (bf16[2,1024,256]{2,1,0:T(8,128)(2,1)}, bf16[2,1024,256]{2,1,0:T(8,128)(2,1)}, u32[]{:S(2)}, u32[]{:S(2)}) collective-permute-start(bf16[2,1024,256]{2,1,0:T(8,128)(2,1)} %slice.47), channel_id=1, source_target_pairs={{0,6},{2,0},{4,2},{6,4},{1,7},{3,1},{5,3},{7,5},{8,14},{10,8},{12,... | collective-permute-start | bytes 3145736 | tf_op jit(solution)/shard_map/ppermute | solution.py:35
  111.6 25.0 %all-to-all-start.1 = ((bf16[8,256,256]{2,1,0:T(8,128)(2,1)}), bf16[8,256,256]{2,1,0:T(8,128)(2,1)}, u32[]{:S(2)}, u32[]{:S(2)}) async-start(bf16[8,256,256]{2,1,0:T(8,128)(2,1)} %combine_0_3_0.1), calls=%async_computation.1 | async-start | bytes 2097152 | tf_op jit(solution)/shard_map/all_to_all | solution.py:31
  116.0 1.3 copy-start.9
  135.3 1.3 copy-start.2
  136.6 34.2 %all-to-all-start.2 = ((bf16[16,256,256]{2,1,0:T(8,128)(2,1)}), bf16[16,256,256]{2,1,0:T(8,128)(2,1)S(1)}, u32[]{:S(2)}, u32[]{:S(2)}) async-start(bf16[16,256,256]{2,1,0:T(8,128)(2,1)} %copy-done.2), calls=%async_computation.2 | async-start | bytes 4194304 | tf_op jit(solution)/shard_map/all_to_all | solution.py:31
  156.4 4.3 %collective-permute-start.14 = (bf16[2,1024,256]{2,1,0:T(8,128)(2,1)}, bf16[2,1024,256]{2,1,0:T(8,128)(2,1)S(1)}, u32[]{:S(2)}, u32[]{:S(2)}) collective-permute-start(bf16[2,1024,256]{2,1,0:T(8,128)(2,1)} %collective-permute-done.12.refs_2_), channel_id=1, source_target_pairs={{0,1},{1,0},{2,3},{3,2},{4,5},{5,4},{6,7},{7,6},{8,9},{9,8},{10,11... | collective-permute-start | bytes 3145736 | tf_op jit(solution)/shard_map/ppermute | solution.py:35
  156.4 4.5 %collective-permute-start.15 = (bf16[2,1024,256]{2,1,0:T(8,128)(2,1)}, bf16[2,1024,256]{2,1,0:T(8,128)(2,1)}, u32[]{:S(2)}, u32[]{:S(2)}) collective-permute-start(bf16[2,1024,256]{2,1,0:T(8,128)(2,1)} %collective-permute-done.13.refs_3_), channel_id=1, source_target_pairs={{0,1},{1,0},{2,3},{3,2},{4,5},{5,4},{6,7},{7,6},{8,9},{9,8},{10,11... | collective-permute-start | bytes 3145736 | tf_op jit(solution)/shard_map/ppermute | solution.py:35
  170.8 19.9 %all-to-all-start.3 = ((bf16[8,256,256]{2,1,0:T(8,128)(2,1)}), bf16[8,256,256]{2,1,0:T(8,128)(2,1)S(1)}, u32[]{:S(2)}, u32[]{:S(2)}) async-start(bf16[8,256,256]{2,1,0:T(8,128)(2,1)} %combine_3_0_0.1), calls=%async_computation.3 | async-start | bytes 2097152 | tf_op jit(solution)/shard_map/all_to_all | solution.py:31
